TPU v7x, 128 devices: a whole 4x4x4 slice. The times are simulated.
128 devices in a mesh: row: 8 (over x_lo, y), col: 16 (over x_hi, z, core).
Axes of the slice: x: 4 (x_hi: 2, x_lo: 2; x = x_hi * 2 + x_lo), y: 4, z: 4, core: 2. Of those that a mesh axis runs over, the one named last changes fastest.
Arguments:
- vectors: float32 [65536, 2048], P('row', 'col'), may hold values from -6 to 6
- panel_one: float32 [65536, 256], P('row', 'col'), may hold values from -100 to 100
- panel_two: float32 [65536, 256], P('row', 'col'), may hold values from -100 to 100
Outputs:
- rotated: float32 [65536, 2048], P('row', 'col')
All inputs are finite; a program needn't handle non-finite values.
Results may differ from a plain program's by a relative error of at most 0.000092.
Values sent between devices are 32-bit elements; how exact they have to be, the bound alone decides.
No kernel may reach another device: no remote copies, remote signals or barrier semaphores. Data moves between devices by JAX's collectives and lax.ppermute only.
A program may use at most 192 MiB of HBM per device.

v0:
```python
import jax
import jax.numpy as jnp
from jax import lax
from jax.sharding import PartitionSpec as P


def inner_rows(left, right):
    return lax.dot_general(left, right, (((0,), (0,)), ((), ())), precision=lax.Precision.HIGHEST)


def times_rows(left, right):
    return jnp.dot(left, right, precision=lax.Precision.HIGHEST)


def triangle(gramian):
    eye_mask = jnp.eye(gramian.shape[0], dtype=jnp.float32)
    return jnp.triu(gramian, 1) + gramian * eye_mask * 0.5


def invert_upper(factor):
    order = factor.shape[0]
    eye_mask = jnp.eye(order, dtype=jnp.float32)
    diag_values = jnp.sum(factor * eye_mask, axis=1)
    blocks = (1.0 / diag_values).reshape(order, 1, 1)
    width = 1
    while width < order:
        count = order // (2 * width)
        tiled = factor.reshape(count, 2 * width, count, 2 * width)
        picker = jnp.eye(count, dtype=jnp.float32)
        diag_blocks = jnp.einsum("aibj,ab->aij", tiled, picker, precision=lax.Precision.HIGHEST)
        upper_part = diag_blocks[:, :width, width:]
        first_inv = blocks[0::2]
        second_inv = blocks[1::2]
        coupled = jnp.einsum("aij,ajk->aik", first_inv, upper_part, precision=lax.Precision.HIGHEST)
        coupled = -jnp.einsum("aij,ajk->aik", coupled, second_inv, precision=lax.Precision.HIGHEST)
        zero_part = jnp.zeros((count, width, width), jnp.float32)
        top_half = jnp.concatenate([first_inv, coupled], axis=2)
        low_half = jnp.concatenate([zero_part, second_inv], axis=2)
        blocks = jnp.concatenate([top_half, low_half], axis=1)
        width = 2 * width
    return blocks[0]


def solve_upper(factor, right_side):
    return times_rows(invert_upper(factor), right_side)


def reduce_all(partials):
    totals = lax.psum(partials, "row")
    return totals


def apply_panel(current, mirror):
    gramian, projection = reduce_all((inner_rows(mirror, mirror), inner_rows(mirror, current)))
    solved = solve_upper(triangle(gramian), projection)
    return current - times_rows(mirror, solved)


def per_device(vectors, panel_one, panel_two):
    mirror_one, mirror_two = (
        lax.all_gather(panel_one, "col", axis=1, tiled=True),
        lax.all_gather(panel_two, "col", axis=1, tiled=True),
    )
    middle = apply_panel(vectors, mirror_two)
    result = apply_panel(middle, mirror_one)
    return result


def solution(mesh):
    in_specs = (P("row", "col"), P("row", "col"), P("row", "col"))
    out_specs = P("row", "col")
    return jax.shard_map(
        per_device, mesh=mesh, in_specs=in_specs, out_specs=out_specs, check_vma=False
    )
```

profile of v0, /device:TPU:0, one launch (start us, length us, event | category | flops | bytes accessed | tf_op | source)
XLA Modules:
  0.0 471.5 jit_solution(9876713803105695559)
XLA Ops:
  6.5 0.7 all-gather.3.cloned.1.call-update
  7.3 0.7 all-gather.5.cloned.1.call-update
  8.1 5.6 %copy.67 = f32[8192,128]{0,1:T(8,128)} copy(f32[8192,128]{1,0:T(8,128)} %param.3) | data formatting | bytes 8388608 | tf_op args[0]
  13.7 71.7 %all-gather.3.cloned.1.call-done = f32[8192,256]{0,1:T(8,128)} async-done(((f32[8192,16]{0,1:T(8,128)}), f32[8192,256]{0,1:T(8,128)}) %all-gather.3.cloned.1.call-update) | async-done | bytes 8388624 | tf_op jit(solution)/shard_map/all_gather | solution.py:62
  85.5 10.6 %fusion.135 = f32[256,128]{1,0:T(8,128)} fusion(f32[8192,256]{0,1:T(8,128)} %all-gather.3.cloned.1.call-done, f32[8192,128]{1,0:T(8,128)} %param.3), kind=kOutput, calls=%fused_computation.193 | convolution fusion | flops 3221225472 | bytes 12713984 | tf_op jit(solution)/shard_map/dot_general | solution.py:8
  96.0 7.6 %fusion.134 = f32[256,256]{1,0:T(8,128)} fusion(f32[8192,256]{0,1:T(8,128)S(1)} %copy-done), kind=kOutput, calls=%fused_computation.192 | convolution fusion | flops 6442450944 | bytes 8650752 | tf_op jit(solution)/shard_map/dot_general | solution.py:8
  103.6 0.3 all-reduce.21.cloned.1.call-start
  103.9 54.9 %all-gather.5.cloned.1.call-done = f32[8192,256]{0,1:T(8,128)} async-done(((f32[8192,16]{0,1:T(8,128)}), f32[8192,256]{0,1:T(8,128)}) %all-gather.5.cloned.1.call-update) | async-done | bytes 8388624 | tf_op jit(solution)/shard_map/all_gather | solution.py:61
  158.8 11.3 %fusion.136 = f32[256,256]{1,0:T(8,128)} fusion(f32[8192,256]{0,1:T(8,128)} %all-gather.5.cloned.1.call-done), kind=kOutput, calls=%fused_computation.194 | convolution fusion | flops 6442450944 | bytes 8650752 | tf_op jit(solution)/shard_map/dot_general | solution.py:8
  170.0 63.5 %all-reduce.23.cloned.1.call-done = (f32[256,128]{1,0:T(8,128)}, f32[256,256]{1,0:T(8,128)}) async-done(((f32[256,128]{1,0:T(8,128)}, f32[256,256]{1,0:T(8,128)}), (f32[256,128]{1,0:T(8,128)}, f32[256,256]{1,0:T(8,128)})) %all-reduce.23.cloned.1.call-update) | async-done | bytes 393232 | tf_op jit(solution)/shard_map/psum | solution.py:49
  233.5 1.7 fusion.120
  235.7 18.1 %reshape.124 = f32[128,2,128,2]{3,2,1,0:T(8,128)} reshape(f32[256,256]{1,0:T(8,128)S(1)} %get-tuple-element.14) | data formatting | bytes 524288 | tf_op jit(solution)/shard_map/reshape | solution.py:28
  253.8 8.9 %fusion.20 = f32[128,1,2,2]{3,1,2,0:T(1,128)S(1)} fusion(f32[128,2,128,2]{3,2,1,0:T(8,128)} %reshape.124, pred[128,128,1,1]{1,0,2,3:T(32,128)(4,1)S(1)} %fusion.60), kind=kOutput, calls=%fused_computation.44 | convolution fusion | flops 786432 | bytes 280576 | tf_op jit(solution)/shard_map/aibj,ab->aij/dot_general | solution.py:30
  263.1 10.1 %reshape.125 = f32[64,4,64,4]{3,2,1,0:T(8,128)} reshape(f32[256,256]{1,0:T(8,128)S(1)} %get-tuple-element.14) | data formatting | bytes 524288 | tf_op jit(solution)/shard_map/reshape | solution.py:28
  273.2 4.1 reshape.126
  277.4 0.6 reshape.127
  278.0 0.3 reshape.128
  278.3 1.1 reshape.129
  279.3 0.8 reshape.130
  280.4 6.3 %fusion.28 = f32[64,1,4,4]{3,1,2,0:T(1,128)S(1)} fusion(f32[64,4,64,4]{3,2,1,0:T(8,128)} %reshape.125, pred[64,64,1,1]{1,0,2,3:T(32,128)(4,1)S(1)} %fusion.65), kind=kOutput, calls=%fused_computation.70 | convolution fusion | flops 786432 | bytes 270336 | tf_op jit(solution)/shard_map/aibj,ab->aij/dot_general | solution.py:30
  286.8 0.6 fusion.58
  287.4 0.6 convolution_negate_fusion.13
  288.3 1.5 fusion.63
  289.8 0.4 fusion.50
  290.2 0.4 convolution_negate_fusion.12
  290.7 0.8 fusion.68
  291.5 0.3 fusion.48
  292.2 0.6 fusion.73
  292.8 0.3 fusion.46
  293.4 0.6 fusion.78
  294.1 0.3 fusion.44
  294.7 0.6 fusion.83
  295.3 0.3 fusion.42
  295.9 1.2 fusion.41
  297.3 0.5 fusion.9
  297.9 5.4 %fusion.1 = f32[8192,128]{0,1:T(8,128)S(1)} fusion(f32[8192,128]{0,1:T(8,128)S(1)} %copy-done.5, f32[256,128]{1,0:T(8,128)S(1)} %fusion.9, f32[8192,256]{0,1:T(8,128)S(1)} %bitcast.135), kind=kOutput, calls=%fused_computation.3 | convolution fusion | flops 3222274048 | bytes 16908288 | tf_op jit(solution)/shard_map/dot_general | solution.py:12
  303.4 2.0 copy-done.1
  305.4 9.1 %convolution_bitcast_fusion.2 = f32[256,128]{0,1:T(8,128)} fusion(f32[8192,128]{0,1:T(8,128)S(1)} %fusion.1, f32[8192,256]{0,1:T(8,128)S(1)} %bitcast.131), kind=kOutput, calls=%fused_computation.4 | convolution fusion | flops 3221225472 | bytes 12713984 | tf_op jit(solution)/shard_map/dot_general | solution.py:8
  314.5 74.2 %all-reduce.21.cloned.1.call-done = (f32[256,128]{0,1:T(8,128)}, f32[256,256]{1,0:T(8,128)}) async-done(((f32[256,128]{0,1:T(8,128)}, f32[256,256]{1,0:T(8,128)}), (f32[256,128]{0,1:T(8,128)}, f32[256,256]{1,0:T(8,128)})) %all-reduce.21.cloned.1.call-update) | async-done | bytes 393232 | tf_op jit(solution)/shard_map/psum | solution.py:49
  388.7 1.7 fusion.121
  390.9 18.1 %reshape.134 = f32[128,2,128,2]{3,2,1,0:T(8,128)} reshape(f32[256,256]{1,0:T(8,128)S(1)} %get-tuple-element.11) | data formatting | bytes 524288 | tf_op jit(solution)/shard_map/reshape | solution.py:28
  409.0 8.9 %fusion.18 = f32[128,1,2,2]{3,1,2,0:T(1,128)S(1)} fusion(f32[128,2,128,2]{3,2,1,0:T(8,128)} %reshape.134, pred[128,128,1,1]{1,0,2,3:T(32,128)(4,1)S(1)} %fusion.60), kind=kOutput, calls=%fused_computation.42 | convolution fusion | flops 786432 | bytes 280576 | tf_op jit(solution)/shard_map/aibj,ab->aij/dot_general | solution.py:30
  418.4 10.1 %reshape.135 = f32[64,4,64,4]{3,2,1,0:T(8,128)} reshape(f32[256,256]{1,0:T(8,128)S(1)} %get-tuple-element.11) | data formatting | bytes 524288 | tf_op jit(solution)/shard_map/reshape | solution.py:28
  428.4 3.9 reshape.136
  432.3 0.6 reshape.137
  433.0 0.3 reshape.138
  433.2 1.1 reshape.139
  434.3 0.8 reshape.140
  435.4 6.3 %fusion.26 = f32[64,1,4,4]{3,1,2,0:T(1,128)S(1)} fusion(f32[64,4,64,4]{3,2,1,0:T(8,128)} %reshape.135, pred[64,64,1,1]{1,0,2,3:T(32,128)(4,1)S(1)} %fusion.65), kind=kOutput, calls=%fused_computation.68 | convolution fusion | flops 786432 | bytes 270336 | tf_op jit(solution)/shard_map/aibj,ab->aij/dot_general | solution.py:30
  441.8 0.6 fusion.56
  442.4 0.6 convolution_negate_fusion.6
  443.2 1.5 fusion.61
  444.7 0.4 fusion.39
  445.1 0.4 convolution_negate_fusion.5
  445.7 0.8 fusion.66
  446.5 0.3 fusion.37
  447.2 0.6 fusion.71
  448.4 0.6 fusion.76
  449.6 0.6 fusion.81
  450.3 0.3 fusion.31
  450.9 1.0 fusion.30
  452.1 0.6 fusion.5
  452.8 6.2 %fusion = f32[8192,128]{0,1:T(8,128)} fusion(f32[8192,128]{0,1:T(8,128)S(1)} %copy-done.2, f32[256,128]{1,0:T(8,128)S(1)} %fusion.5, f32[8192,256]{0,1:T(8,128)S(1)} %bitcast.133), kind=kOutput, calls=%fused_computation.1 | convolution fusion | flops 3222274048 | bytes 16908288 | tf_op jit(solution)/shard_map/dot_general | solution.py:12
  459.0 5.6 %copy.71 = f32[8192,128]{1,0:T(8,128)} copy(f32[8192,128]{0,1:T(8,128)} %fusion) | data formatting | bytes 8388608 | tf_op jit(solution)/shard_map/sub | solution.py:56
  (106 shorter events, 6.7 us)
Async XLA Ops:
  6.5 78.9 %all-gather.3.cloned.1.call-start = ((), (), s32[]{:S(2)}) async-start(), calls=%async_computation | async-start | bytes 8912896 | tf_op jit(solution)/shard_map/all_gather | solution.py:62
  7.3 151.5 %all-gather.5.cloned.1.call-start = ((), (), s32[]{:S(2)}) async-start(), calls=%async_computation.1 | async-start | bytes 8912896 | tf_op jit(solution)/shard_map/all_gather | solution.py:61
  8.0 225.5 %all-reduce.23.cloned.1.call-start = ((), (), s32[]{:S(2)}) async-start(), calls=%async_computation.3 | async-start | bytes 786432 | tf_op jit(solution)/shard_map/psum | solution.py:49
  85.4 10.6 %copy-start = (f32[8192,256]{0,1:T(8,128)S(1)}, f32[8192,256]{0,1:T(8,128)}, u32[]{:S(2)}) copy-start(f32[8192,256]{0,1:T(8,128)} %all-gather.3.cloned.1.call-done) | copy-start | bytes 25165828
  103.6 285.1 %all-reduce.21.cloned.1.call-start = ((), (), s32[]{:S(2)}) async-start(), calls=%async_computation.2 | async-start | bytes 786432 | tf_op jit(solution)/shard_map/psum | solution.py:49
  280.4 7.8 %copy-start.4 = (f32[32,8,32,8]{3,2,1,0:T(8,128)S(1)}, f32[32,8,32,8]{3,2,1,0:T(8,128)}, u32[]{:S(2)}) copy-start(f32[32,8,32,8]{3,2,1,0:T(8,128)} %reshape.126) | copy-start | bytes 786436
  280.4 13.0 %copy-start.7 = (f32[4,64,4,64]{3,2,1,0:T(4,128)S(1)}, f32[4,64,4,64]{3,2,1,0:T(4,128)}, u32[]{:S(2)}) copy-start(f32[4,64,4,64]{3,2,1,0:T(4,128)} %reshape.129) | copy-start | bytes 786436
  286.8 7.9 %copy-start.9 = (f32[2,128,2,128]{3,2,1,0:T(2,128)S(1)}, f32[2,128,2,128]{3,2,1,0:T(2,128)}, u32[]{:S(2)}) copy-start(f32[2,128,2,128]{3,2,1,0:T(2,128)} %reshape.130) | copy-start | bytes 786436
  286.8 10.5 %copy-start.11 = (f32[256,128]{1,0:T(8,128)S(1)}, f32[256,128]{1,0:T(8,128)}, u32[]{:S(2)}) copy-start(f32[256,128]{1,0:T(8,128)} %get-tuple-element.7) | copy-start | bytes 393220
  286.8 11.1 %slice-start.4 = ((s8[8388608]{0:T(1024)(128)(4,1)}), s8[4194304]{0:T(1024)(128)(4,1)S(1)}, s32[]{:S(2)}) async-start(s8[8388608]{0:T(1024)(128)(4,1)} %bitcast.134), calls=%async_computation.8 | async-start | bytes 8388608
  286.8 11.1 %copy-start.5 = (f32[8192,128]{0,1:T(8,128)S(1)}, f32[8192,128]{0,1:T(8,128)}, u32[]{:S(2)}) copy-start(f32[8192,128]{0,1:T(8,128)} %copy.67) | copy-start | bytes 12582916
  290.7 7.2 %slice-start.5 = ((s8[8388608]{0:T(1024)(128)(4,1)}), s8[4194304]{0:T(1024)(128)(4,1)S(1)}, s32[]{:S(2)}) async-start(s8[8388608]{0:T(1024)(128)(4,1)} %bitcast.134), calls=%async_computation.9 | async-start | bytes 8388608
  295.9 9.5 %slice-start = ((s8[8388608]{0:T(1024)(128)(4,1)}), s8[4194304]{0:T(1024)(128)(4,1)S(1)}, s32[]{:S(2)}) async-start(s8[8388608]{0:T(1024)(128)(4,1)} %bitcast.130), calls=%async_computation.4 | async-start | bytes 8388608
  297.9 7.5 %slice-start.1 = ((s8[8388608]{0:T(1024)(128)(4,1)}), s8[4194304]{0:T(1024)(128)(4,1)S(1)}, s32[]{:S(2)}) async-start(s8[8388608]{0:T(1024)(128)(4,1)} %bitcast.130), calls=%async_computation.5 | async-start | bytes 8388608
  303.3 2.0 copy-start.1
  435.4 7.8 %copy-start.3 = (f32[32,8,32,8]{3,2,1,0:T(8,128)S(1)}, f32[32,8,32,8]{3,2,1,0:T(8,128)}, u32[]{:S(2)}) copy-start(f32[32,8,32,8]{3,2,1,0:T(8,128)} %reshape.136) | copy-start | bytes 786436
  435.4 13.0 %copy-start.6 = (f32[4,64,4,64]{3,2,1,0:T(4,128)S(1)}, f32[4,64,4,64]{3,2,1,0:T(4,128)}, u32[]{:S(2)}) copy-start(f32[4,64,4,64]{3,2,1,0:T(4,128)} %reshape.139) | copy-start | bytes 786436
  441.7 7.9 %copy-start.8 = (f32[2,128,2,128]{3,2,1,0:T(2,128)S(1)}, f32[2,128,2,128]{3,2,1,0:T(2,128)}, u32[]{:S(2)}) copy-start(f32[2,128,2,128]{3,2,1,0:T(2,128)} %reshape.140) | copy-start | bytes 786436
  441.7 10.4 %copy-start.10 = (f32[256,128]{0,1:T(8,128)S(1)}, f32[256,128]{0,1:T(8,128)}, u32[]{:S(2)}) copy-start(f32[256,128]{0,1:T(8,128)} %get-tuple-element.5) | copy-start | bytes 393220
  441.8 11.0 %slice-start.2 = ((s8[8388608]{0:T(1024)(128)(4,1)}), s8[4194304]{0:T(1024)(128)(4,1)S(1)}, s32[]{:S(2)}) async-start(s8[8388608]{0:T(1024)(128)(4,1)} %bitcast.132), calls=%async_computation.6 | async-start | bytes 8388608
  441.8 11.0 %copy-start.2 = (f32[8192,128]{0,1:T(8,128)S(1)}, f32[8192,128]{0,1:T(8,128)}, u32[]{:S(2)}) copy-start(f32[8192,128]{0,1:T(8,128)} %copy-done.1) | copy-start | bytes 12582916
  445.7 7.1 %slice-start.3 = ((s8[8388608]{0:T(1024)(128)(4,1)}), s8[4194304]{0:T(1024)(128)(4,1)S(1)}, s32[]{:S(2)}) async-start(s8[8388608]{0:T(1024)(128)(4,1)} %bitcast.132), calls=%async_computation.7 | async-start | bytes 8388608
Sparse Core Ops, SparseCore 0:
  9.8 75.5 all-gather.2
  87.9 70.8 all-gather.4
  161.3 72.1 all-reduce.22
  314.6 74.0 all-reduce.20
where the time goes:
time: 480 us; the launch traced here: 472 us
  waiting for transfers between devices  266 us (55%)
  matrix products  101 us (21%)
  local copies, waits for them, and re-layouts  85.5 us (18%)
  between operations  14.4 us (3%)
  other arithmetic  5.02 us (1%)
    psum x2, waiting for transfers between devices, reduce_all(): totals = lax.psum(partials, 'row')  138 us
    all_gather x1, waiting for transfers between devices, per_device(): lax.all_gather(panel_two, 'col', axis=1, tiled=True)  71.7 us
    reshape x14, local copies, waits for them, and re-layouts, invert_upper(): tiled = factor.reshape(count, 2 * width, count, 2 * width)  69.9 us
    all_gather x1, waiting for transfers between devices, per_device(): lax.all_gather(panel_one, 'col', axis=1, tiled=True)  54.9 us
    dot_general x14, matrix products, invert_upper(): jnp.einsum('aibj,ab->aij', tiled, picker, precision=lax.Precision.HIGHEST)  38.9 us
    dot_general x4, matrix products, inner_rows(): lax.dot_general(left, right, (((0,), (0,)), ((), ())), precision=lax.Prec...  38.5 us
    dot_general x4, matrix products, times_rows(): return jnp.dot(left, right, precision=lax.Precision.HIGHEST)  12.8 us
  transfers between devices with their start and end apart: 4, of which 4 were waited for; matrix products, arithmetic and copies ran while one was open for 7% of the time, Pallas kernels for 0%

commit v1 on v0

v1 whole, which is shorter than its diff:
```python
import functools

import jax
import jax.numpy as jnp
from jax import lax
from jax.experimental import pallas as pl
from jax.experimental.pallas import tpu as pltpu
from jax.sharding import PartitionSpec as P

F32 = jnp.float32
BF16 = jnp.bfloat16
HIGHEST = lax.Precision.HIGHEST
PLANES, DEPTH, CORES = 2, 4, 2
CHIPS = PLANES * DEPTH
WIDE = 128
TILE = 512
PIECES = ((0, 0), (0, 1), (1, 1), (0, 2), (0, 3)), ((1, 2), (1, 3), (2, 2), (2, 3), (3, 3))


def split3(value):
    high = value.astype(BF16)
    rest = value - high.astype(F32)
    middle = rest.astype(BF16)
    low = (rest - middle.astype(F32)).astype(BF16)
    return high, middle, low


def nn(left, right):
    return lax.dot_general(left, right, (((1,), (0,)), ((), ())), preferred_element_type=F32)


def nt(left, right):
    return lax.dot_general(left, right, (((1,), (1,)), ((), ())), preferred_element_type=F32)


def full(left, right):
    return lax.dot_general(
        left, right, (((1,), (0,)), ((), ())), precision=HIGHEST, preferred_element_type=F32
    )


def gram_kernel(where_ref, *refs):
    steps = pl.num_programs(0)
    step = pl.program_id(0)
    whole = refs[0:4]
    early = refs[4:8]
    late = refs[8:12]
    own_ref, other_ref, out_ref, high, middle, low, even, skew, proj = refs[12:]
    core = where_ref[CHIPS]
    panel = high.shape[0] // 2
    group = whole[0].shape[0] // 4

    def place(slot, ref):
        value = ref[...]
        chip = where_ref[slot]
        for part in range(2):
            for swap in range(2):
                row = (2 * part + swap) * group
                first, second, third = split3(value[row : row + group])
                start = pl.multiple_of(
                    part * panel + chip * 2 * group + group * (core ^ swap), group
                )
                high[pl.ds(start, group), :] = first
                middle[pl.ds(start, group), :] = second
                low[pl.ds(start, group), :] = third

    for slot in range(4):
        place(slot, whole[slot])

    @pl.when(step < steps // 2)
    def _():
        for slot in range(4):
            place(4 + slot, early[slot])

    @pl.when(step >= steps // 2)
    def _():
        for slot in range(4):
            place(4 + slot, late[slot])

    @pl.when(step == 0)
    def _():
        even[...] = jnp.zeros_like(even)
        skew[...] = jnp.zeros_like(skew)
        proj[...] = jnp.zeros_like(proj)

    one, two, three = high[...], middle[...], low[...]
    even[:panel] += nt(one[:panel], one) + nt(two[:panel], two)
    even[panel:, panel:] += nt(one[panel:], one[panel:]) + nt(two[panel:], two[panel:])
    skew[...] += nt(one, two) + nt(one, three)
    current = jnp.concatenate([own_ref[...], other_ref[...]], axis=1)
    first, second, third = split3(current)
    proj[...] += (
        (nn(one, third) + nn(three, first) + nn(two, second))
        + (nn(one, second) + nn(two, first))
        + nn(one, first)
    )

    @pl.when(step == steps - 1)
    def _():
        rows = 2 * panel
        out_ref[core, 0:rows, :] = proj[:, :WIDE]
        out_ref[1 - core, 0:rows, :] = proj[:, WIDE:]
        for part in range(2):
            for place_at, (i, j) in enumerate(PIECES[part]):
                at_i, at_j = slice(i * WIDE, (i + 1) * WIDE), slice(j * WIDE, (j + 1) * WIDE)
                block = even[at_i, at_j] + (skew[at_i, at_j] + skew[at_j, at_i].T)
                start = rows + place_at * WIDE
                out_ref[part, start : start + WIDE, :] = block


def solve_kernel(where_ref, mine_ref, other_ref, own_ref, partner_ref, both):
    core = where_ref[CHIPS]
    both[core] = mine_ref[...]
    both[1 - core] = other_ref[...]
    count = 4
    size = count * WIDE
    panel = size // 2
    base = 16

    def block(i, j):
        for part in range(2):
            if (i, j) in PIECES[part]:
                start = size + PIECES[part].index((i, j)) * WIDE
                return both[part, start : start + WIDE, :]

    row = lax.broadcasted_iota(jnp.int32, (WIDE, WIDE), 0)
    column = lax.broadcasted_iota(jnp.int32, (WIDE, WIDE), 1)
    same = (row // base) == (column // base)
    diagonals = []
    for i in range(count):
        value = block(i, i)
        diagonals.append(
            jnp.where(row < column, value, jnp.where(row == column, value * 0.5, 0.0))
        )
    lane = lax.broadcasted_iota(jnp.int32, (base, WIDE), 1) % base
    ones = jnp.where(same, 1.0, 0.0).astype(F32)
    spread = []
    for i in range(count):
        flipped = jnp.where(same, diagonals[i], 0.0).T
        folded = flipped[0:base]
        for k in range(1, WIDE // base):
            folded = folded + flipped[k * base : (k + 1) * base]
        stacked = jnp.concatenate([jnp.where(lane == k, folded, 0.0) for k in range(base)], axis=0)
        spread.append(full(stacked, ones))
    wide_lane = lax.broadcasted_iota(jnp.int32, (1, size), 1) % base
    wide_row = lax.broadcasted_iota(jnp.int32, (base, size), 0)
    solved = jnp.zeros((base, size), F32)
    for i in range(base - 1, -1, -1):
        factor = jnp.concatenate([s[i * base : (i + 1) * base] for s in spread], axis=1)
        total = jnp.sum(factor * solved, axis=0, keepdims=True)
        line = (jnp.where(wide_lane == i, 1.0, 0.0) - total) / factor[i : i + 1]
        solved = jnp.where(wide_row == i, line, solved)

    big_row = lax.broadcasted_iota(jnp.int32, (panel, panel), 0)
    big_column = lax.broadcasted_iota(jnp.int32, (panel, panel), 1)
    inverses = []
    for half in range(2):
        left, right = 2 * half, 2 * half + 1
        top = jnp.concatenate([diagonals[left], block(left, right)], axis=1)
        bottom = jnp.concatenate([jnp.zeros((WIDE, WIDE), F32), diagonals[right]], axis=1)
        factor = jnp.concatenate([top, bottom], axis=0)
        lines = solved[:, half * panel : (half + 1) * panel]
        tiled = jnp.concatenate([lines] * (panel // base), axis=0)
        inverse = jnp.where((big_row // base) == (big_column // base), tiled, 0.0)
        width = base
        while width < panel:
            picked = (
                ((big_row // width) % 2 == 0) & (big_column // width == big_row // width + 1)
            )
            coupling = jnp.where(picked, factor, 0.0)
            inverse = inverse - full(full(inverse, coupling), inverse)
            width *= 2
        inverses.append(inverse)
    corner = jnp.concatenate(
        [
            jnp.concatenate([block(0, 2), block(0, 3)], axis=1),
            jnp.concatenate([block(1, 2), block(1, 3)], axis=1),
        ],
        axis=0,
    )
    right_side = jnp.concatenate([mine_ref[0:size, :], other_ref[0:size, :]], axis=1)
    second = full(inverses[1], right_side[panel:])
    first = full(inverses[0], right_side[:panel] - full(corner, second))
    own_ref[0:panel, :] = first[:, :WIDE]
    own_ref[panel:, :] = second[:, :WIDE]
    partner_ref[0:panel, :] = first[:, WIDE:]
    partner_ref[panel:, :] = second[:, WIDE:]


def apply_kernel(where_ref, *refs):
    steps = pl.num_programs(0)
    step = pl.program_id(0)
    whole = refs[0:4]
    early = refs[4:8]
    late = refs[8:12]
    current_own, current_other, solved_own, solved_other, out_own, out_other, high, middle, low = refs[12:]
    core = where_ref[CHIPS]
    panel = solved_own.shape[0] // 2
    group = whole[0].shape[0] // 4

    @pl.when(step == 0)
    def _():
        for slot in range(CHIPS):
            chip = where_ref[slot]
            for part in range(2):
                for swap in range(2):
                    start = pl.multiple_of(
                        part * panel + chip * 2 * group + group * (core ^ swap), group
                    )
                    lines = jnp.concatenate(
                        [solved_own[pl.ds(start, group), :], solved_other[pl.ds(start, group), :]],
                        axis=1,
                    )
                    first, second, third = split3(lines)
                    at = slot * 4 * group + (2 * part + swap) * group
                    high[at : at + group, :] = first
                    middle[at : at + group, :] = second
                    low[at : at + group, :] = third

    def run(refs8):
        value = jnp.concatenate([r[...] for r in refs8], axis=0)
        one, two, three = split3(value)
        first, second, third = high[...], middle[...], low[...]

        def tn(left, right):
            return lax.dot_general(
                left, right, (((0,), (0,)), ((), ())), preferred_element_type=F32
            )

        change = (
            (tn(one, third) + tn(three, first) + tn(two, second))
            + (tn(one, second) + tn(two, first))
            + tn(one, first)
        )
        out_own[...] = current_own[...] - change[:, :WIDE]
        out_other[...] = current_other[...] - change[:, WIDE:]

    @pl.when(step < steps // 2)
    def _():
        run(list(whole) + list(early))

    @pl.when(step >= steps // 2)
    def _():
        run(list(whole) + list(late))


def piece_specs(chunk, half_steps):
    whole = [pl.BlockSpec((chunk, TILE), lambda j, w: (0, j))] * 4
    early = [pl.BlockSpec((chunk, TILE), lambda j, w: (0, jnp.minimum(j, half_steps - 1)))] * 4
    late = [pl.BlockSpec((chunk, TILE), lambda j, w: (0, jnp.maximum(j - half_steps, 0)))] * 4
    return whole + early + late


def per_device(vectors, panel_one, panel_two):
    rows, columns = vectors.shape
    group = panel_one.shape[1]
    half = rows // 2
    quarter = half // 2
    chunk = 4 * group
    size = 2 * group * CHIPS * CORES
    steps = half // TILE
    at = lax.axis_index("col")
    core, depth, plane = at % CORES, (at // CORES) % DEPTH, at // (CORES * DEPTH)

    def permute(value, move):
        pairs = []
        for source in range(CHIPS * CORES):
            k, z, x = source % CORES, (source // CORES) % DEPTH, source // (CORES * DEPTH)
            k, z, x = move(k, z, x)
            pairs.append((source, (x * DEPTH + z % DEPTH) * CORES + k))
        return lax.ppermute(value, "col", pairs)

    def core_swap(value):
        return permute(value, lambda k, z, x: (1 - k, z, x))

    def up(value):
        return permute(value, lambda k, z, x: (k, z + 1, x))

    def down(value):
        return permute(value, lambda k, z, x: (k, z - 1, x))

    def across(value):
        return permute(value, lambda k, z, x: (k, z, 1 - x))

    flat = jnp.stack([panel_one.T, panel_two.T])
    keep = lax.dynamic_slice_in_dim(flat, core * half, half, 2)
    give = lax.dynamic_slice_in_dim(flat, (1 - core) * half, half, 2)
    got = core_swap(give)
    chunk_own = jnp.stack([keep, got], axis=1).reshape(chunk, half)

    away = across(chunk_own)
    below = up(chunk_own)
    above = down(chunk_own)
    far_late = down(above[:, quarter:])
    away_below_early = up(away[:, :quarter])
    far_early = up(below[:, :quarter])
    away_above_early = down(away[:, :quarter])
    away_below_late = across(below[:, quarter:])
    away_above_late = across(above[:, quarter:])
    away_far_late = across(far_late)
    away_far_early = up(away_below_early)

    pieces = (
        chunk_own, below, above, away,
        far_early, away_below_early, away_above_early, away_far_early,
        far_late, away_below_late, away_above_late, away_far_late,
    )
    chips = []
    for x_step, z_step in ((0, 0), (0, -1), (0, 1), (1, 0), (0, 2), (1, -1), (1, 1), (1, 2)):
        chips.append(jnp.bitwise_xor(plane, x_step) * DEPTH + (depth + z_step) % DEPTH)
    where = jnp.stack(chips + [core]).astype(jnp.int32)

    given = lax.dynamic_slice_in_dim(vectors, (1 - core) * half, half, 0)
    other = core_swap(given)

    piece_in = piece_specs(chunk, steps // 2)
    own_spec = pl.BlockSpec((TILE, columns), lambda j, w: (w[CHIPS] * steps + j, 0))
    other_spec = pl.BlockSpec((TILE, columns), lambda j, w: (j, 0))
    length = size + 5 * WIDE
    gathered = pl.pallas_call(
        gram_kernel,
        out_shape=jax.ShapeDtypeStruct((2, length, WIDE), F32),
        grid_spec=pltpu.PrefetchScalarGridSpec(
            num_scalar_prefetch=1,
            grid=(steps,),
            in_specs=piece_in + [own_spec, other_spec],
            out_specs=pl.BlockSpec((2, length, WIDE), lambda j, w: (0, 0, 0)),
            scratch_shapes=[pltpu.VMEM((size, TILE), BF16)] * 3
            + [pltpu.VMEM((size, size), F32)] * 2
            + [pltpu.VMEM((size, 2 * WIDE), F32)],
        ),
        compiler_params=pltpu.CompilerParams(
            dimension_semantics=("arbitrary",), vmem_limit_bytes=40 << 20
        ),
        name="gram",
    )(where, *pieces, vectors, other)

    mine = lax.dynamic_index_in_dim(gathered, core, 0, keepdims=False)
    send = lax.dynamic_index_in_dim(gathered, 1 - core, 0, keepdims=False)
    mine = mine + core_swap(send)
    members = lax.axis_size("row")
    parts = lax.all_to_all(mine.reshape(members, length // members, WIDE), "row", 0, 0)
    total = jnp.sum(parts, axis=0)
    spread = jnp.broadcast_to(total[None], (members,) + total.shape)
    mine = lax.all_to_all(spread, "row", 0, 0).reshape(length, WIDE)
    theirs = core_swap(mine)

    solved_own, solved_other = pl.pallas_call(
        solve_kernel,
        out_shape=[jax.ShapeDtypeStruct((size, WIDE), F32)] * 2,
        grid_spec=pltpu.PrefetchScalarGridSpec(
            num_scalar_prefetch=1,
            grid=(1,),
            in_specs=[pl.BlockSpec((length, WIDE), lambda j, w: (0, 0))] * 2,
            out_specs=[pl.BlockSpec((size, WIDE), lambda j, w: (0, 0))] * 2,
            scratch_shapes=[pltpu.VMEM((2, length, WIDE), F32)],
        ),
        compiler_params=pltpu.CompilerParams(vmem_limit_bytes=32 << 20),
        name="solve",
    )(where, mine, theirs)

    result_own, result_other = pl.pallas_call(
        apply_kernel,
        out_shape=[jax.ShapeDtypeStruct((half, columns), F32)] * 2,
        grid_spec=pltpu.PrefetchScalarGridSpec(
            num_scalar_prefetch=1,
            grid=(steps,),
            in_specs=piece_in
            + [own_spec, other_spec]
            + [pl.BlockSpec((size, WIDE), lambda j, w: (0, 0))] * 2,
            out_specs=[pl.BlockSpec((TILE, columns), lambda j, w: (j, 0))] * 2,
            scratch_shapes=[pltpu.VMEM((size, 2 * WIDE), BF16)] * 3,
        ),
        compiler_params=pltpu.CompilerParams(
            dimension_semantics=("arbitrary",), vmem_limit_bytes=40 << 20
        ),
        name="apply",
    )(where, *pieces, vectors, other, solved_own, solved_other)

    returned = core_swap(result_other)
    result = jnp.zeros((rows, columns), F32)
    result = lax.dynamic_update_slice_in_dim(result, result_own, core * half, 0)
    return lax.dynamic_update_slice_in_dim(result, returned, (1 - core) * half, 0)


def solution(mesh):
    specs = (P("row", "col"), P("row", "col"), P("row", "col"))
    return jax.shard_map(
        per_device, mesh=mesh, in_specs=specs, out_specs=P("row", "col"), check_vma=False
    )
```

time: 480 us -> 167 us (0.35); the launches traced: 472 us -> 165 us
  waiting for transfers between devices: 266 us -> 54.1 us
  matrix products: 101 us -> 0 us
  local copies, waits for them, and re-layouts: 85.5 us -> 11.6 us
  Pallas kernels: 0 us -> 42.1 us
  blocking collectives: 0 us -> 28.7 us
  starting transfers between devices: 0.34 us -> 24.7 us
  between operations: 14.4 us -> 0.18 us
    psum x2 -> x0, waiting for transfers between devices: 138 us -> none  [reduce_all(): totals = lax.psum(partials, 'row')]
    all_gather x2 -> x0, waiting for transfers between devices: 127 us -> none  [the longest x1 71.7 us: per_device(): lax.all_gather(panel_two, 'col', axis=1, tiled=True)]
    dot_general x50 -> x0, matrix products: 101 us -> none  [the longest x14 38.9 us: invert_upper(): jnp.einsum('aibj,ab->aij', tiled, picker, precision=lax.Precision.HIGHEST)]
    reshape x14 -> x0, local copies, waits for them, and re-layouts: 69.9 us -> none  [invert_upper(): tiled = factor.reshape(count, 2 * width, count, 2 * width)]
    ppermute x0 -> x16, waiting for transfers between devices: none -> 54.1 us  [permute(): return lax.ppermute(value, 'col', pairs)]
    pallas_call x0 -> x3, Pallas kernels: none -> 42.1 us  [the longest x1 21 us: per_device(): pl.pallas_call(gram_kernel, out_shape=jax.ShapeDtypeStruct((2, length, WI...]
    all_to_all x0 -> x2, blocking collectives: none -> 28.7 us  [the longest x1 15.6 us: per_device(): lax.all_to_all(mine.reshape(members, length // members, WIDE), 'row', 0, 0)]
    ppermute x0 -> x16, starting transfers between devices: none -> 24.7 us  [permute(): return lax.ppermute(value, 'col', pairs)]
  transfers between devices with their start and end apart: 4 -> 16, of which waited for: 4 -> 11; matrix products, arithmetic and copies ran while one was open for 7% -> 2% of each run, Pallas kernels for 0% -> 0%
where the time goes in v1:
time: 167 us; the launch traced here: 165 us
  waiting for transfers between devices  54.1 us (32%)
  Pallas kernels  42.1 us (25%)
  blocking collectives  28.7 us (17%)
  starting transfers between devices  24.7 us (15%)
  local copies, waits for them, and re-layouts  11.6 us (7%)
  other arithmetic  3.73 us (2%)
    ppermute x16, waiting for transfers between devices, permute(): return lax.ppermute(value, 'col', pairs)  54.1 us
    ppermute x16, starting transfers between devices, permute(): return lax.ppermute(value, 'col', pairs)  24.7 us
    pallas_call x1, Pallas kernels, per_device(): pl.pallas_call(gram_kernel, out_shape=jax.ShapeDtypeStruct((2, length, WI...  21 us
    all_to_all x1, blocking collectives, per_device(): lax.all_to_all(mine.reshape(members, length // members, WIDE), 'row', 0, 0)  15.6 us
    all_to_all x1, blocking collectives, per_device(): mine = lax.all_to_all(spread, 'row', 0, 0).reshape(length, WIDE)  13.1 us
    pallas_call x1, Pallas kernels, per_device(): pl.pallas_call(apply_kernel, out_shape=[jax.ShapeDtypeStruct((half, colum...  11.6 us
    pallas_call x1, Pallas kernels, per_device(): pl.pallas_call(solve_kernel, out_shape=[jax.ShapeDtypeStruct((size, WIDE)...  9.62 us
    unnamed x24, local copies, waits for them, and re-layouts  6.02 us
  transfers between devices with their start and end apart: 16, of which 11 were waited for; matrix products, arithmetic and copies ran while one was open for 2% of the time, Pallas kernels for 0%

profile of v1, /device:TPU:0, one launch (start us, length us, event | category | flops | bytes accessed | tf_op | source)
XLA Modules:
  0.0 165.2 jit_solution(4594063091058237066)
XLA Ops:
  0.0 1.3 fusion.2
  1.3 0.1 collective-permute-start
  1.4 1.9 %collective-permute-done = f32[2,16,4096]{2,1,0:T(8,128)S(1)} collective-permute-done((f32[2,16,4096]{2,1,0:T(8,128)S(1)}, f32[2,16,4096]{2,1,0:T(8,128)S(1)}, u32[]{:S(2)}, u32[]{:S(2)}) %collective-permute-start) | collective-permute-done | bytes 524320 | tf_op jit(solution)/shard_map/ppermute | solution.py:271
  3.3 0.1 pad_maximum_fusion
  3.3 0.1 copy.4
  3.4 3.2 %collective-permute-start.3 = (f32[64,4096]{1,0:T(8,128)S(1)}, f32[64,4096]{1,0:T(8,128)S(1)}, u32[]{:S(2)}, u32[]{:S(2)}) collective-permute-start(f32[64,4096]{1,0:T(8,128)S(1)} %bitcast.25), channel_id=1, source_target_pairs={{0,8},{1,9},{2,10},{3,11},{4,12},{5,13},{6,14},{7,15},{8,0},{9,1},... | collective-permute-start | bytes 3145736 | tf_op jit(solution)/shard_map/ppermute | solution.py:271
  6.6 4.0 %collective-permute-start.2 = (f32[64,4096]{1,0:T(8,128)S(1)}, f32[64,4096]{1,0:T(8,128)S(1)}, u32[]{:S(2)}, u32[]{:S(2)}) collective-permute-start(f32[64,4096]{1,0:T(8,128)S(1)} %bitcast.26), channel_id=1, source_target_pairs={{0,6},{1,7},{2,0},{3,1},{4,2},{5,3},{6,4},{7,5},{8,14},{9,15},{10,... | collective-permute-start | bytes 3145736 | tf_op jit(solution)/shard_map/ppermute | solution.py:271
  10.6 0.0 copy-done.10
  10.6 1.5 constant_dynamic-slice_fusion
  12.1 0.0 collective-permute-start.12
  12.1 0.0 collective-permute-start.1
  12.1 18.1 %collective-permute-done.3.refs_3_ = f32[64,4096]{1,0:T(8,128)S(1)} collective-permute-done((f32[64,4096]{1,0:T(8,128)S(1)}, f32[64,4096]{1,0:T(8,128)S(1)}, u32[]{:S(2)}, u32[]{:S(2)}) %collective-permute-start.3) | collective-permute-done | bytes 1048608 | tf_op jit(solution)/shard_map/ppermute | solution.py:271
  30.2 4.2 %collective-permute-start.6 = (f32[64,2048]{1,0:T(8,128)S(1)}, f32[64,2048]{1,0:T(8,128)S(1)}, u32[]{:S(2)}, u32[]{:S(2)}) collective-permute-start(f32[64,2048]{1,0:T(8,128)S(1)} %slice.19), channel_id=1, source_target_pairs={{0,6},{1,7},{2,0},{3,1},{4,2},{5,3},{6,4},{7,5},{8,14},{9,15},{10,... | collective-permute-start | bytes 1572872 | tf_op jit(solution)/shard_map/ppermute | solution.py:271
  34.4 0.0 collective-permute-start.5
  34.4 0.0 collective-permute-done.2.refs_2_
  34.5 3.1 %collective-permute-start.10 = (f32[64,2048]{1,0:T(8,128)S(1)}, f32[64,2048]{1,0:T(8,128)S(1)}, u32[]{:S(2)}, u32[]{:S(2)}) collective-permute-start(f32[64,2048]{1,0:T(8,128)S(1)} %slice.20), channel_id=1, source_target_pairs={{0,8},{1,9},{2,10},{3,11},{4,12},{5,13},{6,14},{7,15},{8,0},{9,1},... | collective-permute-start | bytes 1572872 | tf_op jit(solution)/shard_map/ppermute | solution.py:271
  37.6 1.7 %collective-permute-done.1.refs_1_ = f32[64,4096]{1,0:T(8,128)S(1)} collective-permute-done((f32[64,4096]{1,0:T(8,128)S(1)}, f32[64,4096]{1,0:T(8,128)S(1)}, u32[]{:S(2)}, u32[]{:S(2)}) %collective-permute-start.1) | collective-permute-done | bytes 1048608 | tf_op jit(solution)/shard_map/ppermute | solution.py:271
  39.3 0.0 copy-done
  39.3 1.5 collective-permute-start.8
  40.8 1.1 fusion.3
  41.9 4.9 %collective-permute-done.6.refs_6_ = f32[64,2048]{1,0:T(8,128)S(1)} collective-permute-done((f32[64,2048]{1,0:T(8,128)S(1)}, f32[64,2048]{1,0:T(8,128)S(1)}, u32[]{:S(2)}, u32[]{:S(2)}) %collective-permute-start.6) | collective-permute-done | bytes 524320 | tf_op jit(solution)/shard_map/ppermute | solution.py:271
  46.8 0.8 copy-done.4
  47.6 3.0 %collective-permute-start.9 = (f32[64,2048]{1,0:T(8,128)}, f32[64,2048]{1,0:T(8,128)}, u32[]{:S(2)}, u32[]{:S(2)}) collective-permute-start(f32[64,2048]{1,0:T(8,128)} %get-tuple-element.13), channel_id=1, source_target_pairs={{0,8},{1,9},{2,10},{3,11},{4,12},{5,13},{6,14},{7,15},{8,0},{9,1},... | collective-permute-start | bytes 1572872 | tf_op jit(solution)/shard_map/ppermute | solution.py:271
  50.7 0.0 collective-permute-done.5.refs_5_
  50.7 0.4 collective-permute-start.4
  51.0 0.0 collective-permute-done.10.refs_10_
  51.0 0.8 copy-done.7
  51.9 1.9 %collective-permute-start.7 = (f32[64,2048]{1,0:T(8,128)}, f32[64,2048]{1,0:T(8,128)}, u32[]{:S(2)}, u32[]{:S(2)}) collective-permute-start(f32[64,2048]{1,0:T(8,128)} %collective-permute-done.5.refs_5_), channel_id=1, source_target_pairs={{0,2},{1,3},{2,4},{3,5},{4,6},{5,7},{6,0},{7,1},{8,10},{9,11},{10,... | collective-permute-start | bytes 1572872 | tf_op jit(solution)/shard_map/ppermute | solution.py:271
  53.8 2.5 %collective-permute-done.8.refs_8_ = f32[64,2048]{1,0:T(8,128)} collective-permute-done((f32[64,2048]{1,0:T(8,128)S(1)}, f32[64,2048]{1,0:T(8,128)}, u32[]{:S(2)}, u32[]{:S(2)}) %collective-permute-start.8) | collective-permute-done | bytes 524320 | tf_op jit(solution)/shard_map/ppermute | solution.py:271
  56.3 3.0 %collective-permute-start.11 = (f32[64,2048]{1,0:T(8,128)}, f32[64,2048]{1,0:T(8,128)}, u32[]{:S(2)}, u32[]{:S(2)}) collective-permute-start(f32[64,2048]{1,0:T(8,128)} %collective-permute-done.8.refs_8_), channel_id=1, source_target_pairs={{0,8},{1,9},{2,10},{3,11},{4,12},{5,13},{6,14},{7,15},{8,0},{9,1},... | collective-permute-start | bytes 1572872 | tf_op jit(solution)/shard_map/ppermute | solution.py:271
  59.3 0.1 stack.57.where_ref
  59.4 1.9 %collective-permute-done.9.refs_9_ = f32[64,2048]{1,0:T(8,128)} collective-permute-done((f32[64,2048]{1,0:T(8,128)}, f32[64,2048]{1,0:T(8,128)}, u32[]{:S(2)}, u32[]{:S(2)}) %collective-permute-start.9) | collective-permute-done | bytes 524320 | tf_op jit(solution)/shard_map/ppermute | solution.py:271
  61.3 6.2 %collective-permute-done.4.refs_4_ = f32[64,2048]{1,0:T(8,128)} collective-permute-done((f32[64,2048]{1,0:T(8,128)}, f32[64,2048]{1,0:T(8,128)}, u32[]{:S(2)}, u32[]{:S(2)}) %collective-permute-start.4) | collective-permute-done | bytes 524320 | tf_op jit(solution)/shard_map/ppermute | solution.py:271
  67.5 0.0 collective-permute-done.12.refs_13_
  67.5 9.0 %collective-permute-done.7.refs_7_ = f32[64,2048]{1,0:T(8,128)} collective-permute-done((f32[64,2048]{1,0:T(8,128)}, f32[64,2048]{1,0:T(8,128)}, u32[]{:S(2)}, u32[]{:S(2)}) %collective-permute-start.7) | collective-permute-done | bytes 524320 | tf_op jit(solution)/shard_map/ppermute | solution.py:271
  76.5 0.0 collective-permute-done.11.refs_11_
  76.5 1.2 copy-done.1
  77.8 1.0 copy-done.5
  78.8 1.0 copy-done.8
  79.8 21.0 %gram.1 = f32[2,1152,128]{2,1,0:T(8,128)S(1)} custom-call(s32[9]{0:T(128)S(1)} %stack.57.where_ref, f32[64,4096]{1,0:T(8,128)S(1)} %bitcast.28, f32[64,4096]{1,0:T(8,128)S(1)} %collective-permute-done.1.refs_1_, f32[64,4096]{1,0:T(8,128)S(1)} %copy-done.1, f32[64,4096]{1,0:T(8,128)S(1)} %collective-permute-done.3.refs_3_, ...), custom_call_target="tpu_custom_call" | custom-call | tf_op jit(solution)/shard_map/gram/pallas_call | solution.py:320
  100.8 0.0 copy-start.3
  100.8 1.0 copy-done.3
  101.8 0.9 dynamic-slice_bitcast_fusion
  102.7 0.0 collective-permute-start.13
  102.7 2.3 %collective-permute-done.13 = f32[1152,128]{1,0:T(8,128)} collective-permute-done((f32[1152,128]{1,0:T(8,128)}, f32[1152,128]{1,0:T(8,128)}, u32[]{:S(2)}, u32[]{:S(2)}) %collective-permute-start.13) | collective-permute-done | bytes 589856 | tf_op jit(solution)/shard_map/ppermute | solution.py:271
  105.0 1.3 bitcast_add_fusion
  106.4 15.6 %all_to_all.10 = f32[8,144,128]{2,1,0:T(8,128)} all-to-all(f32[8,144,128]{2,1,0:T(8,128)S(1)} %bitcast.32), channel_id=1, replica_groups=mesh['row'=8,'col'=16] {'row'}, dimensions={0} | all-to-all | bytes 1179648 | tf_op jit(solution)/shard_map/all_to_all | solution.py:342
  121.9 1.1 reduce_sum.9
  123.0 0.0 copy-start.2
  123.0 0.0 copy-start.6
  123.1 0.0 copy-start.9
  123.1 13.1 %all_to_all.11 = f32[8,144,128]{2,1,0:T(8,128)S(1)} all-to-all(f32[8,144,128]{2,1,0:T(8,128)S(1)} %broadcast_in_dim.10), channel_id=1, replica_groups=mesh['row'=8,'col'=16] {'row'}, dimensions={0} | all-to-all | bytes 1179648 | tf_op jit(solution)/shard_map/all_to_all | solution.py:345
  136.2 0.0 collective-permute-start.14
  136.2 2.0 %collective-permute-done.14.other_ref = f32[1152,128]{1,0:T(8,128)S(1)} collective-permute-done((f32[1152,128]{1,0:T(8,128)S(1)}, f32[1152,128]{1,0:T(8,128)S(1)}, u32[]{:S(2)}, u32[]{:S(2)}) %collective-permute-start.14) | collective-permute-done | bytes 589856 | tf_op jit(solution)/shard_map/ppermute | solution.py:271
  138.2 9.6 %solve.1 = (f32[512,128]{1,0:T(8,128)S(1)}, f32[512,128]{1,0:T(8,128)S(1)}) custom-call(s32[9]{0:T(128)S(1)} %stack.57.where_ref, f32[1152,128]{1,0:T(8,128)S(1)} %bitcast.31, f32[1152,128]{1,0:T(8,128)S(1)} %collective-permute-done.14.other_ref), custom_call_target="tpu_custom_call" | custom-call | tf_op jit(solution)/shard_map/solve/pallas_call | solution.py:348
  147.9 0.0 copy-done.2
  147.9 11.6 %apply.1 = (f32[4096,128]{1,0:T(8,128)S(1)}, f32[4096,128]{1,0:T(8,128)S(1)}) custom-call(s32[9]{0:T(128)S(1)} %stack.57.where_ref, f32[64,4096]{1,0:T(8,128)S(1)} %bitcast.29, f32[64,4096]{1,0:T(8,128)S(1)} %collective-permute-done.1.refs_1_, f32[64,4096]{1,0:T(8,128)S(1)} %copy-done.2, f32[64,4096]{1,0:T(8,128)S(1)} %collective-permute-done.3.refs_3_, ...), custom_call_target="tpu_custom_call" | custom-call | tf_op jit(solution)/shard_map/apply/pallas_call | solution.py:362
  159.5 0.2 collective-permute-start.15
  159.7 0.3 broadcast_in_dim.4
  159.9 0.2 constant_dynamic-update-slice_fusion.1
  160.1 0.0 copy-start.11
  160.1 3.6 %collective-permute-done.15 = f32[4096,128]{1,0:T(8,128)S(1)} collective-permute-done((f32[4096,128]{1,0:T(8,128)S(1)}, f32[4096,128]{1,0:T(8,128)S(1)}, u32[]{:S(2)}, u32[]{:S(2)}) %collective-permute-start.15) | collective-permute-done | bytes 2097184 | tf_op jit(solution)/shard_map/ppermute | solution.py:271
  163.7 0.0 copy-done.11
  163.7 1.5 constant_dynamic-update-slice_fusion
  (12 shorter events, 0.1 us)
Async XLA Ops:
  1.3 2.0 %collective-permute-start = (f32[2,16,4096]{2,1,0:T(8,128)S(1)}, f32[2,16,4096]{2,1,0:T(8,128)S(1)}, u32[]{:S(2)}, u32[]{:S(2)}) collective-permute-start(f32[2,16,4096]{2,1,0:T(8,128)S(1)} %get-tuple-element.16), channel_id=1, source_target_pairs={{0,1},{1,0},{2,3},{3,2},{4,5},{5,4},{6,7},{7,6},{8,9},{9,8},{10,11... | collective-permute-start | bytes 1572872 | tf_op jit(solution)/shard_map/ppermute | solution.py:271
  3.3 7.4 %copy-start.10 = (f32[8192,128]{1,0:T(8,128)S(1)}, f32[8192,128]{1,0:T(8,128)}, u32[]{:S(2)}) copy-start(f32[8192,128]{1,0:T(8,128)} %refs_12_.3) | copy-start | bytes 12582916
  3.4 26.8 %collective-permute-start.3 = (f32[64,4096]{1,0:T(8,128)S(1)}, f32[64,4096]{1,0:T(8,128)S(1)}, u32[]{:S(2)}, u32[]{:S(2)}) collective-permute-start(f32[64,4096]{1,0:T(8,128)S(1)} %bitcast.25), channel_id=1, source_target_pairs={{0,8},{1,9},{2,10},{3,11},{4,12},{5,13},{6,14},{7,15},{8,0},{9,1},... | collective-permute-start | bytes 3145736 | tf_op jit(solution)/shard_map/ppermute | solution.py:271
  6.6 27.8 %collective-permute-start.2 = (f32[64,4096]{1,0:T(8,128)S(1)}, f32[64,4096]{1,0:T(8,128)S(1)}, u32[]{:S(2)}, u32[]{:S(2)}) collective-permute-start(f32[64,4096]{1,0:T(8,128)S(1)} %bitcast.26), channel_id=1, source_target_pairs={{0,6},{1,7},{2,0},{3,1},{4,2},{5,3},{6,4},{7,5},{8,14},{9,15},{10,... | collective-permute-start | bytes 3145736 | tf_op jit(solution)/shard_map/ppermute | solution.py:271
  12.1 55.4 %collective-permute-start.12 = (f32[4096,128]{1,0:T(8,128)}, f32[4096,128]{1,0:T(8,128)}, u32[]{:S(2)}, u32[]{:S(2)}) collective-permute-start(f32[4096,128]{1,0:T(8,128)} %constant_dynamic-slice_fusion), channel_id=1, source_target_pairs={{0,1},{1,0},{2,3},{3,2},{4,5},{5,4},{6,7},{7,6},{8,9},{9,8},{10,11... | collective-permute-start | bytes 6291464 | tf_op jit(solution)/shard_map/ppermute | solution.py:271
  12.1 27.2 %collective-permute-start.1 = (f32[64,4096]{1,0:T(8,128)S(1)}, f32[64,4096]{1,0:T(8,128)S(1)}, u32[]{:S(2)}, u32[]{:S(2)}) collective-permute-start(f32[64,4096]{1,0:T(8,128)S(1)} %bitcast.27), channel_id=1, source_target_pairs={{0,2},{1,3},{2,4},{3,5},{4,6},{5,7},{6,0},{7,1},{8,10},{9,11},{10,... | collective-permute-start | bytes 3145736 | tf_op jit(solution)/shard_map/ppermute | solution.py:271
  30.2 16.6 %collective-permute-start.6 = (f32[64,2048]{1,0:T(8,128)S(1)}, f32[64,2048]{1,0:T(8,128)S(1)}, u32[]{:S(2)}, u32[]{:S(2)}) collective-permute-start(f32[64,2048]{1,0:T(8,128)S(1)} %slice.19), channel_id=1, source_target_pairs={{0,6},{1,7},{2,0},{3,1},{4,2},{5,3},{6,4},{7,5},{8,14},{9,15},{10,... | collective-permute-start | bytes 1572872 | tf_op jit(solution)/shard_map/ppermute | solution.py:271
  34.4 16.3 %collective-permute-start.5 = (f32[64,2048]{1,0:T(8,128)S(1)}, f32[64,2048]{1,0:T(8,128)}, u32[]{:S(2)}, u32[]{:S(2)}) collective-permute-start(f32[64,2048]{1,0:T(8,128)S(1)} %slice.19), channel_id=1, source_target_pairs={{0,2},{1,3},{2,4},{3,5},{4,6},{5,7},{6,0},{7,1},{8,10},{9,11},{10,... | collective-permute-start | bytes 1572872 | tf_op jit(solution)/shard_map/ppermute | solution.py:271
  34.4 4.8 %copy-start = (f32[64,4096]{1,0:T(8,128)}, f32[64,4096]{1,0:T(8,128)S(1)}, u32[]{:S(2)}) copy-start(f32[64,4096]{1,0:T(8,128)S(1)} %collective-permute-done.2.refs_2_) | copy-start | bytes 3145732
  34.5 16.6 %collective-permute-start.10 = (f32[64,2048]{1,0:T(8,128)S(1)}, f32[64,2048]{1,0:T(8,128)S(1)}, u32[]{:S(2)}, u32[]{:S(2)}) collective-permute-start(f32[64,2048]{1,0:T(8,128)S(1)} %slice.20), channel_id=1, source_target_pairs={{0,8},{1,9},{2,10},{3,11},{4,12},{5,13},{6,14},{7,15},{8,0},{9,1},... | collective-permute-start | bytes 1572872 | tf_op jit(solution)/shard_map/ppermute | solution.py:271
  39.3 17.0 %collective-permute-start.8 = (f32[64,2048]{1,0:T(8,128)S(1)}, f32[64,2048]{1,0:T(8,128)}, u32[]{:S(2)}, u32[]{:S(2)}) collective-permute-start(f32[64,2048]{1,0:T(8,128)S(1)} %slice.20), channel_id=1, source_target_pairs={{0,6},{1,7},{2,0},{3,1},{4,2},{5,3},{6,4},{7,5},{8,14},{9,15},{10,... | collective-permute-start | bytes 1572872 | tf_op jit(solution)/shard_map/ppermute | solution.py:271
  46.8 0.8 copy-start.4
  47.6 13.7 %collective-permute-start.9 = (f32[64,2048]{1,0:T(8,128)}, f32[64,2048]{1,0:T(8,128)}, u32[]{:S(2)}, u32[]{:S(2)}) collective-permute-start(f32[64,2048]{1,0:T(8,128)} %get-tuple-element.13), channel_id=1, source_target_pairs={{0,8},{1,9},{2,10},{3,11},{4,12},{5,13},{6,14},{7,15},{8,0},{9,1},... | collective-permute-start | bytes 1572872 | tf_op jit(solution)/shard_map/ppermute | solution.py:271
  50.7 16.8 %collective-permute-start.4 = (f32[64,2048]{1,0:T(8,128)}, f32[64,2048]{1,0:T(8,128)}, u32[]{:S(2)}, u32[]{:S(2)}) collective-permute-start(f32[64,2048]{1,0:T(8,128)} %get-tuple-element.14), channel_id=1, source_target_pairs={{0,2},{1,3},{2,4},{3,5},{4,6},{5,7},{6,0},{7,1},{8,10},{9,11},{10,... | collective-permute-start | bytes 1572872 | tf_op jit(solution)/shard_map/ppermute | solution.py:271
  51.0 0.8 copy-start.7
  51.9 24.7 %collective-permute-start.7 = (f32[64,2048]{1,0:T(8,128)}, f32[64,2048]{1,0:T(8,128)}, u32[]{:S(2)}, u32[]{:S(2)}) collective-permute-start(f32[64,2048]{1,0:T(8,128)} %collective-permute-done.5.refs_5_), channel_id=1, source_target_pairs={{0,2},{1,3},{2,4},{3,5},{4,6},{5,7},{6,0},{7,1},{8,10},{9,11},{10,... | collective-permute-start | bytes 1572872 | tf_op jit(solution)/shard_map/ppermute | solution.py:271
  56.3 20.2 %collective-permute-start.11 = (f32[64,2048]{1,0:T(8,128)}, f32[64,2048]{1,0:T(8,128)}, u32[]{:S(2)}, u32[]{:S(2)}) collective-permute-start(f32[64,2048]{1,0:T(8,128)} %collective-permute-done.8.refs_8_), channel_id=1, source_target_pairs={{0,8},{1,9},{2,10},{3,11},{4,12},{5,13},{6,14},{7,15},{8,0},{9,1},... | collective-permute-start | bytes 1572872 | tf_op jit(solution)/shard_map/ppermute | solution.py:271
  76.5 1.2 copy-start.1
  77.8 1.0 copy-start.5
  78.8 1.0 copy-start.8
  100.8 1.0 copy-start.3
  102.7 2.3 %collective-permute-start.13 = (f32[1152,128]{1,0:T(8,128)}, f32[1152,128]{1,0:T(8,128)}, u32[]{:S(2)}, u32[]{:S(2)}) collective-permute-start(f32[1152,128]{1,0:T(8,128)} %dynamic-slice_bitcast_fusion), channel_id=1, source_target_pairs={{0,1},{1,0},{2,3},{3,2},{4,5},{5,4},{6,7},{7,6},{8,9},{9,8},{10,11... | collective-permute-start | bytes 1769480 | tf_op jit(solution)/shard_map/ppermute | solution.py:271
  123.0 24.8 %copy-start.2 = (f32[64,4096]{1,0:T(8,128)S(1)}, f32[64,4096]{1,0:T(8,128)}, u32[]{:S(2)}) copy-start(f32[64,4096]{1,0:T(8,128)} %copy-done) | copy-start | bytes 3145732
  123.0 24.8 %copy-start.6 = (f32[64,2048]{1,0:T(8,128)S(1)}, f32[64,2048]{1,0:T(8,128)}, u32[]{:S(2)}) copy-start(f32[64,2048]{1,0:T(8,128)} %copy-done.4) | copy-start | bytes 1572868
  123.1 24.8 %copy-start.9 = (f32[64,2048]{1,0:T(8,128)S(1)}, f32[64,2048]{1,0:T(8,128)}, u32[]{:S(2)}) copy-start(f32[64,2048]{1,0:T(8,128)} %copy-done.7) | copy-start | bytes 1572868
  136.2 2.0 %collective-permute-start.14 = (f32[1152,128]{1,0:T(8,128)S(1)}, f32[1152,128]{1,0:T(8,128)S(1)}, u32[]{:S(2)}, u32[]{:S(2)}) collective-permute-start(f32[1152,128]{1,0:T(8,128)S(1)} %bitcast.30), channel_id=1, source_target_pairs={{0,1},{1,0},{2,3},{3,2},{4,5},{5,4},{6,7},{7,6},{8,9},{9,8},{10,11... | collective-permute-start | bytes 1769480 | tf_op jit(solution)/shard_map/ppermute | solution.py:271
  159.5 4.2 %collective-permute-start.15 = (f32[4096,128]{1,0:T(8,128)S(1)}, f32[4096,128]{1,0:T(8,128)S(1)}, u32[]{:S(2)}, u32[]{:S(2)}) collective-permute-start(f32[4096,128]{1,0:T(8,128)S(1)} %get-tuple-element.12), channel_id=1, source_target_pairs={{0,1},{1,0},{2,3},{3,2},{4,5},{5,4},{6,7},{7,6},{8,9},{9,8},{10,11... | collective-permute-start | bytes 6291464 | tf_op jit(solution)/shard_map/ppermute | solution.py:271
  160.1 3.6 %copy-start.11 = (f32[8192,128]{1,0:T(8,128)}, f32[8192,128]{1,0:T(8,128)S(1)}, u32[]{:S(2)}) copy-start(f32[8192,128]{1,0:T(8,128)S(1)} %constant_dynamic-update-slice_fusion.1) | copy-start | bytes 12582916

commit v2 on v1

v2 whole, which is shorter than its diff:
```python
import functools

import jax
import jax.numpy as jnp
from jax import lax
from jax.experimental import pallas as pl
from jax.experimental.pallas import tpu as pltpu
from jax.sharding import PartitionSpec as P

F32 = jnp.float32
BF16 = jnp.bfloat16
HIGHEST = lax.Precision.HIGHEST
PLANES, DEPTH, CORES = 2, 4, 2
CHIPS = PLANES * DEPTH
WIDE = 128
TILE = 512
PIECES = ((0, 0), (0, 1), (1, 1), (0, 2), (0, 3)), ((1, 2), (1, 3), (2, 2), (2, 3), (3, 3))


def split3(value):
    high = value.astype(BF16)
    rest = value - high.astype(F32)
    middle = rest.astype(BF16)
    low = (rest - middle.astype(F32)).astype(BF16)
    return high, middle, low


def nn(left, right):
    return lax.dot_general(left, right, (((1,), (0,)), ((), ())), preferred_element_type=F32)


def nt(left, right):
    return lax.dot_general(left, right, (((1,), (1,)), ((), ())), preferred_element_type=F32)


def full(left, right):
    return lax.dot_general(
        left, right, (((1,), (0,)), ((), ())), precision=HIGHEST, preferred_element_type=F32
    )


def gram_kernel(where_ref, *refs, pieces, first):
    steps = pl.num_programs(0)
    step = pl.program_id(0)
    panels, rest = refs[:pieces], refs[pieces:]
    if first:
        own_ref, other_ref, out_ref, high, middle, low, even, skew, proj = rest
    else:
        own_ref, other_ref, before_ref, out_ref, high, middle, low, even, skew, proj = rest
    core = where_ref[CHIPS]
    lines = panels[0].shape[0]
    half = even.shape[1]
    start_row = high.shape[0] - half

    for index, ref in enumerate(panels):
        parts = split3(ref[...])
        begin = pl.multiple_of((index // 2) * 2 * lines + lines * (core ^ (index % 2)), lines)
        for target, value in zip((high, middle, low), parts):
            target[pl.ds(begin, lines), :] = value

    @pl.when(step == 0)
    def _():
        even[...] = jnp.zeros_like(even)
        skew[...] = jnp.zeros_like(skew)
        proj[...] = jnp.zeros_like(proj)

    one, two, three = high[start_row:, :], middle[start_row:, :], low[start_row:, :]
    skew[...] += nt(one, two) + nt(one, three)
    if first:
        even[...] += nt(one, one) + nt(two, two)
    else:
        even[half:, :] += nt(one, one) + nt(two, two)
        one_a, two_a, three_a = high[:half, :], middle[:half, :], low[:half, :]
        even[:half, :] += (
            (nt(one_a, three) + nt(three_a, one) + nt(two_a, two))
            + (nt(one_a, two) + nt(two_a, one))
            + nt(one_a, one)
        )
    current = jnp.concatenate([own_ref[...], other_ref[...]], axis=1)
    x_one, x_two, x_three = split3(current)
    proj[...] += (
        (nn(one, x_three) + nn(three, x_one) + nn(two, x_two))
        + (nn(one, x_two) + nn(two, x_one))
        + nn(one, x_one)
    )

    @pl.when(step == steps - 1)
    def _():
        def corner(i, j):
            at_i, at_j = slice(i * WIDE, (i + 1) * WIDE), slice(j * WIDE, (j + 1) * WIDE)
            base = even.shape[0] - half
            return (
                even[base + i * WIDE : base + (i + 1) * WIDE, at_j]
                + skew[at_i, at_j]
                + skew[at_j, at_i].T
            )

        if first:
            out_ref[core, 0:half, :] = proj[:, :WIDE]
            out_ref[1 - core, 0:half, :] = proj[:, WIDE:]
            for place, (i, j) in enumerate(((0, 0), (0, 1), (1, 1))):
                begin = half + place * WIDE
                out_ref[0, begin : begin + WIDE, :] = corner(i, j)
                out_ref[1, begin : begin + WIDE, :] = jnp.zeros((WIDE, WIDE), F32)
        else:
            out_ref[0, 0:half, :] = before_ref[0, 0:half, :]
            out_ref[1, 0:half, :] = before_ref[1, 0:half, :]
            out_ref[core, half : 2 * half, :] = proj[:, :WIDE]
            out_ref[1 - core, half : 2 * half, :] = proj[:, WIDE:]
            for part in range(2):
                for place, (i, j) in enumerate(PIECES[part]):
                    begin = 2 * half + place * WIDE
                    if j < 2:
                        source = half + ((0, 0), (0, 1), (1, 1)).index((i, j)) * WIDE
                        block = before_ref[0, source : source + WIDE, :]
                    elif i < 2:
                        block = even[i * WIDE : (i + 1) * WIDE, (j - 2) * WIDE : (j - 1) * WIDE]
                    else:
                        block = corner(i - 2, j - 2)
                    out_ref[part, begin : begin + WIDE, :] = block


def solve_kernel(where_ref, mine_ref, other_ref, own_ref, partner_ref, both, rows_done, ordered, sides):
    core = where_ref[CHIPS]
    both[core] = mine_ref[...]
    both[1 - core] = other_ref[...]
    count = 4
    size = count * WIDE
    panel = size // 2
    base = 16

    def relative(i, j):
        for part in range(2):
            if (i, j) in PIECES[part]:
                start = size + PIECES[part].index((i, j)) * WIDE
                return both[part, start : start + WIDE, :]

    group = size // (2 * CORES * CHIPS)

    def target(index):
        slot, at_core, part = index // (2 * CORES), (index // 2) % CORES, index % 2
        start = part * panel + where_ref[slot] * CORES * group + at_core * group
        return pl.ds(pl.multiple_of(start, group), group)

    for i in range(count):
        strip = jnp.concatenate(
            [relative(i, j) if i <= j else relative(j, i).T for j in range(count)], axis=1
        )
        for k in range(WIDE // group):
            rows_done[target(i * (WIDE // group) + k), :] = strip[k * group : (k + 1) * group]
    for i in range(count):
        strip = jnp.concatenate(
            [
                rows_done[j * WIDE : (j + 1) * WIDE, i * WIDE : (i + 1) * WIDE].T
                for j in range(count)
            ],
            axis=1,
        )
        for k in range(WIDE // group):
            ordered[target(i * (WIDE // group) + k), :] = strip[k * group : (k + 1) * group]
    for index in range(size // group):
        at = slice(index * group, (index + 1) * group)
        sides[target(index), :] = jnp.concatenate([mine_ref[at, :], other_ref[at, :]], axis=1)

    def block(i, j):
        return ordered[i * WIDE : (i + 1) * WIDE, j * WIDE : (j + 1) * WIDE]

    row = lax.broadcasted_iota(jnp.int32, (WIDE, WIDE), 0)
    column = lax.broadcasted_iota(jnp.int32, (WIDE, WIDE), 1)
    same = (row // base) == (column // base)
    diagonals = []
    for i in range(count):
        value = block(i, i)
        diagonals.append(
            jnp.where(row < column, value, jnp.where(row == column, value * 0.5, 0.0))
        )
    lane = lax.broadcasted_iota(jnp.int32, (base, WIDE), 1) % base
    ones = jnp.where(same, 1.0, 0.0).astype(F32)
    spread = []
    for i in range(count):
        flipped = jnp.where(same, diagonals[i], 0.0).T
        folded = flipped[0:base]
        for k in range(1, WIDE // base):
            folded = folded + flipped[k * base : (k + 1) * base]
        stacked = jnp.concatenate([jnp.where(lane == k, folded, 0.0) for k in range(base)], axis=0)
        spread.append(full(stacked, ones))
    wide_lane = lax.broadcasted_iota(jnp.int32, (1, size), 1) % base
    wide_row = lax.broadcasted_iota(jnp.int32, (base, size), 0)
    solved = jnp.zeros((base, size), F32)
    for i in range(base - 1, -1, -1):
        factor = jnp.concatenate([s[i * base : (i + 1) * base] for s in spread], axis=1)
        total = jnp.sum(factor * solved, axis=0, keepdims=True)
        line = (jnp.where(wide_lane == i, 1.0, 0.0) - total) / factor[i : i + 1]
        solved = jnp.where(wide_row == i, line, solved)

    big_row = lax.broadcasted_iota(jnp.int32, (panel, panel), 0)
    big_column = lax.broadcasted_iota(jnp.int32, (panel, panel), 1)
    inverses = []
    for half in range(2):
        left, right = 2 * half, 2 * half + 1
        top = jnp.concatenate([diagonals[left], block(left, right)], axis=1)
        bottom = jnp.concatenate([jnp.zeros((WIDE, WIDE), F32), diagonals[right]], axis=1)
        factor = jnp.concatenate([top, bottom], axis=0)
        lines = solved[:, half * panel : (half + 1) * panel]
        tiled = jnp.concatenate([lines] * (panel // base), axis=0)
        inverse = jnp.where((big_row // base) == (big_column // base), tiled, 0.0)
        width = base
        while width < panel:
            picked = (
                ((big_row // width) % 2 == 0) & (big_column // width == big_row // width + 1)
            )
            coupling = jnp.where(picked, factor, 0.0)
            inverse = inverse - full(full(inverse, coupling), inverse)
            width *= 2
        inverses.append(inverse)
    corner = jnp.concatenate(
        [
            jnp.concatenate([block(0, 2), block(0, 3)], axis=1),
            jnp.concatenate([block(1, 2), block(1, 3)], axis=1),
        ],
        axis=0,
    )
    right_side = sides[...]
    second = full(inverses[1], right_side[panel:])
    first = full(inverses[0], right_side[:panel] - full(corner, second))
    own_ref[0:panel, :] = first[:, :WIDE]
    own_ref[panel:, :] = second[:, :WIDE]
    partner_ref[0:panel, :] = first[:, WIDE:]
    partner_ref[panel:, :] = second[:, WIDE:]


def apply_kernel(where_ref, *refs):
    step = pl.program_id(0)
    panels = refs[: 2 * CHIPS]
    current_own, current_other, solved_own, solved_other, out_own, out_other, high, middle, low = refs[
        2 * CHIPS :
    ]
    core = where_ref[CHIPS]
    panel = solved_own.shape[0] // 2
    group = panels[0].shape[0] // 2

    @pl.when(step == 0)
    def _():
        for index in range(2 * CHIPS):
            chip = where_ref[index // 2]
            for part in range(2):
                start = pl.multiple_of(
                    part * panel + chip * 2 * group + group * (core ^ (index % 2)), group
                )
                lines = jnp.concatenate(
                    [solved_own[pl.ds(start, group), :], solved_other[pl.ds(start, group), :]],
                    axis=1,
                )
                at = (2 * index + part) * group
                for target, value in zip((high, middle, low), split3(lines)):
                    target[at : at + group, :] = value

    value = jnp.concatenate([r[...] for r in panels], axis=0)
    one, two, three = split3(value)
    first, second, third = high[...], middle[...], low[...]

    def tn(left, right):
        return lax.dot_general(left, right, (((0,), (0,)), ((), ())), preferred_element_type=F32)

    change = (
        (tn(one, third) + tn(three, first) + tn(two, second))
        + (tn(one, second) + tn(two, first))
        + tn(one, first)
    )
    out_own[...] = current_own[...] - change[:, :WIDE]
    out_other[...] = current_other[...] - change[:, WIDE:]


def per_device(vectors, panel_one, panel_two):
    rows, columns = vectors.shape
    group = panel_one.shape[1]
    half = rows // 2
    size = 2 * group * CHIPS * CORES
    steps = half // TILE
    at = lax.axis_index("col")
    core, depth, plane = at % CORES, (at // CORES) % DEPTH, at // (CORES * DEPTH)

    def permute(value, move):
        pairs = []
        for source in range(CHIPS * CORES):
            k, z, x = source % CORES, (source // CORES) % DEPTH, source // (CORES * DEPTH)
            k, z, x = move(k, z, x)
            pairs.append((source, (x * DEPTH + z % DEPTH) * CORES + k))
        return lax.ppermute(value, "col", pairs)

    def core_swap(value):
        return permute(value, lambda k, z, x: (1 - k, z, x))

    def up(value):
        return permute(value, lambda k, z, x: (k, z + 1, x))

    def down(value):
        return permute(value, lambda k, z, x: (k, z - 1, x))

    def across(value):
        return permute(value, lambda k, z, x: (k, z, 1 - x))

    def half_of(which):
        picked = [lax.dynamic_slice_in_dim(v.T, which * half, half, 1) for v in (panel_one, panel_two)]
        return jnp.concatenate(picked, axis=0)

    a_own = half_of(core)
    b_own = core_swap(half_of(1 - core))
    given = lax.dynamic_slice_in_dim(vectors, (1 - core) * half, half, 0)
    other = core_swap(given)

    a_away, a_below, a_above = across(a_own), up(a_own), down(a_own)
    b_away, b_below, b_above = across(b_own), up(b_own), down(b_own)
    a_away_below = up(a_away)
    a_away_above = down(a_away)
    a_far = up(a_below)
    b_away_below = across(b_below)
    b_far = down(b_above)
    b_away_above = across(b_above)
    a_away_far = up(a_away_below)
    b_away_far = across(b_far)

    near = (a_own, b_own, a_below, b_below, a_above, b_above, a_away, b_away)
    distant = (
        a_far, b_far, a_away_below, b_away_below,
        a_away_above, b_away_above, a_away_far, b_away_far,
    )
    chips = []
    for x_step, z_step in ((0, 0), (0, -1), (0, 1), (1, 0), (0, 2), (1, -1), (1, 1), (1, 2)):
        chips.append(jnp.bitwise_xor(plane, x_step) * DEPTH + (depth + z_step) % DEPTH)
    where = jnp.stack(chips + [core]).astype(jnp.int32)

    lines = 2 * group
    piece = pl.BlockSpec((lines, TILE), lambda j, w: (0, j))
    own_spec = pl.BlockSpec((TILE, columns), lambda j, w: (w[CHIPS] * steps + j, 0))
    other_spec = pl.BlockSpec((TILE, columns), lambda j, w: (j, 0))
    length = size + 5 * WIDE
    span = size // 2

    def gram(first, pieces, extra):
        rows_out = span + 3 * WIDE if first else length
        extra_specs = [pl.BlockSpec(v.shape, lambda j, w: (0, 0, 0)) for v in extra]
        height = span if first else size
        units = 10 if first else 16
        return pl.pallas_call(
            functools.partial(gram_kernel, pieces=len(pieces), first=first),
            out_shape=jax.ShapeDtypeStruct((2, rows_out, WIDE), F32),
            grid_spec=pltpu.PrefetchScalarGridSpec(
                num_scalar_prefetch=1,
                grid=(steps,),
                in_specs=[piece] * len(pieces) + [own_spec, other_spec] + extra_specs,
                out_specs=pl.BlockSpec((2, rows_out, WIDE), lambda j, w: (0, 0, 0)),
                scratch_shapes=[pltpu.VMEM((height, TILE), BF16)] * 3
                + [
                    pltpu.VMEM((height, span), F32),
                    pltpu.VMEM((span, span), F32),
                    pltpu.VMEM((span, 2 * WIDE), F32),
                ],
            ),
            compiler_params=pltpu.CompilerParams(
                dimension_semantics=("arbitrary",), vmem_limit_bytes=32 << 20
            ),
            cost_estimate=pl.CostEstimate(
                flops=2 * units * span * span * half,
                bytes_accessed=4 * half * (height + columns * 2),
                transcendentals=0,
            ),
            name="gram_near" if first else "gram_far",
        )(where, *pieces, vectors, other, *extra)

    before = gram(True, near, ())
    gathered = gram(False, near + distant, (before,))

    mine = lax.dynamic_index_in_dim(gathered, core, 0, keepdims=False)
    send = lax.dynamic_index_in_dim(gathered, 1 - core, 0, keepdims=False)
    mine = mine + core_swap(send)
    members = lax.axis_size("row")
    parts = lax.all_to_all(mine.reshape(members, length // members, WIDE), "row", 0, 0)
    total = jnp.sum(parts, axis=0)
    spread = jnp.broadcast_to(total[None], (members,) + total.shape)
    mine = lax.all_to_all(spread, "row", 0, 0).reshape(length, WIDE)
    theirs = core_swap(mine)

    solved_own, solved_other = pl.pallas_call(
        solve_kernel,
        out_shape=[jax.ShapeDtypeStruct((size, WIDE), F32)] * 2,
        grid_spec=pltpu.PrefetchScalarGridSpec(
            num_scalar_prefetch=1,
            grid=(1,),
            in_specs=[pl.BlockSpec((length, WIDE), lambda j, w: (0, 0))] * 2,
            out_specs=[pl.BlockSpec((size, WIDE), lambda j, w: (0, 0))] * 2,
            scratch_shapes=[pltpu.VMEM((2, length, WIDE), F32)]
            + [pltpu.VMEM((size, size), F32)] * 2
            + [pltpu.VMEM((size, 2 * WIDE), F32)],
        ),
        compiler_params=pltpu.CompilerParams(vmem_limit_bytes=32 << 20),
        name="solve",
    )(where, mine, theirs)

    result_own, result_other = pl.pallas_call(
        apply_kernel,
        out_shape=[jax.ShapeDtypeStruct((half, columns), F32)] * 2,
        grid_spec=pltpu.PrefetchScalarGridSpec(
            num_scalar_prefetch=1,
            grid=(steps,),
            in_specs=[piece] * (2 * CHIPS)
            + [own_spec, other_spec]
            + [pl.BlockSpec((size, WIDE), lambda j, w: (0, 0))] * 2,
            out_specs=[pl.BlockSpec((TILE, columns), lambda j, w: (j, 0))] * 2,
            scratch_shapes=[pltpu.VMEM((size, 2 * WIDE), BF16)] * 3,
        ),
        compiler_params=pltpu.CompilerParams(
            dimension_semantics=("arbitrary",), vmem_limit_bytes=40 << 20
        ),
        name="apply",
    )(where, *near, *distant, vectors, other, solved_own, solved_other)

    returned = core_swap(result_other)
    result = jnp.zeros((rows, columns), F32)
    result = lax.dynamic_update_slice_in_dim(result, result_own, core * half, 0)
    return lax.dynamic_update_slice_in_dim(result, returned, (1 - core) * half, 0)


def solution(mesh):
    specs = (P("row", "col"), P("row", "col"), P("row", "col"))
    return jax.shard_map(
        per_device, mesh=mesh, in_specs=specs, out_specs=P("row", "col"), check_vma=False
    )
```

time: 167 us -> 167 us (level)
  waiting for transfers between devices: 54.1 us -> 44.9 us
  Pallas kernels: 42.1 us -> 46.2 us
  local copies, waits for them, and re-layouts: 11.6 us -> 15.1 us
  starting transfers between devices: 24.7 us -> 27.7 us
  other arithmetic: 3.73 us -> 1.23 us
    ppermute x16 -> x19, waiting for transfers between devices: 54.1 us -> 44.9 us  [permute(): return lax.ppermute(value, 'col', pairs)]
    unnamed x24 -> x42, local copies, waits for them, and re-layouts: 6.02 us -> 9.79 us
    pallas_call x1 -> x2, Pallas kernels: 21 us -> 24.6 us  [gram(): pl.pallas_call(functools.partial(gram_kernel, pieces=len(pieces), first=f...]
    ppermute x16 -> x19, starting transfers between devices: 24.7 us -> 27.7 us  [permute(): return lax.ppermute(value, 'col', pairs)]
    dynamic_slice x1, local copies, waits for them, and re-layouts: 1.45 us -> 3.13 us  [per_device(): given = lax.dynamic_slice_in_dim(vectors, (1 - core) * half, half, 0)]
  transfers between devices with their start and end apart: 16 -> 19, of which waited for: 11 -> 8; matrix products, arithmetic and copies ran while one was open for 2% -> 0% of each run, Pallas kernels for 0% -> 6%
where the time goes in v2:
time: 167 us; the launch traced here: 165 us
  Pallas kernels  46.2 us (28%)
  waiting for transfers between devices  44.9 us (27%)
  blocking collectives  29.5 us (18%)
  starting transfers between devices  27.7 us (17%)
  local copies, waits for them, and re-layouts  15.1 us (9%)
    ppermute x19, waiting for transfers between devices, permute(): return lax.ppermute(value, 'col', pairs)  44.9 us
    ppermute x19, starting transfers between devices, permute(): return lax.ppermute(value, 'col', pairs)  27.7 us
    pallas_call x2, Pallas kernels, gram(): pl.pallas_call(functools.partial(gram_kernel, pieces=len(pieces), first=f...  24.6 us
    all_to_all x1, blocking collectives, per_device(): lax.all_to_all(mine.reshape(members, length // members, WIDE), 'row', 0, 0)  16.4 us
    all_to_all x1, blocking collectives, per_device(): mine = lax.all_to_all(spread, 'row', 0, 0).reshape(length, WIDE)  13.1 us
    pallas_call x1, Pallas kernels, per_device(): pl.pallas_call(apply_kernel, out_shape=[jax.ShapeDtypeStruct((half, colum...  11.5 us
    pallas_call x1, Pallas kernels, per_device(): pl.pallas_call(solve_kernel, out_shape=[jax.ShapeDtypeStruct((size, WIDE)...  10.2 us
    unnamed x42, local copies, waits for them, and re-layouts  9.79 us
  transfers between devices with their start and end apart: 19, of which 8 were waited for; matrix products, arithmetic and copies ran while one was open for 0% of the time, Pallas kernels for 6%

profile of v2, /device:TPU:0, one launch (start us, length us, event | category | flops | bytes accessed | tf_op | source)
XLA Modules:
  0.0 164.9 jit_solution(17620451620029004501)
XLA Ops:
  0.0 3.1 %constant_dynamic-slice_fusion = f32[4096,128]{1,0:T(8,128)} fusion(f32[8192,128]{1,0:T(8,128)} %refs_16_.3, s32[]{:T(128)S(6)} %select_n.69), kind=kLoop, calls=%fused_computation.10 | loop fusion | bytes 4194308 | tf_op jit(solution)/shard_map/dynamic_slice | solution.py:309
  3.1 0.0 collective-permute-start.15
  3.1 0.0 copy-done.19
  3.1 0.1 dynamic-slice_bitcast_fusion.1
  3.3 3.2 %collective-permute-start.5 = (f32[32,4096]{1,0:T(8,128)S(1)}, f32[32,4096]{1,0:T(8,128)S(1)}, u32[]{:S(2)}, u32[]{:S(2)}) collective-permute-start(f32[32,4096]{1,0:T(8,128)S(1)} %pad_maximum_fusion.refs_0_), channel_id=1, source_target_pairs={{0,8},{1,9},{2,10},{3,11},{4,12},{5,13},{6,14},{7,15},{8,0},{9,1},... | collective-permute-start | bytes 1572872 | tf_op jit(solution)/shard_map/ppermute | solution.py:289
  6.5 0.3 collective-permute-start
  6.8 4.0 %collective-permute-start.3 = (f32[32,4096]{1,0:T(8,128)S(1)}, f32[32,4096]{1,0:T(8,128)S(1)}, u32[]{:S(2)}, u32[]{:S(2)}) collective-permute-start(f32[32,4096]{1,0:T(8,128)S(1)} %pad_maximum_fusion.refs_0_), channel_id=1, source_target_pairs={{0,6},{1,7},{2,0},{3,1},{4,2},{5,3},{6,4},{7,5},{8,14},{9,15},{10,... | collective-permute-start | bytes 1572872 | tf_op jit(solution)/shard_map/ppermute | solution.py:289
  10.8 0.0 collective-permute-start.1
  10.8 8.3 %collective-permute-done.5.refs_6_ = f32[32,4096]{1,0:T(8,128)S(1)} collective-permute-done((f32[32,4096]{1,0:T(8,128)S(1)}, f32[32,4096]{1,0:T(8,128)S(1)}, u32[]{:S(2)}, u32[]{:S(2)}) %collective-permute-start.5) | collective-permute-done | bytes 524320 | tf_op jit(solution)/shard_map/ppermute | solution.py:289
  19.2 4.1 %collective-permute-start.11 = (f32[32,4096]{1,0:T(8,128)S(1)}, f32[32,4096]{1,0:T(8,128)S(1)}, u32[]{:S(2)}, u32[]{:S(2)}) collective-permute-start(f32[32,4096]{1,0:T(8,128)S(1)} %collective-permute-done.5.refs_6_), channel_id=1, source_target_pairs={{0,6},{1,7},{2,0},{3,1},{4,2},{5,3},{6,4},{7,5},{8,14},{9,15},{10,... | collective-permute-start | bytes 1572872 | tf_op jit(solution)/shard_map/ppermute | solution.py:289
  23.3 0.0 collective-permute-done.refs_1_
  23.3 0.4 collective-permute-start.4
  23.7 0.0 collective-permute-done.3.refs_4_
  23.7 0.8 copy-done.7
  24.5 1.6 collective-permute-start.9
  26.1 0.0 collective-permute-done.1.refs_2_
  26.1 3.0 %collective-permute-start.6 = (f32[32,4096]{1,0:T(8,128)S(1)}, f32[32,4096]{1,0:T(8,128)S(1)}, u32[]{:S(2)}, u32[]{:S(2)}) collective-permute-start(f32[32,4096]{1,0:T(8,128)S(1)} %collective-permute-done.refs_1_), channel_id=1, source_target_pairs={{0,8},{1,9},{2,10},{3,11},{4,12},{5,13},{6,14},{7,15},{8,0},{9,1},... | collective-permute-start | bytes 1572872 | tf_op jit(solution)/shard_map/ppermute | solution.py:289
  29.2 6.5 %collective-permute-done.11.refs_12_ = f32[32,4096]{1,0:T(8,128)S(1)} collective-permute-done((f32[32,4096]{1,0:T(8,128)S(1)}, f32[32,4096]{1,0:T(8,128)S(1)}, u32[]{:S(2)}, u32[]{:S(2)}) %collective-permute-start.11) | collective-permute-done | bytes 524320 | tf_op jit(solution)/shard_map/ppermute | solution.py:289
  35.7 0.8 copy-done.11
  36.5 0.3 collective-permute-start.2
  36.8 0.8 copy-done.3
  37.6 7.9 %collective-permute-done.4.refs_5_ = f32[32,4096]{1,0:T(8,128)} collective-permute-done((f32[32,4096]{1,0:T(8,128)S(1)}, f32[32,4096]{1,0:T(8,128)}, u32[]{:S(2)}, u32[]{:S(2)}) %collective-permute-start.4) | collective-permute-done | bytes 524320 | tf_op jit(solution)/shard_map/ppermute | solution.py:289
  45.6 3.8 %collective-permute-start.8 = (f32[32,4096]{1,0:T(8,128)}, f32[32,4096]{1,0:T(8,128)}, u32[]{:S(2)}, u32[]{:S(2)}) collective-permute-start(f32[32,4096]{1,0:T(8,128)} %collective-permute-done.4.refs_5_), channel_id=1, source_target_pairs={{0,6},{1,7},{2,0},{3,1},{4,2},{5,3},{6,4},{7,5},{8,14},{9,15},{10,... | collective-permute-start | bytes 1572872 | tf_op jit(solution)/shard_map/ppermute | solution.py:289
  49.4 0.0 collective-permute-done.9.refs_10_
  49.4 0.0 collective-permute-start.7
  49.4 0.0 collective-permute-done.6.refs_7_
  49.4 0.8 copy-done.14
  50.2 3.0 %collective-permute-start.12 = (f32[32,4096]{1,0:T(8,128)}, f32[32,4096]{1,0:T(8,128)}, u32[]{:S(2)}, u32[]{:S(2)}) collective-permute-start(f32[32,4096]{1,0:T(8,128)} %collective-permute-done.4.refs_5_), channel_id=1, source_target_pairs={{0,8},{1,9},{2,10},{3,11},{4,12},{5,13},{6,14},{7,15},{8,0},{9,1},... | collective-permute-start | bytes 1572872 | tf_op jit(solution)/shard_map/ppermute | solution.py:289
  53.3 0.0 collective-permute-done.2.refs_3_
  53.3 0.0 collective-permute-start.13
  53.3 6.6 %collective-permute-done.8.refs_9_ = f32[32,4096]{1,0:T(8,128)} collective-permute-done((f32[32,4096]{1,0:T(8,128)}, f32[32,4096]{1,0:T(8,128)}, u32[]{:S(2)}, u32[]{:S(2)}) %collective-permute-start.8) | collective-permute-done | bytes 524320 | tf_op jit(solution)/shard_map/ppermute | solution.py:289
  59.9 3.0 %collective-permute-start.10 = (f32[32,4096]{1,0:T(8,128)}, f32[32,4096]{1,0:T(8,128)}, u32[]{:S(2)}, u32[]{:S(2)}) collective-permute-start(f32[32,4096]{1,0:T(8,128)} %collective-permute-done.2.refs_3_), channel_id=1, source_target_pairs={{0,8},{1,9},{2,10},{3,11},{4,12},{5,13},{6,14},{7,15},{8,0},{9,1},... | collective-permute-start | bytes 1572872 | tf_op jit(solution)/shard_map/ppermute | solution.py:289
  62.9 0.0 collective-permute-done.15.refs_9_.refs_17_
  62.9 0.5 collective-permute-start.14
  63.4 0.1 stack.39.where_ref
  63.5 2.3 %copy-done = f32[8192,128]{1,0:T(8,128)S(1)} copy-done((f32[8192,128]{1,0:T(8,128)S(1)}, f32[8192,128]{1,0:T(8,128)}, u32[]{:S(2)}) %copy-start) | copy-done | bytes 4194328
  65.8 1.0 copy-done.4
  66.9 1.0 copy-done.8
  67.9 1.0 copy-done.15
  69.0 9.9 %gram_near.1.refs_18_ = f32[2,640,128]{2,1,0:T(8,128)S(1)} custom-call(s32[9]{0:T(128)S(1)} %stack.39.where_ref, f32[32,4096]{1,0:T(8,128)S(1)} %pad_maximum_fusion.refs_0_, f32[32,4096]{1,0:T(8,128)S(1)} %copy-done.4, f32[32,4096]{1,0:T(8,128)} %collective-permute-done.1.refs_2_, f32[32,4096]{1,0:T(8,128)} %collective-permute-done.2.refs_3_, ...), custom_call_target="tpu_custom_call" | custom-call | flops 5368709120 | bytes 8388608 | tf_op jit(solution)/shard_map/gram_near/pallas_call | solution.py:345
  78.9 0.0 collective-permute-done.7.refs_8_
  78.9 0.0 collective-permute-done.13.refs_14_
  78.9 0.0 collective-permute-done.12.refs_13_
  78.9 0.0 collective-permute-done.10.refs_11_
  78.9 8.0 %collective-permute-done.14.refs_15_ = f32[32,4096]{1,0:T(8,128)} collective-permute-done((f32[32,4096]{1,0:T(8,128)}, f32[32,4096]{1,0:T(8,128)}, u32[]{:S(2)}, u32[]{:S(2)}) %collective-permute-start.14) | collective-permute-done | bytes 524320 | tf_op jit(solution)/shard_map/ppermute | solution.py:289
  86.9 0.0 copy-done.1
  86.9 14.6 %gram_far.1 = f32[2,1152,128]{2,1,0:T(8,128)S(1)} custom-call(s32[9]{0:T(128)S(1)} %stack.39.where_ref, f32[32,4096]{1,0:T(8,128)S(1)} %pad_maximum_fusion.refs_0_, f32[32,4096]{1,0:T(8,128)S(1)} %copy-done.5, f32[32,4096]{1,0:T(8,128)} %collective-permute-done.1.refs_2_, f32[32,4096]{1,0:T(8,128)} %collective-permute-done.2.refs_3_, ...), custom_call_target="tpu_custom_call" | custom-call | flops 8589934592 | bytes 12582912 | tf_op jit(solution)/shard_map/gram_far/pallas_call | solution.py:345
  101.6 1.0 copy-done.2
  102.7 0.1 collective-permute-start.16
  102.8 2.0 %collective-permute-done.16 = f32[1152,128]{1,0:T(8,128)S(1)} collective-permute-done((f32[1152,128]{1,0:T(8,128)S(1)}, f32[1152,128]{1,0:T(8,128)S(1)}, u32[]{:S(2)}, u32[]{:S(2)}) %collective-permute-start.16) | collective-permute-done | bytes 589856 | tf_op jit(solution)/shard_map/ppermute | solution.py:289
  104.7 1.1 bitcast_add_fusion
  105.9 16.4 %all_to_all.10 = f32[8,144,128]{2,1,0:T(8,128)S(1)} all-to-all(f32[8,144,128]{2,1,0:T(8,128)S(1)} %bitcast.25), channel_id=1, replica_groups=mesh['row'=8,'col'=16] {'row'}, dimensions={0} | all-to-all | bytes 1179648 | tf_op jit(solution)/shard_map/all_to_all | solution.py:378
  122.4 13.1 %all_to_all.11 = f32[8,144,128]{2,1,0:T(8,128)S(1)} all-to-all(f32[8,144,128]{2,1,0:T(8,128)S(1)} %broadcast_in_dim.10), channel_id=1, replica_groups=mesh['row'=8,'col'=16] {'row'}, dimensions={0} | all-to-all | bytes 1179648 | tf_op jit(solution)/shard_map/all_to_all | solution.py:381
  135.5 0.0 collective-permute-start.17
  135.5 2.0 %collective-permute-done.17.other_ref = f32[1152,128]{1,0:T(8,128)S(1)} collective-permute-done((f32[1152,128]{1,0:T(8,128)S(1)}, f32[1152,128]{1,0:T(8,128)S(1)}, u32[]{:S(2)}, u32[]{:S(2)}) %collective-permute-start.17) | collective-permute-done | bytes 589856 | tf_op jit(solution)/shard_map/ppermute | solution.py:289
  137.5 10.2 %solve.1 = (f32[512,128]{1,0:T(8,128)S(1)}, f32[512,128]{1,0:T(8,128)S(1)}) custom-call(s32[9]{0:T(128)S(1)} %stack.39.where_ref, f32[1152,128]{1,0:T(8,128)S(1)} %bitcast.24, f32[1152,128]{1,0:T(8,128)S(1)} %collective-permute-done.17.other_ref), custom_call_target="tpu_custom_call" | custom-call | tf_op jit(solution)/shard_map/solve/pallas_call | solution.py:384
  147.8 11.5 %apply.1 = (f32[4096,128]{1,0:T(8,128)S(1)}, f32[4096,128]{1,0:T(8,128)S(1)}) custom-call(s32[9]{0:T(128)S(1)} %stack.39.where_ref, f32[32,4096]{1,0:T(8,128)S(1)} %pad_maximum_fusion.refs_0_, f32[32,4096]{1,0:T(8,128)S(1)} %copy-done.6, f32[32,4096]{1,0:T(8,128)} %collective-permute-done.1.refs_2_, f32[32,4096]{1,0:T(8,128)} %collective-permute-done.2.refs_3_, ...), custom_call_target="tpu_custom_call" | custom-call | tf_op jit(solution)/shard_map/apply/pallas_call | solution.py:400
  159.2 0.2 collective-permute-start.18
  159.4 0.3 broadcast_in_dim.4
  159.7 0.2 constant_dynamic-update-slice_fusion.1
  159.9 0.0 copy-start.18
  159.9 3.6 %collective-permute-done.18 = f32[4096,128]{1,0:T(8,128)S(1)} collective-permute-done((f32[4096,128]{1,0:T(8,128)S(1)}, f32[4096,128]{1,0:T(8,128)S(1)}, u32[]{:S(2)}, u32[]{:S(2)}) %collective-permute-start.18) | collective-permute-done | bytes 2097184 | tf_op jit(solution)/shard_map/ppermute | solution.py:289
  163.5 0.0 copy-done.18
  163.5 1.5 constant_dynamic-update-slice_fusion
  (34 shorter events, 0.2 us)
Async XLA Ops:
  0.0 3.1 %copy-start.19 = (f32[8192,16]{0,1:T(8,128)S(1)}, f32[8192,16]{0,1:T(8,128)}, u32[]{:S(2)}) copy-start(f32[8192,16]{0,1:T(8,128)} %param.5) | copy-start | bytes 1572868
  0.0 3.1 %copy-start.20 = (f32[8192,16]{0,1:T(8,128)S(1)}, f32[8192,16]{0,1:T(8,128)}, u32[]{:S(2)}) copy-start(f32[8192,16]{0,1:T(8,128)} %param.4) | copy-start | bytes 1572868
  3.1 59.8 %collective-permute-start.15 = (f32[4096,128]{1,0:T(8,128)}, f32[4096,128]{1,0:T(8,128)S(1)}, u32[]{:S(2)}, u32[]{:S(2)}) collective-permute-start(f32[4096,128]{1,0:T(8,128)} %constant_dynamic-slice_fusion), channel_id=1, source_target_pairs={{0,1},{1,0},{2,3},{3,2},{4,5},{5,4},{6,7},{7,6},{8,9},{9,8},{10,11... | collective-permute-start | bytes 6291464 | tf_op jit(solution)/shard_map/ppermute | solution.py:289
  3.3 15.9 %collective-permute-start.5 = (f32[32,4096]{1,0:T(8,128)S(1)}, f32[32,4096]{1,0:T(8,128)S(1)}, u32[]{:S(2)}, u32[]{:S(2)}) collective-permute-start(f32[32,4096]{1,0:T(8,128)S(1)} %pad_maximum_fusion.refs_0_), channel_id=1, source_target_pairs={{0,8},{1,9},{2,10},{3,11},{4,12},{5,13},{6,14},{7,15},{8,0},{9,1},... | collective-permute-start | bytes 1572872 | tf_op jit(solution)/shard_map/ppermute | solution.py:289
  6.5 16.8 %collective-permute-start = (f32[32,4096]{1,0:T(8,128)S(1)}, f32[32,4096]{1,0:T(8,128)S(1)}, u32[]{:S(2)}, u32[]{:S(2)}) collective-permute-start(f32[32,4096]{1,0:T(8,128)S(1)} %pad_maximum_fusion.1), channel_id=1, source_target_pairs={{0,1},{1,0},{2,3},{3,2},{4,5},{5,4},{6,7},{7,6},{8,9},{9,8},{10,11... | collective-permute-start | bytes 1572872 | tf_op jit(solution)/shard_map/ppermute | solution.py:289
  6.8 16.9 %collective-permute-start.3 = (f32[32,4096]{1,0:T(8,128)S(1)}, f32[32,4096]{1,0:T(8,128)S(1)}, u32[]{:S(2)}, u32[]{:S(2)}) collective-permute-start(f32[32,4096]{1,0:T(8,128)S(1)} %pad_maximum_fusion.refs_0_), channel_id=1, source_target_pairs={{0,6},{1,7},{2,0},{3,1},{4,2},{5,3},{6,4},{7,5},{8,14},{9,15},{10,... | collective-permute-start | bytes 1572872 | tf_op jit(solution)/shard_map/ppermute | solution.py:289
  10.8 15.3 %collective-permute-start.1 = (f32[32,4096]{1,0:T(8,128)S(1)}, f32[32,4096]{1,0:T(8,128)}, u32[]{:S(2)}, u32[]{:S(2)}) collective-permute-start(f32[32,4096]{1,0:T(8,128)S(1)} %pad_maximum_fusion.refs_0_), channel_id=1, source_target_pairs={{0,2},{1,3},{2,4},{3,5},{4,6},{5,7},{6,0},{7,1},{8,10},{9,11},{10,... | collective-permute-start | bytes 1572872 | tf_op jit(solution)/shard_map/ppermute | solution.py:289
  19.2 16.5 %collective-permute-start.11 = (f32[32,4096]{1,0:T(8,128)S(1)}, f32[32,4096]{1,0:T(8,128)S(1)}, u32[]{:S(2)}, u32[]{:S(2)}) collective-permute-start(f32[32,4096]{1,0:T(8,128)S(1)} %collective-permute-done.5.refs_6_), channel_id=1, source_target_pairs={{0,6},{1,7},{2,0},{3,1},{4,2},{5,3},{6,4},{7,5},{8,14},{9,15},{10,... | collective-permute-start | bytes 1572872 | tf_op jit(solution)/shard_map/ppermute | solution.py:289
  23.3 22.3 %collective-permute-start.4 = (f32[32,4096]{1,0:T(8,128)S(1)}, f32[32,4096]{1,0:T(8,128)}, u32[]{:S(2)}, u32[]{:S(2)}) collective-permute-start(f32[32,4096]{1,0:T(8,128)S(1)} %collective-permute-done.refs_1_), channel_id=1, source_target_pairs={{0,6},{1,7},{2,0},{3,1},{4,2},{5,3},{6,4},{7,5},{8,14},{9,15},{10,... | collective-permute-start | bytes 1572872 | tf_op jit(solution)/shard_map/ppermute | solution.py:289
  23.7 0.8 copy-start.7
  24.5 24.9 %collective-permute-start.9 = (f32[32,4096]{1,0:T(8,128)S(1)}, f32[32,4096]{1,0:T(8,128)}, u32[]{:S(2)}, u32[]{:S(2)}) collective-permute-start(f32[32,4096]{1,0:T(8,128)S(1)} %collective-permute-done.5.refs_6_), channel_id=1, source_target_pairs={{0,2},{1,3},{2,4},{3,5},{4,6},{5,7},{6,0},{7,1},{8,10},{9,11},{10,... | collective-permute-start | bytes 1572872 | tf_op jit(solution)/shard_map/ppermute | solution.py:289
  26.1 23.3 %collective-permute-start.6 = (f32[32,4096]{1,0:T(8,128)S(1)}, f32[32,4096]{1,0:T(8,128)S(1)}, u32[]{:S(2)}, u32[]{:S(2)}) collective-permute-start(f32[32,4096]{1,0:T(8,128)S(1)} %collective-permute-done.refs_1_), channel_id=1, source_target_pairs={{0,8},{1,9},{2,10},{3,11},{4,12},{5,13},{6,14},{7,15},{8,0},{9,1},... | collective-permute-start | bytes 1572872 | tf_op jit(solution)/shard_map/ppermute | solution.py:289
  35.6 0.8 copy-start.11
  36.5 16.8 %collective-permute-start.2 = (f32[32,4096]{1,0:T(8,128)S(1)}, f32[32,4096]{1,0:T(8,128)}, u32[]{:S(2)}, u32[]{:S(2)}) collective-permute-start(f32[32,4096]{1,0:T(8,128)S(1)} %collective-permute-done.refs_1_), channel_id=1, source_target_pairs={{0,2},{1,3},{2,4},{3,5},{4,6},{5,7},{6,0},{7,1},{8,10},{9,11},{10,... | collective-permute-start | bytes 1572872 | tf_op jit(solution)/shard_map/ppermute | solution.py:289
  36.8 0.9 copy-start.3
  45.6 14.3 %collective-permute-start.8 = (f32[32,4096]{1,0:T(8,128)}, f32[32,4096]{1,0:T(8,128)}, u32[]{:S(2)}, u32[]{:S(2)}) collective-permute-start(f32[32,4096]{1,0:T(8,128)} %collective-permute-done.4.refs_5_), channel_id=1, source_target_pairs={{0,6},{1,7},{2,0},{3,1},{4,2},{5,3},{6,4},{7,5},{8,14},{9,15},{10,... | collective-permute-start | bytes 1572872 | tf_op jit(solution)/shard_map/ppermute | solution.py:289
  49.4 29.5 %collective-permute-start.7 = (f32[32,4096]{1,0:T(8,128)}, f32[32,4096]{1,0:T(8,128)}, u32[]{:S(2)}, u32[]{:S(2)}) collective-permute-start(f32[32,4096]{1,0:T(8,128)} %collective-permute-done.1.refs_2_), channel_id=1, source_target_pairs={{0,2},{1,3},{2,4},{3,5},{4,6},{5,7},{6,0},{7,1},{8,10},{9,11},{10,... | collective-permute-start | bytes 1572872 | tf_op jit(solution)/shard_map/ppermute | solution.py:289
  49.4 0.8 copy-start.14
  50.2 28.7 %collective-permute-start.12 = (f32[32,4096]{1,0:T(8,128)}, f32[32,4096]{1,0:T(8,128)}, u32[]{:S(2)}, u32[]{:S(2)}) collective-permute-start(f32[32,4096]{1,0:T(8,128)} %collective-permute-done.4.refs_5_), channel_id=1, source_target_pairs={{0,8},{1,9},{2,10},{3,11},{4,12},{5,13},{6,14},{7,15},{8,0},{9,1},... | collective-permute-start | bytes 1572872 | tf_op jit(solution)/shard_map/ppermute | solution.py:289
  53.3 25.6 %collective-permute-start.13 = (f32[32,4096]{1,0:T(8,128)}, f32[32,4096]{1,0:T(8,128)}, u32[]{:S(2)}, u32[]{:S(2)}) collective-permute-start(f32[32,4096]{1,0:T(8,128)} %collective-permute-done.9.refs_10_), channel_id=1, source_target_pairs={{0,2},{1,3},{2,4},{3,5},{4,6},{5,7},{6,0},{7,1},{8,10},{9,11},{10,... | collective-permute-start | bytes 1572872 | tf_op jit(solution)/shard_map/ppermute | solution.py:289
  59.9 19.0 %collective-permute-start.10 = (f32[32,4096]{1,0:T(8,128)}, f32[32,4096]{1,0:T(8,128)}, u32[]{:S(2)}, u32[]{:S(2)}) collective-permute-start(f32[32,4096]{1,0:T(8,128)} %collective-permute-done.2.refs_3_), channel_id=1, source_target_pairs={{0,8},{1,9},{2,10},{3,11},{4,12},{5,13},{6,14},{7,15},{8,0},{9,1},... | collective-permute-start | bytes 1572872 | tf_op jit(solution)/shard_map/ppermute | solution.py:289
  62.9 24.0 %copy-start.1 = (f32[4096,128]{1,0:T(8,128)}, f32[4096,128]{1,0:T(8,128)S(1)}, u32[]{:S(2)}) copy-start(f32[4096,128]{1,0:T(8,128)S(1)} %collective-permute-done.15.refs_9_.refs_17_) | copy-start | bytes 6291460
  62.9 24.0 %collective-permute-start.14 = (f32[32,4096]{1,0:T(8,128)}, f32[32,4096]{1,0:T(8,128)}, u32[]{:S(2)}, u32[]{:S(2)}) collective-permute-start(f32[32,4096]{1,0:T(8,128)} %collective-permute-done.8.refs_9_), channel_id=1, source_target_pairs={{0,8},{1,9},{2,10},{3,11},{4,12},{5,13},{6,14},{7,15},{8,0},{9,1},... | collective-permute-start | bytes 1572872 | tf_op jit(solution)/shard_map/ppermute | solution.py:289
  63.5 2.3 %copy-start = (f32[8192,128]{1,0:T(8,128)S(1)}, f32[8192,128]{1,0:T(8,128)}, u32[]{:S(2)}) copy-start(f32[8192,128]{1,0:T(8,128)} %refs_16_.3) | copy-start | bytes 12582916
  65.8 1.0 copy-start.4
  66.9 1.0 copy-start.8
  67.9 1.0 copy-start.15
  68.9 18.0 %copy-start.5 = (f32[32,4096]{1,0:T(8,128)S(1)}, f32[32,4096]{1,0:T(8,128)}, u32[]{:S(2)}) copy-start(f32[32,4096]{1,0:T(8,128)} %copy-done.3) | copy-start | bytes 1572868
  68.9 18.0 %copy-start.9 = (f32[32,4096]{1,0:T(8,128)S(1)}, f32[32,4096]{1,0:T(8,128)}, u32[]{:S(2)}) copy-start(f32[32,4096]{1,0:T(8,128)} %copy-done.7) | copy-start | bytes 1572868
  68.9 18.0 %copy-start.12 = (f32[32,4096]{1,0:T(8,128)S(1)}, f32[32,4096]{1,0:T(8,128)}, u32[]{:S(2)}) copy-start(f32[32,4096]{1,0:T(8,128)} %copy-done.11) | copy-start | bytes 1572868
  69.0 18.0 %copy-start.16 = (f32[32,4096]{1,0:T(8,128)S(1)}, f32[32,4096]{1,0:T(8,128)}, u32[]{:S(2)}) copy-start(f32[32,4096]{1,0:T(8,128)} %copy-done.14) | copy-start | bytes 1572868
  101.6 1.0 copy-start.2
  102.7 2.1 %collective-permute-start.16 = (f32[1152,128]{1,0:T(8,128)S(1)}, f32[1152,128]{1,0:T(8,128)S(1)}, u32[]{:S(2)}, u32[]{:S(2)}) collective-permute-start(f32[1152,128]{1,0:T(8,128)S(1)} %dynamic-slice_bitcast_fusion), channel_id=1, source_target_pairs={{0,1},{1,0},{2,3},{3,2},{4,5},{5,4},{6,7},{7,6},{8,9},{9,8},{10,11... | collective-permute-start | bytes 1769480 | tf_op jit(solution)/shard_map/ppermute | solution.py:289
  122.3 25.4 %copy-start.6 = (f32[32,4096]{1,0:T(8,128)S(1)}, f32[32,4096]{1,0:T(8,128)}, u32[]{:S(2)}) copy-start(f32[32,4096]{1,0:T(8,128)} %copy-done.3) | copy-start | bytes 1572868
  122.3 25.4 %copy-start.10 = (f32[32,4096]{1,0:T(8,128)S(1)}, f32[32,4096]{1,0:T(8,128)}, u32[]{:S(2)}) copy-start(f32[32,4096]{1,0:T(8,128)} %copy-done.7) | copy-start | bytes 1572868
  122.3 25.4 %copy-start.13 = (f32[32,4096]{1,0:T(8,128)S(1)}, f32[32,4096]{1,0:T(8,128)}, u32[]{:S(2)}) copy-start(f32[32,4096]{1,0:T(8,128)} %copy-done.11) | copy-start | bytes 1572868
  122.3 25.4 %copy-start.17 = (f32[32,4096]{1,0:T(8,128)S(1)}, f32[32,4096]{1,0:T(8,128)}, u32[]{:S(2)}) copy-start(f32[32,4096]{1,0:T(8,128)} %copy-done.14) | copy-start | bytes 1572868
  135.5 2.0 %collective-permute-start.17 = (f32[1152,128]{1,0:T(8,128)S(1)}, f32[1152,128]{1,0:T(8,128)S(1)}, u32[]{:S(2)}, u32[]{:S(2)}) collective-permute-start(f32[1152,128]{1,0:T(8,128)S(1)} %bitcast.23), channel_id=1, source_target_pairs={{0,1},{1,0},{2,3},{3,2},{4,5},{5,4},{6,7},{7,6},{8,9},{9,8},{10,11... | collective-permute-start | bytes 1769480 | tf_op jit(solution)/shard_map/ppermute | solution.py:289
  159.2 4.2 %collective-permute-start.18 = (f32[4096,128]{1,0:T(8,128)S(1)}, f32[4096,128]{1,0:T(8,128)S(1)}, u32[]{:S(2)}, u32[]{:S(2)}) collective-permute-start(f32[4096,128]{1,0:T(8,128)S(1)} %get-tuple-element.12), channel_id=1, source_target_pairs={{0,1},{1,0},{2,3},{3,2},{4,5},{5,4},{6,7},{7,6},{8,9},{9,8},{10,11... | collective-permute-start | bytes 6291464 | tf_op jit(solution)/shard_map/ppermute | solution.py:289
  159.9 3.6 %copy-start.18 = (f32[8192,128]{1,0:T(8,128)}, f32[8192,128]{1,0:T(8,128)S(1)}, u32[]{:S(2)}) copy-start(f32[8192,128]{1,0:T(8,128)S(1)} %constant_dynamic-update-slice_fusion.1) | copy-start | bytes 12582916

commit v3 on v2

--- a/solution.py
+++ b/solution.py
@@ -304,19 +304,31 @@
         picked = [lax.dynamic_slice_in_dim(v.T, which * half, half, 1) for v in (panel_one, panel_two)]
         return jnp.concatenate(picked, axis=0)
 
+    barrier = lax.optimization_barrier
     a_own = half_of(core)
-    b_own = core_swap(half_of(1 - core))
-    given = lax.dynamic_slice_in_dim(vectors, (1 - core) * half, half, 0)
+    swapped = half_of(1 - core)
+    b_own = core_swap(swapped)
+    offset, _ = barrier(((1 - core) * half, swapped))
+    given = lax.dynamic_slice_in_dim(vectors, offset, half, 0)
     other = core_swap(given)
 
-    a_away, a_below, a_above = across(a_own), up(a_own), down(a_own)
-    b_away, b_below, b_above = across(b_own), up(b_own), down(b_own)
+    a_own, b_own, given = barrier((a_own, b_own, given))
+    a_away, a_below, a_above, b_away = across(a_own), up(a_own), down(a_own), across(b_own)
+    b_hold, other = barrier((b_own, other))
+    b_below = up(b_hold)
+
+    a_away, a_below, a_above, b_hold = barrier((a_away, a_below, a_above, b_hold))
+    b_above = down(b_hold)
     a_away_below = up(a_away)
-    a_away_above = down(a_away)
     a_far = up(a_below)
+
+    b_away, b_below, b_above, a_hold = barrier((b_away, b_below, b_above, a_away))
     b_away_below = across(b_below)
     b_far = down(b_above)
-    b_away_above = across(b_above)
+    a_away_above = down(a_hold)
+
+    a_away_below, b_above_hold = barrier((a_away_below, b_above))
+    b_away_above = across(b_above_hold)
     a_away_far = up(a_away_below)
     b_away_far = across(b_far)
 
@@ -358,7 +370,7 @@
                 ],
             ),
             compiler_params=pltpu.CompilerParams(
-                dimension_semantics=("arbitrary",), vmem_limit_bytes=32 << 20
+                dimension_semantics=("arbitrary",), vmem_limit_bytes=56 << 20
             ),
             cost_estimate=pl.CostEstimate(
                 flops=2 * units * span * span * half,
@@ -410,7 +422,7 @@
             scratch_shapes=[pltpu.VMEM((size, 2 * WIDE), BF16)] * 3,
         ),
         compiler_params=pltpu.CompilerParams(
-            dimension_semantics=("arbitrary",), vmem_limit_bytes=40 << 20
+            dimension_semantics=("arbitrary",), vmem_limit_bytes=56 << 20
         ),
         name="apply",
     )(where, *near, *distant, vectors, other, solved_own, solved_other)

time: 167 us -> 178 us (1.066)
  waiting for transfers between devices: 44.9 us -> 60.2 us
  local copies, waits for them, and re-layouts: 15.1 us -> 9.44 us
  Pallas kernels: 46.2 us -> 51.8 us
  starting transfers between devices: 27.7 us -> 23.4 us
    ppermute x19, waiting for transfers between devices: 44.9 us -> 60.2 us  [permute(): return lax.ppermute(value, 'col', pairs)]
    unnamed x42 -> x24, local copies, waits for them, and re-layouts: 9.79 us -> 2.77 us
    ppermute x19, starting transfers between devices: 27.7 us -> 23.4 us  [permute(): return lax.ppermute(value, 'col', pairs)]
    pallas_call x2, Pallas kernels: 24.6 us -> 28.2 us  [gram(): pl.pallas_call(functools.partial(gram_kernel, pieces=len(pieces), first=f...]
    pallas_call x1, Pallas kernels: 11.5 us -> 13.4 us  [per_device(): pl.pallas_call(apply_kernel, out_shape=[jax.ShapeDtypeStruct((half, colum...]
  transfers between devices with their start and end apart: 19 -> 19, of which waited for: 8 -> 14; matrix products, arithmetic and copies ran while one was open for 0% -> 1% of each run, Pallas kernels for 6% -> 7%
where the time goes in v3:
time: 178 us; the launch traced here: 176 us
  waiting for transfers between devices  60.2 us (34%)
  Pallas kernels  51.8 us (29%)
  blocking collectives  29.4 us (17%)
  starting transfers between devices  23.4 us (13%)
  local copies, waits for them, and re-layouts  9.44 us (5%)
  other arithmetic  2.05 us (1%)
    ppermute x19, waiting for transfers between devices, permute(): return lax.ppermute(value, 'col', pairs)  60.2 us
    pallas_call x2, Pallas kernels, gram(): pl.pallas_call(functools.partial(gram_kernel, pieces=len(pieces), first=f...  28.2 us
    ppermute x19, starting transfers between devices, permute(): return lax.ppermute(value, 'col', pairs)  23.4 us
    all_to_all x1, blocking collectives, per_device(): lax.all_to_all(mine.reshape(members, length // members, WIDE), 'row', 0, 0)  16.4 us
    pallas_call x1, Pallas kernels, per_device(): pl.pallas_call(apply_kernel, out_shape=[jax.ShapeDtypeStruct((half, colum...  13.4 us
    all_to_all x1, blocking collectives, per_device(): mine = lax.all_to_all(spread, 'row', 0, 0).reshape(length, WIDE)  13 us
    pallas_call x1, Pallas kernels, per_device(): pl.pallas_call(solve_kernel, out_shape=[jax.ShapeDtypeStruct((size, WIDE)...  10.2 us
  transfers between devices with their start and end apart: 19, of which 14 were waited for; matrix products, arithmetic and copies ran while one was open for 1% of the time, Pallas kernels for 7%

profile of v3, /device:TPU:0, one launch (start us, length us, event | category | flops | bytes accessed | tf_op | source)
XLA Modules:
  0.0 176.4 jit_solution(5736744190667695752)
XLA Ops:
  0.0 1.3 dynamic-slice_bitcast_fusion.1
  1.3 0.8 pad_maximum_fusion.1
  2.1 1.8 constant_dynamic-slice_fusion
  3.9 0.1 collective-permute-start.4
  3.9 0.5 collective-permute-start
  4.5 0.0 copy-start.4
  4.5 4.2 %collective-permute-done.refs_1_ = f32[32,4096]{1,0:T(8,128)S(1)} collective-permute-done((f32[32,4096]{1,0:T(8,128)}, f32[32,4096]{1,0:T(8,128)S(1)}, u32[]{:S(2)}, u32[]{:S(2)}) %collective-permute-start) | collective-permute-done | bytes 524320 | tf_op jit(solution)/shard_map/ppermute | solution.py:289
  8.7 4.1 %collective-permute-start.3 = (f32[32,4096]{1,0:T(8,128)S(1)}, f32[32,4096]{1,0:T(8,128)S(1)}, u32[]{:S(2)}, u32[]{:S(2)}) collective-permute-start(f32[32,4096]{1,0:T(8,128)S(1)} %pad_maximum_fusion.refs_0_), channel_id=1, source_target_pairs={{0,6},{1,7},{2,0},{3,1},{4,2},{5,3},{6,4},{7,5},{8,14},{9,15},{10,... | collective-permute-start | bytes 1572872 | tf_op jit(solution)/shard_map/ppermute | solution.py:289
  12.8 0.0 collective-permute-start.2
  12.8 3.0 %collective-permute-start.1 = (f32[32,4096]{1,0:T(8,128)S(1)}, f32[32,4096]{1,0:T(8,128)}, u32[]{:S(2)}, u32[]{:S(2)}) collective-permute-start(f32[32,4096]{1,0:T(8,128)S(1)} %pad_maximum_fusion.refs_0_), channel_id=1, source_target_pairs={{0,8},{1,9},{2,10},{3,11},{4,12},{5,13},{6,14},{7,15},{8,0},{9,1},... | collective-permute-start | bytes 1572872 | tf_op jit(solution)/shard_map/ppermute | solution.py:289
  15.9 0.5 collective-permute-start.5
  16.4 0.0 collective-permute-done.4.refs_9_.refs_17_
  16.4 8.2 %collective-permute-done.3.refs_4_ = f32[32,4096]{1,0:T(8,128)S(1)} collective-permute-done((f32[32,4096]{1,0:T(8,128)S(1)}, f32[32,4096]{1,0:T(8,128)S(1)}, u32[]{:S(2)}, u32[]{:S(2)}) %collective-permute-start.3) | collective-permute-done | bytes 524320 | tf_op jit(solution)/shard_map/ppermute | solution.py:289
  24.5 3.4 %collective-permute-done.2.refs_2_ = f32[32,4096]{1,0:T(8,128)S(1)} collective-permute-done((f32[32,4096]{1,0:T(8,128)S(1)}, f32[32,4096]{1,0:T(8,128)S(1)}, u32[]{:S(2)}, u32[]{:S(2)}) %collective-permute-start.2) | collective-permute-done | bytes 524320 | tf_op jit(solution)/shard_map/ppermute | solution.py:289
  27.9 1.3 collective-permute-done.1.refs_6_
  29.2 3.3 %collective-permute-start.7 = (f32[32,4096]{1,0:T(8,128)S(1)}, f32[32,4096]{1,0:T(8,128)}, u32[]{:S(2)}, u32[]{:S(2)}) collective-permute-start(f32[32,4096]{1,0:T(8,128)S(1)} %collective-permute-done.refs_1_), channel_id=1, source_target_pairs={{0,6},{1,7},{2,0},{3,1},{4,2},{5,3},{6,4},{7,5},{8,14},{9,15},{10,... | collective-permute-start | bytes 1572872 | tf_op jit(solution)/shard_map/ppermute | solution.py:289
  32.5 0.0 copy-done.7
  32.5 0.0 collective-permute-start.6
  32.5 0.0 collective-permute-start.10
  32.5 1.4 collective-permute-start.8
  33.9 5.6 %collective-permute-done.5.refs_7_ = f32[32,4096]{1,0:T(8,128)S(1)} collective-permute-done((f32[32,4096]{1,0:T(8,128)S(1)}, f32[32,4096]{1,0:T(8,128)S(1)}, u32[]{:S(2)}, u32[]{:S(2)}) %collective-permute-start.5) | collective-permute-done | bytes 524320 | tf_op jit(solution)/shard_map/ppermute | solution.py:289
  39.5 2.1 %collective-permute-done.7.refs_5_ = f32[32,4096]{1,0:T(8,128)} collective-permute-done((f32[32,4096]{1,0:T(8,128)S(1)}, f32[32,4096]{1,0:T(8,128)}, u32[]{:S(2)}, u32[]{:S(2)}) %collective-permute-start.7) | collective-permute-done | bytes 524320 | tf_op jit(solution)/shard_map/ppermute | solution.py:289
  41.6 7.1 %collective-permute-done.6.refs_3_ = f32[32,4096]{1,0:T(8,128)} collective-permute-done((f32[32,4096]{1,0:T(8,128)S(1)}, f32[32,4096]{1,0:T(8,128)}, u32[]{:S(2)}, u32[]{:S(2)}) %collective-permute-start.6) | collective-permute-done | bytes 524320 | tf_op jit(solution)/shard_map/ppermute | solution.py:289
  48.7 0.0 copy-done.9
  48.7 0.0 collective-permute-start.9
  48.7 11.2 %collective-permute-done.10.refs_10_ = f32[32,4096]{1,0:T(8,128)} collective-permute-done((f32[32,4096]{1,0:T(8,128)}, f32[32,4096]{1,0:T(8,128)}, u32[]{:S(2)}, u32[]{:S(2)}) %collective-permute-start.10) | collective-permute-done | bytes 524320 | tf_op jit(solution)/shard_map/ppermute | solution.py:289
  59.9 3.0 %collective-permute-start.13 = (f32[32,4096]{1,0:T(8,128)}, f32[32,4096]{1,0:T(8,128)}, u32[]{:S(2)}, u32[]{:S(2)}) collective-permute-start(f32[32,4096]{1,0:T(8,128)} %collective-permute-done.7.refs_5_), channel_id=1, source_target_pairs={{0,8},{1,9},{2,10},{3,11},{4,12},{5,13},{6,14},{7,15},{8,0},{9,1},... | collective-permute-start | bytes 1572872 | tf_op jit(solution)/shard_map/ppermute | solution.py:289
  62.9 0.0 collective-permute-start.14
  62.9 3.2 %collective-permute-start.12 = (f32[32,4096]{1,0:T(8,128)}, f32[32,4096]{1,0:T(8,128)}, u32[]{:S(2)}, u32[]{:S(2)}) collective-permute-start(f32[32,4096]{1,0:T(8,128)} %collective-permute-done.1.refs_6_), channel_id=1, source_target_pairs={{0,6},{1,7},{2,0},{3,1},{4,2},{5,3},{6,4},{7,5},{8,14},{9,15},{10,... | collective-permute-start | bytes 1572872 | tf_op jit(solution)/shard_map/ppermute | solution.py:289
  66.2 4.9 %collective-permute-done.8.refs_8_ = f32[32,4096]{1,0:T(8,128)S(1)} collective-permute-done((f32[32,4096]{1,0:T(8,128)S(1)}, f32[32,4096]{1,0:T(8,128)S(1)}, u32[]{:S(2)}, u32[]{:S(2)}) %collective-permute-start.8) | collective-permute-done | bytes 524320 | tf_op jit(solution)/shard_map/ppermute | solution.py:289
  71.0 0.0 copy-done.10
  71.0 3.0 %collective-permute-start.11 = (f32[32,4096]{1,0:T(8,128)}, f32[32,4096]{1,0:T(8,128)}, u32[]{:S(2)}, u32[]{:S(2)}) collective-permute-start(f32[32,4096]{1,0:T(8,128)} %collective-permute-done.6.refs_3_), channel_id=1, source_target_pairs={{0,8},{1,9},{2,10},{3,11},{4,12},{5,13},{6,14},{7,15},{8,0},{9,1},... | collective-permute-start | bytes 1572872 | tf_op jit(solution)/shard_map/ppermute | solution.py:289
  74.1 0.0 copy-done.11
  74.1 0.0 collective-permute-done.9.refs_9_
  74.1 0.9 collective-permute-start.15
  74.9 0.6 stack.39.where_ref
  75.5 0.0 copy-done.4
  75.5 0.0 copy-done.8
  75.5 11.9 %gram_near.1.refs_18_ = f32[2,640,128]{2,1,0:T(8,128)} custom-call(s32[9]{0:T(128)} %stack.39.where_ref, f32[32,4096]{1,0:T(8,128)} %copy-done.4, f32[32,4096]{1,0:T(8,128)} %copy-done.7, f32[32,4096]{1,0:T(8,128)} %copy-done.9, f32[32,4096]{1,0:T(8,128)} %collective-permute-done.6.refs_3_, f32[32,4096]{1,0:T(8,128)} %copy-done.8, ...), custom_call_target="tpu_custom_call" | custom-call | flops 5368709120 | bytes 8388608 | tf_op jit(solution)/shard_map/gram_near/pallas_call | solution.py:357
  87.5 0.0 collective-permute-done.13.refs_13_
  87.5 0.0 collective-permute-done.14.refs_14_
  87.5 0.0 collective-permute-done.12.refs_12_
  87.5 0.2 collective-permute-done.11.refs_11_
  87.7 5.7 %collective-permute-done.15.refs_15_ = f32[32,4096]{1,0:T(8,128)} collective-permute-done((f32[32,4096]{1,0:T(8,128)}, f32[32,4096]{1,0:T(8,128)}, u32[]{:S(2)}, u32[]{:S(2)}) %collective-permute-start.15) | collective-permute-done | bytes 524320 | tf_op jit(solution)/shard_map/ppermute | solution.py:289
  93.4 16.3 %gram_far.1 = f32[2,1152,128]{2,1,0:T(8,128)} custom-call(s32[9]{0:T(128)} %stack.39.where_ref, f32[32,4096]{1,0:T(8,128)} %copy-done.4, f32[32,4096]{1,0:T(8,128)} %copy-done.7, f32[32,4096]{1,0:T(8,128)} %copy-done.9, f32[32,4096]{1,0:T(8,128)} %collective-permute-done.6.refs_3_, f32[32,4096]{1,0:T(8,128)} %copy-done.8, ...), custom_call_target="tpu_custom_call" | custom-call | flops 8589934592 | bytes 12582912 | tf_op jit(solution)/shard_map/gram_far/pallas_call | solution.py:357
  109.6 1.1 dynamic-slice_bitcast_fusion
  110.7 0.1 collective-permute-start.16
  110.8 2.0 %collective-permute-done.16 = f32[1152,128]{1,0:T(8,128)S(1)} collective-permute-done((f32[1152,128]{1,0:T(8,128)S(1)}, f32[1152,128]{1,0:T(8,128)S(1)}, u32[]{:S(2)}, u32[]{:S(2)}) %collective-permute-start.16) | collective-permute-done | bytes 589856 | tf_op jit(solution)/shard_map/ppermute | solution.py:289
  112.8 1.2 bitcast_add_fusion
  114.0 16.4 %all_to_all.10 = f32[8,144,128]{2,1,0:T(8,128)S(1)} all-to-all(f32[8,144,128]{2,1,0:T(8,128)S(1)} %bitcast.25), channel_id=1, replica_groups=mesh['row'=8,'col'=16] {'row'}, dimensions={0} | all-to-all | bytes 1179648 | tf_op jit(solution)/shard_map/all_to_all | solution.py:390
  130.5 13.0 %all_to_all.11 = f32[8,144,128]{2,1,0:T(8,128)S(1)} all-to-all(f32[8,144,128]{2,1,0:T(8,128)S(1)} %broadcast_in_dim.10), channel_id=1, replica_groups=mesh['row'=8,'col'=16] {'row'}, dimensions={0} | all-to-all | bytes 1179648 | tf_op jit(solution)/shard_map/all_to_all | solution.py:393
  143.5 0.0 collective-permute-start.17
  143.5 2.0 %collective-permute-done.17.other_ref = f32[1152,128]{1,0:T(8,128)S(1)} collective-permute-done((f32[1152,128]{1,0:T(8,128)S(1)}, f32[1152,128]{1,0:T(8,128)S(1)}, u32[]{:S(2)}, u32[]{:S(2)}) %collective-permute-start.17) | collective-permute-done | bytes 589856 | tf_op jit(solution)/shard_map/ppermute | solution.py:289
  145.5 10.2 %solve.1 = (f32[512,128]{1,0:T(8,128)S(1)}, f32[512,128]{1,0:T(8,128)S(1)}) custom-call(s32[9]{0:T(128)S(1)} %copy-done.2, f32[1152,128]{1,0:T(8,128)S(1)} %bitcast.24, f32[1152,128]{1,0:T(8,128)S(1)} %collective-permute-done.17.other_ref), custom_call_target="tpu_custom_call" | custom-call | tf_op jit(solution)/shard_map/solve/pallas_call | solution.py:396
  155.7 0.7 copy-done
  156.4 0.7 copy-done.1
  157.1 13.4 %apply.1 = (f32[4096,128]{1,0:T(8,128)}, f32[4096,128]{1,0:T(8,128)}) custom-call(s32[9]{0:T(128)} %stack.39.where_ref, f32[32,4096]{1,0:T(8,128)} %copy-done.4, f32[32,4096]{1,0:T(8,128)} %copy-done.7, f32[32,4096]{1,0:T(8,128)} %copy-done.9, f32[32,4096]{1,0:T(8,128)} %collective-permute-done.6.refs_3_, f32[32,4096]{1,0:T(8,128)} %copy-done.8, ...), custom_call_target="tpu_custom_call" | custom-call | tf_op jit(solution)/shard_map/apply/pallas_call | solution.py:412
  170.5 0.2 collective-permute-start.18
  170.8 0.3 broadcast_in_dim.4
  171.0 1.3 copy-done.5
  172.4 0.2 constant_dynamic-update-slice_fusion.1
  172.5 0.0 copy-start.3
  172.5 2.4 %collective-permute-done.18 = f32[4096,128]{1,0:T(8,128)S(1)} collective-permute-done((f32[4096,128]{1,0:T(8,128)}, f32[4096,128]{1,0:T(8,128)S(1)}, u32[]{:S(2)}, u32[]{:S(2)}) %collective-permute-start.18) | collective-permute-done | bytes 2097184 | tf_op jit(solution)/shard_map/ppermute | solution.py:289
  175.0 1.5 constant_dynamic-update-slice_fusion
  (16 shorter events, 0.1 us)
Async XLA Ops:
  3.9 12.5 %collective-permute-start.4 = (f32[4096,128]{1,0:T(8,128)S(1)}, f32[4096,128]{1,0:T(8,128)S(1)}, u32[]{:S(2)}, u32[]{:S(2)}) collective-permute-start(f32[4096,128]{1,0:T(8,128)S(1)} %constant_dynamic-slice_fusion), channel_id=1, source_target_pairs={{0,1},{1,0},{2,3},{3,2},{4,5},{5,4},{6,7},{7,6},{8,9},{9,8},{10,11... | collective-permute-start | bytes 6291464 | tf_op jit(solution)/shard_map/ppermute | solution.py:289
  3.9 4.7 %collective-permute-start = (f32[32,4096]{1,0:T(8,128)}, f32[32,4096]{1,0:T(8,128)S(1)}, u32[]{:S(2)}, u32[]{:S(2)}) collective-permute-start(f32[32,4096]{1,0:T(8,128)} %pad_maximum_fusion.1), channel_id=1, source_target_pairs={{0,1},{1,0},{2,3},{3,2},{4,5},{5,4},{6,7},{7,6},{8,9},{9,8},{10,11... | collective-permute-start | bytes 1572872 | tf_op jit(solution)/shard_map/ppermute | solution.py:289
  4.5 71.1 %copy-start.4 = (f32[32,4096]{1,0:T(8,128)}, f32[32,4096]{1,0:T(8,128)S(1)}, u32[]{:S(2)}) copy-start(f32[32,4096]{1,0:T(8,128)S(1)} %pad_maximum_fusion.refs_0_) | copy-start | bytes 1572868
  8.7 23.8 %copy-start.7 = (f32[32,4096]{1,0:T(8,128)}, f32[32,4096]{1,0:T(8,128)S(1)}, u32[]{:S(2)}) copy-start(f32[32,4096]{1,0:T(8,128)S(1)} %collective-permute-done.refs_1_) | copy-start | bytes 1572868
  8.7 15.8 %collective-permute-start.3 = (f32[32,4096]{1,0:T(8,128)S(1)}, f32[32,4096]{1,0:T(8,128)S(1)}, u32[]{:S(2)}, u32[]{:S(2)}) collective-permute-start(f32[32,4096]{1,0:T(8,128)S(1)} %pad_maximum_fusion.refs_0_), channel_id=1, source_target_pairs={{0,6},{1,7},{2,0},{3,1},{4,2},{5,3},{6,4},{7,5},{8,14},{9,15},{10,... | collective-permute-start | bytes 1572872 | tf_op jit(solution)/shard_map/ppermute | solution.py:289
  12.8 15.1 %collective-permute-start.2 = (f32[32,4096]{1,0:T(8,128)S(1)}, f32[32,4096]{1,0:T(8,128)S(1)}, u32[]{:S(2)}, u32[]{:S(2)}) collective-permute-start(f32[32,4096]{1,0:T(8,128)S(1)} %pad_maximum_fusion.refs_0_), channel_id=1, source_target_pairs={{0,2},{1,3},{2,4},{3,5},{4,6},{5,7},{6,0},{7,1},{8,10},{9,11},{10,... | collective-permute-start | bytes 1572872 | tf_op jit(solution)/shard_map/ppermute | solution.py:289
  12.8 16.4 %collective-permute-start.1 = (f32[32,4096]{1,0:T(8,128)S(1)}, f32[32,4096]{1,0:T(8,128)}, u32[]{:S(2)}, u32[]{:S(2)}) collective-permute-start(f32[32,4096]{1,0:T(8,128)S(1)} %pad_maximum_fusion.refs_0_), channel_id=1, source_target_pairs={{0,8},{1,9},{2,10},{3,11},{4,12},{5,13},{6,14},{7,15},{8,0},{9,1},... | collective-permute-start | bytes 1572872 | tf_op jit(solution)/shard_map/ppermute | solution.py:289
  15.9 23.6 %collective-permute-start.5 = (f32[32,4096]{1,0:T(8,128)S(1)}, f32[32,4096]{1,0:T(8,128)S(1)}, u32[]{:S(2)}, u32[]{:S(2)}) collective-permute-start(f32[32,4096]{1,0:T(8,128)S(1)} %collective-permute-done.refs_1_), channel_id=1, source_target_pairs={{0,8},{1,9},{2,10},{3,11},{4,12},{5,13},{6,14},{7,15},{8,0},{9,1},... | collective-permute-start | bytes 1572872 | tf_op jit(solution)/shard_map/ppermute | solution.py:289
  16.4 59.2 %copy-start.6 = (f32[4096,128]{1,0:T(8,128)}, f32[4096,128]{1,0:T(8,128)S(1)}, u32[]{:S(2)}) copy-start(f32[4096,128]{1,0:T(8,128)S(1)} %collective-permute-done.4.refs_9_.refs_17_) | copy-start | bytes 6291460
  24.5 51.0 %copy-start.8 = (f32[32,4096]{1,0:T(8,128)}, f32[32,4096]{1,0:T(8,128)S(1)}, u32[]{:S(2)}) copy-start(f32[32,4096]{1,0:T(8,128)S(1)} %collective-permute-done.3.refs_4_) | copy-start | bytes 1572868
  27.9 20.7 %copy-start.9 = (f32[32,4096]{1,0:T(8,128)}, f32[32,4096]{1,0:T(8,128)S(1)}, u32[]{:S(2)}) copy-start(f32[32,4096]{1,0:T(8,128)S(1)} %collective-permute-done.2.refs_2_) | copy-start | bytes 1572868
  29.2 12.3 %collective-permute-start.7 = (f32[32,4096]{1,0:T(8,128)S(1)}, f32[32,4096]{1,0:T(8,128)}, u32[]{:S(2)}, u32[]{:S(2)}) collective-permute-start(f32[32,4096]{1,0:T(8,128)S(1)} %collective-permute-done.refs_1_), channel_id=1, source_target_pairs={{0,6},{1,7},{2,0},{3,1},{4,2},{5,3},{6,4},{7,5},{8,14},{9,15},{10,... | collective-permute-start | bytes 1572872 | tf_op jit(solution)/shard_map/ppermute | solution.py:289
  32.5 16.2 %collective-permute-start.6 = (f32[32,4096]{1,0:T(8,128)S(1)}, f32[32,4096]{1,0:T(8,128)}, u32[]{:S(2)}, u32[]{:S(2)}) collective-permute-start(f32[32,4096]{1,0:T(8,128)S(1)} %collective-permute-done.refs_1_), channel_id=1, source_target_pairs={{0,2},{1,3},{2,4},{3,5},{4,6},{5,7},{6,0},{7,1},{8,10},{9,11},{10,... | collective-permute-start | bytes 1572872 | tf_op jit(solution)/shard_map/ppermute | solution.py:289
  32.5 27.4 %collective-permute-start.10 = (f32[32,4096]{1,0:T(8,128)}, f32[32,4096]{1,0:T(8,128)}, u32[]{:S(2)}, u32[]{:S(2)}) collective-permute-start(f32[32,4096]{1,0:T(8,128)} %collective-permute-done.1.refs_6_), channel_id=1, source_target_pairs={{0,2},{1,3},{2,4},{3,5},{4,6},{5,7},{6,0},{7,1},{8,10},{9,11},{10,... | collective-permute-start | bytes 1572872 | tf_op jit(solution)/shard_map/ppermute | solution.py:289
  32.5 38.5 %collective-permute-start.8 = (f32[32,4096]{1,0:T(8,128)S(1)}, f32[32,4096]{1,0:T(8,128)S(1)}, u32[]{:S(2)}, u32[]{:S(2)}) collective-permute-start(f32[32,4096]{1,0:T(8,128)S(1)} %collective-permute-done.2.refs_2_), channel_id=1, source_target_pairs={{0,2},{1,3},{2,4},{3,5},{4,6},{5,7},{6,0},{7,1},{8,10},{9,11},{10,... | collective-permute-start | bytes 1572872 | tf_op jit(solution)/shard_map/ppermute | solution.py:289
  39.5 31.6 %copy-start.10 = (f32[32,4096]{1,0:T(8,128)}, f32[32,4096]{1,0:T(8,128)S(1)}, u32[]{:S(2)}) copy-start(f32[32,4096]{1,0:T(8,128)S(1)} %collective-permute-done.5.refs_7_) | copy-start | bytes 1572868
  48.7 25.4 %collective-permute-start.9 = (f32[32,4096]{1,0:T(8,128)}, f32[32,4096]{1,0:T(8,128)}, u32[]{:S(2)}, u32[]{:S(2)}) collective-permute-start(f32[32,4096]{1,0:T(8,128)} %collective-permute-done.7.refs_5_), channel_id=1, source_target_pairs={{0,6},{1,7},{2,0},{3,1},{4,2},{5,3},{6,4},{7,5},{8,14},{9,15},{10,... | collective-permute-start | bytes 1572872 | tf_op jit(solution)/shard_map/ppermute | solution.py:289
  59.9 27.6 %collective-permute-start.13 = (f32[32,4096]{1,0:T(8,128)}, f32[32,4096]{1,0:T(8,128)}, u32[]{:S(2)}, u32[]{:S(2)}) collective-permute-start(f32[32,4096]{1,0:T(8,128)} %collective-permute-done.7.refs_5_), channel_id=1, source_target_pairs={{0,8},{1,9},{2,10},{3,11},{4,12},{5,13},{6,14},{7,15},{8,0},{9,1},... | collective-permute-start | bytes 1572872 | tf_op jit(solution)/shard_map/ppermute | solution.py:289
  62.9 24.5 %collective-permute-start.14 = (f32[32,4096]{1,0:T(8,128)}, f32[32,4096]{1,0:T(8,128)}, u32[]{:S(2)}, u32[]{:S(2)}) collective-permute-start(f32[32,4096]{1,0:T(8,128)} %collective-permute-done.10.refs_10_), channel_id=1, source_target_pairs={{0,2},{1,3},{2,4},{3,5},{4,6},{5,7},{6,0},{7,1},{8,10},{9,11},{10,... | collective-permute-start | bytes 1572872 | tf_op jit(solution)/shard_map/ppermute | solution.py:289
  62.9 24.5 %collective-permute-start.12 = (f32[32,4096]{1,0:T(8,128)}, f32[32,4096]{1,0:T(8,128)}, u32[]{:S(2)}, u32[]{:S(2)}) collective-permute-start(f32[32,4096]{1,0:T(8,128)} %collective-permute-done.1.refs_6_), channel_id=1, source_target_pairs={{0,6},{1,7},{2,0},{3,1},{4,2},{5,3},{6,4},{7,5},{8,14},{9,15},{10,... | collective-permute-start | bytes 1572872 | tf_op jit(solution)/shard_map/ppermute | solution.py:289
  71.0 3.0 %copy-start.11 = (f32[32,4096]{1,0:T(8,128)}, f32[32,4096]{1,0:T(8,128)S(1)}, u32[]{:S(2)}) copy-start(f32[32,4096]{1,0:T(8,128)S(1)} %collective-permute-done.8.refs_8_) | copy-start | bytes 1572868
  71.0 16.7 %collective-permute-start.11 = (f32[32,4096]{1,0:T(8,128)}, f32[32,4096]{1,0:T(8,128)}, u32[]{:S(2)}, u32[]{:S(2)}) collective-permute-start(f32[32,4096]{1,0:T(8,128)} %collective-permute-done.6.refs_3_), channel_id=1, source_target_pairs={{0,8},{1,9},{2,10},{3,11},{4,12},{5,13},{6,14},{7,15},{8,0},{9,1},... | collective-permute-start | bytes 1572872 | tf_op jit(solution)/shard_map/ppermute | solution.py:289
  74.1 19.3 %collective-permute-start.15 = (f32[32,4096]{1,0:T(8,128)}, f32[32,4096]{1,0:T(8,128)}, u32[]{:S(2)}, u32[]{:S(2)}) collective-permute-start(f32[32,4096]{1,0:T(8,128)} %collective-permute-done.9.refs_9_), channel_id=1, source_target_pairs={{0,8},{1,9},{2,10},{3,11},{4,12},{5,13},{6,14},{7,15},{8,0},{9,1},... | collective-permute-start | bytes 1572872 | tf_op jit(solution)/shard_map/ppermute | solution.py:289
  110.7 2.1 %collective-permute-start.16 = (f32[1152,128]{1,0:T(8,128)S(1)}, f32[1152,128]{1,0:T(8,128)S(1)}, u32[]{:S(2)}, u32[]{:S(2)}) collective-permute-start(f32[1152,128]{1,0:T(8,128)S(1)} %dynamic-slice_bitcast_fusion), channel_id=1, source_target_pairs={{0,1},{1,0},{2,3},{3,2},{4,5},{5,4},{6,7},{7,6},{8,9},{9,8},{10,11... | collective-permute-start | bytes 1769480 | tf_op jit(solution)/shard_map/ppermute | solution.py:289
  114.0 31.5 %copy-start.2 = (s32[9]{0:T(128)S(1)}, s32[9]{0:T(128)}, u32[]{:S(2)}) copy-start(s32[9]{0:T(128)} %stack.39.where_ref) | copy-start | bytes 112
  143.5 2.0 %collective-permute-start.17 = (f32[1152,128]{1,0:T(8,128)S(1)}, f32[1152,128]{1,0:T(8,128)S(1)}, u32[]{:S(2)}, u32[]{:S(2)}) collective-permute-start(f32[1152,128]{1,0:T(8,128)S(1)} %bitcast.23), channel_id=1, source_target_pairs={{0,1},{1,0},{2,3},{3,2},{4,5},{5,4},{6,7},{7,6},{8,9},{9,8},{10,11... | collective-permute-start | bytes 1769480 | tf_op jit(solution)/shard_map/ppermute | solution.py:289
  155.7 0.7 copy-start
  156.4 0.7 copy-start.1
  170.5 4.5 %collective-permute-start.18 = (f32[4096,128]{1,0:T(8,128)}, f32[4096,128]{1,0:T(8,128)S(1)}, u32[]{:S(2)}, u32[]{:S(2)}) collective-permute-start(f32[4096,128]{1,0:T(8,128)} %get-tuple-element.42), channel_id=1, source_target_pairs={{0,1},{1,0},{2,3},{3,2},{4,5},{5,4},{6,7},{7,6},{8,9},{9,8},{10,11... | collective-permute-start | bytes 6291464 | tf_op jit(solution)/shard_map/ppermute | solution.py:289
  170.8 1.6 copy-start.5
  172.5 2.5 %copy-start.3 = (f32[8192,128]{1,0:T(8,128)}, f32[8192,128]{1,0:T(8,128)S(1)}, u32[]{:S(2)}) copy-start(f32[8192,128]{1,0:T(8,128)S(1)} %constant_dynamic-update-slice_fusion.1) | copy-start | bytes 12582916

commit v4 on v2

--- a/solution.py
+++ b/solution.py
@@ -14,6 +14,7 @@
 CHIPS = PLANES * DEPTH
 WIDE = 128
 TILE = 512
+LIMIT = 24 << 20
 PIECES = ((0, 0), (0, 1), (1, 1), (0, 2), (0, 3)), ((1, 2), (1, 3), (2, 2), (2, 3), (3, 3))
 
 
@@ -39,24 +40,51 @@
     )
 
 
-def gram_kernel(where_ref, *refs, pieces, first):
+def each_far(step, steps, refs, place):
+    up_ref, down_ref, across_ref, end_up_ref, end_across_ref = refs
+    chunk = down_ref.shape[0]
+    early = step < steps // 2
+
+    @pl.when(early)
+    def _():
+        place(4, up_ref[:chunk])
+        place(5, up_ref[chunk:])
+        place(6, down_ref[...])
+        place(7, end_up_ref[...])
+
+    @pl.when(jnp.logical_not(early))
+    def _():
+        place(4, down_ref[...])
+        place(5, across_ref[:chunk])
+        place(6, across_ref[chunk:])
+        place(7, end_across_ref[...])
+
+
+def gram_kernel(where_ref, *refs, first):
     steps = pl.num_programs(0)
     step = pl.program_id(0)
-    panels, rest = refs[:pieces], refs[pieces:]
+    count = 4 if first else 9
+    panels, rest = refs[:count], refs[count:]
     if first:
         own_ref, other_ref, out_ref, high, middle, low, even, skew, proj = rest
     else:
-        own_ref, other_ref, before_ref, out_ref, high, middle, low, even, skew, proj = rest
+        own_ref, other_ref, before_ref, keep_ref, send_ref, high, middle, low, even, skew, proj = rest
     core = where_ref[CHIPS]
-    lines = panels[0].shape[0]
+    lines = panels[0].shape[0] // 2
     half = even.shape[1]
     start_row = high.shape[0] - half
 
-    for index, ref in enumerate(panels):
-        parts = split3(ref[...])
-        begin = pl.multiple_of((index // 2) * 2 * lines + lines * (core ^ (index % 2)), lines)
-        for target, value in zip((high, middle, low), parts):
-            target[pl.ds(begin, lines), :] = value
+    def place(slot, value):
+        parts = split3(value)
+        for swap in range(2):
+            begin = pl.multiple_of(slot * 2 * lines + lines * (core ^ swap), lines)
+            for target, part in zip((high, middle, low), parts):
+                target[pl.ds(begin, lines), :] = part[swap * lines : (swap + 1) * lines]
+
+    for slot in range(4):
+        place(slot, panels[slot][...])
+    if not first:
+        each_far(step, steps, panels[4:], place)
 
     @pl.when(step == 0)
     def _():
@@ -96,28 +124,39 @@
             )
 
         if first:
-            out_ref[core, 0:half, :] = proj[:, :WIDE]
-            out_ref[1 - core, 0:half, :] = proj[:, WIDE:]
-            for place, (i, j) in enumerate(((0, 0), (0, 1), (1, 1))):
-                begin = half + place * WIDE
+            out_ref[0, 0:half, :] = proj[:, :WIDE]
+            out_ref[1, 0:half, :] = proj[:, WIDE:]
+            for at, (i, j) in enumerate(((0, 0), (0, 1), (1, 1))):
+                begin = half + at * WIDE
                 out_ref[0, begin : begin + WIDE, :] = corner(i, j)
                 out_ref[1, begin : begin + WIDE, :] = jnp.zeros((WIDE, WIDE), F32)
         else:
-            out_ref[0, 0:half, :] = before_ref[0, 0:half, :]
-            out_ref[1, 0:half, :] = before_ref[1, 0:half, :]
-            out_ref[core, half : 2 * half, :] = proj[:, :WIDE]
-            out_ref[1 - core, half : 2 * half, :] = proj[:, WIDE:]
-            for part in range(2):
-                for place, (i, j) in enumerate(PIECES[part]):
-                    begin = 2 * half + place * WIDE
+            keep_ref[0:half, :] = before_ref[0, 0:half, :]
+            send_ref[0:half, :] = before_ref[1, 0:half, :]
+            keep_ref[half : 2 * half, :] = proj[:, :WIDE]
+            send_ref[half : 2 * half, :] = proj[:, WIDE:]
+
+            def blocks(part, target):
+                for at, (i, j) in enumerate(PIECES[part]):
+                    begin = 2 * half + at * WIDE
                     if j < 2:
-                        source = half + ((0, 0), (0, 1), (1, 1)).index((i, j)) * WIDE
-                        block = before_ref[0, source : source + WIDE, :]
+                        index = half + ((0, 0), (0, 1), (1, 1)).index((i, j)) * WIDE
+                        block = before_ref[0, index : index + WIDE, :]
                     elif i < 2:
                         block = even[i * WIDE : (i + 1) * WIDE, (j - 2) * WIDE : (j - 1) * WIDE]
                     else:
                         block = corner(i - 2, j - 2)
-                    out_ref[part, begin : begin + WIDE, :] = block
+                    target[begin : begin + WIDE, :] = block
+
+            @pl.when(core == 0)
+            def _():
+                blocks(0, keep_ref)
+                blocks(1, send_ref)
+
+            @pl.when(core != 0)
+            def _():
+                blocks(1, keep_ref)
+                blocks(0, send_ref)
 
 
 def solve_kernel(where_ref, mine_ref, other_ref, own_ref, partner_ref, both, rows_done, ordered, sides):
@@ -231,13 +270,13 @@
 
 def apply_kernel(where_ref, *refs):
     step = pl.program_id(0)
-    panels = refs[: 2 * CHIPS]
-    current_own, current_other, solved_own, solved_other, out_own, out_other, high, middle, low = refs[
-        2 * CHIPS :
-    ]
+    steps = pl.num_programs(0)
+    panels = refs[:9]
+    current_own, current_other, solved_own, solved_other, out_own, out_other, high, middle, low, merged = refs[9:]
     core = where_ref[CHIPS]
     panel = solved_own.shape[0] // 2
-    group = panels[0].shape[0] // 2
+    chunk = panels[0].shape[0]
+    group = chunk // 4
 
     @pl.when(step == 0)
     def _():
@@ -255,8 +294,13 @@
                 for target, value in zip((high, middle, low), split3(lines)):
                     target[at : at + group, :] = value
 
-    value = jnp.concatenate([r[...] for r in panels], axis=0)
-    one, two, three = split3(value)
+    def place(slot, value):
+        merged[slot * chunk : (slot + 1) * chunk, :] = value
+
+    for slot in range(4):
+        place(slot, panels[slot][...])
+    each_far(step, steps, panels[4:], place)
+    one, two, three = split3(merged[...])
     first, second, third = high[...], middle[...], low[...]
 
     def tn(left, right):
@@ -276,6 +320,8 @@
     group = panel_one.shape[1]
     half = rows // 2
     size = 2 * group * CHIPS * CORES
+    quarter = half // 2
+    chunk = 4 * group
     steps = half // TILE
     at = lax.axis_index("col")
     core, depth, plane = at % CORES, (at // CORES) % DEPTH, at // (CORES * DEPTH)
@@ -306,50 +352,58 @@
 
     a_own = half_of(core)
     b_own = core_swap(half_of(1 - core))
+    own = jnp.concatenate([a_own, b_own], axis=0)
     given = lax.dynamic_slice_in_dim(vectors, (1 - core) * half, half, 0)
     other = core_swap(given)
 
-    a_away, a_below, a_above = across(a_own), up(a_own), down(a_own)
-    b_away, b_below, b_above = across(b_own), up(b_own), down(b_own)
-    a_away_below = up(a_away)
-    a_away_above = down(a_away)
-    a_far = up(a_below)
-    b_away_below = across(b_below)
-    b_far = down(b_above)
-    b_away_above = across(b_above)
-    a_away_far = up(a_away_below)
-    b_away_far = across(b_far)
-
-    near = (a_own, b_own, a_below, b_below, a_above, b_above, a_away, b_away)
-    distant = (
-        a_far, b_far, a_away_below, b_away_below,
-        a_away_above, b_away_above, a_away_far, b_away_far,
-    )
+    away, below, above = across(own), up(own), down(own)
+    near = (own, below, above, away)
+    sent_up = up(jnp.concatenate([below[:, :quarter], away[:, :quarter]], axis=0))
+    sent_down = down(jnp.concatenate([above[:, quarter:], away[:, :quarter]], axis=0))
+    sent_across = across(jnp.concatenate([below[:, quarter:], above[:, quarter:]], axis=0))
     chips = []
     for x_step, z_step in ((0, 0), (0, -1), (0, 1), (1, 0), (0, 2), (1, -1), (1, 1), (1, 2)):
         chips.append(jnp.bitwise_xor(plane, x_step) * DEPTH + (depth + z_step) % DEPTH)
     where = jnp.stack(chips + [core]).astype(jnp.int32)
 
-    lines = 2 * group
-    piece = pl.BlockSpec((lines, TILE), lambda j, w: (0, j))
+    turn = steps // 2
+    whole = [pl.BlockSpec((chunk, TILE), lambda j, w: (0, j))] * 4
+
+    def early(lines):
+        return pl.BlockSpec((lines, TILE), lambda j, w: (0, jnp.minimum(j, turn - 1)))
+
+    def late(lines):
+        return pl.BlockSpec((lines, TILE), lambda j, w: (0, jnp.maximum(j - turn, 0)))
+
+    both = pl.BlockSpec(
+        (chunk, TILE), lambda j, w: (jnp.where(j < turn, 1, 0), jnp.where(j < turn, j, j - turn))
+    )
+    parts_far = [early(2 * chunk), both, late(2 * chunk), early(chunk), late(chunk)]
     own_spec = pl.BlockSpec((TILE, columns), lambda j, w: (w[CHIPS] * steps + j, 0))
     other_spec = pl.BlockSpec((TILE, columns), lambda j, w: (j, 0))
     length = size + 5 * WIDE
     span = size // 2
 
     def gram(first, pieces, extra):
-        rows_out = span + 3 * WIDE if first else length
-        extra_specs = [pl.BlockSpec(v.shape, lambda j, w: (0, 0, 0)) for v in extra]
+        if first:
+            shapes = [jax.ShapeDtypeStruct((2, span + 3 * WIDE, WIDE), F32)]
+        else:
+            shapes = [jax.ShapeDtypeStruct((length, WIDE), F32)] * 2
         height = span if first else size
         units = 10 if first else 16
         return pl.pallas_call(
-            functools.partial(gram_kernel, pieces=len(pieces), first=first),
-            out_shape=jax.ShapeDtypeStruct((2, rows_out, WIDE), F32),
+            functools.partial(gram_kernel, first=first),
+            out_shape=shapes,
             grid_spec=pltpu.PrefetchScalarGridSpec(
                 num_scalar_prefetch=1,
                 grid=(steps,),
-                in_specs=[piece] * len(pieces) + [own_spec, other_spec] + extra_specs,
-                out_specs=pl.BlockSpec((2, rows_out, WIDE), lambda j, w: (0, 0, 0)),
+                in_specs=whole
+                + ([] if first else parts_far)
+                + [own_spec, other_spec]
+                + [pl.BlockSpec(v.shape, lambda j, w: (0, 0, 0)) for v in extra],
+                out_specs=[
+                    pl.BlockSpec(v.shape, lambda j, w, n=len(v.shape): (0,) * n) for v in shapes
+                ],
                 scratch_shapes=[pltpu.VMEM((height, TILE), BF16)] * 3
                 + [
                     pltpu.VMEM((height, span), F32),
@@ -358,22 +412,23 @@
                 ],
             ),
             compiler_params=pltpu.CompilerParams(
-                dimension_semantics=("arbitrary",), vmem_limit_bytes=32 << 20
+                dimension_semantics=("arbitrary",), vmem_limit_bytes=LIMIT
             ),
             cost_estimate=pl.CostEstimate(
-                flops=2 * units * span * span * half,
+                flops=2 * 6 * units * span * span * half,
                 bytes_accessed=4 * half * (height + columns * 2),
                 transcendentals=0,
             ),
             name="gram_near" if first else "gram_far",
         )(where, *pieces, vectors, other, *extra)
 
-    before = gram(True, near, ())
-    gathered = gram(False, near + distant, (before,))
-
-    mine = lax.dynamic_index_in_dim(gathered, core, 0, keepdims=False)
-    send = lax.dynamic_index_in_dim(gathered, 1 - core, 0, keepdims=False)
-    mine = mine + core_swap(send)
+    (before,) = gram(True, near, ())
+    before, sent_up, sent_down = lax.optimization_barrier((before, sent_up, sent_down))
+    end_up = up(sent_up[chunk:])
+    end_across = across(sent_down[:chunk])
+    far = (sent_up, sent_down, sent_across, end_up, end_across)
+    kept, sent = gram(False, near + far, (before,))
+    mine = kept + core_swap(sent)
     members = lax.axis_size("row")
     parts = lax.all_to_all(mine.reshape(members, length // members, WIDE), "row", 0, 0)
     total = jnp.sum(parts, axis=0)
@@ -403,17 +458,19 @@
         grid_spec=pltpu.PrefetchScalarGridSpec(
             num_scalar_prefetch=1,
             grid=(steps,),
-            in_specs=[piece] * (2 * CHIPS)
+            in_specs=whole
+            + parts_far
             + [own_spec, other_spec]
             + [pl.BlockSpec((size, WIDE), lambda j, w: (0, 0))] * 2,
             out_specs=[pl.BlockSpec((TILE, columns), lambda j, w: (j, 0))] * 2,
-            scratch_shapes=[pltpu.VMEM((size, 2 * WIDE), BF16)] * 3,
+            scratch_shapes=[pltpu.VMEM((size, 2 * WIDE), BF16)] * 3
+            + [pltpu.VMEM((size, TILE), F32)],
         ),
         compiler_params=pltpu.CompilerParams(
-            dimension_semantics=("arbitrary",), vmem_limit_bytes=40 << 20
+            dimension_semantics=("arbitrary",), vmem_limit_bytes=LIMIT
         ),
         name="apply",
-    )(where, *near, *distant, vectors, other, solved_own, solved_other)
+    )(where, *near, *far, vectors, other, solved_own, solved_other)
 
     returned = core_swap(result_other)
     result = jnp.zeros((rows, columns), F32)

time: 167 us -> 167 us (level)
  starting transfers between devices: 27.7 us -> 13.2 us
  waiting for transfers between devices: 44.9 us -> 58.8 us
    ppermute x19 -> x13, starting transfers between devices: 27.7 us -> 13.2 us  [permute(): return lax.ppermute(value, 'col', pairs)]
    ppermute x19 -> x13, waiting for transfers between devices: 44.9 us -> 58.8 us  [permute(): return lax.ppermute(value, 'col', pairs)]
    unnamed x42 -> x26, local copies, waits for them, and re-layouts: 9.79 us -> 7.97 us
  transfers between devices with their start and end apart: 19 -> 13, of which waited for: 8 -> 10; matrix products, arithmetic and copies ran while one was open for 0% -> 3% of each run, Pallas kernels for 6% -> 6%
where the time goes in v4:
time: 167 us; the launch traced here: 165 us
  waiting for transfers between devices  58.8 us (35%)
  Pallas kernels  46.7 us (28%)
  blocking collectives  28.7 us (17%)
  local copies, waits for them, and re-layouts  15.6 us (9%)
  starting transfers between devices  13.2 us (8%)
    ppermute x13, waiting for transfers between devices, permute(): return lax.ppermute(value, 'col', pairs)  58.8 us
    pallas_call x2, Pallas kernels, gram(): pl.pallas_call(functools.partial(gram_kernel, first=first), out_shape=sha...  24.9 us
    all_to_all x1, blocking collectives, per_device(): lax.all_to_all(mine.reshape(members, length // members, WIDE), 'row', 0, 0)  15.7 us
    ppermute x13, starting transfers between devices, permute(): return lax.ppermute(value, 'col', pairs)  13.2 us
    all_to_all x1, blocking collectives, per_device(): mine = lax.all_to_all(spread, 'row', 0, 0).reshape(length, WIDE)  13 us
    pallas_call x1, Pallas kernels, per_device(): pl.pallas_call(apply_kernel, out_shape=[jax.ShapeDtypeStruct((half, colum...  11.6 us
    pallas_call x1, Pallas kernels, per_device(): pl.pallas_call(solve_kernel, out_shape=[jax.ShapeDtypeStruct((size, WIDE)...  10.2 us
    unnamed x26, local copies, waits for them, and re-layouts  7.97 us
  transfers between devices with their start and end apart: 13, of which 10 were waited for; matrix products, arithmetic and copies ran while one was open for 3% of the time, Pallas kernels for 6%

profile of v4, /device:TPU:0, one launch (start us, length us, event | category | flops | bytes accessed | tf_op | source)
XLA Modules:
  0.0 164.9 jit_solution(3610394887260408195)
XLA Ops:
  0.0 1.3 dynamic-slice_bitcast_fusion.2
  1.3 0.1 collective-permute-start
  1.4 3.1 %constant_dynamic-slice_fusion = f32[4096,128]{1,0:T(8,128)} fusion(f32[8192,128]{1,0:T(8,128)} %refs_9_.3, s32[]{:T(128)S(6)} %select_n.62), kind=kLoop, calls=%fused_computation.11 | loop fusion | bytes 4194308 | tf_op jit(solution)/shard_map/dynamic_slice | solution.py:356
  4.5 0.5 collective-permute-start.4
  4.9 0.0 collective-permute-done
  4.9 0.1 pad_maximum_fusion.2.refs_0_
  5.0 3.2 %collective-permute-start.3 = (f32[64,4096]{1,0:T(8,128)S(1)}, f32[64,4096]{1,0:T(8,128)S(1)}, u32[]{:S(2)}, u32[]{:S(2)}) collective-permute-start(f32[64,4096]{1,0:T(8,128)S(1)} %pad_maximum_fusion.2.refs_0_), channel_id=1, source_target_pairs={{0,8},{1,9},{2,10},{3,11},{4,12},{5,13},{6,14},{7,15},{8,0},{9,1},... | collective-permute-start | bytes 3145736 | tf_op jit(solution)/shard_map/ppermute | solution.py:335
  8.2 4.0 %collective-permute-start.2 = (f32[64,4096]{1,0:T(8,128)S(1)}, f32[64,4096]{1,0:T(8,128)}, u32[]{:S(2)}, u32[]{:S(2)}) collective-permute-start(f32[64,4096]{1,0:T(8,128)S(1)} %pad_maximum_fusion.2.refs_0_), channel_id=1, source_target_pairs={{0,6},{1,7},{2,0},{3,1},{4,2},{5,3},{6,4},{7,5},{8,14},{9,15},{10,... | collective-permute-start | bytes 3145736 | tf_op jit(solution)/shard_map/ppermute | solution.py:335
  12.2 0.0 collective-permute-start.1
  12.2 0.1 stack.39.where_ref
  12.3 19.4 %collective-permute-done.3.refs_3_ = f32[64,4096]{1,0:T(8,128)S(1)} collective-permute-done((f32[64,4096]{1,0:T(8,128)S(1)}, f32[64,4096]{1,0:T(8,128)S(1)}, u32[]{:S(2)}, u32[]{:S(2)}) %collective-permute-start.3) | collective-permute-done | bytes 1048608 | tf_op jit(solution)/shard_map/ppermute | solution.py:335
  31.7 0.0 copy-start
  31.7 2.8 %collective-permute-done.2.refs_2_ = f32[64,4096]{1,0:T(8,128)} collective-permute-done((f32[64,4096]{1,0:T(8,128)S(1)}, f32[64,4096]{1,0:T(8,128)}, u32[]{:S(2)}, u32[]{:S(2)}) %collective-permute-start.2) | collective-permute-done | bytes 1048608 | tf_op jit(solution)/shard_map/ppermute | solution.py:335
  34.6 1.1 slice.28
  35.6 2.3 %collective-permute-done.1.refs_1_ = f32[64,4096]{1,0:T(8,128)S(1)} collective-permute-done((f32[64,4096]{1,0:T(8,128)S(1)}, f32[64,4096]{1,0:T(8,128)S(1)}, u32[]{:S(2)}, u32[]{:S(2)}) %collective-permute-start.1) | collective-permute-done | bytes 1048608 | tf_op jit(solution)/shard_map/ppermute | solution.py:335
  38.0 0.1 fusion
  38.1 0.4 pad_maximum_fusion.3
  38.5 0.6 collective-permute-start.7
  39.0 1.7 %collective-permute-start.6 = (f32[128,2048]{1,0:T(8,128)S(1)}, f32[128,2048]{1,0:T(8,128)S(1)}, u32[]{:S(2)}, u32[]{:S(2)}) collective-permute-start(f32[128,2048]{1,0:T(8,128)S(1)} %get-tuple-element.26), channel_id=1, source_target_pairs={{0,6},{1,7},{2,0},{3,1},{4,2},{5,3},{6,4},{7,5},{8,14},{9,15},{10,... | collective-permute-start | bytes 3145736 | tf_op jit(solution)/shard_map/ppermute | solution.py:335
  40.7 0.4 collective-permute-start.5
  41.1 0.0 collective-permute-done.4.refs_5_.refs_10_
  41.1 0.0 copy-done
  41.1 10.0 %gram_near.1.refs_11_ = f32[2,640,128]{2,1,0:T(8,128)S(1)} custom-call(s32[9]{0:T(128)S(1)} %stack.39.where_ref, f32[64,4096]{1,0:T(8,128)S(1)} %pad_maximum_fusion.2.refs_0_, f32[64,4096]{1,0:T(8,128)S(1)} %collective-permute-done.1.refs_1_, f32[64,4096]{1,0:T(8,128)} %collective-permute-done.2.refs_2_, f32[64,4096]{1,0:T(8,128)S(1)} %collective-permute-done.3.refs_3_, ...), custom_call_target="tpu_custom_call" | custom-call | flops 32212254720 | bytes 8388608 | tf_op jit(solution)/shard_map/gram_near/pallas_call | solution.py:394
  51.1 11.3 %collective-permute-done.6.refs_5_ = f32[128,2048]{1,0:T(8,128)S(1)} collective-permute-done((f32[128,2048]{1,0:T(8,128)S(1)}, f32[128,2048]{1,0:T(8,128)S(1)}, u32[]{:S(2)}, u32[]{:S(2)}) %collective-permute-start.6) | collective-permute-done | bytes 1048608 | tf_op jit(solution)/shard_map/ppermute | solution.py:335
  62.4 0.0 copy-start.2
  62.4 3.3 %collective-permute-done.5.refs_4_ = f32[128,2048]{1,0:T(8,128)S(1)} collective-permute-done((f32[128,2048]{1,0:T(8,128)S(1)}, f32[128,2048]{1,0:T(8,128)S(1)}, u32[]{:S(2)}, u32[]{:S(2)}) %collective-permute-start.5) | collective-permute-done | bytes 1048608 | tf_op jit(solution)/shard_map/ppermute | solution.py:335
  65.7 0.0 copy-start.4
  65.8 2.5 %collective-permute-start.9 = (f32[64,2048]{1,0:T(8,128)S(1)}, f32[64,2048]{1,0:T(8,128)S(1)}, u32[]{:S(2)}, u32[]{:S(2)}) collective-permute-start(f32[64,2048]{1,0:T(8,128)S(1)} %slice.25), channel_id=1, source_target_pairs={{0,8},{1,9},{2,10},{3,11},{4,12},{5,13},{6,14},{7,15},{8,0},{9,1},... | collective-permute-start | bytes 1572872 | tf_op jit(solution)/shard_map/ppermute | solution.py:335
  68.3 0.0 collective-permute-start.8
  68.3 0.0 collective-permute-done.7.refs_6_
  68.3 0.0 copy-start.6
  68.3 10.7 %collective-permute-done.9.refs_8_ = f32[64,2048]{1,0:T(8,128)S(1)} collective-permute-done((f32[64,2048]{1,0:T(8,128)S(1)}, f32[64,2048]{1,0:T(8,128)S(1)}, u32[]{:S(2)}, u32[]{:S(2)}) %collective-permute-start.9) | collective-permute-done | bytes 524320 | tf_op jit(solution)/shard_map/ppermute | solution.py:335
  79.0 0.0 copy-start.8
  79.0 1.4 collective-permute-done.8.refs_7_
  80.4 14.9 %gram_far.1 = (f32[1152,128]{1,0:T(8,128)S(1)}, f32[1152,128]{1,0:T(8,128)S(1)}) custom-call(s32[9]{0:T(128)S(1)} %stack.39.where_ref, f32[64,4096]{1,0:T(8,128)S(1)} %pad_maximum_fusion.2.refs_0_, f32[64,4096]{1,0:T(8,128)S(1)} %collective-permute-done.1.refs_1_, f32[64,4096]{1,0:T(8,128)} %collective-permute-done.2.refs_2_, ...), custom_call_target="tpu_custom_call" | custom-call | flops 51539607552 | bytes 12582912 | tf_op jit(solution)/shard_map/gram_far/pallas_call | solution.py:394
  95.4 0.0 copy-done.2
  95.4 0.0 copy-done.4
  95.4 0.0 copy-done.6
  95.4 0.0 copy-done.8
  95.4 0.0 copy-done.10
  95.4 0.1 collective-permute-start.10
  95.5 2.0 %collective-permute-done.10 = f32[1152,128]{1,0:T(8,128)S(1)} collective-permute-done((f32[1152,128]{1,0:T(8,128)S(1)}, f32[1152,128]{1,0:T(8,128)S(1)}, u32[]{:S(2)}, u32[]{:S(2)}) %collective-permute-start.10) | collective-permute-done | bytes 589856 | tf_op jit(solution)/shard_map/ppermute | solution.py:335
  97.5 0.1 add.94
  97.6 15.7 %all_to_all.10 = f32[8,144,128]{2,1,0:T(8,128)} all-to-all(f32[8,144,128]{2,1,0:T(8,128)S(1)} %bitcast.21), channel_id=1, replica_groups=mesh['row'=8,'col'=16] {'row'}, dimensions={0} | all-to-all | bytes 1179648 | tf_op jit(solution)/shard_map/all_to_all | solution.py:433
  113.3 1.1 reduce_sum.9
  114.4 13.0 %all_to_all.11 = f32[8,144,128]{2,1,0:T(8,128)S(1)} all-to-all(f32[8,144,128]{2,1,0:T(8,128)S(1)} %broadcast_in_dim.10), channel_id=1, replica_groups=mesh['row'=8,'col'=16] {'row'}, dimensions={0} | all-to-all | bytes 1179648 | tf_op jit(solution)/shard_map/all_to_all | solution.py:436
  127.4 0.0 collective-permute-start.11
  127.4 2.0 %collective-permute-done.11.other_ref = f32[1152,128]{1,0:T(8,128)S(1)} collective-permute-done((f32[1152,128]{1,0:T(8,128)S(1)}, f32[1152,128]{1,0:T(8,128)S(1)}, u32[]{:S(2)}, u32[]{:S(2)}) %collective-permute-start.11) | collective-permute-done | bytes 589856 | tf_op jit(solution)/shard_map/ppermute | solution.py:335
  129.4 10.2 %solve.1 = (f32[512,128]{1,0:T(8,128)S(1)}, f32[512,128]{1,0:T(8,128)S(1)}) custom-call(s32[9]{0:T(128)S(1)} %stack.39.where_ref, f32[1152,128]{1,0:T(8,128)S(1)} %bitcast.20, f32[1152,128]{1,0:T(8,128)S(1)} %collective-permute-done.11.other_ref), custom_call_target="tpu_custom_call" | custom-call | tf_op jit(solution)/shard_map/solve/pallas_call | solution.py:439
  139.6 0.0 copy-start.1
  139.6 2.2 %copy-done.1 = f32[8192,128]{1,0:T(8,128)S(1)} copy-done((f32[8192,128]{1,0:T(8,128)S(1)}, f32[8192,128]{1,0:T(8,128)}, u32[]{:S(2)}) %copy-start.1) | copy-done | bytes 4194328
  141.8 1.2 copy-done.3
  143.0 1.2 copy-done.5
  144.3 1.2 copy-done.7
  145.5 1.0 copy-done.9
  146.5 1.0 copy-done.11
  147.6 11.6 %apply.1 = (f32[4096,128]{1,0:T(8,128)S(1)}, f32[4096,128]{1,0:T(8,128)S(1)}) custom-call(s32[9]{0:T(128)S(1)} %stack.39.where_ref, f32[64,4096]{1,0:T(8,128)S(1)} %pad_maximum_fusion.2.refs_0_, f32[64,4096]{1,0:T(8,128)S(1)} %collective-permute-done.1.refs_1_, f32[64,4096]{1,0:T(8,128)} %collective-permute-done.2.refs_2_, ...), custom_call_target="tpu_custom_call" | custom-call | tf_op jit(solution)/shard_map/apply/pallas_call | solution.py:455
  159.2 0.2 collective-permute-start.12
  159.4 0.3 broadcast_in_dim.4
  159.7 0.2 constant_dynamic-update-slice_fusion.1
  159.9 0.0 copy-start.12
  159.9 3.5 %collective-permute-done.12 = f32[4096,128]{1,0:T(8,128)S(1)} collective-permute-done((f32[4096,128]{1,0:T(8,128)S(1)}, f32[4096,128]{1,0:T(8,128)S(1)}, u32[]{:S(2)}, u32[]{:S(2)}) %collective-permute-start.12) | collective-permute-done | bytes 2097184 | tf_op jit(solution)/shard_map/ppermute | solution.py:335
  163.4 0.0 copy-done.12
  163.4 1.5 constant_dynamic-update-slice_fusion
  (11 shorter events, 0.2 us)
Async XLA Ops:
  1.3 3.6 %collective-permute-start = (f32[32,4096]{1,0:T(8,128)S(1)}, f32[32,4096]{1,0:T(8,128)S(1)}, u32[]{:S(2)}, u32[]{:S(2)}) collective-permute-start(f32[32,4096]{1,0:T(8,128)S(1)} %pad_maximum_fusion.4), channel_id=1, source_target_pairs={{0,1},{1,0},{2,3},{3,2},{4,5},{5,4},{6,7},{7,6},{8,9},{9,8},{10,11... | collective-permute-start | bytes 1572872 | tf_op jit(solution)/shard_map/ppermute | solution.py:335
  4.5 36.6 %collective-permute-start.4 = (f32[4096,128]{1,0:T(8,128)}, f32[4096,128]{1,0:T(8,128)}, u32[]{:S(2)}, u32[]{:S(2)}) collective-permute-start(f32[4096,128]{1,0:T(8,128)} %constant_dynamic-slice_fusion), channel_id=1, source_target_pairs={{0,1},{1,0},{2,3},{3,2},{4,5},{5,4},{6,7},{7,6},{8,9},{9,8},{10,11... | collective-permute-start | bytes 6291464 | tf_op jit(solution)/shard_map/ppermute | solution.py:335
  5.0 26.7 %collective-permute-start.3 = (f32[64,4096]{1,0:T(8,128)S(1)}, f32[64,4096]{1,0:T(8,128)S(1)}, u32[]{:S(2)}, u32[]{:S(2)}) collective-permute-start(f32[64,4096]{1,0:T(8,128)S(1)} %pad_maximum_fusion.2.refs_0_), channel_id=1, source_target_pairs={{0,8},{1,9},{2,10},{3,11},{4,12},{5,13},{6,14},{7,15},{8,0},{9,1},... | collective-permute-start | bytes 3145736 | tf_op jit(solution)/shard_map/ppermute | solution.py:335
  8.2 26.4 %collective-permute-start.2 = (f32[64,4096]{1,0:T(8,128)S(1)}, f32[64,4096]{1,0:T(8,128)}, u32[]{:S(2)}, u32[]{:S(2)}) collective-permute-start(f32[64,4096]{1,0:T(8,128)S(1)} %pad_maximum_fusion.2.refs_0_), channel_id=1, source_target_pairs={{0,6},{1,7},{2,0},{3,1},{4,2},{5,3},{6,4},{7,5},{8,14},{9,15},{10,... | collective-permute-start | bytes 3145736 | tf_op jit(solution)/shard_map/ppermute | solution.py:335
  12.2 25.7 %collective-permute-start.1 = (f32[64,4096]{1,0:T(8,128)S(1)}, f32[64,4096]{1,0:T(8,128)S(1)}, u32[]{:S(2)}, u32[]{:S(2)}) collective-permute-start(f32[64,4096]{1,0:T(8,128)S(1)} %pad_maximum_fusion.2.refs_0_), channel_id=1, source_target_pairs={{0,2},{1,3},{2,4},{3,5},{4,6},{5,7},{6,0},{7,1},{8,10},{9,11},{10,... | collective-permute-start | bytes 3145736 | tf_op jit(solution)/shard_map/ppermute | solution.py:335
  31.7 9.3 %copy-start = (f32[8192,128]{1,0:T(8,128)S(1)}, f32[8192,128]{1,0:T(8,128)}, u32[]{:S(2)}) copy-start(f32[8192,128]{1,0:T(8,128)} %refs_9_.3) | copy-start | bytes 12582916
  38.5 29.8 %collective-permute-start.7 = (f32[128,2048]{1,0:T(8,128)S(1)}, f32[128,2048]{1,0:T(8,128)S(1)}, u32[]{:S(2)}, u32[]{:S(2)}) collective-permute-start(f32[128,2048]{1,0:T(8,128)S(1)} %get-tuple-element.25), channel_id=1, source_target_pairs={{0,8},{1,9},{2,10},{3,11},{4,12},{5,13},{6,14},{7,15},{8,0},{9,1},... | collective-permute-start | bytes 3145736 | tf_op jit(solution)/shard_map/ppermute | solution.py:335
  39.0 23.3 %collective-permute-start.6 = (f32[128,2048]{1,0:T(8,128)S(1)}, f32[128,2048]{1,0:T(8,128)S(1)}, u32[]{:S(2)}, u32[]{:S(2)}) collective-permute-start(f32[128,2048]{1,0:T(8,128)S(1)} %get-tuple-element.26), channel_id=1, source_target_pairs={{0,6},{1,7},{2,0},{3,1},{4,2},{5,3},{6,4},{7,5},{8,14},{9,15},{10,... | collective-permute-start | bytes 3145736 | tf_op jit(solution)/shard_map/ppermute | solution.py:335
  40.7 25.0 %collective-permute-start.5 = (f32[128,2048]{1,0:T(8,128)S(1)}, f32[128,2048]{1,0:T(8,128)S(1)}, u32[]{:S(2)}, u32[]{:S(2)}) collective-permute-start(f32[128,2048]{1,0:T(8,128)S(1)} %get-tuple-element.27), channel_id=1, source_target_pairs={{0,2},{1,3},{2,4},{3,5},{4,6},{5,7},{6,0},{7,1},{8,10},{9,11},{10,... | collective-permute-start | bytes 3145736 | tf_op jit(solution)/shard_map/ppermute | solution.py:335
  62.4 33.0 %copy-start.2 = (f32[128,2048]{1,0:T(8,128)}, f32[128,2048]{1,0:T(8,128)S(1)}, u32[]{:S(2)}) copy-start(f32[128,2048]{1,0:T(8,128)S(1)} %collective-permute-done.6.refs_5_) | copy-start | bytes 3145732
  65.7 29.7 %copy-start.4 = (f32[128,2048]{1,0:T(8,128)}, f32[128,2048]{1,0:T(8,128)S(1)}, u32[]{:S(2)}) copy-start(f32[128,2048]{1,0:T(8,128)S(1)} %collective-permute-done.5.refs_4_) | copy-start | bytes 3145732
  65.8 13.2 %collective-permute-start.9 = (f32[64,2048]{1,0:T(8,128)S(1)}, f32[64,2048]{1,0:T(8,128)S(1)}, u32[]{:S(2)}, u32[]{:S(2)}) collective-permute-start(f32[64,2048]{1,0:T(8,128)S(1)} %slice.25), channel_id=1, source_target_pairs={{0,8},{1,9},{2,10},{3,11},{4,12},{5,13},{6,14},{7,15},{8,0},{9,1},... | collective-permute-start | bytes 1572872 | tf_op jit(solution)/shard_map/ppermute | solution.py:335
  68.3 12.1 %collective-permute-start.8 = (f32[64,2048]{1,0:T(8,128)S(1)}, f32[64,2048]{1,0:T(8,128)S(1)}, u32[]{:S(2)}, u32[]{:S(2)}) collective-permute-start(f32[64,2048]{1,0:T(8,128)S(1)} %slice.24), channel_id=1, source_target_pairs={{0,2},{1,3},{2,4},{3,5},{4,6},{5,7},{6,0},{7,1},{8,10},{9,11},{10,... | collective-permute-start | bytes 1572872 | tf_op jit(solution)/shard_map/ppermute | solution.py:335
  68.3 27.1 %copy-start.6 = (f32[128,2048]{1,0:T(8,128)}, f32[128,2048]{1,0:T(8,128)S(1)}, u32[]{:S(2)}) copy-start(f32[128,2048]{1,0:T(8,128)S(1)} %collective-permute-done.7.refs_6_) | copy-start | bytes 3145732
  79.0 16.4 %copy-start.8 = (f32[64,2048]{1,0:T(8,128)}, f32[64,2048]{1,0:T(8,128)S(1)}, u32[]{:S(2)}) copy-start(f32[64,2048]{1,0:T(8,128)S(1)} %collective-permute-done.9.refs_8_) | copy-start | bytes 1572868
  80.4 15.0 %copy-start.10 = (f32[64,2048]{1,0:T(8,128)}, f32[64,2048]{1,0:T(8,128)S(1)}, u32[]{:S(2)}) copy-start(f32[64,2048]{1,0:T(8,128)S(1)} %collective-permute-done.8.refs_7_) | copy-start | bytes 1572868
  95.4 2.1 %collective-permute-start.10 = (f32[1152,128]{1,0:T(8,128)S(1)}, f32[1152,128]{1,0:T(8,128)S(1)}, u32[]{:S(2)}, u32[]{:S(2)}) collective-permute-start(f32[1152,128]{1,0:T(8,128)S(1)} %get-tuple-element.18), channel_id=1, source_target_pairs={{0,1},{1,0},{2,3},{3,2},{4,5},{5,4},{6,7},{7,6},{8,9},{9,8},{10,11... | collective-permute-start | bytes 1769480 | tf_op jit(solution)/shard_map/ppermute | solution.py:335
  127.4 2.0 %collective-permute-start.11 = (f32[1152,128]{1,0:T(8,128)S(1)}, f32[1152,128]{1,0:T(8,128)S(1)}, u32[]{:S(2)}, u32[]{:S(2)}) collective-permute-start(f32[1152,128]{1,0:T(8,128)S(1)} %bitcast.19), channel_id=1, source_target_pairs={{0,1},{1,0},{2,3},{3,2},{4,5},{5,4},{6,7},{7,6},{8,9},{9,8},{10,11... | collective-permute-start | bytes 1769480 | tf_op jit(solution)/shard_map/ppermute | solution.py:335
  139.6 2.2 %copy-start.1 = (f32[8192,128]{1,0:T(8,128)S(1)}, f32[8192,128]{1,0:T(8,128)}, u32[]{:S(2)}) copy-start(f32[8192,128]{1,0:T(8,128)} %refs_9_.3) | copy-start | bytes 12582916
  141.8 1.2 copy-start.3
  143.0 1.2 copy-start.5
  144.3 1.2 copy-start.7
  145.5 1.0 copy-start.9
  146.5 1.0 copy-start.11
  159.2 4.2 %collective-permute-start.12 = (f32[4096,128]{1,0:T(8,128)S(1)}, f32[4096,128]{1,0:T(8,128)S(1)}, u32[]{:S(2)}, u32[]{:S(2)}) collective-permute-start(f32[4096,128]{1,0:T(8,128)S(1)} %get-tuple-element.22), channel_id=1, source_target_pairs={{0,1},{1,0},{2,3},{3,2},{4,5},{5,4},{6,7},{7,6},{8,9},{9,8},{10,11... | collective-permute-start | bytes 6291464 | tf_op jit(solution)/shard_map/ppermute | solution.py:335
  159.9 3.5 %copy-start.12 = (f32[8192,128]{1,0:T(8,128)}, f32[8192,128]{1,0:T(8,128)S(1)}, u32[]{:S(2)}) copy-start(f32[8192,128]{1,0:T(8,128)S(1)} %constant_dynamic-update-slice_fusion.1) | copy-start | bytes 12582916

commit v5 on v4

--- a/solution.py
+++ b/solution.py
@@ -18,12 +18,9 @@
 PIECES = ((0, 0), (0, 1), (1, 1), (0, 2), (0, 3)), ((1, 2), (1, 3), (2, 2), (2, 3), (3, 3))
 
 
-def split3(value):
+def split2(value):
     high = value.astype(BF16)
-    rest = value - high.astype(F32)
-    middle = rest.astype(BF16)
-    low = (rest - middle.astype(F32)).astype(BF16)
-    return high, middle, low
+    return high, (value - high.astype(F32)).astype(BF16)
 
 
 def nn(left, right):
@@ -66,19 +63,19 @@
     count = 4 if first else 9
     panels, rest = refs[:count], refs[count:]
     if first:
-        own_ref, other_ref, out_ref, high, middle, low, even, skew, proj = rest
+        own_ref, other_ref, out_ref, high, low, even, skew, proj = rest
     else:
-        own_ref, other_ref, before_ref, keep_ref, send_ref, high, middle, low, even, skew, proj = rest
+        own_ref, other_ref, before_ref, keep_ref, send_ref, high, low, even, skew, proj = rest
     core = where_ref[CHIPS]
     lines = panels[0].shape[0] // 2
     half = even.shape[1]
     start_row = high.shape[0] - half
 
     def place(slot, value):
-        parts = split3(value)
+        parts = split2(value)
         for swap in range(2):
             begin = pl.multiple_of(slot * 2 * lines + lines * (core ^ swap), lines)
-            for target, part in zip((high, middle, low), parts):
+            for target, part in zip((high, low), parts):
                 target[pl.ds(begin, lines), :] = part[swap * lines : (swap + 1) * lines]
 
     for slot in range(4):
@@ -92,25 +89,16 @@
         skew[...] = jnp.zeros_like(skew)
         proj[...] = jnp.zeros_like(proj)
 
-    one, two, three = high[start_row:, :], middle[start_row:, :], low[start_row:, :]
-    skew[...] += nt(one, two) + nt(one, three)
+    one, two = high[start_row:, :], low[start_row:, :]
+    skew[...] += nt(one, two)
     if first:
-        even[...] += nt(one, one) + nt(two, two)
+        even[...] += nt(one, one)
     else:
-        even[half:, :] += nt(one, one) + nt(two, two)
-        one_a, two_a, three_a = high[:half, :], middle[:half, :], low[:half, :]
-        even[:half, :] += (
-            (nt(one_a, three) + nt(three_a, one) + nt(two_a, two))
-            + (nt(one_a, two) + nt(two_a, one))
-            + nt(one_a, one)
-        )
-    current = jnp.concatenate([own_ref[...], other_ref[...]], axis=1)
-    x_one, x_two, x_three = split3(current)
-    proj[...] += (
-        (nn(one, x_three) + nn(three, x_one) + nn(two, x_two))
-        + (nn(one, x_two) + nn(two, x_one))
-        + nn(one, x_one)
-    )
+        even[half:, :] += nt(one, one)
+        one_a, two_a = high[:half, :], low[:half, :]
+        even[:half, :] += (nt(one_a, two) + nt(two_a, one)) + nt(one_a, one)
+    x_one, x_two = split2(jnp.concatenate([own_ref[...], other_ref[...]], axis=1))
+    proj[...] += (nn(one, x_two) + nn(two, x_one)) + nn(one, x_one)
 
     @pl.when(step == steps - 1)
     def _():
@@ -159,7 +147,7 @@
                 blocks(0, send_ref)
 
 
-def solve_kernel(where_ref, mine_ref, other_ref, own_ref, partner_ref, both, rows_done, ordered, sides):
+def solve(where_ref, mine_ref, other_ref, solved_ref, both, rows_done, ordered, sides):
     core = where_ref[CHIPS]
     both[core] = mine_ref[...]
     both[1 - core] = other_ref[...]
@@ -262,36 +250,32 @@
     right_side = sides[...]
     second = full(inverses[1], right_side[panel:])
     first = full(inverses[0], right_side[:panel] - full(corner, second))
-    own_ref[0:panel, :] = first[:, :WIDE]
-    own_ref[panel:, :] = second[:, :WIDE]
-    partner_ref[0:panel, :] = first[:, WIDE:]
-    partner_ref[panel:, :] = second[:, WIDE:]
+    solved_ref[0:panel, :] = first
+    solved_ref[panel:, :] = second
 
 
 def apply_kernel(where_ref, *refs):
     step = pl.program_id(0)
     steps = pl.num_programs(0)
     panels = refs[:9]
-    current_own, current_other, solved_own, solved_other, out_own, out_other, high, middle, low, merged = refs[9:]
+    current_own, current_other, mine_ref, theirs_ref, out_own, out_other = refs[9:15]
+    solved, high, low, merged, both, rows_done, ordered, sides = refs[15:]
     core = where_ref[CHIPS]
-    panel = solved_own.shape[0] // 2
+    panel = solved.shape[0] // 2
     chunk = panels[0].shape[0]
     group = chunk // 4
 
     @pl.when(step == 0)
     def _():
+        solve(where_ref, mine_ref, theirs_ref, solved, both, rows_done, ordered, sides)
         for index in range(2 * CHIPS):
             chip = where_ref[index // 2]
             for part in range(2):
                 start = pl.multiple_of(
                     part * panel + chip * 2 * group + group * (core ^ (index % 2)), group
                 )
-                lines = jnp.concatenate(
-                    [solved_own[pl.ds(start, group), :], solved_other[pl.ds(start, group), :]],
-                    axis=1,
-                )
                 at = (2 * index + part) * group
-                for target, value in zip((high, middle, low), split3(lines)):
+                for target, value in zip((high, low), split2(solved[pl.ds(start, group), :])):
                     target[at : at + group, :] = value
 
     def place(slot, value):
@@ -300,17 +284,13 @@
     for slot in range(4):
         place(slot, panels[slot][...])
     each_far(step, steps, panels[4:], place)
-    one, two, three = split3(merged[...])
-    first, second, third = high[...], middle[...], low[...]
+    one, two = split2(merged[...])
+    first, second = high[...], low[...]
 
     def tn(left, right):
         return lax.dot_general(left, right, (((0,), (0,)), ((), ())), preferred_element_type=F32)
 
-    change = (
-        (tn(one, third) + tn(three, first) + tn(two, second))
-        + (tn(one, second) + tn(two, first))
-        + tn(one, first)
-    )
+    change = (tn(one, second) + tn(two, first)) + tn(one, first)
     out_own[...] = current_own[...] - change[:, :WIDE]
     out_other[...] = current_other[...] - change[:, WIDE:]
 
@@ -353,14 +333,14 @@
     a_own = half_of(core)
     b_own = core_swap(half_of(1 - core))
     own = jnp.concatenate([a_own, b_own], axis=0)
-    given = lax.dynamic_slice_in_dim(vectors, (1 - core) * half, half, 0)
-    other = core_swap(given)
-
     away, below, above = across(own), up(own), down(own)
     near = (own, below, above, away)
-    sent_up = up(jnp.concatenate([below[:, :quarter], away[:, :quarter]], axis=0))
-    sent_down = down(jnp.concatenate([above[:, quarter:], away[:, :quarter]], axis=0))
-    sent_across = across(jnp.concatenate([below[:, quarter:], above[:, quarter:]], axis=0))
+    to_up = jnp.concatenate([below[:, :quarter], away[:, :quarter]], axis=0)
+    to_down = jnp.concatenate([above[:, quarter:], away[:, :quarter]], axis=0)
+    to_across = jnp.concatenate([below[:, quarter:], above[:, quarter:]], axis=0)
+    sent_up, sent_down, sent_across = up(to_up), down(to_down), across(to_across)
+    other = core_swap(vectors)
+
     chips = []
     for x_step, z_step in ((0, 0), (0, -1), (0, 1), (1, 0), (0, 2), (1, -1), (1, 1), (1, 2)):
         chips.append(jnp.bitwise_xor(plane, x_step) * DEPTH + (depth + z_step) % DEPTH)
@@ -380,7 +360,6 @@
     )
     parts_far = [early(2 * chunk), both, late(2 * chunk), early(chunk), late(chunk)]
     own_spec = pl.BlockSpec((TILE, columns), lambda j, w: (w[CHIPS] * steps + j, 0))
-    other_spec = pl.BlockSpec((TILE, columns), lambda j, w: (j, 0))
     length = size + 5 * WIDE
     span = size // 2
 
@@ -399,12 +378,12 @@
                 grid=(steps,),
                 in_specs=whole
                 + ([] if first else parts_far)
-                + [own_spec, other_spec]
+                + [own_spec, own_spec]
                 + [pl.BlockSpec(v.shape, lambda j, w: (0, 0, 0)) for v in extra],
                 out_specs=[
                     pl.BlockSpec(v.shape, lambda j, w, n=len(v.shape): (0,) * n) for v in shapes
                 ],
-                scratch_shapes=[pltpu.VMEM((height, TILE), BF16)] * 3
+                scratch_shapes=[pltpu.VMEM((height, TILE), BF16)] * 2
                 + [
                     pltpu.VMEM((height, span), F32),
                     pltpu.VMEM((span, span), F32),
@@ -415,7 +394,7 @@
                 dimension_semantics=("arbitrary",), vmem_limit_bytes=LIMIT
             ),
             cost_estimate=pl.CostEstimate(
-                flops=2 * 6 * units * span * span * half,
+                flops=2 * 3 * units * span * span * half,
                 bytes_accessed=4 * half * (height + columns * 2),
                 transcendentals=0,
             ),
@@ -436,22 +415,6 @@
     mine = lax.all_to_all(spread, "row", 0, 0).reshape(length, WIDE)
     theirs = core_swap(mine)
 
-    solved_own, solved_other = pl.pallas_call(
-        solve_kernel,
-        out_shape=[jax.ShapeDtypeStruct((size, WIDE), F32)] * 2,
-        grid_spec=pltpu.PrefetchScalarGridSpec(
-            num_scalar_prefetch=1,
-            grid=(1,),
-            in_specs=[pl.BlockSpec((length, WIDE), lambda j, w: (0, 0))] * 2,
-            out_specs=[pl.BlockSpec((size, WIDE), lambda j, w: (0, 0))] * 2,
-            scratch_shapes=[pltpu.VMEM((2, length, WIDE), F32)]
-            + [pltpu.VMEM((size, size), F32)] * 2
-            + [pltpu.VMEM((size, 2 * WIDE), F32)],
-        ),
-        compiler_params=pltpu.CompilerParams(vmem_limit_bytes=32 << 20),
-        name="solve",
-    )(where, mine, theirs)
-
     result_own, result_other = pl.pallas_call(
         apply_kernel,
         out_shape=[jax.ShapeDtypeStruct((half, columns), F32)] * 2,
@@ -460,17 +423,20 @@
             grid=(steps,),
             in_specs=whole
             + parts_far
-            + [own_spec, other_spec]
-            + [pl.BlockSpec((size, WIDE), lambda j, w: (0, 0))] * 2,
+            + [own_spec, own_spec]
+            + [pl.BlockSpec((length, WIDE), lambda j, w: (0, 0))] * 2,
             out_specs=[pl.BlockSpec((TILE, columns), lambda j, w: (j, 0))] * 2,
-            scratch_shapes=[pltpu.VMEM((size, 2 * WIDE), BF16)] * 3
-            + [pltpu.VMEM((size, TILE), F32)],
+            scratch_shapes=[pltpu.VMEM((size, 2 * WIDE), F32)]
+            + [pltpu.VMEM((size, 2 * WIDE), BF16)] * 2
+            + [pltpu.VMEM((size, TILE), F32), pltpu.VMEM((2, length, WIDE), F32)]
+            + [pltpu.VMEM((size, size), F32)] * 2
+            + [pltpu.VMEM((size, 2 * WIDE), F32)],
         ),
         compiler_params=pltpu.CompilerParams(
-            dimension_semantics=("arbitrary",), vmem_limit_bytes=LIMIT
+            dimension_semantics=("arbitrary",), vmem_limit_bytes=58 << 20
         ),
-        name="apply",
-    )(where, *near, *far, vectors, other, solved_own, solved_other)
+        name="solve_apply",
+    )(where, *near, *far, vectors, other, mine, theirs)
 
     returned = core_swap(result_other)
     result = jnp.zeros((rows, columns), F32)

time: 167 us -> 154 us (0.922)
  local copies, waits for them, and re-layouts: 15.6 us -> 6.51 us
  Pallas kernels: 46.7 us -> 40.4 us
  waiting for transfers between devices: 58.8 us -> 62.9 us
    pallas_call x1, Pallas kernels: 11.6 us -> 22.1 us  [per_device(): pl.pallas_call(apply_kernel, out_shape=[jax.ShapeDtypeStruct((half, colum...]
    pallas_call x1 -> x0, Pallas kernels: 10.2 us -> none  [per_device(): pl.pallas_call(solve_kernel, out_shape=[jax.ShapeDtypeStruct((size, WIDE)...]
    pallas_call x2, Pallas kernels: 24.9 us -> 18.3 us  [gram(): pl.pallas_call(functools.partial(gram_kernel, first=first), out_shape=sha...]
    unnamed x26 -> x28, local copies, waits for them, and re-layouts: 7.97 us -> 1.98 us
    ppermute x13, waiting for transfers between devices: 58.8 us -> 62.9 us  [permute(): return lax.ppermute(value, 'col', pairs)]
    dynamic_slice x1 -> x0, local copies, waits for them, and re-layouts: 3.05 us -> none  [per_device(): given = lax.dynamic_slice_in_dim(vectors, (1 - core) * half, half, 0)]
  transfers between devices with their start and end apart: 13 -> 13, of which waited for: 10 -> 11; matrix products, arithmetic and copies ran while one was open for 3% -> 2% of each run, Pallas kernels for 6% -> 5%
where the time goes in v5:
time: 154 us; the launch traced here: 153 us
  waiting for transfers between devices  62.9 us (41%)
  Pallas kernels  40.4 us (26%)
  blocking collectives  28.5 us (19%)
  starting transfers between devices  13.4 us (9%)
  local copies, waits for them, and re-layouts  6.51 us (4%)
    ppermute x13, waiting for transfers between devices, permute(): return lax.ppermute(value, 'col', pairs)  62.9 us
    pallas_call x1, Pallas kernels, per_device(): pl.pallas_call(apply_kernel, out_shape=[jax.ShapeDtypeStruct((half, colum...  22.1 us
    pallas_call x2, Pallas kernels, gram(): pl.pallas_call(functools.partial(gram_kernel, first=first), out_shape=sha...  18.3 us
    all_to_all x1, blocking collectives, per_device(): lax.all_to_all(mine.reshape(members, length // members, WIDE), 'row', 0, 0)  15.5 us
    ppermute x13, starting transfers between devices, permute(): return lax.ppermute(value, 'col', pairs)  13.4 us
    all_to_all x1, blocking collectives, per_device(): mine = lax.all_to_all(spread, 'row', 0, 0).reshape(length, WIDE)  13 us
  transfers between devices with their start and end apart: 13, of which 11 were waited for; matrix products, arithmetic and copies ran while one was open for 2% of the time, Pallas kernels for 5%

profile of v5, /device:TPU:0, one launch (start us, length us, event | category | flops | bytes accessed | tf_op | source)
XLA Modules:
  0.0 152.6 jit_solution(16838984564929139784)
XLA Ops:
  0.0 0.0 collective-permute-start.4
  0.0 1.3 dynamic-slice_bitcast_fusion.2
  1.3 0.6 collective-permute-start
  1.9 6.0 %collective-permute-done = f32[32,4096]{1,0:T(8,128)S(1)} collective-permute-done((f32[32,4096]{1,0:T(8,128)S(1)}, f32[32,4096]{1,0:T(8,128)S(1)}, u32[]{:S(2)}, u32[]{:S(2)}) %collective-permute-start) | collective-permute-done | bytes 524320 | tf_op jit(solution)/shard_map/ppermute | solution.py:315
  7.9 0.1 pad_maximum_fusion.2.refs_0_
  8.0 0.0 copy-start.1
  8.0 3.2 %collective-permute-start.3 = (f32[64,4096]{1,0:T(8,128)S(1)}, f32[64,4096]{1,0:T(8,128)S(1)}, u32[]{:S(2)}, u32[]{:S(2)}) collective-permute-start(f32[64,4096]{1,0:T(8,128)S(1)} %pad_maximum_fusion.2.refs_0_), channel_id=1, source_target_pairs={{0,8},{1,9},{2,10},{3,11},{4,12},{5,13},{6,14},{7,15},{8,0},{9,1},... | collective-permute-start | bytes 3145736 | tf_op jit(solution)/shard_map/ppermute | solution.py:315
  11.2 4.0 %collective-permute-start.2 = (f32[64,4096]{1,0:T(8,128)S(1)}, f32[64,4096]{1,0:T(8,128)}, u32[]{:S(2)}, u32[]{:S(2)}) collective-permute-start(f32[64,4096]{1,0:T(8,128)S(1)} %pad_maximum_fusion.2.refs_0_), channel_id=1, source_target_pairs={{0,6},{1,7},{2,0},{3,1},{4,2},{5,3},{6,4},{7,5},{8,14},{9,15},{10,... | collective-permute-start | bytes 3145736 | tf_op jit(solution)/shard_map/ppermute | solution.py:315
  15.2 0.0 collective-permute-start.1
  15.2 0.1 stack.39.where_ref
  15.3 0.0 copy-start.9
  15.3 19.5 %collective-permute-done.3.refs_3_ = f32[64,4096]{1,0:T(8,128)S(1)} collective-permute-done((f32[64,4096]{1,0:T(8,128)S(1)}, f32[64,4096]{1,0:T(8,128)S(1)}, u32[]{:S(2)}, u32[]{:S(2)}) %collective-permute-start.3) | collective-permute-done | bytes 1048608 | tf_op jit(solution)/shard_map/ppermute | solution.py:315
  34.8 0.0 copy-start.3
  34.8 0.0 copy-start
  34.8 2.8 %collective-permute-done.2.refs_2_ = f32[64,4096]{1,0:T(8,128)} collective-permute-done((f32[64,4096]{1,0:T(8,128)S(1)}, f32[64,4096]{1,0:T(8,128)}, u32[]{:S(2)}, u32[]{:S(2)}) %collective-permute-start.2) | collective-permute-done | bytes 1048608 | tf_op jit(solution)/shard_map/ppermute | solution.py:315
  37.7 1.1 slice.28
  38.7 2.3 %collective-permute-done.1.refs_1_ = f32[64,4096]{1,0:T(8,128)S(1)} collective-permute-done((f32[64,4096]{1,0:T(8,128)S(1)}, f32[64,4096]{1,0:T(8,128)S(1)}, u32[]{:S(2)}, u32[]{:S(2)}) %collective-permute-start.1) | collective-permute-done | bytes 1048608 | tf_op jit(solution)/shard_map/ppermute | solution.py:315
  41.1 0.0 copy-start.2
  41.1 0.1 fusion
  41.1 0.4 pad_maximum_fusion.3
  41.5 0.1 collective-permute-start.5
  41.6 3.2 %collective-permute-start.6 = (f32[128,2048]{1,0:T(8,128)S(1)}, f32[128,2048]{1,0:T(8,128)S(1)}, u32[]{:S(2)}, u32[]{:S(2)}) collective-permute-start(f32[128,2048]{1,0:T(8,128)S(1)} %get-tuple-element.22), channel_id=1, source_target_pairs={{0,6},{1,7},{2,0},{3,1},{4,2},{5,3},{6,4},{7,5},{8,14},{9,15},{10,... | collective-permute-start | bytes 3145736 | tf_op jit(solution)/shard_map/ppermute | solution.py:315
  44.8 0.5 collective-permute-start.7
  45.3 0.0 collective-permute-done.4.refs_5_.refs_10_
  45.3 0.0 copy-done
  45.3 8.2 %gram_near.1.refs_11_ = f32[2,640,128]{2,1,0:T(8,128)S(1)} custom-call(s32[9]{0:T(128)S(1)} %stack.39.where_ref, f32[64,4096]{1,0:T(8,128)S(1)} %pad_maximum_fusion.2.refs_0_, f32[64,4096]{1,0:T(8,128)S(1)} %collective-permute-done.1.refs_1_, f32[64,4096]{1,0:T(8,128)} %collective-permute-done.2.refs_2_, f32[64,4096]{1,0:T(8,128)S(1)} %collective-permute-done.3.refs_3_, ...), custom_call_target="tpu_custom_call" | custom-call | flops 16106127360 | bytes 8388608 | tf_op jit(solution)/shard_map/gram_near/pallas_call | solution.py:373
  53.5 13.0 %collective-permute-done.5.refs_4_ = f32[128,2048]{1,0:T(8,128)S(1)} collective-permute-done((f32[128,2048]{1,0:T(8,128)S(1)}, f32[128,2048]{1,0:T(8,128)S(1)}, u32[]{:S(2)}, u32[]{:S(2)}) %collective-permute-start.5) | collective-permute-done | bytes 1048608 | tf_op jit(solution)/shard_map/ppermute | solution.py:315
  66.5 0.0 copy-start.4
  66.5 0.0 collective-permute-done.6.refs_5_
  66.6 0.1 collective-permute-start.8
  66.7 1.4 collective-permute-start.9
  68.1 2.2 %collective-permute-done.7.refs_6_ = f32[128,2048]{1,0:T(8,128)S(1)} collective-permute-done((f32[128,2048]{1,0:T(8,128)S(1)}, f32[128,2048]{1,0:T(8,128)S(1)}, u32[]{:S(2)}, u32[]{:S(2)}) %collective-permute-start.7) | collective-permute-done | bytes 1048608 | tf_op jit(solution)/shard_map/ppermute | solution.py:315
  70.3 9.1 %collective-permute-done.8.refs_7_ = f32[64,2048]{1,0:T(8,128)S(1)} collective-permute-done((f32[64,2048]{1,0:T(8,128)S(1)}, f32[64,2048]{1,0:T(8,128)S(1)}, u32[]{:S(2)}, u32[]{:S(2)}) %collective-permute-start.8) | collective-permute-done | bytes 524320 | tf_op jit(solution)/shard_map/ppermute | solution.py:315
  79.4 1.3 collective-permute-done.9.refs_8_
  80.7 0.0 copy-done.1
  80.7 0.0 copy-done.9
  80.7 0.0 copy-done.3
  80.7 0.0 copy-done.2
  80.8 0.0 copy-start.8
  80.8 10.1 %gram_far.1 = (f32[1152,128]{1,0:T(8,128)S(1)}, f32[1152,128]{1,0:T(8,128)S(1)}) custom-call(s32[9]{0:T(128)S(1)} %stack.39.where_ref, f32[64,4096]{1,0:T(8,128)S(1)} %pad_maximum_fusion.2.refs_0_, f32[64,4096]{1,0:T(8,128)S(1)} %collective-permute-done.1.refs_1_, f32[64,4096]{1,0:T(8,128)} %collective-permute-done.2.refs_2_, ...), custom_call_target="tpu_custom_call" | custom-call | flops 25769803776 | bytes 12582912 | tf_op jit(solution)/shard_map/gram_far/pallas_call | solution.py:373
  90.9 0.0 copy-done.4
  90.9 0.0 copy-done.5
  90.9 0.0 copy-done.6
  90.9 0.0 copy-done.7
  90.9 0.0 copy-done.8
  90.9 0.1 collective-permute-start.10
  91.0 2.0 %collective-permute-done.10 = f32[1152,128]{1,0:T(8,128)S(1)} collective-permute-done((f32[1152,128]{1,0:T(8,128)S(1)}, f32[1152,128]{1,0:T(8,128)S(1)}, u32[]{:S(2)}, u32[]{:S(2)}) %collective-permute-start.10) | collective-permute-done | bytes 589856 | tf_op jit(solution)/shard_map/ppermute | solution.py:315
  93.0 0.1 add.93
  93.1 15.5 %all_to_all.10 = f32[8,144,128]{2,1,0:T(8,128)S(1)} all-to-all(f32[8,144,128]{2,1,0:T(8,128)S(1)} %bitcast.19), channel_id=1, replica_groups=mesh['row'=8,'col'=16] {'row'}, dimensions={0} | all-to-all | bytes 1179648 | tf_op jit(solution)/shard_map/all_to_all | solution.py:412
  108.7 13.0 %all_to_all.11 = f32[8,144,128]{2,1,0:T(8,128)S(1)} all-to-all(f32[8,144,128]{2,1,0:T(8,128)S(1)} %broadcast_in_dim.10), channel_id=1, replica_groups=mesh['row'=8,'col'=16] {'row'}, dimensions={0} | all-to-all | bytes 1179648 | tf_op jit(solution)/shard_map/all_to_all | solution.py:415
  121.7 0.0 collective-permute-start.11
  121.7 2.0 %collective-permute-done.11.refs_12_ = f32[1152,128]{1,0:T(8,128)S(1)} collective-permute-done((f32[1152,128]{1,0:T(8,128)S(1)}, f32[1152,128]{1,0:T(8,128)S(1)}, u32[]{:S(2)}, u32[]{:S(2)}) %collective-permute-start.11) | collective-permute-done | bytes 589856 | tf_op jit(solution)/shard_map/ppermute | solution.py:315
  123.7 0.0 copy-done.11
  123.7 0.8 copy-done.13
  124.5 22.1 %solve_apply.1 = (f32[4096,128]{1,0:T(8,128)}, f32[4096,128]{1,0:T(8,128)}) custom-call(s32[9]{0:T(128)} %copy-done.9, f32[64,4096]{1,0:T(8,128)} %copy-done.1, f32[64,4096]{1,0:T(8,128)} %copy-done.2, f32[64,4096]{1,0:T(8,128)} %collective-permute-done.2.refs_2_, f32[64,4096]{1,0:T(8,128)} %copy-done.3, f32[128,2048]{1,0:T(8,128)} %copy-done.4, ...), custom_call_target="tpu_custom_call" | custom-call | tf_op jit(solution)/shard_map/solve_apply/pallas_call | solution.py:418
  146.6 0.0 copy-start.12
  146.7 0.2 collective-permute-start.12
  146.9 0.3 broadcast_in_dim.4
  147.2 1.1 copy-done.12
  148.2 0.2 constant_dynamic-update-slice_fusion.1
  148.4 0.0 copy-start.10
  148.4 2.7 %collective-permute-done.12 = f32[4096,128]{1,0:T(8,128)S(1)} collective-permute-done((f32[4096,128]{1,0:T(8,128)}, f32[4096,128]{1,0:T(8,128)S(1)}, u32[]{:S(2)}, u32[]{:S(2)}) %collective-permute-start.12) | collective-permute-done | bytes 2097184 | tf_op jit(solution)/shard_map/ppermute | solution.py:315
  151.1 0.0 copy-done.10
  151.1 1.5 constant_dynamic-update-slice_fusion
  (11 shorter events, 0.2 us)
Async XLA Ops:
  0.0 45.3 %collective-permute-start.4 = (f32[8192,128]{1,0:T(8,128)}, f32[8192,128]{1,0:T(8,128)}, u32[]{:S(2)}, u32[]{:S(2)}) collective-permute-start(f32[8192,128]{1,0:T(8,128)} %refs_9_.3), channel_id=1, source_target_pairs={{0,1},{1,0},{2,3},{3,2},{4,5},{5,4},{6,7},{7,6},{8,9},{9,8},{10,11... | collective-permute-start | bytes 12582920 | tf_op jit(solution)/shard_map/ppermute | solution.py:315
  1.3 6.6 %collective-permute-start = (f32[32,4096]{1,0:T(8,128)S(1)}, f32[32,4096]{1,0:T(8,128)S(1)}, u32[]{:S(2)}, u32[]{:S(2)}) collective-permute-start(f32[32,4096]{1,0:T(8,128)S(1)} %pad_maximum_fusion.4), channel_id=1, source_target_pairs={{0,1},{1,0},{2,3},{3,2},{4,5},{5,4},{6,7},{7,6},{8,9},{9,8},{10,11... | collective-permute-start | bytes 1572872 | tf_op jit(solution)/shard_map/ppermute | solution.py:315
  8.0 72.8 %copy-start.1 = (f32[64,4096]{1,0:T(8,128)}, f32[64,4096]{1,0:T(8,128)S(1)}, u32[]{:S(2)}) copy-start(f32[64,4096]{1,0:T(8,128)S(1)} %pad_maximum_fusion.2.refs_0_) | copy-start | bytes 3145732
  8.0 26.8 %collective-permute-start.3 = (f32[64,4096]{1,0:T(8,128)S(1)}, f32[64,4096]{1,0:T(8,128)S(1)}, u32[]{:S(2)}, u32[]{:S(2)}) collective-permute-start(f32[64,4096]{1,0:T(8,128)S(1)} %pad_maximum_fusion.2.refs_0_), channel_id=1, source_target_pairs={{0,8},{1,9},{2,10},{3,11},{4,12},{5,13},{6,14},{7,15},{8,0},{9,1},... | collective-permute-start | bytes 3145736 | tf_op jit(solution)/shard_map/ppermute | solution.py:315
  11.2 26.5 %collective-permute-start.2 = (f32[64,4096]{1,0:T(8,128)S(1)}, f32[64,4096]{1,0:T(8,128)}, u32[]{:S(2)}, u32[]{:S(2)}) collective-permute-start(f32[64,4096]{1,0:T(8,128)S(1)} %pad_maximum_fusion.2.refs_0_), channel_id=1, source_target_pairs={{0,6},{1,7},{2,0},{3,1},{4,2},{5,3},{6,4},{7,5},{8,14},{9,15},{10,... | collective-permute-start | bytes 3145736 | tf_op jit(solution)/shard_map/ppermute | solution.py:315
  15.2 25.9 %collective-permute-start.1 = (f32[64,4096]{1,0:T(8,128)S(1)}, f32[64,4096]{1,0:T(8,128)S(1)}, u32[]{:S(2)}, u32[]{:S(2)}) collective-permute-start(f32[64,4096]{1,0:T(8,128)S(1)} %pad_maximum_fusion.2.refs_0_), channel_id=1, source_target_pairs={{0,2},{1,3},{2,4},{3,5},{4,6},{5,7},{6,0},{7,1},{8,10},{9,11},{10,... | collective-permute-start | bytes 3145736 | tf_op jit(solution)/shard_map/ppermute | solution.py:315
  15.3 65.4 %copy-start.9 = (s32[9]{0:T(128)}, s32[9]{0:T(128)S(1)}, u32[]{:S(2)}) copy-start(s32[9]{0:T(128)S(1)} %stack.39.where_ref) | copy-start | bytes 112
  34.8 46.0 %copy-start.3 = (f32[64,4096]{1,0:T(8,128)}, f32[64,4096]{1,0:T(8,128)S(1)}, u32[]{:S(2)}) copy-start(f32[64,4096]{1,0:T(8,128)S(1)} %collective-permute-done.3.refs_3_) | copy-start | bytes 3145732
  34.8 10.5 %copy-start = (f32[8192,128]{1,0:T(8,128)S(1)}, f32[8192,128]{1,0:T(8,128)}, u32[]{:S(2)}) copy-start(f32[8192,128]{1,0:T(8,128)} %refs_9_.3) | copy-start | bytes 12582916
  41.1 39.7 %copy-start.2 = (f32[64,4096]{1,0:T(8,128)}, f32[64,4096]{1,0:T(8,128)S(1)}, u32[]{:S(2)}) copy-start(f32[64,4096]{1,0:T(8,128)S(1)} %collective-permute-done.1.refs_1_) | copy-start | bytes 3145732
  41.5 25.0 %collective-permute-start.5 = (f32[128,2048]{1,0:T(8,128)S(1)}, f32[128,2048]{1,0:T(8,128)S(1)}, u32[]{:S(2)}, u32[]{:S(2)}) collective-permute-start(f32[128,2048]{1,0:T(8,128)S(1)} %get-tuple-element.23), channel_id=1, source_target_pairs={{0,2},{1,3},{2,4},{3,5},{4,6},{5,7},{6,0},{7,1},{8,10},{9,11},{10,... | collective-permute-start | bytes 3145736 | tf_op jit(solution)/shard_map/ppermute | solution.py:315
  41.6 24.9 %collective-permute-start.6 = (f32[128,2048]{1,0:T(8,128)S(1)}, f32[128,2048]{1,0:T(8,128)S(1)}, u32[]{:S(2)}, u32[]{:S(2)}) collective-permute-start(f32[128,2048]{1,0:T(8,128)S(1)} %get-tuple-element.22), channel_id=1, source_target_pairs={{0,6},{1,7},{2,0},{3,1},{4,2},{5,3},{6,4},{7,5},{8,14},{9,15},{10,... | collective-permute-start | bytes 3145736 | tf_op jit(solution)/shard_map/ppermute | solution.py:315
  44.8 25.5 %collective-permute-start.7 = (f32[128,2048]{1,0:T(8,128)S(1)}, f32[128,2048]{1,0:T(8,128)S(1)}, u32[]{:S(2)}, u32[]{:S(2)}) collective-permute-start(f32[128,2048]{1,0:T(8,128)S(1)} %get-tuple-element.21), channel_id=1, source_target_pairs={{0,8},{1,9},{2,10},{3,11},{4,12},{5,13},{6,14},{7,15},{8,0},{9,1},... | collective-permute-start | bytes 3145736 | tf_op jit(solution)/shard_map/ppermute | solution.py:315
  66.5 24.3 %copy-start.4 = (f32[128,2048]{1,0:T(8,128)}, f32[128,2048]{1,0:T(8,128)S(1)}, u32[]{:S(2)}) copy-start(f32[128,2048]{1,0:T(8,128)S(1)} %collective-permute-done.5.refs_4_) | copy-start | bytes 3145732
  66.5 24.4 %copy-start.5 = (f32[128,2048]{1,0:T(8,128)}, f32[128,2048]{1,0:T(8,128)S(1)}, u32[]{:S(2)}) copy-start(f32[128,2048]{1,0:T(8,128)S(1)} %collective-permute-done.6.refs_5_) | copy-start | bytes 3145732
  66.6 12.8 %collective-permute-start.8 = (f32[64,2048]{1,0:T(8,128)S(1)}, f32[64,2048]{1,0:T(8,128)S(1)}, u32[]{:S(2)}, u32[]{:S(2)}) collective-permute-start(f32[64,2048]{1,0:T(8,128)S(1)} %slice.24), channel_id=1, source_target_pairs={{0,2},{1,3},{2,4},{3,5},{4,6},{5,7},{6,0},{7,1},{8,10},{9,11},{10,... | collective-permute-start | bytes 1572872 | tf_op jit(solution)/shard_map/ppermute | solution.py:315
  66.7 14.0 %collective-permute-start.9 = (f32[64,2048]{1,0:T(8,128)S(1)}, f32[64,2048]{1,0:T(8,128)S(1)}, u32[]{:S(2)}, u32[]{:S(2)}) collective-permute-start(f32[64,2048]{1,0:T(8,128)S(1)} %slice.25), channel_id=1, source_target_pairs={{0,8},{1,9},{2,10},{3,11},{4,12},{5,13},{6,14},{7,15},{8,0},{9,1},... | collective-permute-start | bytes 1572872 | tf_op jit(solution)/shard_map/ppermute | solution.py:315
  70.3 20.6 %copy-start.6 = (f32[128,2048]{1,0:T(8,128)}, f32[128,2048]{1,0:T(8,128)S(1)}, u32[]{:S(2)}) copy-start(f32[128,2048]{1,0:T(8,128)S(1)} %collective-permute-done.7.refs_6_) | copy-start | bytes 3145732
  79.4 11.5 %copy-start.7 = (f32[64,2048]{1,0:T(8,128)}, f32[64,2048]{1,0:T(8,128)S(1)}, u32[]{:S(2)}) copy-start(f32[64,2048]{1,0:T(8,128)S(1)} %collective-permute-done.8.refs_7_) | copy-start | bytes 1572868
  80.8 10.2 %copy-start.8 = (f32[64,2048]{1,0:T(8,128)}, f32[64,2048]{1,0:T(8,128)S(1)}, u32[]{:S(2)}) copy-start(f32[64,2048]{1,0:T(8,128)S(1)} %collective-permute-done.9.refs_8_) | copy-start | bytes 1572868
  90.9 2.1 %collective-permute-start.10 = (f32[1152,128]{1,0:T(8,128)S(1)}, f32[1152,128]{1,0:T(8,128)S(1)}, u32[]{:S(2)}, u32[]{:S(2)}) collective-permute-start(f32[1152,128]{1,0:T(8,128)S(1)} %get-tuple-element.16), channel_id=1, source_target_pairs={{0,1},{1,0},{2,3},{3,2},{4,5},{5,4},{6,7},{7,6},{8,9},{9,8},{10,11... | collective-permute-start | bytes 1769480 | tf_op jit(solution)/shard_map/ppermute | solution.py:315
  121.7 2.0 %copy-start.11 = (f32[8,144,128]{2,1,0:T(8,128)}, f32[8,144,128]{2,1,0:T(8,128)S(1)}, u32[]{:S(2)}) copy-start(f32[8,144,128]{2,1,0:T(8,128)S(1)} %all_to_all.11) | copy-start | bytes 1769476
  121.7 2.0 %collective-permute-start.11 = (f32[1152,128]{1,0:T(8,128)S(1)}, f32[1152,128]{1,0:T(8,128)S(1)}, u32[]{:S(2)}, u32[]{:S(2)}) collective-permute-start(f32[1152,128]{1,0:T(8,128)S(1)} %bitcast.20), channel_id=1, source_target_pairs={{0,1},{1,0},{2,3},{3,2},{4,5},{5,4},{6,7},{7,6},{8,9},{9,8},{10,11... | collective-permute-start | bytes 1769480 | tf_op jit(solution)/shard_map/ppermute | solution.py:315
  123.7 0.8 copy-start.13
  146.6 1.6 %copy-start.12 = (f32[4096,128]{1,0:T(8,128)S(1)}, f32[4096,128]{1,0:T(8,128)}, u32[]{:S(2)}) copy-start(f32[4096,128]{1,0:T(8,128)} %get-tuple-element.17) | copy-start | bytes 6291460
  146.7 4.5 %collective-permute-start.12 = (f32[4096,128]{1,0:T(8,128)}, f32[4096,128]{1,0:T(8,128)S(1)}, u32[]{:S(2)}, u32[]{:S(2)}) collective-permute-start(f32[4096,128]{1,0:T(8,128)} %get-tuple-element.18), channel_id=1, source_target_pairs={{0,1},{1,0},{2,3},{3,2},{4,5},{5,4},{6,7},{7,6},{8,9},{9,8},{10,11... | collective-permute-start | bytes 6291464 | tf_op jit(solution)/shard_map/ppermute | solution.py:315
  148.4 2.7 %copy-start.10 = (f32[8192,128]{1,0:T(8,128)}, f32[8192,128]{1,0:T(8,128)S(1)}, u32[]{:S(2)}) copy-start(f32[8192,128]{1,0:T(8,128)S(1)} %constant_dynamic-update-slice_fusion.1) | copy-start | bytes 12582916

commit v6 on v5

--- a/solution.py
+++ b/solution.py
@@ -13,7 +13,7 @@
 PLANES, DEPTH, CORES = 2, 4, 2
 CHIPS = PLANES * DEPTH
 WIDE = 128
-TILE = 512
+TILE = 1024
 LIMIT = 24 << 20
 PIECES = ((0, 0), (0, 1), (1, 1), (0, 2), (0, 3)), ((1, 2), (1, 3), (2, 2), (2, 3), (3, 3))
 
@@ -220,26 +220,29 @@
         line = (jnp.where(wide_lane == i, 1.0, 0.0) - total) / factor[i : i + 1]
         solved = jnp.where(wide_row == i, line, solved)
 
-    big_row = lax.broadcasted_iota(jnp.int32, (panel, panel), 0)
-    big_column = lax.broadcasted_iota(jnp.int32, (panel, panel), 1)
+    def three(left, right):
+        return (nn(left[0], right[1]) + nn(left[1], right[0])) + nn(left[0], right[0])
+
+    small = []
+    for i in range(count):
+        tiled = jnp.concatenate([solved[:, i * WIDE : (i + 1) * WIDE]] * (WIDE // base), axis=0)
+        small.append(jnp.where(same, tiled, 0.0))
+    width = base
+    while width < WIDE:
+        picked = ((row // width) % 2 == 0) & (column // width == row // width + 1)
+        for i in range(count):
+            inverse = split2(small[i])
+            coupling = split2(jnp.where(picked, diagonals[i], 0.0))
+            small[i] = small[i] - three(split2(three(inverse, coupling)), inverse)
+        width *= 2
     inverses = []
     for half in range(2):
-        left, right = 2 * half, 2 * half + 1
-        top = jnp.concatenate([diagonals[left], block(left, right)], axis=1)
-        bottom = jnp.concatenate([jnp.zeros((WIDE, WIDE), F32), diagonals[right]], axis=1)
-        factor = jnp.concatenate([top, bottom], axis=0)
-        lines = solved[:, half * panel : (half + 1) * panel]
-        tiled = jnp.concatenate([lines] * (panel // base), axis=0)
-        inverse = jnp.where((big_row // base) == (big_column // base), tiled, 0.0)
-        width = base
-        while width < panel:
-            picked = (
-                ((big_row // width) % 2 == 0) & (big_column // width == big_row // width + 1)
-            )
-            coupling = jnp.where(picked, factor, 0.0)
-            inverse = inverse - full(full(inverse, coupling), inverse)
-            width *= 2
-        inverses.append(inverse)
+        left, right = small[2 * half], small[2 * half + 1]
+        coupling = split2(block(2 * half, 2 * half + 1))
+        corner = -three(split2(three(split2(left), coupling)), split2(right))
+        top = jnp.concatenate([left, corner], axis=1)
+        bottom = jnp.concatenate([jnp.zeros((WIDE, WIDE), F32), right], axis=1)
+        inverses.append(split2(jnp.concatenate([top, bottom], axis=0)))
     corner = jnp.concatenate(
         [
             jnp.concatenate([block(0, 2), block(0, 3)], axis=1),
@@ -248,8 +251,10 @@
         axis=0,
     )
     right_side = sides[...]
-    second = full(inverses[1], right_side[panel:])
-    first = full(inverses[0], right_side[:panel] - full(corner, second))
+    second = three(inverses[1], split2(right_side[panel:]))
+    first = three(
+        inverses[0], split2(right_side[:panel] - three(split2(corner), split2(second)))
+    )
     solved_ref[0:panel, :] = first
     solved_ref[panel:, :] = second
 
@@ -339,7 +344,8 @@
     to_down = jnp.concatenate([above[:, quarter:], away[:, :quarter]], axis=0)
     to_across = jnp.concatenate([below[:, quarter:], above[:, quarter:]], axis=0)
     sent_up, sent_down, sent_across = up(to_up), down(to_down), across(to_across)
-    other = core_swap(vectors)
+    vectors_late, _ = lax.optimization_barrier((vectors, own))
+    other = core_swap(vectors_late)
 
     chips = []
     for x_step, z_step in ((0, 0), (0, -1), (0, 1), (1, 0), (0, 2), (1, -1), (1, 1), (1, 2)):
@@ -415,6 +421,7 @@
     mine = lax.all_to_all(spread, "row", 0, 0).reshape(length, WIDE)
     theirs = core_swap(mine)
 
+    far_held = [pltpu.with_memory_space_constraint(v, pltpu.HBM) for v in far]
     result_own, result_other = pl.pallas_call(
         apply_kernel,
         out_shape=[jax.ShapeDtypeStruct((half, columns), F32)] * 2,
@@ -433,10 +440,10 @@
             + [pltpu.VMEM((size, 2 * WIDE), F32)],
         ),
         compiler_params=pltpu.CompilerParams(
-            dimension_semantics=("arbitrary",), vmem_limit_bytes=58 << 20
+            dimension_semantics=("arbitrary",), vmem_limit_bytes=LIMIT
         ),
         name="solve_apply",
-    )(where, *near, *far, vectors, other, mine, theirs)
+    )(where, *near, *far_held, vectors, other, mine, theirs)
 
     returned = core_swap(result_other)
     result = jnp.zeros((rows, columns), F32)

time: 154 us -> 138 us (0.90)
  Pallas kernels: 40.4 us -> 27 us
  local copies, waits for them, and re-layouts: 6.51 us -> 4.56 us
    pallas_call x1, Pallas kernels: 22.1 us -> 11.6 us  [per_device(): pl.pallas_call(apply_kernel, out_shape=[jax.ShapeDtypeStruct((half, colum...]
    pallas_call x2, Pallas kernels: 18.3 us -> 15.4 us  [gram(): pl.pallas_call(functools.partial(gram_kernel, first=first), out_shape=sha...]
    unnamed x28 -> x12, local copies, waits for them, and re-layouts: 1.98 us -> 0.02 us
where the time goes in v6:
time: 138 us; the launch traced here: 137 us
  waiting for transfers between devices  62.3 us (45%)
  blocking collectives  28.6 us (21%)
  Pallas kernels  27 us (20%)
  starting transfers between devices  12.6 us (9%)
  local copies, waits for them, and re-layouts  4.56 us (3%)
  other arithmetic  1.64 us (1%)
    ppermute x13, waiting for transfers between devices, permute(): return lax.ppermute(value, 'col', pairs)  62.3 us
    all_to_all x1, blocking collectives, per_device(): lax.all_to_all(mine.reshape(members, length // members, WIDE), 'row', 0, 0)  15.6 us
    pallas_call x2, Pallas kernels, gram(): pl.pallas_call(functools.partial(gram_kernel, first=first), out_shape=sha...  15.4 us
    all_to_all x1, blocking collectives, per_device(): mine = lax.all_to_all(spread, 'row', 0, 0).reshape(length, WIDE)  13 us
    ppermute x13, starting transfers between devices, permute(): return lax.ppermute(value, 'col', pairs)  12.6 us
    pallas_call x1, Pallas kernels, per_device(): pl.pallas_call(apply_kernel, out_shape=[jax.ShapeDtypeStruct((half, colum...  11.6 us
  transfers between devices with their start and end apart: 13, of which 11 were waited for; matrix products, arithmetic and copies ran while one was open for 2% of the time, Pallas kernels for 5%

profile of v6, /device:TPU:0, one launch (start us, length us, event | category | flops | bytes accessed | tf_op | source)
XLA Modules:
  0.0 136.9 jit_solution(13873750554945399483)
XLA Ops:
  0.0 1.3 dynamic-slice_bitcast_fusion.2
  1.3 0.1 collective-permute-start
  1.4 1.9 %collective-permute-done = f32[32,4096]{1,0:T(8,128)S(1)} collective-permute-done((f32[32,4096]{1,0:T(8,128)S(1)}, f32[32,4096]{1,0:T(8,128)S(1)}, u32[]{:S(2)}, u32[]{:S(2)}) %collective-permute-start) | collective-permute-done | bytes 524320 | tf_op jit(solution)/shard_map/ppermute | solution.py:320
  3.3 0.1 pad_maximum_fusion.2.refs_0_
  3.4 0.2 collective-permute-start.4
  3.6 3.1 %collective-permute-start.3 = (f32[64,4096]{1,0:T(8,128)S(1)}, f32[64,4096]{1,0:T(8,128)S(1)}, u32[]{:S(2)}, u32[]{:S(2)}) collective-permute-start(f32[64,4096]{1,0:T(8,128)S(1)} %pad_maximum_fusion.2.refs_0_), channel_id=1, source_target_pairs={{0,8},{1,9},{2,10},{3,11},{4,12},{5,13},{6,14},{7,15},{8,0},{9,1},... | collective-permute-start | bytes 3145736 | tf_op jit(solution)/shard_map/ppermute | solution.py:320
  6.7 4.0 %collective-permute-start.2 = (f32[64,4096]{1,0:T(8,128)S(1)}, f32[64,4096]{1,0:T(8,128)}, u32[]{:S(2)}, u32[]{:S(2)}) collective-permute-start(f32[64,4096]{1,0:T(8,128)S(1)} %pad_maximum_fusion.2.refs_0_), channel_id=1, source_target_pairs={{0,6},{1,7},{2,0},{3,1},{4,2},{5,3},{6,4},{7,5},{8,14},{9,15},{10,... | collective-permute-start | bytes 3145736 | tf_op jit(solution)/shard_map/ppermute | solution.py:320
  10.7 0.0 collective-permute-start.1
  10.8 0.1 stack.39.where_ref
  10.8 19.7 %collective-permute-done.3.refs_3_ = f32[64,4096]{1,0:T(8,128)S(1)} collective-permute-done((f32[64,4096]{1,0:T(8,128)S(1)}, f32[64,4096]{1,0:T(8,128)S(1)}, u32[]{:S(2)}, u32[]{:S(2)}) %collective-permute-start.3) | collective-permute-done | bytes 1048608 | tf_op jit(solution)/shard_map/ppermute | solution.py:320
  30.6 2.8 %collective-permute-done.2.refs_2_ = f32[64,4096]{1,0:T(8,128)} collective-permute-done((f32[64,4096]{1,0:T(8,128)S(1)}, f32[64,4096]{1,0:T(8,128)}, u32[]{:S(2)}, u32[]{:S(2)}) %collective-permute-start.2) | collective-permute-done | bytes 1048608 | tf_op jit(solution)/shard_map/ppermute | solution.py:320
  33.4 1.1 slice.28
  34.5 2.3 %collective-permute-done.1.refs_1_ = f32[64,4096]{1,0:T(8,128)S(1)} collective-permute-done((f32[64,4096]{1,0:T(8,128)S(1)}, f32[64,4096]{1,0:T(8,128)S(1)}, u32[]{:S(2)}, u32[]{:S(2)}) %collective-permute-start.1) | collective-permute-done | bytes 1048608 | tf_op jit(solution)/shard_map/ppermute | solution.py:320
  36.8 0.1 fusion
  36.9 0.4 pad_maximum_fusion.3
  37.3 0.1 collective-permute-start.5
  37.4 3.2 %collective-permute-start.6 = (f32[128,2048]{1,0:T(8,128)S(1)}, f32[128,2048]{1,0:T(8,128)S(1)}, u32[]{:S(2)}, u32[]{:S(2)}) collective-permute-start(f32[128,2048]{1,0:T(8,128)S(1)} %get-tuple-element.24), channel_id=1, source_target_pairs={{0,6},{1,7},{2,0},{3,1},{4,2},{5,3},{6,4},{7,5},{8,14},{9,15},{10,... | collective-permute-start | bytes 3145736 | tf_op jit(solution)/shard_map/ppermute | solution.py:320
  40.6 0.5 collective-permute-start.7
  41.1 0.0 collective-permute-done.4.refs_5_.refs_10_
  41.1 6.5 %gram_near.1.refs_11_ = f32[2,640,128]{2,1,0:T(8,128)S(1)} custom-call(s32[9]{0:T(128)S(1)} %stack.39.where_ref, f32[64,4096]{1,0:T(8,128)S(1)} %pad_maximum_fusion.2.refs_0_, f32[64,4096]{1,0:T(8,128)S(1)} %collective-permute-done.1.refs_1_, f32[64,4096]{1,0:T(8,128)} %collective-permute-done.2.refs_2_, f32[64,4096]{1,0:T(8,128)S(1)} %collective-permute-done.3.refs_3_, ...), custom_call_target="tpu_custom_call" | custom-call | flops 16106127360 | bytes 8388608 | tf_op jit(solution)/shard_map/gram_near/pallas_call | solution.py:379
  47.6 14.9 %collective-permute-done.5.refs_4_ = f32[128,2048]{1,0:T(8,128)S(1)} collective-permute-done((f32[128,2048]{1,0:T(8,128)S(1)}, f32[128,2048]{1,0:T(8,128)S(1)}, u32[]{:S(2)}, u32[]{:S(2)}) %collective-permute-start.5) | collective-permute-done | bytes 1048608 | tf_op jit(solution)/shard_map/ppermute | solution.py:320
  62.5 0.0 copy-start
  62.5 0.0 collective-permute-done.6.refs_5_
  62.5 0.0 copy-start.1
  62.6 0.1 collective-permute-start.8
  62.7 1.0 collective-permute-start.9
  63.7 2.4 %collective-permute-done.7.refs_6_ = f32[128,2048]{1,0:T(8,128)S(1)} collective-permute-done((f32[128,2048]{1,0:T(8,128)S(1)}, f32[128,2048]{1,0:T(8,128)S(1)}, u32[]{:S(2)}, u32[]{:S(2)}) %collective-permute-start.7) | collective-permute-done | bytes 1048608 | tf_op jit(solution)/shard_map/ppermute | solution.py:320
  66.1 0.0 copy-start.2
  66.1 9.6 %collective-permute-done.8.refs_7_ = f32[64,2048]{1,0:T(8,128)S(1)} collective-permute-done((f32[64,2048]{1,0:T(8,128)S(1)}, f32[64,2048]{1,0:T(8,128)S(1)}, u32[]{:S(2)}, u32[]{:S(2)}) %collective-permute-start.8) | collective-permute-done | bytes 524320 | tf_op jit(solution)/shard_map/ppermute | solution.py:320
  75.7 0.0 copy-start.3
  75.7 1.0 collective-permute-done.9.refs_8_
  76.7 0.0 copy-start.4
  76.7 8.9 %gram_far.1 = (f32[1152,128]{1,0:T(8,128)S(1)}, f32[1152,128]{1,0:T(8,128)S(1)}) custom-call(s32[9]{0:T(128)S(1)} %stack.39.where_ref, f32[64,4096]{1,0:T(8,128)S(1)} %pad_maximum_fusion.2.refs_0_, f32[64,4096]{1,0:T(8,128)S(1)} %collective-permute-done.1.refs_1_, f32[64,4096]{1,0:T(8,128)} %collective-permute-done.2.refs_2_, ...), custom_call_target="tpu_custom_call" | custom-call | flops 25769803776 | bytes 12582912 | tf_op jit(solution)/shard_map/gram_far/pallas_call | solution.py:379
  85.6 0.0 copy-done
  85.7 0.0 copy-done.1
  85.7 0.0 copy-done.2
  85.7 0.0 copy-done.3
  85.7 0.0 copy-done.4
  85.7 0.1 collective-permute-start.10
  85.8 2.0 %collective-permute-done.10 = f32[1152,128]{1,0:T(8,128)S(1)} collective-permute-done((f32[1152,128]{1,0:T(8,128)S(1)}, f32[1152,128]{1,0:T(8,128)S(1)}, u32[]{:S(2)}, u32[]{:S(2)}) %collective-permute-start.10) | collective-permute-done | bytes 589856 | tf_op jit(solution)/shard_map/ppermute | solution.py:320
  87.8 0.1 add.93
  87.8 15.6 %all_to_all.10 = f32[8,144,128]{2,1,0:T(8,128)} all-to-all(f32[8,144,128]{2,1,0:T(8,128)S(1)} %bitcast.21), channel_id=1, replica_groups=mesh['row'=8,'col'=16] {'row'}, dimensions={0} | all-to-all | bytes 1179648 | tf_op jit(solution)/shard_map/all_to_all | solution.py:418
  103.4 1.1 reduce_sum.9
  104.6 13.0 %all_to_all.11 = f32[8,144,128]{2,1,0:T(8,128)S(1)} all-to-all(f32[8,144,128]{2,1,0:T(8,128)S(1)} %broadcast_in_dim.10), channel_id=1, replica_groups=mesh['row'=8,'col'=16] {'row'}, dimensions={0} | all-to-all | bytes 1179648 | tf_op jit(solution)/shard_map/all_to_all | solution.py:421
  117.6 0.0 collective-permute-start.11
  117.6 2.0 %collective-permute-done.11.refs_12_ = f32[1152,128]{1,0:T(8,128)S(1)} collective-permute-done((f32[1152,128]{1,0:T(8,128)S(1)}, f32[1152,128]{1,0:T(8,128)S(1)}, u32[]{:S(2)}, u32[]{:S(2)}) %collective-permute-start.11) | collective-permute-done | bytes 589856 | tf_op jit(solution)/shard_map/ppermute | solution.py:320
  119.6 11.6 %solve_apply.1 = (f32[4096,128]{1,0:T(8,128)S(1)}, f32[4096,128]{1,0:T(8,128)S(1)}) custom-call(s32[9]{0:T(128)S(1)} %stack.39.where_ref, f32[64,4096]{1,0:T(8,128)S(1)} %pad_maximum_fusion.2.refs_0_, f32[64,4096]{1,0:T(8,128)S(1)} %collective-permute-done.1.refs_1_, f32[64,4096]{1,0:T(8,128)} %collective-permute-done.2.refs_2_, ...), custom_call_target="tpu_custom_call" | custom-call | tf_op jit(solution)/shard_map/solve_apply/pallas_call | solution.py:425
  131.2 0.2 collective-permute-start.12
  131.4 0.3 broadcast_in_dim.4
  131.7 0.2 constant_dynamic-update-slice_fusion.1
  131.9 0.0 copy-start.5
  131.9 3.5 %collective-permute-done.12 = f32[4096,128]{1,0:T(8,128)S(1)} collective-permute-done((f32[4096,128]{1,0:T(8,128)S(1)}, f32[4096,128]{1,0:T(8,128)S(1)}, u32[]{:S(2)}, u32[]{:S(2)}) %collective-permute-start.12) | collective-permute-done | bytes 2097184 | tf_op jit(solution)/shard_map/ppermute | solution.py:320
  135.5 0.0 copy-done.5
  135.5 1.5 %constant_dynamic-update-slice_fusion = f32[8192,128]{1,0:T(8,128)} fusion(f32[8192,128]{1,0:T(8,128)} %copy-done.5, f32[4096,128]{1,0:T(8,128)S(1)} %collective-permute-done.12, s32[]{:T(128)S(6)} %select_n.61), kind=kLoop, calls=%fused_computation.9 | loop fusion | bytes 4194308 | tf_op jit(solution)/shard_map/dynamic_update_slice | solution.py:451
  (5 shorter events, 0.2 us)
Async XLA Ops:
  1.3 2.0 %collective-permute-start = (f32[32,4096]{1,0:T(8,128)S(1)}, f32[32,4096]{1,0:T(8,128)S(1)}, u32[]{:S(2)}, u32[]{:S(2)}) collective-permute-start(f32[32,4096]{1,0:T(8,128)S(1)} %pad_maximum_fusion.4), channel_id=1, source_target_pairs={{0,1},{1,0},{2,3},{3,2},{4,5},{5,4},{6,7},{7,6},{8,9},{9,8},{10,11... | collective-permute-start | bytes 1572872 | tf_op jit(solution)/shard_map/ppermute | solution.py:320
  3.4 37.7 %collective-permute-start.4 = (f32[8192,128]{1,0:T(8,128)}, f32[8192,128]{1,0:T(8,128)}, u32[]{:S(2)}, u32[]{:S(2)}) collective-permute-start(f32[8192,128]{1,0:T(8,128)} %refs_9_.3), channel_id=1, source_target_pairs={{0,1},{1,0},{2,3},{3,2},{4,5},{5,4},{6,7},{7,6},{8,9},{9,8},{10,11... | collective-permute-start | bytes 12582920 | tf_op jit(solution)/shard_map/ppermute | solution.py:320
  3.6 26.9 %collective-permute-start.3 = (f32[64,4096]{1,0:T(8,128)S(1)}, f32[64,4096]{1,0:T(8,128)S(1)}, u32[]{:S(2)}, u32[]{:S(2)}) collective-permute-start(f32[64,4096]{1,0:T(8,128)S(1)} %pad_maximum_fusion.2.refs_0_), channel_id=1, source_target_pairs={{0,8},{1,9},{2,10},{3,11},{4,12},{5,13},{6,14},{7,15},{8,0},{9,1},... | collective-permute-start | bytes 3145736 | tf_op jit(solution)/shard_map/ppermute | solution.py:320
  6.7 26.7 %collective-permute-start.2 = (f32[64,4096]{1,0:T(8,128)S(1)}, f32[64,4096]{1,0:T(8,128)}, u32[]{:S(2)}, u32[]{:S(2)}) collective-permute-start(f32[64,4096]{1,0:T(8,128)S(1)} %pad_maximum_fusion.2.refs_0_), channel_id=1, source_target_pairs={{0,6},{1,7},{2,0},{3,1},{4,2},{5,3},{6,4},{7,5},{8,14},{9,15},{10,... | collective-permute-start | bytes 3145736 | tf_op jit(solution)/shard_map/ppermute | solution.py:320
  10.7 26.1 %collective-permute-start.1 = (f32[64,4096]{1,0:T(8,128)S(1)}, f32[64,4096]{1,0:T(8,128)S(1)}, u32[]{:S(2)}, u32[]{:S(2)}) collective-permute-start(f32[64,4096]{1,0:T(8,128)S(1)} %pad_maximum_fusion.2.refs_0_), channel_id=1, source_target_pairs={{0,2},{1,3},{2,4},{3,5},{4,6},{5,7},{6,0},{7,1},{8,10},{9,11},{10,... | collective-permute-start | bytes 3145736 | tf_op jit(solution)/shard_map/ppermute | solution.py:320
  37.3 25.3 %collective-permute-start.5 = (f32[128,2048]{1,0:T(8,128)S(1)}, f32[128,2048]{1,0:T(8,128)S(1)}, u32[]{:S(2)}, u32[]{:S(2)}) collective-permute-start(f32[128,2048]{1,0:T(8,128)S(1)} %get-tuple-element.25), channel_id=1, source_target_pairs={{0,2},{1,3},{2,4},{3,5},{4,6},{5,7},{6,0},{7,1},{8,10},{9,11},{10,... | collective-permute-start | bytes 3145736 | tf_op jit(solution)/shard_map/ppermute | solution.py:320
  37.4 25.2 %collective-permute-start.6 = (f32[128,2048]{1,0:T(8,128)S(1)}, f32[128,2048]{1,0:T(8,128)S(1)}, u32[]{:S(2)}, u32[]{:S(2)}) collective-permute-start(f32[128,2048]{1,0:T(8,128)S(1)} %get-tuple-element.24), channel_id=1, source_target_pairs={{0,6},{1,7},{2,0},{3,1},{4,2},{5,3},{6,4},{7,5},{8,14},{9,15},{10,... | collective-permute-start | bytes 3145736 | tf_op jit(solution)/shard_map/ppermute | solution.py:320
  40.6 25.5 %collective-permute-start.7 = (f32[128,2048]{1,0:T(8,128)S(1)}, f32[128,2048]{1,0:T(8,128)S(1)}, u32[]{:S(2)}, u32[]{:S(2)}) collective-permute-start(f32[128,2048]{1,0:T(8,128)S(1)} %get-tuple-element.23), channel_id=1, source_target_pairs={{0,8},{1,9},{2,10},{3,11},{4,12},{5,13},{6,14},{7,15},{8,0},{9,1},... | collective-permute-start | bytes 3145736 | tf_op jit(solution)/shard_map/ppermute | solution.py:320
  62.5 23.1 %copy-start = (f32[128,2048]{1,0:T(8,128)}, f32[128,2048]{1,0:T(8,128)S(1)}, u32[]{:S(2)}) copy-start(f32[128,2048]{1,0:T(8,128)S(1)} %collective-permute-done.5.refs_4_) | copy-start | bytes 3145732
  62.5 23.1 %copy-start.1 = (f32[128,2048]{1,0:T(8,128)}, f32[128,2048]{1,0:T(8,128)S(1)}, u32[]{:S(2)}) copy-start(f32[128,2048]{1,0:T(8,128)S(1)} %collective-permute-done.6.refs_5_) | copy-start | bytes 3145732
  62.6 13.1 %collective-permute-start.8 = (f32[64,2048]{1,0:T(8,128)S(1)}, f32[64,2048]{1,0:T(8,128)S(1)}, u32[]{:S(2)}, u32[]{:S(2)}) collective-permute-start(f32[64,2048]{1,0:T(8,128)S(1)} %slice.24), channel_id=1, source_target_pairs={{0,2},{1,3},{2,4},{3,5},{4,6},{5,7},{6,0},{7,1},{8,10},{9,11},{10,... | collective-permute-start | bytes 1572872 | tf_op jit(solution)/shard_map/ppermute | solution.py:320
  62.7 14.0 %collective-permute-start.9 = (f32[64,2048]{1,0:T(8,128)S(1)}, f32[64,2048]{1,0:T(8,128)S(1)}, u32[]{:S(2)}, u32[]{:S(2)}) collective-permute-start(f32[64,2048]{1,0:T(8,128)S(1)} %slice.25), channel_id=1, source_target_pairs={{0,8},{1,9},{2,10},{3,11},{4,12},{5,13},{6,14},{7,15},{8,0},{9,1},... | collective-permute-start | bytes 1572872 | tf_op jit(solution)/shard_map/ppermute | solution.py:320
  66.1 19.6 %copy-start.2 = (f32[128,2048]{1,0:T(8,128)}, f32[128,2048]{1,0:T(8,128)S(1)}, u32[]{:S(2)}) copy-start(f32[128,2048]{1,0:T(8,128)S(1)} %collective-permute-done.7.refs_6_) | copy-start | bytes 3145732
  75.7 10.0 %copy-start.3 = (f32[64,2048]{1,0:T(8,128)}, f32[64,2048]{1,0:T(8,128)S(1)}, u32[]{:S(2)}) copy-start(f32[64,2048]{1,0:T(8,128)S(1)} %collective-permute-done.8.refs_7_) | copy-start | bytes 1572868
  76.7 8.9 %copy-start.4 = (f32[64,2048]{1,0:T(8,128)}, f32[64,2048]{1,0:T(8,128)S(1)}, u32[]{:S(2)}) copy-start(f32[64,2048]{1,0:T(8,128)S(1)} %collective-permute-done.9.refs_8_) | copy-start | bytes 1572868
  85.7 2.1 %collective-permute-start.10 = (f32[1152,128]{1,0:T(8,128)S(1)}, f32[1152,128]{1,0:T(8,128)S(1)}, u32[]{:S(2)}, u32[]{:S(2)}) collective-permute-start(f32[1152,128]{1,0:T(8,128)S(1)} %get-tuple-element.18), channel_id=1, source_target_pairs={{0,1},{1,0},{2,3},{3,2},{4,5},{5,4},{6,7},{7,6},{8,9},{9,8},{10,11... | collective-permute-start | bytes 1769480 | tf_op jit(solution)/shard_map/ppermute | solution.py:320
  117.6 2.0 %collective-permute-start.11 = (f32[1152,128]{1,0:T(8,128)S(1)}, f32[1152,128]{1,0:T(8,128)S(1)}, u32[]{:S(2)}, u32[]{:S(2)}) collective-permute-start(f32[1152,128]{1,0:T(8,128)S(1)} %bitcast.19), channel_id=1, source_target_pairs={{0,1},{1,0},{2,3},{3,2},{4,5},{5,4},{6,7},{7,6},{8,9},{9,8},{10,11... | collective-permute-start | bytes 1769480 | tf_op jit(solution)/shard_map/ppermute | solution.py:320
  131.2 4.2 %collective-permute-start.12 = (f32[4096,128]{1,0:T(8,128)S(1)}, f32[4096,128]{1,0:T(8,128)S(1)}, u32[]{:S(2)}, u32[]{:S(2)}) collective-permute-start(f32[4096,128]{1,0:T(8,128)S(1)} %get-tuple-element.20), channel_id=1, source_target_pairs={{0,1},{1,0},{2,3},{3,2},{4,5},{5,4},{6,7},{7,6},{8,9},{9,8},{10,11... | collective-permute-start | bytes 6291464 | tf_op jit(solution)/shard_map/ppermute | solution.py:320
  131.9 3.6 %copy-start.5 = (f32[8192,128]{1,0:T(8,128)}, f32[8192,128]{1,0:T(8,128)S(1)}, u32[]{:S(2)}) copy-start(f32[8192,128]{1,0:T(8,128)S(1)} %constant_dynamic-update-slice_fusion.1) | copy-start | bytes 12582916

commit v7 on v6

--- a/solution.py
+++ b/solution.py
@@ -60,28 +60,30 @@
 def gram_kernel(where_ref, *refs, first):
     steps = pl.num_programs(0)
     step = pl.program_id(0)
-    count = 4 if first else 9
+    count = 8 if first else 13
     panels, rest = refs[:count], refs[count:]
     if first:
         own_ref, other_ref, out_ref, high, low, even, skew, proj = rest
     else:
         own_ref, other_ref, before_ref, keep_ref, send_ref, high, low, even, skew, proj = rest
     core = where_ref[CHIPS]
-    lines = panels[0].shape[0] // 2
+    lines = panels[0].shape[0]
     half = even.shape[1]
     start_row = high.shape[0] - half
 
+    def place_half(slot, swap, value):
+        begin = pl.multiple_of(slot * 2 * lines + lines * (core ^ swap), lines)
+        for target, part in zip((high, low), split2(value)):
+            target[pl.ds(begin, lines), :] = part
+
     def place(slot, value):
-        parts = split2(value)
-        for swap in range(2):
-            begin = pl.multiple_of(slot * 2 * lines + lines * (core ^ swap), lines)
-            for target, part in zip((high, low), parts):
-                target[pl.ds(begin, lines), :] = part[swap * lines : (swap + 1) * lines]
-
-    for slot in range(4):
-        place(slot, panels[slot][...])
+        place_half(slot, 0, value[:lines])
+        place_half(slot, 1, value[lines:])
+
+    for index in range(8):
+        place_half(index // 2, index % 2, panels[index][...])
     if not first:
-        each_far(step, steps, panels[4:], place)
+        each_far(step, steps, panels[8:], place)
 
     @pl.when(step == 0)
     def _():
@@ -262,12 +264,12 @@
 def apply_kernel(where_ref, *refs):
     step = pl.program_id(0)
     steps = pl.num_programs(0)
-    panels = refs[:9]
-    current_own, current_other, mine_ref, theirs_ref, out_own, out_other = refs[9:15]
-    solved, high, low, merged, both, rows_done, ordered, sides = refs[15:]
+    panels = refs[:13]
+    current_own, current_other, mine_ref, theirs_ref, out_own, out_other = refs[13:19]
+    solved, high, low, merged, both, rows_done, ordered, sides = refs[19:]
     core = where_ref[CHIPS]
     panel = solved.shape[0] // 2
-    chunk = panels[0].shape[0]
+    chunk = 2 * panels[0].shape[0]
     group = chunk // 4
 
     @pl.when(step == 0)
@@ -286,9 +288,9 @@
     def place(slot, value):
         merged[slot * chunk : (slot + 1) * chunk, :] = value
 
-    for slot in range(4):
-        place(slot, panels[slot][...])
-    each_far(step, steps, panels[4:], place)
+    for index in range(8):
+        merged[index * chunk // 2 : (index + 1) * chunk // 2, :] = panels[index][...]
+    each_far(step, steps, panels[8:], place)
     one, two = split2(merged[...])
     first, second = high[...], low[...]
 
@@ -338,13 +340,23 @@
     a_own = half_of(core)
     b_own = core_swap(half_of(1 - core))
     own = jnp.concatenate([a_own, b_own], axis=0)
-    away, below, above = across(own), up(own), down(own)
-    near = (own, below, above, away)
-    to_up = jnp.concatenate([below[:, :quarter], away[:, :quarter]], axis=0)
-    to_down = jnp.concatenate([above[:, quarter:], away[:, :quarter]], axis=0)
-    to_across = jnp.concatenate([below[:, quarter:], above[:, quarter:]], axis=0)
+    a_away, a_below, a_above = across(a_own), up(a_own), down(a_own)
+    b_away, b_below, b_above = across(b_own), up(b_own), down(b_own)
+    near = (a_own, b_own, a_below, b_below, a_above, b_above, a_away, b_away)
+
+    def early_half(*values):
+        return [v[:, :quarter] for v in values]
+
+    def late_half(*values):
+        return [v[:, quarter:] for v in values]
+
+    to_up = jnp.concatenate(early_half(a_below, b_below, a_away, b_away), axis=0)
+    to_down = jnp.concatenate(
+        late_half(a_above, b_above) + early_half(a_away, b_away), axis=0
+    )
+    to_across = jnp.concatenate(late_half(a_below, b_below, a_above, b_above), axis=0)
     sent_up, sent_down, sent_across = up(to_up), down(to_down), across(to_across)
-    vectors_late, _ = lax.optimization_barrier((vectors, own))
+    vectors_late, _ = lax.optimization_barrier((vectors, to_up))
     other = core_swap(vectors_late)
 
     chips = []
@@ -353,7 +365,7 @@
     where = jnp.stack(chips + [core]).astype(jnp.int32)
 
     turn = steps // 2
-    whole = [pl.BlockSpec((chunk, TILE), lambda j, w: (0, j))] * 4
+    whole = [pl.BlockSpec((chunk // 2, TILE), lambda j, w: (0, j))] * 8
 
     def early(lines):
         return pl.BlockSpec((lines, TILE), lambda j, w: (0, jnp.minimum(j, turn - 1)))
@@ -421,7 +433,7 @@
     mine = lax.all_to_all(spread, "row", 0, 0).reshape(length, WIDE)
     theirs = core_swap(mine)
 
-    far_held = [pltpu.with_memory_space_constraint(v, pltpu.HBM) for v in far]
+    held = [pltpu.with_memory_space_constraint(v, pltpu.HBM) for v in near + far]
     result_own, result_other = pl.pallas_call(
         apply_kernel,
         out_shape=[jax.ShapeDtypeStruct((half, columns), F32)] * 2,
@@ -443,7 +455,7 @@
             dimension_semantics=("arbitrary",), vmem_limit_bytes=LIMIT
         ),
         name="solve_apply",
-    )(where, *near, *far_held, vectors, other, mine, theirs)
+    )(where, *held, vectors, other, mine, theirs)
 
     returned = core_swap(result_other)
     result = jnp.zeros((rows, columns), F32)

time: 138 us -> 139 us (level)
  waiting for transfers between devices: 62.3 us -> 47.1 us
  starting transfers between devices: 12.6 us -> 20.5 us
  local copies, waits for them, and re-layouts: 4.56 us -> 11.5 us
    ppermute x13 -> x16, waiting for transfers between devices: 62.3 us -> 47.1 us  [permute(): return lax.ppermute(value, 'col', pairs)]
    unnamed x12 -> x40, local copies, waits for them, and re-layouts: 0.02 us -> 7.99 us
    ppermute x13 -> x16, starting transfers between devices: 12.6 us -> 20.5 us  [permute(): return lax.ppermute(value, 'col', pairs)]
  transfers between devices with their start and end apart: 13 -> 16, of which waited for: 11 -> 11; matrix products, arithmetic and copies ran while one was open for 2% -> 1% of each run, Pallas kernels for 5% -> 5%
where the time goes in v7:
time: 139 us; the launch traced here: 138 us
  waiting for transfers between devices  47.1 us (34%)
  blocking collectives  29.2 us (21%)
  Pallas kernels  27.6 us (20%)
  starting transfers between devices  20.5 us (15%)
  local copies, waits for them, and re-layouts  11.5 us (8%)
  other arithmetic  1.52 us (1%)
    ppermute x16, waiting for transfers between devices, permute(): return lax.ppermute(value, 'col', pairs)  47.1 us
    ppermute x16, starting transfers between devices, permute(): return lax.ppermute(value, 'col', pairs)  20.5 us
    all_to_all x1, blocking collectives, per_device(): lax.all_to_all(mine.reshape(members, length // members, WIDE), 'row', 0, 0)  16.2 us
    pallas_call x2, Pallas kernels, gram(): pl.pallas_call(functools.partial(gram_kernel, first=first), out_shape=sha...  15.5 us
    all_to_all x1, blocking collectives, per_device(): mine = lax.all_to_all(spread, 'row', 0, 0).reshape(length, WIDE)  13 us
    pallas_call x1, Pallas kernels, per_device(): pl.pallas_call(apply_kernel, out_shape=[jax.ShapeDtypeStruct((half, colum...  12.1 us
    unnamed x40, local copies, waits for them, and re-layouts  7.99 us
  transfers between devices with their start and end apart: 16, of which 11 were waited for; matrix products, arithmetic and copies ran while one was open for 1% of the time, Pallas kernels for 5%

profile of v7, /device:TPU:0, one launch (start us, length us, event | category | flops | bytes accessed | tf_op | source)
XLA Modules:
  0.0 137.6 jit_solution(15309557564548573942)
XLA Ops:
  0.0 1.3 dynamic-slice_bitcast_fusion
  1.3 0.1 collective-permute-start
  1.4 0.0 copy-start.2
  1.5 2.1 %collective-permute-start.1 = (f32[32,4096]{1,0:T(8,128)S(1)}, f32[32,4096]{1,0:T(8,128)S(1)}, u32[]{:S(2)}, u32[]{:S(2)}) collective-permute-start(f32[32,4096]{1,0:T(8,128)S(1)} %pad_maximum_fusion.5.refs_0_), channel_id=1, source_target_pairs={{0,2},{1,3},{2,4},{3,5},{4,6},{5,7},{6,0},{7,1},{8,10},{9,11},{10,... | collective-permute-start | bytes 1572872 | tf_op jit(solution)/shard_map/ppermute | solution.py:322
  3.5 3.0 %collective-permute-start.5 = (f32[32,4096]{1,0:T(8,128)S(1)}, f32[32,4096]{1,0:T(8,128)S(1)}, u32[]{:S(2)}, u32[]{:S(2)}) collective-permute-start(f32[32,4096]{1,0:T(8,128)S(1)} %pad_maximum_fusion.5.refs_0_), channel_id=1, source_target_pairs={{0,8},{1,9},{2,10},{3,11},{4,12},{5,13},{6,14},{7,15},{8,0},{9,1},... | collective-permute-start | bytes 1572872 | tf_op jit(solution)/shard_map/ppermute | solution.py:322
  6.6 2.2 %collective-permute-start.3 = (f32[32,4096]{1,0:T(8,128)S(1)}, f32[32,4096]{1,0:T(8,128)S(1)}, u32[]{:S(2)}, u32[]{:S(2)}) collective-permute-start(f32[32,4096]{1,0:T(8,128)S(1)} %pad_maximum_fusion.5.refs_0_), channel_id=1, source_target_pairs={{0,6},{1,7},{2,0},{3,1},{4,2},{5,3},{6,4},{7,5},{8,14},{9,15},{10,... | collective-permute-start | bytes 1572872 | tf_op jit(solution)/shard_map/ppermute | solution.py:322
  8.8 0.0 collective-permute-done.refs_1_
  8.8 0.5 collective-permute-start.6
  9.3 0.0 collective-permute-start.2
  9.3 9.1 %collective-permute-done.1.refs_2_ = f32[32,4096]{1,0:T(8,128)S(1)} collective-permute-done((f32[32,4096]{1,0:T(8,128)S(1)}, f32[32,4096]{1,0:T(8,128)S(1)}, u32[]{:S(2)}, u32[]{:S(2)}) %collective-permute-start.1) | collective-permute-done | bytes 524320 | tf_op jit(solution)/shard_map/ppermute | solution.py:322
  18.4 1.9 %collective-permute-start.4 = (f32[32,4096]{1,0:T(8,128)S(1)}, f32[32,4096]{1,0:T(8,128)S(1)}, u32[]{:S(2)}, u32[]{:S(2)}) collective-permute-start(f32[32,4096]{1,0:T(8,128)S(1)} %collective-permute-done.refs_1_), channel_id=1, source_target_pairs={{0,6},{1,7},{2,0},{3,1},{4,2},{5,3},{6,4},{7,5},{8,14},{9,15},{10,... | collective-permute-start | bytes 1572872 | tf_op jit(solution)/shard_map/ppermute | solution.py:322
  20.4 0.0 collective-permute-done.5.refs_6_
  20.4 0.0 copy-start.6
  20.5 0.3 collective-permute-done.3.refs_4_
  20.8 9.5 %collective-permute-done.6.refs_7_ = f32[32,4096]{1,0:T(8,128)S(1)} collective-permute-done((f32[32,4096]{1,0:T(8,128)S(1)}, f32[32,4096]{1,0:T(8,128)S(1)}, u32[]{:S(2)}, u32[]{:S(2)}) %collective-permute-start.6) | collective-permute-done | bytes 524320 | tf_op jit(solution)/shard_map/ppermute | solution.py:322
  30.3 0.0 collective-permute-done.2.refs_3_
  30.4 0.0 copy-done.6
  30.4 0.0 copy-start.4
  30.4 0.9 copy-done.4
  31.3 0.6 collective-permute-done.4.refs_5_
  32.0 0.0 copy-done.8
  32.0 0.8 copy-done.12
  32.8 0.0 copy-done.15
  32.8 1.4 pad_maximum_fusion.4
  34.1 0.0 collective-permute-start.7
  34.1 0.1 stack.39.where_ref
  34.2 1.5 %collective-permute-start.8 = (f32[128,2048]{1,0:T(8,128)}, f32[128,2048]{1,0:T(8,128)S(1)}, u32[]{:S(2)}, u32[]{:S(2)}) collective-permute-start(f32[128,2048]{1,0:T(8,128)} %get-tuple-element.23), channel_id=1, source_target_pairs={{0,2},{1,3},{2,4},{3,5},{4,6},{5,7},{6,0},{7,1},{8,10},{9,11},{10,... | collective-permute-start | bytes 3145736 | tf_op jit(solution)/shard_map/ppermute | solution.py:322
  35.7 1.9 %collective-permute-start.9 = (f32[128,2048]{1,0:T(8,128)S(1)}, f32[128,2048]{1,0:T(8,128)S(1)}, u32[]{:S(2)}, u32[]{:S(2)}) collective-permute-start(f32[128,2048]{1,0:T(8,128)S(1)} %get-tuple-element.22), channel_id=1, source_target_pairs={{0,6},{1,7},{2,0},{3,1},{4,2},{5,3},{6,4},{7,5},{8,14},{9,15},{10,... | collective-permute-start | bytes 3145736 | tf_op jit(solution)/shard_map/ppermute | solution.py:322
  37.6 2.9 %collective-permute-start.10 = (f32[128,2048]{1,0:T(8,128)S(1)}, f32[128,2048]{1,0:T(8,128)S(1)}, u32[]{:S(2)}, u32[]{:S(2)}) collective-permute-start(f32[128,2048]{1,0:T(8,128)S(1)} %get-tuple-element.21), channel_id=1, source_target_pairs={{0,8},{1,9},{2,10},{3,11},{4,12},{5,13},{6,14},{7,15},{8,0},{9,1},... | collective-permute-start | bytes 3145736 | tf_op jit(solution)/shard_map/ppermute | solution.py:322
  40.5 1.1 collective-permute-done.7.refs_9_.refs_14_
  41.6 1.0 copy-done.5
  42.7 1.0 copy-done.7
  43.7 1.0 copy-done.9
  44.7 1.0 copy-done.11
  45.8 1.0 copy-done.13
  46.8 1.0 copy-done.16
  47.9 6.5 %gram_near.1.refs_15_ = f32[2,640,128]{2,1,0:T(8,128)S(1)} custom-call(s32[9]{0:T(128)S(1)} %stack.39.where_ref, f32[32,4096]{1,0:T(8,128)S(1)} %pad_maximum_fusion.5.refs_0_, f32[32,4096]{1,0:T(8,128)S(1)} %copy-done.16, f32[32,4096]{1,0:T(8,128)S(1)} %collective-permute-done.1.refs_2_, f32[32,4096]{1,0:T(8,128)S(1)} %copy-done.5, ...), custom_call_target="tpu_custom_call" | custom-call | flops 16106127360 | bytes 8388608 | tf_op jit(solution)/shard_map/gram_near/pallas_call | solution.py:391
  54.4 7.1 %collective-permute-done.8.refs_8_ = f32[128,2048]{1,0:T(8,128)S(1)} collective-permute-done((f32[128,2048]{1,0:T(8,128)}, f32[128,2048]{1,0:T(8,128)S(1)}, u32[]{:S(2)}, u32[]{:S(2)}) %collective-permute-start.8) | collective-permute-done | bytes 1048608 | tf_op jit(solution)/shard_map/ppermute | solution.py:322
  61.5 0.0 collective-permute-done.9.refs_9_
  61.6 1.2 collective-permute-start.11
  62.8 2.9 %collective-permute-start.12 = (f32[64,2048]{1,0:T(8,128)S(1)}, f32[64,2048]{1,0:T(8,128)S(1)}, u32[]{:S(2)}, u32[]{:S(2)}) collective-permute-start(f32[64,2048]{1,0:T(8,128)S(1)} %slice.43), channel_id=1, source_target_pairs={{0,8},{1,9},{2,10},{3,11},{4,12},{5,13},{6,14},{7,15},{8,0},{9,1},... | collective-permute-start | bytes 1572872 | tf_op jit(solution)/shard_map/ppermute | solution.py:322
  65.7 0.0 collective-permute-done.10.refs_10_
  65.7 10.9 %collective-permute-done.11.refs_11_ = f32[64,2048]{1,0:T(8,128)S(1)} collective-permute-done((f32[64,2048]{1,0:T(8,128)S(1)}, f32[64,2048]{1,0:T(8,128)S(1)}, u32[]{:S(2)}, u32[]{:S(2)}) %collective-permute-start.11) | collective-permute-done | bytes 524320 | tf_op jit(solution)/shard_map/ppermute | solution.py:322
  76.6 0.7 collective-permute-done.12.refs_12_
  77.3 9.0 %gram_far.1 = (f32[1152,128]{1,0:T(8,128)S(1)}, f32[1152,128]{1,0:T(8,128)S(1)}) custom-call(s32[9]{0:T(128)S(1)} %stack.39.where_ref, f32[32,4096]{1,0:T(8,128)S(1)} %pad_maximum_fusion.5.refs_0_, f32[32,4096]{1,0:T(8,128)S(1)} %copy-done.16, f32[32,4096]{1,0:T(8,128)S(1)} %collective-permute-done.1.refs_2_, f32[32,4096]{1,0:T(8,128)S(1)} %copy-done.5, ...), custom_call_target="tpu_custom_call" | custom-call | flops 25769803776 | bytes 12582912 | tf_op jit(solution)/shard_map/gram_far/pallas_call | solution.py:391
  86.3 0.0 copy-done
  86.3 0.0 copy-done.1
  86.3 0.0 copy-done.14
  86.3 0.0 copy-done.17
  86.3 0.0 copy-done.18
  86.4 0.1 collective-permute-start.13
  86.5 2.0 %collective-permute-done.13 = f32[1152,128]{1,0:T(8,128)S(1)} collective-permute-done((f32[1152,128]{1,0:T(8,128)S(1)}, f32[1152,128]{1,0:T(8,128)S(1)}, u32[]{:S(2)}, u32[]{:S(2)}) %collective-permute-start.13) | collective-permute-done | bytes 589856 | tf_op jit(solution)/shard_map/ppermute | solution.py:322
  88.4 0.1 add.93
  88.5 16.2 %all_to_all.10 = f32[8,144,128]{2,1,0:T(8,128)S(1)} all-to-all(f32[8,144,128]{2,1,0:T(8,128)S(1)} %bitcast.21), channel_id=1, replica_groups=mesh['row'=8,'col'=16] {'row'}, dimensions={0} | all-to-all | bytes 1179648 | tf_op jit(solution)/shard_map/all_to_all | solution.py:430
  104.8 13.0 %all_to_all.11 = f32[8,144,128]{2,1,0:T(8,128)S(1)} all-to-all(f32[8,144,128]{2,1,0:T(8,128)S(1)} %broadcast_in_dim.10), channel_id=1, replica_groups=mesh['row'=8,'col'=16] {'row'}, dimensions={0} | all-to-all | bytes 1179648 | tf_op jit(solution)/shard_map/all_to_all | solution.py:433
  117.8 0.0 collective-permute-start.14
  117.8 2.0 %collective-permute-done.14.refs_16_ = f32[1152,128]{1,0:T(8,128)S(1)} collective-permute-done((f32[1152,128]{1,0:T(8,128)S(1)}, f32[1152,128]{1,0:T(8,128)S(1)}, u32[]{:S(2)}, u32[]{:S(2)}) %collective-permute-start.14) | collective-permute-done | bytes 589856 | tf_op jit(solution)/shard_map/ppermute | solution.py:322
  119.8 12.1 %solve_apply.1 = (f32[4096,128]{1,0:T(8,128)S(1)}, f32[4096,128]{1,0:T(8,128)S(1)}) custom-call(s32[9]{0:T(128)S(1)} %stack.39.where_ref, f32[32,4096]{1,0:T(8,128)} %copy-done.2, f32[32,4096]{1,0:T(8,128)} %copy-done.15, f32[32,4096]{1,0:T(8,128)} %copy-done.3, f32[32,4096]{1,0:T(8,128)} %copy-done.4, f32[32,4096]{1,0:T(8,128)} %copy-done.8, ...), custom_call_target="tpu_custom_call" | custom-call | tf_op jit(solution)/shard_map/solve_apply/pallas_call | solution.py:437
  131.9 0.2 collective-permute-start.15
  132.1 0.3 broadcast_in_dim.4
  132.4 0.2 constant_dynamic-update-slice_fusion.1
  132.6 0.0 copy-start.19
  132.6 3.5 %collective-permute-done.15 = f32[4096,128]{1,0:T(8,128)S(1)} collective-permute-done((f32[4096,128]{1,0:T(8,128)S(1)}, f32[4096,128]{1,0:T(8,128)S(1)}, u32[]{:S(2)}, u32[]{:S(2)}) %collective-permute-start.15) | collective-permute-done | bytes 2097184 | tf_op jit(solution)/shard_map/ppermute | solution.py:322
  136.2 1.5 %constant_dynamic-update-slice_fusion = f32[8192,128]{1,0:T(8,128)} fusion(f32[8192,128]{1,0:T(8,128)} %copy-done.19, f32[4096,128]{1,0:T(8,128)S(1)} %collective-permute-done.15, s32[]{:T(128)S(6)} %select_n.61), kind=kLoop, calls=%fused_computation.11 | loop fusion | bytes 4194308 | tf_op jit(solution)/shard_map/dynamic_update_slice | solution.py:463
  (32 shorter events, 0.4 us)
Async XLA Ops:
  1.3 7.5 %collective-permute-start = (f32[32,4096]{1,0:T(8,128)S(1)}, f32[32,4096]{1,0:T(8,128)S(1)}, u32[]{:S(2)}, u32[]{:S(2)}) collective-permute-start(f32[32,4096]{1,0:T(8,128)S(1)} %pad_maximum_fusion.6), channel_id=1, source_target_pairs={{0,1},{1,0},{2,3},{3,2},{4,5},{5,4},{6,7},{7,6},{8,9},{9,8},{10,11... | collective-permute-start | bytes 1572872 | tf_op jit(solution)/shard_map/ppermute | solution.py:322
  1.4 75.9 %copy-start.2 = (f32[32,4096]{1,0:T(8,128)}, f32[32,4096]{1,0:T(8,128)S(1)}, u32[]{:S(2)}) copy-start(f32[32,4096]{1,0:T(8,128)S(1)} %pad_maximum_fusion.5.refs_0_) | copy-start | bytes 1572868
  1.5 17.0 %collective-permute-start.1 = (f32[32,4096]{1,0:T(8,128)S(1)}, f32[32,4096]{1,0:T(8,128)S(1)}, u32[]{:S(2)}, u32[]{:S(2)}) collective-permute-start(f32[32,4096]{1,0:T(8,128)S(1)} %pad_maximum_fusion.5.refs_0_), channel_id=1, source_target_pairs={{0,2},{1,3},{2,4},{3,5},{4,6},{5,7},{6,0},{7,1},{8,10},{9,11},{10,... | collective-permute-start | bytes 1572872 | tf_op jit(solution)/shard_map/ppermute | solution.py:322
  3.5 16.9 %collective-permute-start.5 = (f32[32,4096]{1,0:T(8,128)S(1)}, f32[32,4096]{1,0:T(8,128)S(1)}, u32[]{:S(2)}, u32[]{:S(2)}) collective-permute-start(f32[32,4096]{1,0:T(8,128)S(1)} %pad_maximum_fusion.5.refs_0_), channel_id=1, source_target_pairs={{0,8},{1,9},{2,10},{3,11},{4,12},{5,13},{6,14},{7,15},{8,0},{9,1},... | collective-permute-start | bytes 1572872 | tf_op jit(solution)/shard_map/ppermute | solution.py:322
  6.6 14.2 %collective-permute-start.3 = (f32[32,4096]{1,0:T(8,128)S(1)}, f32[32,4096]{1,0:T(8,128)S(1)}, u32[]{:S(2)}, u32[]{:S(2)}) collective-permute-start(f32[32,4096]{1,0:T(8,128)S(1)} %pad_maximum_fusion.5.refs_0_), channel_id=1, source_target_pairs={{0,6},{1,7},{2,0},{3,1},{4,2},{5,3},{6,4},{7,5},{8,14},{9,15},{10,... | collective-permute-start | bytes 1572872 | tf_op jit(solution)/shard_map/ppermute | solution.py:322
  8.8 24.0 %copy-start.15 = (f32[32,4096]{1,0:T(8,128)}, f32[32,4096]{1,0:T(8,128)S(1)}, u32[]{:S(2)}) copy-start(f32[32,4096]{1,0:T(8,128)S(1)} %collective-permute-done.refs_1_) | copy-start | bytes 1572868
  8.8 21.5 %collective-permute-start.6 = (f32[32,4096]{1,0:T(8,128)S(1)}, f32[32,4096]{1,0:T(8,128)S(1)}, u32[]{:S(2)}, u32[]{:S(2)}) collective-permute-start(f32[32,4096]{1,0:T(8,128)S(1)} %collective-permute-done.refs_1_), channel_id=1, source_target_pairs={{0,8},{1,9},{2,10},{3,11},{4,12},{5,13},{6,14},{7,15},{8,0},{9,1},... | collective-permute-start | bytes 1572872 | tf_op jit(solution)/shard_map/ppermute | solution.py:322
  9.3 21.1 %collective-permute-start.2 = (f32[32,4096]{1,0:T(8,128)S(1)}, f32[32,4096]{1,0:T(8,128)S(1)}, u32[]{:S(2)}, u32[]{:S(2)}) collective-permute-start(f32[32,4096]{1,0:T(8,128)S(1)} %collective-permute-done.refs_1_), channel_id=1, source_target_pairs={{0,2},{1,3},{2,4},{3,5},{4,6},{5,7},{6,0},{7,1},{8,10},{9,11},{10,... | collective-permute-start | bytes 1572872 | tf_op jit(solution)/shard_map/ppermute | solution.py:322
  18.4 58.9 %copy-start.3 = (f32[32,4096]{1,0:T(8,128)}, f32[32,4096]{1,0:T(8,128)S(1)}, u32[]{:S(2)}) copy-start(f32[32,4096]{1,0:T(8,128)S(1)} %collective-permute-done.1.refs_2_) | copy-start | bytes 1572868
  18.4 13.5 %collective-permute-start.4 = (f32[32,4096]{1,0:T(8,128)S(1)}, f32[32,4096]{1,0:T(8,128)S(1)}, u32[]{:S(2)}, u32[]{:S(2)}) collective-permute-start(f32[32,4096]{1,0:T(8,128)S(1)} %collective-permute-done.refs_1_), channel_id=1, source_target_pairs={{0,6},{1,7},{2,0},{3,1},{4,2},{5,3},{6,4},{7,5},{8,14},{9,15},{10,... | collective-permute-start | bytes 1572872 | tf_op jit(solution)/shard_map/ppermute | solution.py:322
  20.4 10.0 %copy-start.6 = (f32[32,4096]{1,0:T(8,128)}, f32[32,4096]{1,0:T(8,128)S(1)}, u32[]{:S(2)}) copy-start(f32[32,4096]{1,0:T(8,128)S(1)} %collective-permute-done.5.refs_6_) | copy-start | bytes 1572868
  20.8 11.2 %copy-start.8 = (f32[32,4096]{1,0:T(8,128)}, f32[32,4096]{1,0:T(8,128)S(1)}, u32[]{:S(2)}) copy-start(f32[32,4096]{1,0:T(8,128)S(1)} %collective-permute-done.3.refs_4_) | copy-start | bytes 1572868
  30.3 1.7 %copy-start.10 = (f32[32,4096]{1,0:T(8,128)}, f32[32,4096]{1,0:T(8,128)S(1)}, u32[]{:S(2)}) copy-start(f32[32,4096]{1,0:T(8,128)S(1)} %collective-permute-done.6.refs_7_) | copy-start | bytes 1572868
  30.4 0.9 copy-start.4
  32.0 0.8 copy-start.12
  34.1 7.5 %collective-permute-start.7 = (f32[8192,128]{1,0:T(8,128)}, f32[8192,128]{1,0:T(8,128)}, u32[]{:S(2)}, u32[]{:S(2)}) collective-permute-start(f32[8192,128]{1,0:T(8,128)} %refs_13_.3), channel_id=1, source_target_pairs={{0,1},{1,0},{2,3},{3,2},{4,5},{5,4},{6,7},{7,6},{8,9},{9,8},{10,11... | collective-permute-start | bytes 12582920 | tf_op jit(solution)/shard_map/ppermute | solution.py:322
  34.2 27.3 %collective-permute-start.8 = (f32[128,2048]{1,0:T(8,128)}, f32[128,2048]{1,0:T(8,128)S(1)}, u32[]{:S(2)}, u32[]{:S(2)}) collective-permute-start(f32[128,2048]{1,0:T(8,128)} %get-tuple-element.23), channel_id=1, source_target_pairs={{0,2},{1,3},{2,4},{3,5},{4,6},{5,7},{6,0},{7,1},{8,10},{9,11},{10,... | collective-permute-start | bytes 3145736 | tf_op jit(solution)/shard_map/ppermute | solution.py:322
  35.7 25.8 %collective-permute-start.9 = (f32[128,2048]{1,0:T(8,128)S(1)}, f32[128,2048]{1,0:T(8,128)S(1)}, u32[]{:S(2)}, u32[]{:S(2)}) collective-permute-start(f32[128,2048]{1,0:T(8,128)S(1)} %get-tuple-element.22), channel_id=1, source_target_pairs={{0,6},{1,7},{2,0},{3,1},{4,2},{5,3},{6,4},{7,5},{8,14},{9,15},{10,... | collective-permute-start | bytes 3145736 | tf_op jit(solution)/shard_map/ppermute | solution.py:322
  37.6 28.1 %collective-permute-start.10 = (f32[128,2048]{1,0:T(8,128)S(1)}, f32[128,2048]{1,0:T(8,128)S(1)}, u32[]{:S(2)}, u32[]{:S(2)}) collective-permute-start(f32[128,2048]{1,0:T(8,128)S(1)} %get-tuple-element.21), channel_id=1, source_target_pairs={{0,8},{1,9},{2,10},{3,11},{4,12},{5,13},{6,14},{7,15},{8,0},{9,1},... | collective-permute-start | bytes 3145736 | tf_op jit(solution)/shard_map/ppermute | solution.py:322
  41.6 1.0 copy-start.5
  42.7 1.0 copy-start.7
  43.7 1.0 copy-start.9
  44.7 1.0 copy-start.11
  45.8 1.0 copy-start.13
  46.8 1.0 copy-start.16
  61.5 24.8 %copy-start = (f32[128,2048]{1,0:T(8,128)}, f32[128,2048]{1,0:T(8,128)S(1)}, u32[]{:S(2)}) copy-start(f32[128,2048]{1,0:T(8,128)S(1)} %collective-permute-done.8.refs_8_) | copy-start | bytes 3145732
  61.5 24.8 %copy-start.1 = (f32[128,2048]{1,0:T(8,128)}, f32[128,2048]{1,0:T(8,128)S(1)}, u32[]{:S(2)}) copy-start(f32[128,2048]{1,0:T(8,128)S(1)} %collective-permute-done.9.refs_9_) | copy-start | bytes 3145732
  61.6 15.0 %collective-permute-start.11 = (f32[64,2048]{1,0:T(8,128)S(1)}, f32[64,2048]{1,0:T(8,128)S(1)}, u32[]{:S(2)}, u32[]{:S(2)}) collective-permute-start(f32[64,2048]{1,0:T(8,128)S(1)} %slice.42), channel_id=1, source_target_pairs={{0,2},{1,3},{2,4},{3,5},{4,6},{5,7},{6,0},{7,1},{8,10},{9,11},{10,... | collective-permute-start | bytes 1572872 | tf_op jit(solution)/shard_map/ppermute | solution.py:322
  62.8 14.5 %collective-permute-start.12 = (f32[64,2048]{1,0:T(8,128)S(1)}, f32[64,2048]{1,0:T(8,128)S(1)}, u32[]{:S(2)}, u32[]{:S(2)}) collective-permute-start(f32[64,2048]{1,0:T(8,128)S(1)} %slice.43), channel_id=1, source_target_pairs={{0,8},{1,9},{2,10},{3,11},{4,12},{5,13},{6,14},{7,15},{8,0},{9,1},... | collective-permute-start | bytes 1572872 | tf_op jit(solution)/shard_map/ppermute | solution.py:322
  65.7 20.7 %copy-start.14 = (f32[128,2048]{1,0:T(8,128)}, f32[128,2048]{1,0:T(8,128)S(1)}, u32[]{:S(2)}) copy-start(f32[128,2048]{1,0:T(8,128)S(1)} %collective-permute-done.10.refs_10_) | copy-start | bytes 3145732
  76.6 9.7 %copy-start.17 = (f32[64,2048]{1,0:T(8,128)}, f32[64,2048]{1,0:T(8,128)S(1)}, u32[]{:S(2)}) copy-start(f32[64,2048]{1,0:T(8,128)S(1)} %collective-permute-done.11.refs_11_) | copy-start | bytes 1572868
  77.3 9.0 %copy-start.18 = (f32[64,2048]{1,0:T(8,128)}, f32[64,2048]{1,0:T(8,128)S(1)}, u32[]{:S(2)}) copy-start(f32[64,2048]{1,0:T(8,128)S(1)} %collective-permute-done.12.refs_12_) | copy-start | bytes 1572868
  86.4 2.1 %collective-permute-start.13 = (f32[1152,128]{1,0:T(8,128)S(1)}, f32[1152,128]{1,0:T(8,128)S(1)}, u32[]{:S(2)}, u32[]{:S(2)}) collective-permute-start(f32[1152,128]{1,0:T(8,128)S(1)} %get-tuple-element.18), channel_id=1, source_target_pairs={{0,1},{1,0},{2,3},{3,2},{4,5},{5,4},{6,7},{7,6},{8,9},{9,8},{10,11... | collective-permute-start | bytes 1769480 | tf_op jit(solution)/shard_map/ppermute | solution.py:322
  117.8 2.0 %collective-permute-start.14 = (f32[1152,128]{1,0:T(8,128)S(1)}, f32[1152,128]{1,0:T(8,128)S(1)}, u32[]{:S(2)}, u32[]{:S(2)}) collective-permute-start(f32[1152,128]{1,0:T(8,128)S(1)} %bitcast.19), channel_id=1, source_target_pairs={{0,1},{1,0},{2,3},{3,2},{4,5},{5,4},{6,7},{7,6},{8,9},{9,8},{10,11... | collective-permute-start | bytes 1769480 | tf_op jit(solution)/shard_map/ppermute | solution.py:322
  131.9 4.2 %collective-permute-start.15 = (f32[4096,128]{1,0:T(8,128)S(1)}, f32[4096,128]{1,0:T(8,128)S(1)}, u32[]{:S(2)}, u32[]{:S(2)}) collective-permute-start(f32[4096,128]{1,0:T(8,128)S(1)} %get-tuple-element.20), channel_id=1, source_target_pairs={{0,1},{1,0},{2,3},{3,2},{4,5},{5,4},{6,7},{7,6},{8,9},{9,8},{10,11... | collective-permute-start | bytes 6291464 | tf_op jit(solution)/shard_map/ppermute | solution.py:322
  132.6 3.6 %copy-start.19 = (f32[8192,128]{1,0:T(8,128)}, f32[8192,128]{1,0:T(8,128)S(1)}, u32[]{:S(2)}) copy-start(f32[8192,128]{1,0:T(8,128)S(1)} %constant_dynamic-update-slice_fusion.1) | copy-start | bytes 12582916

commit v8 on v7

--- a/solution.py
+++ b/solution.py
@@ -37,40 +37,39 @@
     )
 
 
-def each_far(step, steps, refs, place):
-    up_ref, down_ref, across_ref, end_up_ref, end_across_ref = refs
+def each_middle(early, refs, place):
+    up_ref, down_ref, across_ref = refs
     chunk = down_ref.shape[0]
-    early = step < steps // 2
 
     @pl.when(early)
     def _():
         place(4, up_ref[:chunk])
         place(5, up_ref[chunk:])
         place(6, down_ref[...])
-        place(7, end_up_ref[...])
 
     @pl.when(jnp.logical_not(early))
     def _():
         place(4, down_ref[...])
         place(5, across_ref[:chunk])
         place(6, across_ref[chunk:])
-        place(7, end_across_ref[...])
-
-
-def gram_kernel(where_ref, *refs, first):
-    steps = pl.num_programs(0)
-    step = pl.program_id(0)
-    count = 8 if first else 13
-    panels, rest = refs[:count], refs[count:]
-    if first:
-        own_ref, other_ref, out_ref, high, low, even, skew, proj = rest
-    else:
-        own_ref, other_ref, before_ref, keep_ref, send_ref, high, low, even, skew, proj = rest
-    core = where_ref[CHIPS]
-    lines = panels[0].shape[0]
-    half = even.shape[1]
-    start_row = high.shape[0] - half
-
+
+
+def each_last(early, refs, place):
+    @pl.when(early)
+    def _():
+        place(7, refs[0][...])
+
+    @pl.when(jnp.logical_not(early))
+    def _():
+        place(7, refs[1][...])
+
+
+def each_far(step, steps, refs, place):
+    each_middle(step < steps // 2, refs[:3], place)
+    each_last(step < steps // 2, refs[3:], place)
+
+
+def placer(core, lines, high, low):
     def place_half(slot, swap, value):
         begin = pl.multiple_of(slot * 2 * lines + lines * (core ^ swap), lines)
         for target, part in zip((high, low), split2(value)):
@@ -80,16 +79,34 @@
         place_half(slot, 0, value[:lines])
         place_half(slot, 1, value[lines:])
 
+    return place_half, place
+
+
+def gram_kernel(where_ref, *refs, first):
+    steps = pl.num_programs(0)
+    step = pl.program_id(0)
+    count = 8 if first else 11
+    panels = refs[:count]
+    own_ref, other_ref, out_ref, high, low, even, skew, proj = refs[count:]
+    core = where_ref[CHIPS]
+    half = even.shape[1]
+    start_row = high.shape[0] - half
+    place_half, place = placer(core, panels[0].shape[0], high, low)
+
+    @pl.when(step == 0)
+    def _():
+        even[...] = jnp.zeros_like(even)
+        skew[...] = jnp.zeros_like(skew)
+        proj[...] = jnp.zeros_like(proj)
+        if not first:
+            empty = half // 4
+            high[2 * half - empty :, :] = jnp.zeros((empty, high.shape[1]), BF16)
+            low[2 * half - empty :, :] = jnp.zeros((empty, low.shape[1]), BF16)
+
     for index in range(8):
         place_half(index // 2, index % 2, panels[index][...])
     if not first:
-        each_far(step, steps, panels[8:], place)
-
-    @pl.when(step == 0)
-    def _():
-        even[...] = jnp.zeros_like(even)
-        skew[...] = jnp.zeros_like(skew)
-        proj[...] = jnp.zeros_like(proj)
+        each_middle(step < steps // 2, panels[8:], place)
 
     one, two = high[start_row:, :], low[start_row:, :]
     skew[...] += nt(one, two)
@@ -104,49 +121,83 @@
 
     @pl.when(step == steps - 1)
     def _():
-        def corner(i, j):
-            at_i, at_j = slice(i * WIDE, (i + 1) * WIDE), slice(j * WIDE, (j + 1) * WIDE)
-            base = even.shape[0] - half
-            return (
-                even[base + i * WIDE : base + (i + 1) * WIDE, at_j]
-                + skew[at_i, at_j]
-                + skew[at_j, at_i].T
+        out_ref[0:half, :] = proj[...]
+        out_ref[half : 2 * half, :] = even[start_row:, :] + (skew[...] + skew[...].T)
+        if not first:
+            out_ref[2 * half :, :] = even[:half, :]
+
+
+def last_kernel(where_ref, *refs):
+    steps = pl.num_programs(0)
+    step = pl.program_id(0)
+    panels = refs[:13]
+    own_ref, other_ref, near_ref, middle_ref, keep_ref, send_ref, high, low, gram, proj = refs[13:]
+    core = where_ref[CHIPS]
+    size = gram.shape[1]
+    half = size // 2
+    chunk = gram.shape[0]
+    place_half, place = placer(core, panels[0].shape[0], high, low)
+    for index in range(8):
+        place_half(index // 2, index % 2, panels[index][...])
+    each_far(step, steps, panels[8:], place)
+
+    @pl.when(step == 0)
+    def _():
+        gram[...] = jnp.zeros_like(gram)
+        proj[...] = jnp.zeros_like(proj)
+
+    one, two = high[...], low[...]
+    last, rest = one[size - chunk :], two[size - chunk :]
+    pair = jnp.concatenate([last, rest], axis=0)
+    partial = nt(pair, one)
+    gram[...] += nt(last, two) + (partial[chunk:] + partial[:chunk])
+    x_one, x_two = split2(jnp.concatenate([own_ref[...], other_ref[...]], axis=1))
+    partial = nn(pair, x_one)
+    proj[...] += nn(last, x_two) + (partial[chunk:] + partial[:chunk])
+
+    @pl.when(step == steps - 1)
+    def _():
+        for target, lanes in ((keep_ref, slice(0, WIDE)), (send_ref, slice(WIDE, 2 * WIDE))):
+            target[0:half, :] = near_ref[0:half, lanes]
+            target[half : size - chunk, :] = middle_ref[0 : half - chunk, lanes]
+            target[size - chunk : size, :] = proj[:, lanes]
+
+        def spot(ref, base, i, j):
+            return ref[base + i * WIDE : base + (i + 1) * WIDE, j * WIDE : (j + 1) * WIDE]
+
+        def lower(j):
+            return jnp.concatenate(
+                [jnp.zeros((WIDE - chunk, WIDE), F32), gram[:, j * WIDE : (j + 1) * WIDE]], axis=0
             )
 
-        if first:
-            out_ref[0, 0:half, :] = proj[:, :WIDE]
-            out_ref[1, 0:half, :] = proj[:, WIDE:]
-            for at, (i, j) in enumerate(((0, 0), (0, 1), (1, 1))):
-                begin = half + at * WIDE
-                out_ref[0, begin : begin + WIDE, :] = corner(i, j)
-                out_ref[1, begin : begin + WIDE, :] = jnp.zeros((WIDE, WIDE), F32)
-        else:
-            keep_ref[0:half, :] = before_ref[0, 0:half, :]
-            send_ref[0:half, :] = before_ref[1, 0:half, :]
-            keep_ref[half : 2 * half, :] = proj[:, :WIDE]
-            send_ref[half : 2 * half, :] = proj[:, WIDE:]
-
-            def blocks(part, target):
-                for at, (i, j) in enumerate(PIECES[part]):
-                    begin = 2 * half + at * WIDE
-                    if j < 2:
-                        index = half + ((0, 0), (0, 1), (1, 1)).index((i, j)) * WIDE
-                        block = before_ref[0, index : index + WIDE, :]
-                    elif i < 2:
-                        block = even[i * WIDE : (i + 1) * WIDE, (j - 2) * WIDE : (j - 1) * WIDE]
-                    else:
-                        block = corner(i - 2, j - 2)
-                    target[begin : begin + WIDE, :] = block
-
-            @pl.when(core == 0)
-            def _():
-                blocks(0, keep_ref)
-                blocks(1, send_ref)
-
-            @pl.when(core != 0)
-            def _():
-                blocks(1, keep_ref)
-                blocks(0, send_ref)
+        lane = lax.broadcasted_iota(jnp.int32, (WIDE, WIDE), 1)
+
+        def blocks(part, target):
+            for at, (i, j) in enumerate(PIECES[part]):
+                begin = size + at * WIDE
+                if j < 2:
+                    block = spot(near_ref, half, i, j)
+                elif i < 2:
+                    block = spot(middle_ref, 2 * half, i, j - 2)
+                else:
+                    block = spot(middle_ref, half, i - 2, j - 2)
+                if j == 3:
+                    added = lower(i)
+                    if i == 3:
+                        block = block + added
+                        added = jnp.where(lane < WIDE - chunk, added, 0.0)
+                    block = block + added.T
+                target[begin : begin + WIDE, :] = block
+
+        @pl.when(core == 0)
+        def _():
+            blocks(0, keep_ref)
+            blocks(1, send_ref)
+
+        @pl.when(core != 0)
+        def _():
+            blocks(1, keep_ref)
+            blocks(0, send_ref)
 
 
 def solve(where_ref, mine_ref, other_ref, solved_ref, both, rows_done, ordered, sides):
@@ -381,50 +432,57 @@
     length = size + 5 * WIDE
     span = size // 2
 
-    def gram(first, pieces, extra):
-        if first:
-            shapes = [jax.ShapeDtypeStruct((2, span + 3 * WIDE, WIDE), F32)]
-        else:
-            shapes = [jax.ShapeDtypeStruct((length, WIDE), F32)] * 2
-        height = span if first else size
-        units = 10 if first else 16
+    def products(kernel, pieces, specs, extra, shapes, scratch, units, name):
         return pl.pallas_call(
-            functools.partial(gram_kernel, first=first),
-            out_shape=shapes,
+            kernel,
+            out_shape=[jax.ShapeDtypeStruct(v, F32) for v in shapes],
             grid_spec=pltpu.PrefetchScalarGridSpec(
                 num_scalar_prefetch=1,
                 grid=(steps,),
-                in_specs=whole
-                + ([] if first else parts_far)
+                in_specs=specs
                 + [own_spec, own_spec]
-                + [pl.BlockSpec(v.shape, lambda j, w: (0, 0, 0)) for v in extra],
-                out_specs=[
-                    pl.BlockSpec(v.shape, lambda j, w, n=len(v.shape): (0,) * n) for v in shapes
-                ],
-                scratch_shapes=[pltpu.VMEM((height, TILE), BF16)] * 2
-                + [
-                    pltpu.VMEM((height, span), F32),
-                    pltpu.VMEM((span, span), F32),
-                    pltpu.VMEM((span, 2 * WIDE), F32),
-                ],
+                + [pl.BlockSpec(v.shape, lambda j, w: (0, 0)) for v in extra],
+                out_specs=[pl.BlockSpec(v, lambda j, w: (0, 0)) for v in shapes],
+                scratch_shapes=scratch,
             ),
             compiler_params=pltpu.CompilerParams(
                 dimension_semantics=("arbitrary",), vmem_limit_bytes=LIMIT
             ),
             cost_estimate=pl.CostEstimate(
                 flops=2 * 3 * units * span * span * half,
-                bytes_accessed=4 * half * (height + columns * 2),
+                bytes_accessed=4 * half * (size + columns * 2),
                 transcendentals=0,
             ),
-            name="gram_near" if first else "gram_far",
+            name=name,
         )(where, *pieces, vectors, other, *extra)
 
-    (before,) = gram(True, near, ())
-    before, sent_up, sent_down = lax.optimization_barrier((before, sent_up, sent_down))
+    def split_scratch(height):
+        return [pltpu.VMEM((height, TILE), BF16)] * 2
+
+    square = pltpu.VMEM((span, span), F32)
+    (before,) = products(
+        functools.partial(gram_kernel, first=True), near, whole, (),
+        [(2 * span, span)], split_scratch(span) + [square] * 3, 10, "gram_near",
+    )
+    before, sent_up, sent_down, sent_across = lax.optimization_barrier(
+        (before, sent_up, sent_down, sent_across)
+    )
     end_up = up(sent_up[chunk:])
     end_across = across(sent_down[:chunk])
-    far = (sent_up, sent_down, sent_across, end_up, end_across)
-    kept, sent = gram(False, near + far, (before,))
+    middle = (sent_up, sent_down, sent_across)
+    (between,) = products(
+        functools.partial(gram_kernel, first=False), near + middle, whole + parts_far[:3], (),
+        [(3 * span, span)],
+        split_scratch(size) + [pltpu.VMEM((size, span), F32), square, square], 16, "gram_middle",
+    )
+    end_up, end_across, between = lax.optimization_barrier((end_up, end_across, between))
+    far = middle + (end_up, end_across)
+    kept, sent = products(
+        last_kernel, near + far, whole + parts_far, (before, between),
+        [(length, WIDE)] * 2,
+        split_scratch(size) + [pltpu.VMEM((chunk, size), F32), pltpu.VMEM((chunk, span), F32)],
+        8, "gram_last",
+    )
     mine = kept + core_swap(sent)
     members = lax.axis_size("row")
     parts = lax.all_to_all(mine.reshape(members, length // members, WIDE), "row", 0, 0)

time: 139 us -> 140 us (level)
  Pallas kernels: 27.6 us -> 34.9 us
  waiting for transfers between devices: 47.1 us -> 40.7 us
    pallas_call x2 -> x3, Pallas kernels: 15.5 us -> 22.8 us  [products(): pl.pallas_call(kernel, out_shape=[jax.ShapeDtypeStruct(v, F32) for v in s...]
    ppermute x16, waiting for transfers between devices: 47.1 us -> 40.7 us  [permute(): return lax.ppermute(value, 'col', pairs)]
  transfers between devices with their start and end apart: 16 -> 16, of which waited for: 11 -> 12; matrix products, arithmetic and copies ran while one was open for 1% -> 1% of each run, Pallas kernels for 5% -> 11%
where the time goes in v8:
time: 140 us; the launch traced here: 138 us
  waiting for transfers between devices  40.7 us (29%)
  Pallas kernels  34.9 us (25%)
  blocking collectives  28.7 us (20%)
  starting transfers between devices  20.2 us (14%)
  local copies, waits for them, and re-layouts  11.5 us (8%)
  other arithmetic  1.52 us (1%)
    ppermute x16, waiting for transfers between devices, permute(): return lax.ppermute(value, 'col', pairs)  40.7 us
    pallas_call x3, Pallas kernels, products(): pl.pallas_call(kernel, out_shape=[jax.ShapeDtypeStruct(v, F32) for v in s...  22.8 us
    ppermute x16, starting transfers between devices, permute(): return lax.ppermute(value, 'col', pairs)  20.2 us
    all_to_all x1, blocking collectives, per_device(): lax.all_to_all(mine.reshape(members, length // members, WIDE), 'row', 0, 0)  15.7 us
    all_to_all x1, blocking collectives, per_device(): mine = lax.all_to_all(spread, 'row', 0, 0).reshape(length, WIDE)  13 us
    pallas_call x1, Pallas kernels, per_device(): pl.pallas_call(apply_kernel, out_shape=[jax.ShapeDtypeStruct((half, colum...  12.1 us
    unnamed x40, local copies, waits for them, and re-layouts  7.99 us
  transfers between devices with their start and end apart: 16, of which 12 were waited for; matrix products, arithmetic and copies ran while one was open for 1% of the time, Pallas kernels for 11%

profile of v8, /device:TPU:0, one launch (start us, length us, event | category | flops | bytes accessed | tf_op | source)
XLA Modules:
  0.0 137.8 jit_solution(7255914832392449855)
XLA Ops:
  0.0 1.3 dynamic-slice_bitcast_fusion
  1.3 0.1 collective-permute-start
  1.4 0.0 copy-start.2
  1.5 2.1 %collective-permute-start.1 = (f32[32,4096]{1,0:T(8,128)S(1)}, f32[32,4096]{1,0:T(8,128)S(1)}, u32[]{:S(2)}, u32[]{:S(2)}) collective-permute-start(f32[32,4096]{1,0:T(8,128)S(1)} %pad_maximum_fusion.5.refs_0_), channel_id=1, source_target_pairs={{0,2},{1,3},{2,4},{3,5},{4,6},{5,7},{6,0},{7,1},{8,10},{9,11},{10,... | collective-permute-start | bytes 1572872 | tf_op jit(solution)/shard_map/ppermute | solution.py:373
  3.5 3.0 %collective-permute-start.5 = (f32[32,4096]{1,0:T(8,128)S(1)}, f32[32,4096]{1,0:T(8,128)S(1)}, u32[]{:S(2)}, u32[]{:S(2)}) collective-permute-start(f32[32,4096]{1,0:T(8,128)S(1)} %pad_maximum_fusion.5.refs_0_), channel_id=1, source_target_pairs={{0,8},{1,9},{2,10},{3,11},{4,12},{5,13},{6,14},{7,15},{8,0},{9,1},... | collective-permute-start | bytes 1572872 | tf_op jit(solution)/shard_map/ppermute | solution.py:373
  6.6 2.2 %collective-permute-start.3 = (f32[32,4096]{1,0:T(8,128)S(1)}, f32[32,4096]{1,0:T(8,128)S(1)}, u32[]{:S(2)}, u32[]{:S(2)}) collective-permute-start(f32[32,4096]{1,0:T(8,128)S(1)} %pad_maximum_fusion.5.refs_0_), channel_id=1, source_target_pairs={{0,6},{1,7},{2,0},{3,1},{4,2},{5,3},{6,4},{7,5},{8,14},{9,15},{10,... | collective-permute-start | bytes 1572872 | tf_op jit(solution)/shard_map/ppermute | solution.py:373
  8.8 0.0 collective-permute-done.refs_1_
  8.8 0.5 collective-permute-start.6
  9.3 0.0 collective-permute-start.2
  9.3 9.1 %collective-permute-done.1.refs_2_ = f32[32,4096]{1,0:T(8,128)S(1)} collective-permute-done((f32[32,4096]{1,0:T(8,128)S(1)}, f32[32,4096]{1,0:T(8,128)S(1)}, u32[]{:S(2)}, u32[]{:S(2)}) %collective-permute-start.1) | collective-permute-done | bytes 524320 | tf_op jit(solution)/shard_map/ppermute | solution.py:373
  18.4 1.9 %collective-permute-start.4 = (f32[32,4096]{1,0:T(8,128)S(1)}, f32[32,4096]{1,0:T(8,128)S(1)}, u32[]{:S(2)}, u32[]{:S(2)}) collective-permute-start(f32[32,4096]{1,0:T(8,128)S(1)} %collective-permute-done.refs_1_), channel_id=1, source_target_pairs={{0,6},{1,7},{2,0},{3,1},{4,2},{5,3},{6,4},{7,5},{8,14},{9,15},{10,... | collective-permute-start | bytes 1572872 | tf_op jit(solution)/shard_map/ppermute | solution.py:373
  20.4 0.0 collective-permute-done.5.refs_6_
  20.4 0.0 copy-start.6
  20.5 0.3 collective-permute-done.3.refs_4_
  20.8 9.5 %collective-permute-done.6.refs_7_ = f32[32,4096]{1,0:T(8,128)S(1)} collective-permute-done((f32[32,4096]{1,0:T(8,128)S(1)}, f32[32,4096]{1,0:T(8,128)S(1)}, u32[]{:S(2)}, u32[]{:S(2)}) %collective-permute-start.6) | collective-permute-done | bytes 524320 | tf_op jit(solution)/shard_map/ppermute | solution.py:373
  30.3 0.0 collective-permute-done.2.refs_3_
  30.4 0.0 copy-done.6
  30.4 0.0 copy-start.4
  30.4 0.9 copy-done.4
  31.3 0.6 collective-permute-done.4.refs_5_
  32.0 0.0 copy-done.8
  32.0 0.0 copy-done.10
  32.0 0.8 copy-done.12
  32.8 1.4 pad_maximum_fusion.4
  34.1 0.0 collective-permute-start.7
  34.1 0.1 stack.39.where_ref
  34.2 1.5 %collective-permute-start.8 = (f32[128,2048]{1,0:T(8,128)S(1)}, f32[128,2048]{1,0:T(8,128)S(1)}, u32[]{:S(2)}, u32[]{:S(2)}) collective-permute-start(f32[128,2048]{1,0:T(8,128)S(1)} %get-tuple-element.31), channel_id=1, source_target_pairs={{0,2},{1,3},{2,4},{3,5},{4,6},{5,7},{6,0},{7,1},{8,10},{9,11},{10,... | collective-permute-start | bytes 3145736 | tf_op jit(solution)/shard_map/ppermute | solution.py:373
  35.7 2.8 %collective-permute-start.10 = (f32[128,2048]{1,0:T(8,128)}, f32[128,2048]{1,0:T(8,128)S(1)}, u32[]{:S(2)}, u32[]{:S(2)}) collective-permute-start(f32[128,2048]{1,0:T(8,128)} %get-tuple-element.29), channel_id=1, source_target_pairs={{0,8},{1,9},{2,10},{3,11},{4,12},{5,13},{6,14},{7,15},{8,0},{9,1},... | collective-permute-start | bytes 3145736 | tf_op jit(solution)/shard_map/ppermute | solution.py:373
  38.5 1.9 %collective-permute-start.9 = (f32[128,2048]{1,0:T(8,128)S(1)}, f32[128,2048]{1,0:T(8,128)S(1)}, u32[]{:S(2)}, u32[]{:S(2)}) collective-permute-start(f32[128,2048]{1,0:T(8,128)S(1)} %get-tuple-element.30), channel_id=1, source_target_pairs={{0,6},{1,7},{2,0},{3,1},{4,2},{5,3},{6,4},{7,5},{8,14},{9,15},{10,... | collective-permute-start | bytes 3145736 | tf_op jit(solution)/shard_map/ppermute | solution.py:373
  40.5 1.1 collective-permute-done.7.refs_9_.refs_12_.refs_14_
  41.6 1.0 copy-done.5
  42.7 1.0 copy-done.7
  43.7 1.0 copy-done.9
  44.7 1.0 copy-done.11
  45.8 1.0 copy-done.13
  46.8 1.0 copy-done.16
  47.9 6.6 %gram_near.1.refs_15_ = f32[512,256]{1,0:T(8,128)S(1)} custom-call(s32[9]{0:T(128)S(1)} %stack.39.where_ref, f32[32,4096]{1,0:T(8,128)S(1)} %pad_maximum_fusion.5.refs_0_, f32[32,4096]{1,0:T(8,128)S(1)} %copy-done.16, f32[32,4096]{1,0:T(8,128)S(1)} %collective-permute-done.1.refs_2_, f32[32,4096]{1,0:T(8,128)S(1)} %copy-done.5, f32[32,4096]{1,0:T(8,128)S(1)} %copy-done.9, ...), custom_call_target="tpu_custom_call" | custom-call | flops 16106127360 | bytes 12582912 | tf_op jit(solution)/shard_map/gram_near/pallas_call | solution.py:436
  54.5 8.3 %collective-permute-done.10.refs_10_ = f32[128,2048]{1,0:T(8,128)S(1)} collective-permute-done((f32[128,2048]{1,0:T(8,128)}, f32[128,2048]{1,0:T(8,128)S(1)}, u32[]{:S(2)}, u32[]{:S(2)}) %collective-permute-start.10) | collective-permute-done | bytes 1048608 | tf_op jit(solution)/shard_map/ppermute | solution.py:373
  62.7 0.0 collective-permute-done.8.refs_8_
  62.7 0.8 collective-permute-done.9.refs_9_
  63.6 1.7 %collective-permute-start.11 = (f32[64,2048]{1,0:T(8,128)S(1)}, f32[64,2048]{1,0:T(8,128)S(1)}, u32[]{:S(2)}, u32[]{:S(2)}) collective-permute-start(f32[64,2048]{1,0:T(8,128)S(1)} %slice.42), channel_id=1, source_target_pairs={{0,2},{1,3},{2,4},{3,5},{4,6},{5,7},{6,0},{7,1},{8,10},{9,11},{10,... | collective-permute-start | bytes 1572872 | tf_op jit(solution)/shard_map/ppermute | solution.py:373
  65.3 2.1 %collective-permute-start.12 = (f32[64,2048]{1,0:T(8,128)S(1)}, f32[64,2048]{1,0:T(8,128)S(1)}, u32[]{:S(2)}, u32[]{:S(2)}) collective-permute-start(f32[64,2048]{1,0:T(8,128)S(1)} %slice.43), channel_id=1, source_target_pairs={{0,8},{1,9},{2,10},{3,11},{4,12},{5,13},{6,14},{7,15},{8,0},{9,1},... | collective-permute-start | bytes 1572872 | tf_op jit(solution)/shard_map/ppermute | solution.py:373
  67.4 8.8 %gram_middle.1.refs_16_ = f32[768,256]{1,0:T(8,128)S(1)} custom-call(s32[9]{0:T(128)S(1)} %stack.39.where_ref, f32[32,4096]{1,0:T(8,128)S(1)} %pad_maximum_fusion.5.refs_0_, f32[32,4096]{1,0:T(8,128)S(1)} %copy-done.16, f32[32,4096]{1,0:T(8,128)S(1)} %collective-permute-done.1.refs_2_, f32[32,4096]{1,0:T(8,128)S(1)} %copy-done.5, f32[32,4096]{1,0:T(8,128)S(1)} %copy-done.9, ...), custom_call_target="tpu_custom_call" | custom-call | flops 25769803776 | bytes 12582912 | tf_op jit(solution)/shard_map/gram_middle/pallas_call | solution.py:436
  76.2 1.8 %collective-permute-done.11.refs_11_ = f32[64,2048]{1,0:T(8,128)S(1)} collective-permute-done((f32[64,2048]{1,0:T(8,128)S(1)}, f32[64,2048]{1,0:T(8,128)S(1)}, u32[]{:S(2)}, u32[]{:S(2)}) %collective-permute-start.11) | collective-permute-done | bytes 524320 | tf_op jit(solution)/shard_map/ppermute | solution.py:373
  78.0 1.5 %collective-permute-done.12.refs_12_ = f32[64,2048]{1,0:T(8,128)S(1)} collective-permute-done((f32[64,2048]{1,0:T(8,128)S(1)}, f32[64,2048]{1,0:T(8,128)S(1)}, u32[]{:S(2)}, u32[]{:S(2)}) %collective-permute-start.12) | collective-permute-done | bytes 524320 | tf_op jit(solution)/shard_map/ppermute | solution.py:373
  79.5 0.0 copy-done
  79.6 0.0 copy-done.1
  79.6 0.0 copy-start.18
  79.6 7.4 %gram_last.1 = (f32[1152,128]{1,0:T(8,128)S(1)}, f32[1152,128]{1,0:T(8,128)S(1)}) custom-call(s32[9]{0:T(128)S(1)} %stack.39.where_ref, f32[32,4096]{1,0:T(8,128)S(1)} %pad_maximum_fusion.5.refs_0_, f32[32,4096]{1,0:T(8,128)S(1)} %copy-done.16, f32[32,4096]{1,0:T(8,128)S(1)} %collective-permute-done.1.refs_2_, f32[32,4096]{1,0:T(8,128)S(1)} %copy-done.5, ...), custom_call_target="tpu_custom_call" | custom-call | flops 12884901888 | bytes 12582912 | tf_op jit(solution)/shard_map/gram_last/pallas_call | solution.py:436
  87.0 0.1 collective-permute-start.13
  87.1 2.0 %collective-permute-done.13 = f32[1152,128]{1,0:T(8,128)S(1)} collective-permute-done((f32[1152,128]{1,0:T(8,128)S(1)}, f32[1152,128]{1,0:T(8,128)S(1)}, u32[]{:S(2)}, u32[]{:S(2)}) %collective-permute-start.13) | collective-permute-done | bytes 589856 | tf_op jit(solution)/shard_map/ppermute | solution.py:373
  89.1 0.1 add.93
  89.2 15.7 %all_to_all.10 = f32[8,144,128]{2,1,0:T(8,128)S(1)} all-to-all(f32[8,144,128]{2,1,0:T(8,128)S(1)} %bitcast.21), channel_id=1, replica_groups=mesh['row'=8,'col'=16] {'row'}, dimensions={0} | all-to-all | bytes 1179648 | tf_op jit(solution)/shard_map/all_to_all | solution.py:488
  105.0 13.0 %all_to_all.11 = f32[8,144,128]{2,1,0:T(8,128)S(1)} all-to-all(f32[8,144,128]{2,1,0:T(8,128)S(1)} %broadcast_in_dim.10), channel_id=1, replica_groups=mesh['row'=8,'col'=16] {'row'}, dimensions={0} | all-to-all | bytes 1179648 | tf_op jit(solution)/shard_map/all_to_all | solution.py:491
  118.0 0.0 collective-permute-start.14
  118.0 2.0 %collective-permute-done.14.refs_16_ = f32[1152,128]{1,0:T(8,128)S(1)} collective-permute-done((f32[1152,128]{1,0:T(8,128)S(1)}, f32[1152,128]{1,0:T(8,128)S(1)}, u32[]{:S(2)}, u32[]{:S(2)}) %collective-permute-start.14) | collective-permute-done | bytes 589856 | tf_op jit(solution)/shard_map/ppermute | solution.py:373
  120.0 12.1 %solve_apply.1 = (f32[4096,128]{1,0:T(8,128)S(1)}, f32[4096,128]{1,0:T(8,128)S(1)}) custom-call(s32[9]{0:T(128)S(1)} %stack.39.where_ref, f32[32,4096]{1,0:T(8,128)} %copy-done.2, f32[32,4096]{1,0:T(8,128)} %copy-done.15, f32[32,4096]{1,0:T(8,128)} %copy-done.3, f32[32,4096]{1,0:T(8,128)} %copy-done.4, f32[32,4096]{1,0:T(8,128)} %copy-done.8, ...), custom_call_target="tpu_custom_call" | custom-call | tf_op jit(solution)/shard_map/solve_apply/pallas_call | solution.py:495
  132.1 0.2 collective-permute-start.15
  132.3 0.3 broadcast_in_dim.4
  132.6 0.2 constant_dynamic-update-slice_fusion.1
  132.8 0.0 copy-start.19
  132.8 3.5 %collective-permute-done.15 = f32[4096,128]{1,0:T(8,128)S(1)} collective-permute-done((f32[4096,128]{1,0:T(8,128)S(1)}, f32[4096,128]{1,0:T(8,128)S(1)}, u32[]{:S(2)}, u32[]{:S(2)}) %collective-permute-start.15) | collective-permute-done | bytes 2097184 | tf_op jit(solution)/shard_map/ppermute | solution.py:373
  136.4 0.0 copy-done.19
  136.4 1.5 %constant_dynamic-update-slice_fusion = f32[8192,128]{1,0:T(8,128)} fusion(f32[8192,128]{1,0:T(8,128)} %copy-done.19, f32[4096,128]{1,0:T(8,128)S(1)} %collective-permute-done.15, s32[]{:T(128)S(6)} %select_n.61), kind=kLoop, calls=%fused_computation.11 | loop fusion | bytes 4194308 | tf_op jit(solution)/shard_map/dynamic_update_slice | solution.py:521
  (33 shorter events, 0.4 us)
Async XLA Ops:
  1.3 7.5 %collective-permute-start = (f32[32,4096]{1,0:T(8,128)S(1)}, f32[32,4096]{1,0:T(8,128)S(1)}, u32[]{:S(2)}, u32[]{:S(2)}) collective-permute-start(f32[32,4096]{1,0:T(8,128)S(1)} %pad_maximum_fusion.6), channel_id=1, source_target_pairs={{0,1},{1,0},{2,3},{3,2},{4,5},{5,4},{6,7},{7,6},{8,9},{9,8},{10,11... | collective-permute-start | bytes 1572872 | tf_op jit(solution)/shard_map/ppermute | solution.py:373
  1.4 78.1 %copy-start.2 = (f32[32,4096]{1,0:T(8,128)}, f32[32,4096]{1,0:T(8,128)S(1)}, u32[]{:S(2)}) copy-start(f32[32,4096]{1,0:T(8,128)S(1)} %pad_maximum_fusion.5.refs_0_) | copy-start | bytes 1572868
  1.5 17.0 %collective-permute-start.1 = (f32[32,4096]{1,0:T(8,128)S(1)}, f32[32,4096]{1,0:T(8,128)S(1)}, u32[]{:S(2)}, u32[]{:S(2)}) collective-permute-start(f32[32,4096]{1,0:T(8,128)S(1)} %pad_maximum_fusion.5.refs_0_), channel_id=1, source_target_pairs={{0,2},{1,3},{2,4},{3,5},{4,6},{5,7},{6,0},{7,1},{8,10},{9,11},{10,... | collective-permute-start | bytes 1572872 | tf_op jit(solution)/shard_map/ppermute | solution.py:373
  3.5 16.9 %collective-permute-start.5 = (f32[32,4096]{1,0:T(8,128)S(1)}, f32[32,4096]{1,0:T(8,128)S(1)}, u32[]{:S(2)}, u32[]{:S(2)}) collective-permute-start(f32[32,4096]{1,0:T(8,128)S(1)} %pad_maximum_fusion.5.refs_0_), channel_id=1, source_target_pairs={{0,8},{1,9},{2,10},{3,11},{4,12},{5,13},{6,14},{7,15},{8,0},{9,1},... | collective-permute-start | bytes 1572872 | tf_op jit(solution)/shard_map/ppermute | solution.py:373
  6.6 14.2 %collective-permute-start.3 = (f32[32,4096]{1,0:T(8,128)S(1)}, f32[32,4096]{1,0:T(8,128)S(1)}, u32[]{:S(2)}, u32[]{:S(2)}) collective-permute-start(f32[32,4096]{1,0:T(8,128)S(1)} %pad_maximum_fusion.5.refs_0_), channel_id=1, source_target_pairs={{0,6},{1,7},{2,0},{3,1},{4,2},{5,3},{6,4},{7,5},{8,14},{9,15},{10,... | collective-permute-start | bytes 1572872 | tf_op jit(solution)/shard_map/ppermute | solution.py:373
  8.8 24.0 %copy-start.15 = (f32[32,4096]{1,0:T(8,128)}, f32[32,4096]{1,0:T(8,128)S(1)}, u32[]{:S(2)}) copy-start(f32[32,4096]{1,0:T(8,128)S(1)} %collective-permute-done.refs_1_) | copy-start | bytes 1572868
  8.8 21.5 %collective-permute-start.6 = (f32[32,4096]{1,0:T(8,128)S(1)}, f32[32,4096]{1,0:T(8,128)S(1)}, u32[]{:S(2)}, u32[]{:S(2)}) collective-permute-start(f32[32,4096]{1,0:T(8,128)S(1)} %collective-permute-done.refs_1_), channel_id=1, source_target_pairs={{0,8},{1,9},{2,10},{3,11},{4,12},{5,13},{6,14},{7,15},{8,0},{9,1},... | collective-permute-start | bytes 1572872 | tf_op jit(solution)/shard_map/ppermute | solution.py:373
  9.3 21.1 %collective-permute-start.2 = (f32[32,4096]{1,0:T(8,128)S(1)}, f32[32,4096]{1,0:T(8,128)S(1)}, u32[]{:S(2)}, u32[]{:S(2)}) collective-permute-start(f32[32,4096]{1,0:T(8,128)S(1)} %collective-permute-done.refs_1_), channel_id=1, source_target_pairs={{0,2},{1,3},{2,4},{3,5},{4,6},{5,7},{6,0},{7,1},{8,10},{9,11},{10,... | collective-permute-start | bytes 1572872 | tf_op jit(solution)/shard_map/ppermute | solution.py:373
  18.4 61.1 %copy-start.3 = (f32[32,4096]{1,0:T(8,128)}, f32[32,4096]{1,0:T(8,128)S(1)}, u32[]{:S(2)}) copy-start(f32[32,4096]{1,0:T(8,128)S(1)} %collective-permute-done.1.refs_2_) | copy-start | bytes 1572868
  18.4 13.5 %collective-permute-start.4 = (f32[32,4096]{1,0:T(8,128)S(1)}, f32[32,4096]{1,0:T(8,128)S(1)}, u32[]{:S(2)}, u32[]{:S(2)}) collective-permute-start(f32[32,4096]{1,0:T(8,128)S(1)} %collective-permute-done.refs_1_), channel_id=1, source_target_pairs={{0,6},{1,7},{2,0},{3,1},{4,2},{5,3},{6,4},{7,5},{8,14},{9,15},{10,... | collective-permute-start | bytes 1572872 | tf_op jit(solution)/shard_map/ppermute | solution.py:373
  20.4 10.0 %copy-start.6 = (f32[32,4096]{1,0:T(8,128)}, f32[32,4096]{1,0:T(8,128)S(1)}, u32[]{:S(2)}) copy-start(f32[32,4096]{1,0:T(8,128)S(1)} %collective-permute-done.5.refs_6_) | copy-start | bytes 1572868
  20.8 11.2 %copy-start.8 = (f32[32,4096]{1,0:T(8,128)}, f32[32,4096]{1,0:T(8,128)S(1)}, u32[]{:S(2)}) copy-start(f32[32,4096]{1,0:T(8,128)S(1)} %collective-permute-done.3.refs_4_) | copy-start | bytes 1572868
  30.3 1.7 %copy-start.10 = (f32[32,4096]{1,0:T(8,128)}, f32[32,4096]{1,0:T(8,128)S(1)}, u32[]{:S(2)}) copy-start(f32[32,4096]{1,0:T(8,128)S(1)} %collective-permute-done.6.refs_7_) | copy-start | bytes 1572868
  30.4 0.9 copy-start.4
  32.0 0.8 copy-start.12
  34.1 7.5 %collective-permute-start.7 = (f32[8192,128]{1,0:T(8,128)}, f32[8192,128]{1,0:T(8,128)}, u32[]{:S(2)}, u32[]{:S(2)}) collective-permute-start(f32[8192,128]{1,0:T(8,128)} %refs_13_.3), channel_id=1, source_target_pairs={{0,1},{1,0},{2,3},{3,2},{4,5},{5,4},{6,7},{7,6},{8,9},{9,8},{10,11... | collective-permute-start | bytes 12582920 | tf_op jit(solution)/shard_map/ppermute | solution.py:373
  34.2 28.5 %collective-permute-start.8 = (f32[128,2048]{1,0:T(8,128)S(1)}, f32[128,2048]{1,0:T(8,128)S(1)}, u32[]{:S(2)}, u32[]{:S(2)}) collective-permute-start(f32[128,2048]{1,0:T(8,128)S(1)} %get-tuple-element.31), channel_id=1, source_target_pairs={{0,2},{1,3},{2,4},{3,5},{4,6},{5,7},{6,0},{7,1},{8,10},{9,11},{10,... | collective-permute-start | bytes 3145736 | tf_op jit(solution)/shard_map/ppermute | solution.py:373
  35.7 27.0 %collective-permute-start.10 = (f32[128,2048]{1,0:T(8,128)}, f32[128,2048]{1,0:T(8,128)S(1)}, u32[]{:S(2)}, u32[]{:S(2)}) collective-permute-start(f32[128,2048]{1,0:T(8,128)} %get-tuple-element.29), channel_id=1, source_target_pairs={{0,8},{1,9},{2,10},{3,11},{4,12},{5,13},{6,14},{7,15},{8,0},{9,1},... | collective-permute-start | bytes 3145736 | tf_op jit(solution)/shard_map/ppermute | solution.py:373
  38.5 25.0 %collective-permute-start.9 = (f32[128,2048]{1,0:T(8,128)S(1)}, f32[128,2048]{1,0:T(8,128)S(1)}, u32[]{:S(2)}, u32[]{:S(2)}) collective-permute-start(f32[128,2048]{1,0:T(8,128)S(1)} %get-tuple-element.30), channel_id=1, source_target_pairs={{0,6},{1,7},{2,0},{3,1},{4,2},{5,3},{6,4},{7,5},{8,14},{9,15},{10,... | collective-permute-start | bytes 3145736 | tf_op jit(solution)/shard_map/ppermute | solution.py:373
  41.6 1.0 copy-start.5
  42.7 1.0 copy-start.7
  43.7 1.0 copy-start.9
  44.7 1.0 copy-start.11
  45.8 1.0 copy-start.13
  46.8 1.0 copy-start.16
  62.7 16.8 %copy-start.14 = (f32[128,2048]{1,0:T(8,128)}, f32[128,2048]{1,0:T(8,128)S(1)}, u32[]{:S(2)}) copy-start(f32[128,2048]{1,0:T(8,128)S(1)} %collective-permute-done.10.refs_10_) | copy-start | bytes 3145732
  62.7 16.8 %copy-start = (f32[128,2048]{1,0:T(8,128)}, f32[128,2048]{1,0:T(8,128)S(1)}, u32[]{:S(2)}) copy-start(f32[128,2048]{1,0:T(8,128)S(1)} %collective-permute-done.8.refs_8_) | copy-start | bytes 3145732
  63.5 16.0 %copy-start.1 = (f32[128,2048]{1,0:T(8,128)}, f32[128,2048]{1,0:T(8,128)S(1)}, u32[]{:S(2)}) copy-start(f32[128,2048]{1,0:T(8,128)S(1)} %collective-permute-done.9.refs_9_) | copy-start | bytes 3145732
  63.6 14.4 %collective-permute-start.11 = (f32[64,2048]{1,0:T(8,128)S(1)}, f32[64,2048]{1,0:T(8,128)S(1)}, u32[]{:S(2)}, u32[]{:S(2)}) collective-permute-start(f32[64,2048]{1,0:T(8,128)S(1)} %slice.42), channel_id=1, source_target_pairs={{0,2},{1,3},{2,4},{3,5},{4,6},{5,7},{6,0},{7,1},{8,10},{9,11},{10,... | collective-permute-start | bytes 1572872 | tf_op jit(solution)/shard_map/ppermute | solution.py:373
  65.3 14.2 %collective-permute-start.12 = (f32[64,2048]{1,0:T(8,128)S(1)}, f32[64,2048]{1,0:T(8,128)S(1)}, u32[]{:S(2)}, u32[]{:S(2)}) collective-permute-start(f32[64,2048]{1,0:T(8,128)S(1)} %slice.43), channel_id=1, source_target_pairs={{0,8},{1,9},{2,10},{3,11},{4,12},{5,13},{6,14},{7,15},{8,0},{9,1},... | collective-permute-start | bytes 1572872 | tf_op jit(solution)/shard_map/ppermute | solution.py:373
  78.0 9.0 %copy-start.17 = (f32[64,2048]{1,0:T(8,128)}, f32[64,2048]{1,0:T(8,128)S(1)}, u32[]{:S(2)}) copy-start(f32[64,2048]{1,0:T(8,128)S(1)} %collective-permute-done.11.refs_11_) | copy-start | bytes 1572868
  79.6 7.5 %copy-start.18 = (f32[64,2048]{1,0:T(8,128)}, f32[64,2048]{1,0:T(8,128)S(1)}, u32[]{:S(2)}) copy-start(f32[64,2048]{1,0:T(8,128)S(1)} %collective-permute-done.12.refs_12_) | copy-start | bytes 1572868
  87.0 2.1 %collective-permute-start.13 = (f32[1152,128]{1,0:T(8,128)S(1)}, f32[1152,128]{1,0:T(8,128)S(1)}, u32[]{:S(2)}, u32[]{:S(2)}) collective-permute-start(f32[1152,128]{1,0:T(8,128)S(1)} %get-tuple-element.26), channel_id=1, source_target_pairs={{0,1},{1,0},{2,3},{3,2},{4,5},{5,4},{6,7},{7,6},{8,9},{9,8},{10,11... | collective-permute-start | bytes 1769480 | tf_op jit(solution)/shard_map/ppermute | solution.py:373
  118.0 2.0 %collective-permute-start.14 = (f32[1152,128]{1,0:T(8,128)S(1)}, f32[1152,128]{1,0:T(8,128)S(1)}, u32[]{:S(2)}, u32[]{:S(2)}) collective-permute-start(f32[1152,128]{1,0:T(8,128)S(1)} %bitcast.19), channel_id=1, source_target_pairs={{0,1},{1,0},{2,3},{3,2},{4,5},{5,4},{6,7},{7,6},{8,9},{9,8},{10,11... | collective-permute-start | bytes 1769480 | tf_op jit(solution)/shard_map/ppermute | solution.py:373
  132.1 4.2 %collective-permute-start.15 = (f32[4096,128]{1,0:T(8,128)S(1)}, f32[4096,128]{1,0:T(8,128)S(1)}, u32[]{:S(2)}, u32[]{:S(2)}) collective-permute-start(f32[4096,128]{1,0:T(8,128)S(1)} %get-tuple-element.28), channel_id=1, source_target_pairs={{0,1},{1,0},{2,3},{3,2},{4,5},{5,4},{6,7},{7,6},{8,9},{9,8},{10,11... | collective-permute-start | bytes 6291464 | tf_op jit(solution)/shard_map/ppermute | solution.py:373
  132.8 3.6 %copy-start.19 = (f32[8192,128]{1,0:T(8,128)}, f32[8192,128]{1,0:T(8,128)S(1)}, u32[]{:S(2)}) copy-start(f32[8192,128]{1,0:T(8,128)S(1)} %constant_dynamic-update-slice_fusion.1) | copy-start | bytes 12582916

commit v9 on v7

--- a/solution.py
+++ b/solution.py
@@ -341,6 +341,7 @@
     b_own = core_swap(half_of(1 - core))
     own = jnp.concatenate([a_own, b_own], axis=0)
     a_away, a_below, a_above = across(a_own), up(a_own), down(a_own)
+    b_own, other = lax.optimization_barrier((b_own, core_swap(vectors)))
     b_away, b_below, b_above = across(b_own), up(b_own), down(b_own)
     near = (a_own, b_own, a_below, b_below, a_above, b_above, a_away, b_away)
 
@@ -356,8 +357,6 @@
     )
     to_across = jnp.concatenate(late_half(a_below, b_below, a_above, b_above), axis=0)
     sent_up, sent_down, sent_across = up(to_up), down(to_down), across(to_across)
-    vectors_late, _ = lax.optimization_barrier((vectors, to_up))
-    other = core_swap(vectors_late)
 
     chips = []
     for x_step, z_step in ((0, 0), (0, -1), (0, 1), (1, 0), (0, 2), (1, -1), (1, 1), (1, 2)):
@@ -433,7 +432,9 @@
     mine = lax.all_to_all(spread, "row", 0, 0).reshape(length, WIDE)
     theirs = core_swap(mine)
 
-    held = [pltpu.with_memory_space_constraint(v, pltpu.HBM) for v in near + far]
+    *held, vectors_held, other_held = [
+        pltpu.with_memory_space_constraint(v, pltpu.HBM) for v in near + far + (vectors, other)
+    ]
     result_own, result_other = pl.pallas_call(
         apply_kernel,
         out_shape=[jax.ShapeDtypeStruct((half, columns), F32)] * 2,
@@ -455,7 +456,7 @@
             dimension_semantics=("arbitrary",), vmem_limit_bytes=LIMIT
         ),
         name="solve_apply",
-    )(where, *held, vectors, other, mine, theirs)
+    )(where, *held, vectors_held, other_held, mine, theirs)
 
     returned = core_swap(result_other)
     result = jnp.zeros((rows, columns), F32)

time: 139 us -> 133 us (0.957)
  waiting for transfers between devices: 47.1 us -> 42.2 us
  starting transfers between devices: 20.5 us -> 24.7 us
  local copies, waits for them, and re-layouts: 11.5 us -> 7.75 us
    ppermute x16, waiting for transfers between devices: 47.1 us -> 42.2 us  [permute(): return lax.ppermute(value, 'col', pairs)]
    ppermute x16, starting transfers between devices: 20.5 us -> 24.7 us  [permute(): return lax.ppermute(value, 'col', pairs)]
    unnamed x40 -> x36, local copies, waits for them, and re-layouts: 7.99 us -> 4.22 us
  transfers between devices with their start and end apart: 16 -> 16, of which waited for: 11 -> 10; matrix products, arithmetic and copies ran while one was open for 1% -> 2% of each run, Pallas kernels for 5% -> 5%
where the time goes in v9:
time: 133 us; the launch traced here: 132 us
  waiting for transfers between devices  42.2 us (32%)
  blocking collectives  29.2 us (22%)
  Pallas kernels  27.3 us (21%)
  starting transfers between devices  24.7 us (19%)
  local copies, waits for them, and re-layouts  7.75 us (6%)
    ppermute x16, waiting for transfers between devices, permute(): return lax.ppermute(value, 'col', pairs)  42.2 us
    ppermute x16, starting transfers between devices, permute(): return lax.ppermute(value, 'col', pairs)  24.7 us
    all_to_all x1, blocking collectives, per_device(): lax.all_to_all(mine.reshape(members, length // members, WIDE), 'row', 0, 0)  16.2 us
    pallas_call x2, Pallas kernels, gram(): pl.pallas_call(functools.partial(gram_kernel, first=first), out_shape=sha...  15.1 us
    all_to_all x1, blocking collectives, per_device(): mine = lax.all_to_all(spread, 'row', 0, 0).reshape(length, WIDE)  13 us
    pallas_call x1, Pallas kernels, per_device(): pl.pallas_call(apply_kernel, out_shape=[jax.ShapeDtypeStruct((half, colum...  12.1 us
    unnamed x36, local copies, waits for them, and re-layouts  4.22 us
  transfers between devices with their start and end apart: 16, of which 10 were waited for; matrix products, arithmetic and copies ran while one was open for 2% of the time, Pallas kernels for 5%

profile of v9, /device:TPU:0, one launch (start us, length us, event | category | flops | bytes accessed | tf_op | source)
XLA Modules:
  0.0 131.9 jit_solution(13092010642896918303)
XLA Ops:
  0.0 0.0 collective-permute-start.1
  0.0 1.3 dynamic-slice_bitcast_fusion
  1.3 0.6 collective-permute-start
  1.9 0.0 copy-start.3
  1.9 2.1 %collective-permute-start.2 = (f32[32,4096]{1,0:T(8,128)S(1)}, f32[32,4096]{1,0:T(8,128)S(1)}, u32[]{:S(2)}, u32[]{:S(2)}) collective-permute-start(f32[32,4096]{1,0:T(8,128)S(1)} %pad_maximum_fusion.5.refs_0_), channel_id=1, source_target_pairs={{0,2},{1,3},{2,4},{3,5},{4,6},{5,7},{6,0},{7,1},{8,10},{9,11},{10,... | collective-permute-start | bytes 1572872 | tf_op jit(solution)/shard_map/ppermute | solution.py:322
  4.0 3.0 %collective-permute-start.6 = (f32[32,4096]{1,0:T(8,128)S(1)}, f32[32,4096]{1,0:T(8,128)S(1)}, u32[]{:S(2)}, u32[]{:S(2)}) collective-permute-start(f32[32,4096]{1,0:T(8,128)S(1)} %pad_maximum_fusion.5.refs_0_), channel_id=1, source_target_pairs={{0,8},{1,9},{2,10},{3,11},{4,12},{5,13},{6,14},{7,15},{8,0},{9,1},... | collective-permute-start | bytes 1572872 | tf_op jit(solution)/shard_map/ppermute | solution.py:322
  7.0 2.2 %collective-permute-start.4 = (f32[32,4096]{1,0:T(8,128)S(1)}, f32[32,4096]{1,0:T(8,128)S(1)}, u32[]{:S(2)}, u32[]{:S(2)}) collective-permute-start(f32[32,4096]{1,0:T(8,128)S(1)} %pad_maximum_fusion.5.refs_0_), channel_id=1, source_target_pairs={{0,6},{1,7},{2,0},{3,1},{4,2},{5,3},{6,4},{7,5},{8,14},{9,15},{10,... | collective-permute-start | bytes 1572872 | tf_op jit(solution)/shard_map/ppermute | solution.py:322
  9.3 0.0 collective-permute-done.refs_1_
  9.3 0.0 collective-permute-done.1.refs_9_.refs_14_
  9.3 1.9 %collective-permute-start.7 = (f32[32,4096]{1,0:T(8,128)}, f32[32,4096]{1,0:T(8,128)S(1)}, u32[]{:S(2)}, u32[]{:S(2)}) collective-permute-start(f32[32,4096]{1,0:T(8,128)} %collective-permute-done.refs_1_), channel_id=1, source_target_pairs={{0,8},{1,9},{2,10},{3,11},{4,12},{5,13},{6,14},{7,15},{8,0},{9,1},... | collective-permute-start | bytes 1572872 | tf_op jit(solution)/shard_map/ppermute | solution.py:322
  11.2 1.9 %collective-permute-start.3 = (f32[32,4096]{1,0:T(8,128)}, f32[32,4096]{1,0:T(8,128)S(1)}, u32[]{:S(2)}, u32[]{:S(2)}) collective-permute-start(f32[32,4096]{1,0:T(8,128)} %collective-permute-done.refs_1_), channel_id=1, source_target_pairs={{0,2},{1,3},{2,4},{3,5},{4,6},{5,7},{6,0},{7,1},{8,10},{9,11},{10,... | collective-permute-start | bytes 1572872 | tf_op jit(solution)/shard_map/ppermute | solution.py:322
  13.1 0.1 stack.39.where_ref
  13.2 5.7 %collective-permute-done.2.refs_2_ = f32[32,4096]{1,0:T(8,128)S(1)} collective-permute-done((f32[32,4096]{1,0:T(8,128)S(1)}, f32[32,4096]{1,0:T(8,128)S(1)}, u32[]{:S(2)}, u32[]{:S(2)}) %collective-permute-start.2) | collective-permute-done | bytes 524320 | tf_op jit(solution)/shard_map/ppermute | solution.py:322
  18.9 2.1 %collective-permute-start.5 = (f32[32,4096]{1,0:T(8,128)}, f32[32,4096]{1,0:T(8,128)S(1)}, u32[]{:S(2)}, u32[]{:S(2)}) collective-permute-start(f32[32,4096]{1,0:T(8,128)} %collective-permute-done.refs_1_), channel_id=1, source_target_pairs={{0,6},{1,7},{2,0},{3,1},{4,2},{5,3},{6,4},{7,5},{8,14},{9,15},{10,... | collective-permute-start | bytes 1572872 | tf_op jit(solution)/shard_map/ppermute | solution.py:322
  21.0 0.0 copy-start
  21.0 0.0 collective-permute-done.6.refs_6_
  21.0 0.0 copy-start.7
  21.0 0.1 collective-permute-done.4.refs_4_
  21.2 9.2 %collective-permute-done.7.refs_7_ = f32[32,4096]{1,0:T(8,128)S(1)} collective-permute-done((f32[32,4096]{1,0:T(8,128)}, f32[32,4096]{1,0:T(8,128)S(1)}, u32[]{:S(2)}, u32[]{:S(2)}) %collective-permute-start.7) | collective-permute-done | bytes 524320 | tf_op jit(solution)/shard_map/ppermute | solution.py:322
  30.4 0.0 collective-permute-done.3.refs_3_
  30.4 0.0 copy-start.5
  30.4 1.4 %collective-permute-done.5.refs_5_ = f32[32,4096]{1,0:T(8,128)S(1)} collective-permute-done((f32[32,4096]{1,0:T(8,128)}, f32[32,4096]{1,0:T(8,128)S(1)}, u32[]{:S(2)}, u32[]{:S(2)}) %collective-permute-start.5) | collective-permute-done | bytes 524320 | tf_op jit(solution)/shard_map/ppermute | solution.py:322
  31.8 0.4 pad_maximum_fusion.4
  32.2 0.0 copy-done.7
  32.2 0.0 copy-done.5
  32.2 1.8 %collective-permute-start.8 = (f32[128,2048]{1,0:T(8,128)S(1)}, f32[128,2048]{1,0:T(8,128)S(1)}, u32[]{:S(2)}, u32[]{:S(2)}) collective-permute-start(f32[128,2048]{1,0:T(8,128)S(1)} %get-tuple-element.25), channel_id=1, source_target_pairs={{0,2},{1,3},{2,4},{3,5},{4,6},{5,7},{6,0},{7,1},{8,10},{9,11},{10,... | collective-permute-start | bytes 3145736 | tf_op jit(solution)/shard_map/ppermute | solution.py:322
  34.0 0.0 copy-done.9
  34.0 0.0 copy-done.11
  34.0 1.9 %collective-permute-start.9 = (f32[128,2048]{1,0:T(8,128)S(1)}, f32[128,2048]{1,0:T(8,128)S(1)}, u32[]{:S(2)}, u32[]{:S(2)}) collective-permute-start(f32[128,2048]{1,0:T(8,128)S(1)} %get-tuple-element.24), channel_id=1, source_target_pairs={{0,6},{1,7},{2,0},{3,1},{4,2},{5,3},{6,4},{7,5},{8,14},{9,15},{10,... | collective-permute-start | bytes 3145736 | tf_op jit(solution)/shard_map/ppermute | solution.py:322
  35.9 2.7 %collective-permute-start.10 = (f32[128,2048]{1,0:T(8,128)S(1)}, f32[128,2048]{1,0:T(8,128)S(1)}, u32[]{:S(2)}, u32[]{:S(2)}) collective-permute-start(f32[128,2048]{1,0:T(8,128)S(1)} %get-tuple-element.23), channel_id=1, source_target_pairs={{0,8},{1,9},{2,10},{3,11},{4,12},{5,13},{6,14},{7,15},{8,0},{9,1},... | collective-permute-start | bytes 3145736 | tf_op jit(solution)/shard_map/ppermute | solution.py:322
  38.5 0.0 copy-done
  38.5 1.0 copy-done.6
  39.6 1.0 copy-done.8
  40.6 1.0 copy-done.10
  41.7 1.0 copy-done.12
  42.7 6.2 %gram_near.1.refs_15_ = f32[2,640,128]{2,1,0:T(8,128)S(1)} custom-call(s32[9]{0:T(128)S(1)} %stack.39.where_ref, f32[32,4096]{1,0:T(8,128)S(1)} %pad_maximum_fusion.5.refs_0_, f32[32,4096]{1,0:T(8,128)} %collective-permute-done.refs_1_, f32[32,4096]{1,0:T(8,128)S(1)} %collective-permute-done.2.refs_2_, f32[32,4096]{1,0:T(8,128)S(1)} %copy-done.6, ...), custom_call_target="tpu_custom_call" | custom-call | flops 16106127360 | bytes 8388608 | tf_op jit(solution)/shard_map/gram_near/pallas_call | solution.py:390
  48.9 8.4 %collective-permute-done.8.refs_8_ = f32[128,2048]{1,0:T(8,128)S(1)} collective-permute-done((f32[128,2048]{1,0:T(8,128)S(1)}, f32[128,2048]{1,0:T(8,128)S(1)}, u32[]{:S(2)}, u32[]{:S(2)}) %collective-permute-start.8) | collective-permute-done | bytes 1048608 | tf_op jit(solution)/shard_map/ppermute | solution.py:322
  57.3 0.0 collective-permute-done.9.refs_9_
  57.4 1.7 %collective-permute-start.11 = (f32[64,2048]{1,0:T(8,128)S(1)}, f32[64,2048]{1,0:T(8,128)S(1)}, u32[]{:S(2)}, u32[]{:S(2)}) collective-permute-start(f32[64,2048]{1,0:T(8,128)S(1)} %slice.42), channel_id=1, source_target_pairs={{0,2},{1,3},{2,4},{3,5},{4,6},{5,7},{6,0},{7,1},{8,10},{9,11},{10,... | collective-permute-start | bytes 1572872 | tf_op jit(solution)/shard_map/ppermute | solution.py:322
  59.1 2.6 %collective-permute-start.12 = (f32[64,2048]{1,0:T(8,128)S(1)}, f32[64,2048]{1,0:T(8,128)S(1)}, u32[]{:S(2)}, u32[]{:S(2)}) collective-permute-start(f32[64,2048]{1,0:T(8,128)S(1)} %slice.43), channel_id=1, source_target_pairs={{0,8},{1,9},{2,10},{3,11},{4,12},{5,13},{6,14},{7,15},{8,0},{9,1},... | collective-permute-start | bytes 1572872 | tf_op jit(solution)/shard_map/ppermute | solution.py:322
  61.7 0.0 collective-permute-done.10.refs_10_
  61.7 8.2 %collective-permute-done.11.refs_11_ = f32[64,2048]{1,0:T(8,128)S(1)} collective-permute-done((f32[64,2048]{1,0:T(8,128)S(1)}, f32[64,2048]{1,0:T(8,128)S(1)}, u32[]{:S(2)}, u32[]{:S(2)}) %collective-permute-start.11) | collective-permute-done | bytes 524320 | tf_op jit(solution)/shard_map/ppermute | solution.py:322
  69.9 1.6 %collective-permute-done.12.refs_12_ = f32[64,2048]{1,0:T(8,128)S(1)} collective-permute-done((f32[64,2048]{1,0:T(8,128)S(1)}, f32[64,2048]{1,0:T(8,128)S(1)}, u32[]{:S(2)}, u32[]{:S(2)}) %collective-permute-start.12) | collective-permute-done | bytes 524320 | tf_op jit(solution)/shard_map/ppermute | solution.py:322
  71.6 0.0 copy-done.3
  71.6 0.0 copy-done.4
  71.6 0.0 copy-done.13
  71.6 0.0 copy-start.16
  71.6 8.9 %gram_far.1 = (f32[1152,128]{1,0:T(8,128)S(1)}, f32[1152,128]{1,0:T(8,128)S(1)}) custom-call(s32[9]{0:T(128)S(1)} %stack.39.where_ref, f32[32,4096]{1,0:T(8,128)S(1)} %pad_maximum_fusion.5.refs_0_, f32[32,4096]{1,0:T(8,128)} %collective-permute-done.refs_1_, f32[32,4096]{1,0:T(8,128)S(1)} %collective-permute-done.2.refs_2_, f32[32,4096]{1,0:T(8,128)S(1)} %copy-done.6, ...), custom_call_target="tpu_custom_call" | custom-call | flops 25769803776 | bytes 12582912 | tf_op jit(solution)/shard_map/gram_far/pallas_call | solution.py:390
  80.5 0.0 copy-done.1
  80.5 0.0 copy-done.2
  80.6 0.1 collective-permute-start.13
  80.7 2.0 %collective-permute-done.13 = f32[1152,128]{1,0:T(8,128)S(1)} collective-permute-done((f32[1152,128]{1,0:T(8,128)S(1)}, f32[1152,128]{1,0:T(8,128)S(1)}, u32[]{:S(2)}, u32[]{:S(2)}) %collective-permute-start.13) | collective-permute-done | bytes 589856 | tf_op jit(solution)/shard_map/ppermute | solution.py:322
  82.7 0.1 add.93
  82.7 16.2 %all_to_all.10 = f32[8,144,128]{2,1,0:T(8,128)S(1)} all-to-all(f32[8,144,128]{2,1,0:T(8,128)S(1)} %bitcast.21), channel_id=1, replica_groups=mesh['row'=8,'col'=16] {'row'}, dimensions={0} | all-to-all | bytes 1179648 | tf_op jit(solution)/shard_map/all_to_all | solution.py:429
  99.0 13.0 %all_to_all.11 = f32[8,144,128]{2,1,0:T(8,128)S(1)} all-to-all(f32[8,144,128]{2,1,0:T(8,128)S(1)} %broadcast_in_dim.10), channel_id=1, replica_groups=mesh['row'=8,'col'=16] {'row'}, dimensions={0} | all-to-all | bytes 1179648 | tf_op jit(solution)/shard_map/all_to_all | solution.py:432
  112.0 0.0 collective-permute-start.14
  112.0 2.0 %collective-permute-done.14.refs_16_ = f32[1152,128]{1,0:T(8,128)S(1)} collective-permute-done((f32[1152,128]{1,0:T(8,128)S(1)}, f32[1152,128]{1,0:T(8,128)S(1)}, u32[]{:S(2)}, u32[]{:S(2)}) %collective-permute-start.14) | collective-permute-done | bytes 589856 | tf_op jit(solution)/shard_map/ppermute | solution.py:322
  114.0 12.1 %solve_apply.1 = (f32[4096,128]{1,0:T(8,128)S(1)}, f32[4096,128]{1,0:T(8,128)S(1)}) custom-call(s32[9]{0:T(128)S(1)} %stack.39.where_ref, f32[32,4096]{1,0:T(8,128)} %copy-done.3, f32[32,4096]{1,0:T(8,128)} %collective-permute-done.refs_1_, f32[32,4096]{1,0:T(8,128)} %copy-done.4, f32[32,4096]{1,0:T(8,128)} %copy-done.5, f32[32,4096]{1,0:T(8,128)} %copy-done.9, ...), custom_call_target="tpu_custom_call" | custom-call | tf_op jit(solution)/shard_map/solve_apply/pallas_call | solution.py:438
  126.2 0.2 collective-permute-start.15
  126.4 0.3 broadcast_in_dim.4
  126.6 0.2 constant_dynamic-update-slice_fusion.1
  126.9 0.0 copy-start.17
  126.9 3.5 %collective-permute-done.15 = f32[4096,128]{1,0:T(8,128)S(1)} collective-permute-done((f32[4096,128]{1,0:T(8,128)S(1)}, f32[4096,128]{1,0:T(8,128)S(1)}, u32[]{:S(2)}, u32[]{:S(2)}) %collective-permute-start.15) | collective-permute-done | bytes 2097184 | tf_op jit(solution)/shard_map/ppermute | solution.py:322
  130.4 1.5 %constant_dynamic-update-slice_fusion = f32[8192,128]{1,0:T(8,128)} fusion(f32[8192,128]{1,0:T(8,128)} %copy-done.17, f32[4096,128]{1,0:T(8,128)S(1)} %collective-permute-done.15, s32[]{:T(128)S(6)} %select_n.61), kind=kLoop, calls=%fused_computation.11 | loop fusion | bytes 4194308 | tf_op jit(solution)/shard_map/dynamic_update_slice | solution.py:464
  (28 shorter events, 0.4 us)
Async XLA Ops:
  0.0 9.3 %collective-permute-start.1 = (f32[8192,128]{1,0:T(8,128)}, f32[8192,128]{1,0:T(8,128)}, u32[]{:S(2)}, u32[]{:S(2)}) collective-permute-start(f32[8192,128]{1,0:T(8,128)} %refs_13_.3), channel_id=1, source_target_pairs={{0,1},{1,0},{2,3},{3,2},{4,5},{5,4},{6,7},{7,6},{8,9},{9,8},{10,11... | collective-permute-start | bytes 12582920 | tf_op jit(solution)/shard_map/ppermute | solution.py:322
  1.3 7.9 %collective-permute-start = (f32[32,4096]{1,0:T(8,128)S(1)}, f32[32,4096]{1,0:T(8,128)}, u32[]{:S(2)}, u32[]{:S(2)}) collective-permute-start(f32[32,4096]{1,0:T(8,128)S(1)} %pad_maximum_fusion.6), channel_id=1, source_target_pairs={{0,1},{1,0},{2,3},{3,2},{4,5},{5,4},{6,7},{7,6},{8,9},{9,8},{10,11... | collective-permute-start | bytes 1572872 | tf_op jit(solution)/shard_map/ppermute | solution.py:322
  1.9 69.6 %copy-start.3 = (f32[32,4096]{1,0:T(8,128)}, f32[32,4096]{1,0:T(8,128)S(1)}, u32[]{:S(2)}) copy-start(f32[32,4096]{1,0:T(8,128)S(1)} %pad_maximum_fusion.5.refs_0_) | copy-start | bytes 1572868
  1.9 16.9 %collective-permute-start.2 = (f32[32,4096]{1,0:T(8,128)S(1)}, f32[32,4096]{1,0:T(8,128)S(1)}, u32[]{:S(2)}, u32[]{:S(2)}) collective-permute-start(f32[32,4096]{1,0:T(8,128)S(1)} %pad_maximum_fusion.5.refs_0_), channel_id=1, source_target_pairs={{0,2},{1,3},{2,4},{3,5},{4,6},{5,7},{6,0},{7,1},{8,10},{9,11},{10,... | collective-permute-start | bytes 1572872 | tf_op jit(solution)/shard_map/ppermute | solution.py:322
  4.0 17.0 %collective-permute-start.6 = (f32[32,4096]{1,0:T(8,128)S(1)}, f32[32,4096]{1,0:T(8,128)S(1)}, u32[]{:S(2)}, u32[]{:S(2)}) collective-permute-start(f32[32,4096]{1,0:T(8,128)S(1)} %pad_maximum_fusion.5.refs_0_), channel_id=1, source_target_pairs={{0,8},{1,9},{2,10},{3,11},{4,12},{5,13},{6,14},{7,15},{8,0},{9,1},... | collective-permute-start | bytes 1572872 | tf_op jit(solution)/shard_map/ppermute | solution.py:322
  7.0 14.1 %collective-permute-start.4 = (f32[32,4096]{1,0:T(8,128)S(1)}, f32[32,4096]{1,0:T(8,128)S(1)}, u32[]{:S(2)}, u32[]{:S(2)}) collective-permute-start(f32[32,4096]{1,0:T(8,128)S(1)} %pad_maximum_fusion.5.refs_0_), channel_id=1, source_target_pairs={{0,6},{1,7},{2,0},{3,1},{4,2},{5,3},{6,4},{7,5},{8,14},{9,15},{10,... | collective-permute-start | bytes 1572872 | tf_op jit(solution)/shard_map/ppermute | solution.py:322
  9.3 21.1 %collective-permute-start.7 = (f32[32,4096]{1,0:T(8,128)}, f32[32,4096]{1,0:T(8,128)S(1)}, u32[]{:S(2)}, u32[]{:S(2)}) collective-permute-start(f32[32,4096]{1,0:T(8,128)} %collective-permute-done.refs_1_), channel_id=1, source_target_pairs={{0,8},{1,9},{2,10},{3,11},{4,12},{5,13},{6,14},{7,15},{8,0},{9,1},... | collective-permute-start | bytes 1572872 | tf_op jit(solution)/shard_map/ppermute | solution.py:322
  11.2 19.2 %collective-permute-start.3 = (f32[32,4096]{1,0:T(8,128)}, f32[32,4096]{1,0:T(8,128)S(1)}, u32[]{:S(2)}, u32[]{:S(2)}) collective-permute-start(f32[32,4096]{1,0:T(8,128)} %collective-permute-done.refs_1_), channel_id=1, source_target_pairs={{0,2},{1,3},{2,4},{3,5},{4,6},{5,7},{6,0},{7,1},{8,10},{9,11},{10,... | collective-permute-start | bytes 1572872 | tf_op jit(solution)/shard_map/ppermute | solution.py:322
  18.9 52.7 %copy-start.4 = (f32[32,4096]{1,0:T(8,128)}, f32[32,4096]{1,0:T(8,128)S(1)}, u32[]{:S(2)}) copy-start(f32[32,4096]{1,0:T(8,128)S(1)} %collective-permute-done.2.refs_2_) | copy-start | bytes 1572868
  18.9 12.9 %collective-permute-start.5 = (f32[32,4096]{1,0:T(8,128)}, f32[32,4096]{1,0:T(8,128)S(1)}, u32[]{:S(2)}, u32[]{:S(2)}) collective-permute-start(f32[32,4096]{1,0:T(8,128)} %collective-permute-done.refs_1_), channel_id=1, source_target_pairs={{0,6},{1,7},{2,0},{3,1},{4,2},{5,3},{6,4},{7,5},{8,14},{9,15},{10,... | collective-permute-start | bytes 1572872 | tf_op jit(solution)/shard_map/ppermute | solution.py:322
  21.0 17.6 %copy-start = (f32[8192,128]{1,0:T(8,128)S(1)}, f32[8192,128]{1,0:T(8,128)}, u32[]{:S(2)}) copy-start(f32[8192,128]{1,0:T(8,128)} %refs_13_.3) | copy-start | bytes 12582916
  21.0 11.2 %copy-start.7 = (f32[32,4096]{1,0:T(8,128)}, f32[32,4096]{1,0:T(8,128)S(1)}, u32[]{:S(2)}) copy-start(f32[32,4096]{1,0:T(8,128)S(1)} %collective-permute-done.6.refs_6_) | copy-start | bytes 1572868
  21.1 12.9 %copy-start.9 = (f32[32,4096]{1,0:T(8,128)}, f32[32,4096]{1,0:T(8,128)S(1)}, u32[]{:S(2)}) copy-start(f32[32,4096]{1,0:T(8,128)S(1)} %collective-permute-done.4.refs_4_) | copy-start | bytes 1572868
  30.3 3.7 %copy-start.11 = (f32[32,4096]{1,0:T(8,128)}, f32[32,4096]{1,0:T(8,128)S(1)}, u32[]{:S(2)}) copy-start(f32[32,4096]{1,0:T(8,128)S(1)} %collective-permute-done.7.refs_7_) | copy-start | bytes 1572868
  30.4 1.8 %copy-start.5 = (f32[32,4096]{1,0:T(8,128)}, f32[32,4096]{1,0:T(8,128)S(1)}, u32[]{:S(2)}) copy-start(f32[32,4096]{1,0:T(8,128)S(1)} %collective-permute-done.3.refs_3_) | copy-start | bytes 1572868
  31.8 39.8 %copy-start.13 = (f32[32,4096]{1,0:T(8,128)}, f32[32,4096]{1,0:T(8,128)S(1)}, u32[]{:S(2)}) copy-start(f32[32,4096]{1,0:T(8,128)S(1)} %collective-permute-done.5.refs_5_) | copy-start | bytes 1572868
  32.2 25.1 %collective-permute-start.8 = (f32[128,2048]{1,0:T(8,128)S(1)}, f32[128,2048]{1,0:T(8,128)S(1)}, u32[]{:S(2)}, u32[]{:S(2)}) collective-permute-start(f32[128,2048]{1,0:T(8,128)S(1)} %get-tuple-element.25), channel_id=1, source_target_pairs={{0,2},{1,3},{2,4},{3,5},{4,6},{5,7},{6,0},{7,1},{8,10},{9,11},{10,... | collective-permute-start | bytes 3145736 | tf_op jit(solution)/shard_map/ppermute | solution.py:322
  34.0 23.3 %collective-permute-start.9 = (f32[128,2048]{1,0:T(8,128)S(1)}, f32[128,2048]{1,0:T(8,128)S(1)}, u32[]{:S(2)}, u32[]{:S(2)}) collective-permute-start(f32[128,2048]{1,0:T(8,128)S(1)} %get-tuple-element.24), channel_id=1, source_target_pairs={{0,6},{1,7},{2,0},{3,1},{4,2},{5,3},{6,4},{7,5},{8,14},{9,15},{10,... | collective-permute-start | bytes 3145736 | tf_op jit(solution)/shard_map/ppermute | solution.py:322
  35.9 25.8 %collective-permute-start.10 = (f32[128,2048]{1,0:T(8,128)S(1)}, f32[128,2048]{1,0:T(8,128)S(1)}, u32[]{:S(2)}, u32[]{:S(2)}) collective-permute-start(f32[128,2048]{1,0:T(8,128)S(1)} %get-tuple-element.23), channel_id=1, source_target_pairs={{0,8},{1,9},{2,10},{3,11},{4,12},{5,13},{6,14},{7,15},{8,0},{9,1},... | collective-permute-start | bytes 3145736 | tf_op jit(solution)/shard_map/ppermute | solution.py:322
  38.5 1.0 copy-start.6
  39.6 1.0 copy-start.8
  40.6 1.0 copy-start.10
  41.7 1.0 copy-start.12
  57.3 23.3 %copy-start.1 = (f32[128,2048]{1,0:T(8,128)}, f32[128,2048]{1,0:T(8,128)S(1)}, u32[]{:S(2)}) copy-start(f32[128,2048]{1,0:T(8,128)S(1)} %collective-permute-done.8.refs_8_) | copy-start | bytes 3145732
  57.3 23.2 %copy-start.2 = (f32[128,2048]{1,0:T(8,128)}, f32[128,2048]{1,0:T(8,128)S(1)}, u32[]{:S(2)}) copy-start(f32[128,2048]{1,0:T(8,128)S(1)} %collective-permute-done.9.refs_9_) | copy-start | bytes 3145732
  57.4 12.6 %collective-permute-start.11 = (f32[64,2048]{1,0:T(8,128)S(1)}, f32[64,2048]{1,0:T(8,128)S(1)}, u32[]{:S(2)}, u32[]{:S(2)}) collective-permute-start(f32[64,2048]{1,0:T(8,128)S(1)} %slice.42), channel_id=1, source_target_pairs={{0,2},{1,3},{2,4},{3,5},{4,6},{5,7},{6,0},{7,1},{8,10},{9,11},{10,... | collective-permute-start | bytes 1572872 | tf_op jit(solution)/shard_map/ppermute | solution.py:322
  59.1 12.5 %collective-permute-start.12 = (f32[64,2048]{1,0:T(8,128)S(1)}, f32[64,2048]{1,0:T(8,128)S(1)}, u32[]{:S(2)}, u32[]{:S(2)}) collective-permute-start(f32[64,2048]{1,0:T(8,128)S(1)} %slice.43), channel_id=1, source_target_pairs={{0,8},{1,9},{2,10},{3,11},{4,12},{5,13},{6,14},{7,15},{8,0},{9,1},... | collective-permute-start | bytes 1572872 | tf_op jit(solution)/shard_map/ppermute | solution.py:322
  61.7 18.9 %copy-start.14 = (f32[128,2048]{1,0:T(8,128)}, f32[128,2048]{1,0:T(8,128)S(1)}, u32[]{:S(2)}) copy-start(f32[128,2048]{1,0:T(8,128)S(1)} %collective-permute-done.10.refs_10_) | copy-start | bytes 3145732
  69.9 10.6 %copy-start.15 = (f32[64,2048]{1,0:T(8,128)}, f32[64,2048]{1,0:T(8,128)S(1)}, u32[]{:S(2)}) copy-start(f32[64,2048]{1,0:T(8,128)S(1)} %collective-permute-done.11.refs_11_) | copy-start | bytes 1572868
  71.6 9.0 %copy-start.16 = (f32[64,2048]{1,0:T(8,128)}, f32[64,2048]{1,0:T(8,128)S(1)}, u32[]{:S(2)}) copy-start(f32[64,2048]{1,0:T(8,128)S(1)} %collective-permute-done.12.refs_12_) | copy-start | bytes 1572868
  80.6 2.1 %collective-permute-start.13 = (f32[1152,128]{1,0:T(8,128)S(1)}, f32[1152,128]{1,0:T(8,128)S(1)}, u32[]{:S(2)}, u32[]{:S(2)}) collective-permute-start(f32[1152,128]{1,0:T(8,128)S(1)} %get-tuple-element.20), channel_id=1, source_target_pairs={{0,1},{1,0},{2,3},{3,2},{4,5},{5,4},{6,7},{7,6},{8,9},{9,8},{10,11... | collective-permute-start | bytes 1769480 | tf_op jit(solution)/shard_map/ppermute | solution.py:322
  112.0 2.0 %collective-permute-start.14 = (f32[1152,128]{1,0:T(8,128)S(1)}, f32[1152,128]{1,0:T(8,128)S(1)}, u32[]{:S(2)}, u32[]{:S(2)}) collective-permute-start(f32[1152,128]{1,0:T(8,128)S(1)} %bitcast.19), channel_id=1, source_target_pairs={{0,1},{1,0},{2,3},{3,2},{4,5},{5,4},{6,7},{7,6},{8,9},{9,8},{10,11... | collective-permute-start | bytes 1769480 | tf_op jit(solution)/shard_map/ppermute | solution.py:322
  126.2 4.2 %collective-permute-start.15 = (f32[4096,128]{1,0:T(8,128)S(1)}, f32[4096,128]{1,0:T(8,128)S(1)}, u32[]{:S(2)}, u32[]{:S(2)}) collective-permute-start(f32[4096,128]{1,0:T(8,128)S(1)} %get-tuple-element.22), channel_id=1, source_target_pairs={{0,1},{1,0},{2,3},{3,2},{4,5},{5,4},{6,7},{7,6},{8,9},{9,8},{10,11... | collective-permute-start | bytes 6291464 | tf_op jit(solution)/shard_map/ppermute | solution.py:322
  126.9 3.6 %copy-start.17 = (f32[8192,128]{1,0:T(8,128)}, f32[8192,128]{1,0:T(8,128)S(1)}, u32[]{:S(2)}) copy-start(f32[8192,128]{1,0:T(8,128)S(1)} %constant_dynamic-update-slice_fusion.1) | copy-start | bytes 12582916

commit v10 on v9

--- a/solution.py
+++ b/solution.py
@@ -37,30 +37,34 @@
     )
 
 
-def each_far(step, steps, refs, place):
-    up_ref, down_ref, across_ref, end_up_ref, end_across_ref = refs
-    chunk = down_ref.shape[0]
+def each_far(step, steps, refs, place_half):
     early = step < steps // 2
 
     @pl.when(early)
     def _():
-        place(4, up_ref[:chunk])
-        place(5, up_ref[chunk:])
-        place(6, down_ref[...])
-        place(7, end_up_ref[...])
+        for swap in range(2):
+            up_ref, down_ref, across_ref, end_up_ref, end_across_ref = refs[5 * swap : 5 * swap + 5]
+            lines = down_ref.shape[0]
+            place_half(4, swap, up_ref[:lines])
+            place_half(5, swap, up_ref[lines:])
+            place_half(6, swap, down_ref[...])
+            place_half(7, swap, end_up_ref[...])
 
     @pl.when(jnp.logical_not(early))
     def _():
-        place(4, down_ref[...])
-        place(5, across_ref[:chunk])
-        place(6, across_ref[chunk:])
-        place(7, end_across_ref[...])
+        for swap in range(2):
+            up_ref, down_ref, across_ref, end_up_ref, end_across_ref = refs[5 * swap : 5 * swap + 5]
+            lines = down_ref.shape[0]
+            place_half(4, swap, down_ref[...])
+            place_half(5, swap, across_ref[:lines])
+            place_half(6, swap, across_ref[lines:])
+            place_half(7, swap, end_across_ref[...])
 
 
 def gram_kernel(where_ref, *refs, first):
     steps = pl.num_programs(0)
     step = pl.program_id(0)
-    count = 8 if first else 13
+    count = 8 if first else 18
     panels, rest = refs[:count], refs[count:]
     if first:
         own_ref, other_ref, out_ref, high, low, even, skew, proj = rest
@@ -76,14 +80,10 @@
         for target, part in zip((high, low), split2(value)):
             target[pl.ds(begin, lines), :] = part
 
-    def place(slot, value):
-        place_half(slot, 0, value[:lines])
-        place_half(slot, 1, value[lines:])
-
     for index in range(8):
         place_half(index // 2, index % 2, panels[index][...])
     if not first:
-        each_far(step, steps, panels[8:], place)
+        each_far(step, steps, panels[8:], place_half)
 
     @pl.when(step == 0)
     def _():
@@ -264,9 +264,9 @@
 def apply_kernel(where_ref, *refs):
     step = pl.program_id(0)
     steps = pl.num_programs(0)
-    panels = refs[:13]
-    current_own, current_other, mine_ref, theirs_ref, out_own, out_other = refs[13:19]
-    solved, high, low, merged, both, rows_done, ordered, sides = refs[19:]
+    panels = refs[:18]
+    current_own, current_other, mine_ref, theirs_ref, out_own, out_other = refs[18:24]
+    solved, high, low, merged, both, rows_done, ordered, sides = refs[24:]
     core = where_ref[CHIPS]
     panel = solved.shape[0] // 2
     chunk = 2 * panels[0].shape[0]
@@ -285,12 +285,13 @@
                 for target, value in zip((high, low), split2(solved[pl.ds(start, group), :])):
                     target[at : at + group, :] = value
 
-    def place(slot, value):
-        merged[slot * chunk : (slot + 1) * chunk, :] = value
+    def place_half(slot, swap, value):
+        at = slot * chunk + swap * (chunk // 2)
+        merged[at : at + chunk // 2, :] = value
 
     for index in range(8):
-        merged[index * chunk // 2 : (index + 1) * chunk // 2, :] = panels[index][...]
-    each_far(step, steps, panels[8:], place)
+        place_half(index // 2, index % 2, panels[index][...])
+    each_far(step, steps, panels[8:], place_half)
     one, two = split2(merged[...])
     first, second = high[...], low[...]
 
@@ -340,8 +341,8 @@
     a_own = half_of(core)
     b_own = core_swap(half_of(1 - core))
     own = jnp.concatenate([a_own, b_own], axis=0)
+    a_own, b_own, other = lax.optimization_barrier((a_own, b_own, core_swap(vectors)))
     a_away, a_below, a_above = across(a_own), up(a_own), down(a_own)
-    b_own, other = lax.optimization_barrier((b_own, core_swap(vectors)))
     b_away, b_below, b_above = across(b_own), up(b_own), down(b_own)
     near = (a_own, b_own, a_below, b_below, a_above, b_above, a_away, b_away)
 
@@ -351,12 +352,14 @@
     def late_half(*values):
         return [v[:, quarter:] for v in values]
 
-    to_up = jnp.concatenate(early_half(a_below, b_below, a_away, b_away), axis=0)
-    to_down = jnp.concatenate(
-        late_half(a_above, b_above) + early_half(a_away, b_away), axis=0
-    )
-    to_across = jnp.concatenate(late_half(a_below, b_below, a_above, b_above), axis=0)
-    sent_up, sent_down, sent_across = up(to_up), down(to_down), across(to_across)
+    def second_wave(below, above, away):
+        to_up = jnp.concatenate(early_half(below, away), axis=0)
+        to_down = jnp.concatenate(late_half(above) + early_half(away), axis=0)
+        to_across = jnp.concatenate(late_half(below, above), axis=0)
+        return up(to_up), down(to_down), across(to_across)
+
+    a_sent = second_wave(a_below, a_above, a_away)
+    b_sent = second_wave(b_below, b_above, b_away)
 
     chips = []
     for x_step, z_step in ((0, 0), (0, -1), (0, 1), (1, 0), (0, 2), (1, -1), (1, 1), (1, 2)):
@@ -373,9 +376,9 @@
         return pl.BlockSpec((lines, TILE), lambda j, w: (0, jnp.maximum(j - turn, 0)))
 
     both = pl.BlockSpec(
-        (chunk, TILE), lambda j, w: (jnp.where(j < turn, 1, 0), jnp.where(j < turn, j, j - turn))
+        (chunk // 2, TILE), lambda j, w: (jnp.where(j < turn, 1, 0), jnp.where(j < turn, j, j - turn))
     )
-    parts_far = [early(2 * chunk), both, late(2 * chunk), early(chunk), late(chunk)]
+    parts_far = [early(chunk), both, late(chunk), early(chunk // 2), late(chunk // 2)] * 2
     own_spec = pl.BlockSpec((TILE, columns), lambda j, w: (w[CHIPS] * steps + j, 0))
     length = size + 5 * WIDE
     span = size // 2
@@ -419,10 +422,11 @@
         )(where, *pieces, vectors, other, *extra)
 
     (before,) = gram(True, near, ())
-    before, sent_up, sent_down = lax.optimization_barrier((before, sent_up, sent_down))
-    end_up = up(sent_up[chunk:])
-    end_across = across(sent_down[:chunk])
-    far = (sent_up, sent_down, sent_across, end_up, end_across)
+    lines = chunk // 2
+    far = ()
+    for sent_up, sent_down, sent_across in (a_sent, b_sent):
+        _, sent_up, sent_down = lax.optimization_barrier((before, sent_up, sent_down))
+        far += (sent_up, sent_down, sent_across, up(sent_up[lines:]), across(sent_down[:lines]))
     kept, sent = gram(False, near + far, (before,))
     mine = kept + core_swap(sent)
     members = lax.axis_size("row")

time: 133 us -> 139 us (1.045)
  waiting for transfers between devices: 42.2 us -> 48.7 us
  local copies, waits for them, and re-layouts: 7.75 us -> 3.61 us
  starting transfers between devices: 24.7 us -> 28.4 us
    ppermute x16 -> x21, waiting for transfers between devices: 42.2 us -> 48.7 us  [permute(): return lax.ppermute(value, 'col', pairs)]
    unnamed x36 -> x38, local copies, waits for them, and re-layouts: 4.22 us -> 0.08 us
    ppermute x16 -> x21, starting transfers between devices: 24.7 us -> 28.4 us  [permute(): return lax.ppermute(value, 'col', pairs)]
  transfers between devices with their start and end apart: 16 -> 21, of which waited for: 10 -> 14; matrix products, arithmetic and copies ran while one was open for 2% -> 2% of each run, Pallas kernels for 5% -> 4%
where the time goes in v10:
time: 139 us; the launch traced here: 138 us
  waiting for transfers between devices  48.7 us (35%)
  blocking collectives  28.5 us (21%)
  starting transfers between devices  28.4 us (20%)
  Pallas kernels  27.4 us (20%)
  local copies, waits for them, and re-layouts  3.61 us (3%)
    ppermute x21, waiting for transfers between devices, permute(): return lax.ppermute(value, 'col', pairs)  48.7 us
    ppermute x21, starting transfers between devices, permute(): return lax.ppermute(value, 'col', pairs)  28.4 us
    all_to_all x1, blocking collectives, per_device(): lax.all_to_all(mine.reshape(members, length // members, WIDE), 'row', 0, 0)  15.5 us
    pallas_call x2, Pallas kernels, gram(): pl.pallas_call(functools.partial(gram_kernel, first=first), out_shape=sha...  15.2 us
    all_to_all x1, blocking collectives, per_device(): mine = lax.all_to_all(spread, 'row', 0, 0).reshape(length, WIDE)  13 us
    pallas_call x1, Pallas kernels, per_device(): pl.pallas_call(apply_kernel, out_shape=[jax.ShapeDtypeStruct((half, colum...  12.2 us
  transfers between devices with their start and end apart: 21, of which 14 were waited for; matrix products, arithmetic and copies ran while one was open for 2% of the time, Pallas kernels for 4%

profile of v10, /device:TPU:0, one launch (start us, length us, event | category | flops | bytes accessed | tf_op | source)
XLA Modules:
  0.0 137.5 jit_solution(17392321231542774351)
XLA Ops:
  0.0 0.0 collective-permute-start.1
  0.0 1.3 dynamic-slice_bitcast_fusion
  1.3 0.6 collective-permute-start
  1.9 0.0 copy-start.1
  1.9 6.1 %collective-permute-done.refs_1_ = f32[32,4096]{1,0:T(8,128)} collective-permute-done((f32[32,4096]{1,0:T(8,128)S(1)}, f32[32,4096]{1,0:T(8,128)}, u32[]{:S(2)}, u32[]{:S(2)}) %collective-permute-start) | collective-permute-done | bytes 524320 | tf_op jit(solution)/shard_map/ppermute | solution.py:323
  8.0 0.0 collective-permute-done.1.refs_9_.refs_19_
  8.0 3.1 %collective-permute-start.7 = (f32[32,4096]{1,0:T(8,128)}, f32[32,4096]{1,0:T(8,128)S(1)}, u32[]{:S(2)}, u32[]{:S(2)}) collective-permute-start(f32[32,4096]{1,0:T(8,128)} %collective-permute-done.refs_1_), channel_id=1, source_target_pairs={{0,8},{1,9},{2,10},{3,11},{4,12},{5,13},{6,14},{7,15},{8,0},{9,1},... | collective-permute-start | bytes 1572872 | tf_op jit(solution)/shard_map/ppermute | solution.py:323
  11.2 4.0 %collective-permute-start.5 = (f32[32,4096]{1,0:T(8,128)}, f32[32,4096]{1,0:T(8,128)S(1)}, u32[]{:S(2)}, u32[]{:S(2)}) collective-permute-start(f32[32,4096]{1,0:T(8,128)} %collective-permute-done.refs_1_), channel_id=1, source_target_pairs={{0,6},{1,7},{2,0},{3,1},{4,2},{5,3},{6,4},{7,5},{8,14},{9,15},{10,... | collective-permute-start | bytes 1572872 | tf_op jit(solution)/shard_map/ppermute | solution.py:323
  15.2 0.0 collective-permute-start.3
  15.2 0.1 stack.39.where_ref
  15.3 0.0 collective-permute-start.2
  15.3 3.3 %collective-permute-start.4 = (f32[32,4096]{1,0:T(8,128)S(1)}, f32[32,4096]{1,0:T(8,128)S(1)}, u32[]{:S(2)}, u32[]{:S(2)}) collective-permute-start(f32[32,4096]{1,0:T(8,128)S(1)} %pad_maximum_fusion.4.refs_0_), channel_id=1, source_target_pairs={{0,6},{1,7},{2,0},{3,1},{4,2},{5,3},{6,4},{7,5},{8,14},{9,15},{10,... | collective-permute-start | bytes 1572872 | tf_op jit(solution)/shard_map/ppermute | solution.py:323
  18.6 5.1 %collective-permute-done.7.refs_7_ = f32[32,4096]{1,0:T(8,128)S(1)} collective-permute-done((f32[32,4096]{1,0:T(8,128)}, f32[32,4096]{1,0:T(8,128)S(1)}, u32[]{:S(2)}, u32[]{:S(2)}) %collective-permute-start.7) | collective-permute-done | bytes 524320 | tf_op jit(solution)/shard_map/ppermute | solution.py:323
  23.7 3.1 %collective-permute-start.6 = (f32[32,4096]{1,0:T(8,128)S(1)}, f32[32,4096]{1,0:T(8,128)S(1)}, u32[]{:S(2)}, u32[]{:S(2)}) collective-permute-start(f32[32,4096]{1,0:T(8,128)S(1)} %pad_maximum_fusion.4.refs_0_), channel_id=1, source_target_pairs={{0,8},{1,9},{2,10},{3,11},{4,12},{5,13},{6,14},{7,15},{8,0},{9,1},... | collective-permute-start | bytes 1572872 | tf_op jit(solution)/shard_map/ppermute | solution.py:323
  26.9 1.0 collective-permute-done.5.refs_5_
  27.9 0.0 copy-start
  27.9 3.6 %collective-permute-done.3.refs_3_ = f32[32,4096]{1,0:T(8,128)S(1)} collective-permute-done((f32[32,4096]{1,0:T(8,128)}, f32[32,4096]{1,0:T(8,128)S(1)}, u32[]{:S(2)}, u32[]{:S(2)}) %collective-permute-start.3) | collective-permute-done | bytes 524320 | tf_op jit(solution)/shard_map/ppermute | solution.py:323
  31.5 0.2 pad_maximum_fusion.7
  31.7 0.1 collective-permute-start.13
  31.8 3.2 %collective-permute-start.14 = (f32[64,2048]{1,0:T(8,128)S(1)}, f32[64,2048]{1,0:T(8,128)S(1)}, u32[]{:S(2)}, u32[]{:S(2)}) collective-permute-start(f32[64,2048]{1,0:T(8,128)S(1)} %get-tuple-element.36), channel_id=1, source_target_pairs={{0,6},{1,7},{2,0},{3,1},{4,2},{5,3},{6,4},{7,5},{8,14},{9,15},{10,... | collective-permute-start | bytes 1572872 | tf_op jit(solution)/shard_map/ppermute | solution.py:323
  35.0 3.4 %collective-permute-done.6.refs_6_ = f32[32,4096]{1,0:T(8,128)S(1)} collective-permute-done((f32[32,4096]{1,0:T(8,128)S(1)}, f32[32,4096]{1,0:T(8,128)S(1)}, u32[]{:S(2)}, u32[]{:S(2)}) %collective-permute-start.6) | collective-permute-done | bytes 524320 | tf_op jit(solution)/shard_map/ppermute | solution.py:323
  38.4 3.1 %collective-permute-start.15 = (f32[64,2048]{1,0:T(8,128)S(1)}, f32[64,2048]{1,0:T(8,128)S(1)}, u32[]{:S(2)}, u32[]{:S(2)}) collective-permute-start(f32[64,2048]{1,0:T(8,128)S(1)} %get-tuple-element.35), channel_id=1, source_target_pairs={{0,8},{1,9},{2,10},{3,11},{4,12},{5,13},{6,14},{7,15},{8,0},{9,1},... | collective-permute-start | bytes 1572872 | tf_op jit(solution)/shard_map/ppermute | solution.py:323
  41.5 0.0 collective-permute-done.4.refs_4_
  41.5 0.0 copy-start.6
  41.5 1.2 collective-permute-done.2.refs_2_
  42.7 0.2 pad_maximum_fusion.6
  42.9 0.9 collective-permute-start.8
  43.8 2.4 %collective-permute-start.9 = (f32[64,2048]{1,0:T(8,128)S(1)}, f32[64,2048]{1,0:T(8,128)S(1)}, u32[]{:S(2)}, u32[]{:S(2)}) collective-permute-start(f32[64,2048]{1,0:T(8,128)S(1)} %get-tuple-element.39), channel_id=1, source_target_pairs={{0,6},{1,7},{2,0},{3,1},{4,2},{5,3},{6,4},{7,5},{8,14},{9,15},{10,... | collective-permute-start | bytes 1572872 | tf_op jit(solution)/shard_map/ppermute | solution.py:323
  46.2 7.7 %collective-permute-done.13.refs_13_ = f32[64,2048]{1,0:T(8,128)S(1)} collective-permute-done((f32[64,2048]{1,0:T(8,128)S(1)}, f32[64,2048]{1,0:T(8,128)S(1)}, u32[]{:S(2)}, u32[]{:S(2)}) %collective-permute-start.13) | collective-permute-done | bytes 524320 | tf_op jit(solution)/shard_map/ppermute | solution.py:323
  53.9 0.5 collective-permute-start.10
  54.4 6.2 %gram_near.1.refs_20_ = f32[2,640,128]{2,1,0:T(8,128)S(1)} custom-call(s32[9]{0:T(128)S(1)} %stack.39.where_ref, f32[32,4096]{1,0:T(8,128)S(1)} %pad_maximum_fusion.4.refs_0_, f32[32,4096]{1,0:T(8,128)} %collective-permute-done.refs_1_, f32[32,4096]{1,0:T(8,128)S(1)} %collective-permute-done.2.refs_2_, f32[32,4096]{1,0:T(8,128)S(1)} %collective-permute-done.3.refs_3_, ...), custom_call_target="tpu_custom_call" | custom-call | flops 16106127360 | bytes 8388608 | tf_op jit(solution)/shard_map/gram_near/pallas_call | solution.py:393
  60.6 0.0 collective-permute-done.14.refs_14_
  60.7 0.1 collective-permute-start.16
  60.8 4.4 %collective-permute-done.8.refs_8_ = f32[64,2048]{1,0:T(8,128)S(1)} collective-permute-done((f32[64,2048]{1,0:T(8,128)S(1)}, f32[64,2048]{1,0:T(8,128)S(1)}, u32[]{:S(2)}, u32[]{:S(2)}) %collective-permute-start.8) | collective-permute-done | bytes 524320 | tf_op jit(solution)/shard_map/ppermute | solution.py:323
  65.2 0.0 collective-permute-start.17
  65.2 0.0 collective-permute-done.9.refs_9_
  65.2 0.0 copy-start.11
  65.2 0.1 collective-permute-start.11
  65.3 0.0 collective-permute-done.15.refs_15_
  65.4 3.6 %collective-permute-start.12 = (f32[32,2048]{1,0:T(8,128)S(1)}, f32[32,2048]{1,0:T(8,128)S(1)}, u32[]{:S(2)}, u32[]{:S(2)}) collective-permute-start(f32[32,2048]{1,0:T(8,128)S(1)} %slice.45), channel_id=1, source_target_pairs={{0,8},{1,9},{2,10},{3,11},{4,12},{5,13},{6,14},{7,15},{8,0},{9,1},... | collective-permute-start | bytes 786440 | tf_op jit(solution)/shard_map/ppermute | solution.py:323
  68.9 0.0 collective-permute-done.10.refs_10_
  68.9 2.3 %collective-permute-done.16.refs_16_ = f32[32,2048]{1,0:T(8,128)S(1)} collective-permute-done((f32[32,2048]{1,0:T(8,128)S(1)}, f32[32,2048]{1,0:T(8,128)S(1)}, u32[]{:S(2)}, u32[]{:S(2)}) %collective-permute-start.16) | collective-permute-done | bytes 262176 | tf_op jit(solution)/shard_map/ppermute | solution.py:323
  71.2 3.7 %collective-permute-done.17.refs_17_ = f32[32,2048]{1,0:T(8,128)S(1)} collective-permute-done((f32[32,2048]{1,0:T(8,128)S(1)}, f32[32,2048]{1,0:T(8,128)S(1)}, u32[]{:S(2)}, u32[]{:S(2)}) %collective-permute-start.17) | collective-permute-done | bytes 262176 | tf_op jit(solution)/shard_map/ppermute | solution.py:323
  74.9 0.0 collective-permute-done.11.refs_11_
  75.0 2.8 %collective-permute-done.12.refs_12_ = f32[32,2048]{1,0:T(8,128)S(1)} collective-permute-done((f32[32,2048]{1,0:T(8,128)S(1)}, f32[32,2048]{1,0:T(8,128)S(1)}, u32[]{:S(2)}, u32[]{:S(2)}) %collective-permute-start.12) | collective-permute-done | bytes 262176 | tf_op jit(solution)/shard_map/ppermute | solution.py:323
  77.7 0.0 copy-done.2
  77.7 0.0 copy-done.7
  77.8 0.0 copy-done.6
  77.8 0.0 copy-done.3
  77.8 9.0 %gram_far.1 = (f32[1152,128]{1,0:T(8,128)S(1)}, f32[1152,128]{1,0:T(8,128)S(1)}) custom-call(s32[9]{0:T(128)S(1)} %stack.39.where_ref, f32[32,4096]{1,0:T(8,128)S(1)} %pad_maximum_fusion.4.refs_0_, f32[32,4096]{1,0:T(8,128)} %collective-permute-done.refs_1_, f32[32,4096]{1,0:T(8,128)S(1)} %collective-permute-done.2.refs_2_, ...), custom_call_target="tpu_custom_call" | custom-call | flops 25769803776 | bytes 12582912 | tf_op jit(solution)/shard_map/gram_far/pallas_call | solution.py:393
  86.9 0.1 collective-permute-start.18
  87.0 2.0 %collective-permute-done.18 = f32[1152,128]{1,0:T(8,128)S(1)} collective-permute-done((f32[1152,128]{1,0:T(8,128)S(1)}, f32[1152,128]{1,0:T(8,128)S(1)}, u32[]{:S(2)}, u32[]{:S(2)}) %collective-permute-start.18) | collective-permute-done | bytes 589856 | tf_op jit(solution)/shard_map/ppermute | solution.py:323
  89.0 0.1 add.93
  89.1 15.5 %all_to_all.10 = f32[8,144,128]{2,1,0:T(8,128)S(1)} all-to-all(f32[8,144,128]{2,1,0:T(8,128)S(1)} %bitcast.21), channel_id=1, replica_groups=mesh['row'=8,'col'=16] {'row'}, dimensions={0} | all-to-all | bytes 1179648 | tf_op jit(solution)/shard_map/all_to_all | solution.py:433
  104.7 13.0 %all_to_all.11 = f32[8,144,128]{2,1,0:T(8,128)S(1)} all-to-all(f32[8,144,128]{2,1,0:T(8,128)S(1)} %broadcast_in_dim.10), channel_id=1, replica_groups=mesh['row'=8,'col'=16] {'row'}, dimensions={0} | all-to-all | bytes 1179648 | tf_op jit(solution)/shard_map/all_to_all | solution.py:436
  117.7 0.0 collective-permute-start.19
  117.7 2.0 %collective-permute-done.19.refs_21_ = f32[1152,128]{1,0:T(8,128)S(1)} collective-permute-done((f32[1152,128]{1,0:T(8,128)S(1)}, f32[1152,128]{1,0:T(8,128)S(1)}, u32[]{:S(2)}, u32[]{:S(2)}) %collective-permute-start.19) | collective-permute-done | bytes 589856 | tf_op jit(solution)/shard_map/ppermute | solution.py:323
  119.7 12.2 %solve_apply.1 = (f32[4096,128]{1,0:T(8,128)S(1)}, f32[4096,128]{1,0:T(8,128)S(1)}) custom-call(s32[9]{0:T(128)S(1)} %stack.39.where_ref, f32[32,4096]{1,0:T(8,128)} %copy-done.1, f32[32,4096]{1,0:T(8,128)} %collective-permute-done.refs_1_, f32[32,4096]{1,0:T(8,128)} %copy-done.3, f32[32,4096]{1,0:T(8,128)} %copy-done.2, f32[32,4096]{1,0:T(8,128)} %copy-done.6, ...), custom_call_target="tpu_custom_call" | custom-call | tf_op jit(solution)/shard_map/solve_apply/pallas_call | solution.py:442
  131.8 0.2 collective-permute-start.20
  132.0 0.3 broadcast_in_dim.4
  132.3 0.2 constant_dynamic-update-slice_fusion.1
  132.5 0.0 copy-start.18
  132.5 3.5 %collective-permute-done.20 = f32[4096,128]{1,0:T(8,128)S(1)} collective-permute-done((f32[4096,128]{1,0:T(8,128)S(1)}, f32[4096,128]{1,0:T(8,128)S(1)}, u32[]{:S(2)}, u32[]{:S(2)}) %collective-permute-start.20) | collective-permute-done | bytes 2097184 | tf_op jit(solution)/shard_map/ppermute | solution.py:323
  136.1 1.5 %constant_dynamic-update-slice_fusion = f32[8192,128]{1,0:T(8,128)} fusion(f32[8192,128]{1,0:T(8,128)} %copy-done.18, f32[4096,128]{1,0:T(8,128)S(1)} %collective-permute-done.20, s32[]{:T(128)S(6)} %select_n.61), kind=kLoop, calls=%fused_computation.12 | loop fusion | bytes 4194308 | tf_op jit(solution)/shard_map/dynamic_update_slice | solution.py:468
  (43 shorter events, 0.4 us)
Async XLA Ops:
  0.0 8.0 %collective-permute-start.1 = (f32[8192,128]{1,0:T(8,128)}, f32[8192,128]{1,0:T(8,128)}, u32[]{:S(2)}, u32[]{:S(2)}) collective-permute-start(f32[8192,128]{1,0:T(8,128)} %refs_18_.3), channel_id=1, source_target_pairs={{0,1},{1,0},{2,3},{3,2},{4,5},{5,4},{6,7},{7,6},{8,9},{9,8},{10,11... | collective-permute-start | bytes 12582920 | tf_op jit(solution)/shard_map/ppermute | solution.py:323
  1.3 6.7 %collective-permute-start = (f32[32,4096]{1,0:T(8,128)S(1)}, f32[32,4096]{1,0:T(8,128)}, u32[]{:S(2)}, u32[]{:S(2)}) collective-permute-start(f32[32,4096]{1,0:T(8,128)S(1)} %pad_maximum_fusion.5), channel_id=1, source_target_pairs={{0,1},{1,0},{2,3},{3,2},{4,5},{5,4},{6,7},{7,6},{8,9},{9,8},{10,11... | collective-permute-start | bytes 1572872 | tf_op jit(solution)/shard_map/ppermute | solution.py:323
  1.9 75.8 %copy-start.1 = (f32[32,4096]{1,0:T(8,128)}, f32[32,4096]{1,0:T(8,128)S(1)}, u32[]{:S(2)}) copy-start(f32[32,4096]{1,0:T(8,128)S(1)} %pad_maximum_fusion.4.refs_0_) | copy-start | bytes 1572868
  8.0 15.7 %collective-permute-start.7 = (f32[32,4096]{1,0:T(8,128)}, f32[32,4096]{1,0:T(8,128)S(1)}, u32[]{:S(2)}, u32[]{:S(2)}) collective-permute-start(f32[32,4096]{1,0:T(8,128)} %collective-permute-done.refs_1_), channel_id=1, source_target_pairs={{0,8},{1,9},{2,10},{3,11},{4,12},{5,13},{6,14},{7,15},{8,0},{9,1},... | collective-permute-start | bytes 1572872 | tf_op jit(solution)/shard_map/ppermute | solution.py:323
  11.2 16.7 %collective-permute-start.5 = (f32[32,4096]{1,0:T(8,128)}, f32[32,4096]{1,0:T(8,128)S(1)}, u32[]{:S(2)}, u32[]{:S(2)}) collective-permute-start(f32[32,4096]{1,0:T(8,128)} %collective-permute-done.refs_1_), channel_id=1, source_target_pairs={{0,6},{1,7},{2,0},{3,1},{4,2},{5,3},{6,4},{7,5},{8,14},{9,15},{10,... | collective-permute-start | bytes 1572872 | tf_op jit(solution)/shard_map/ppermute | solution.py:323
  15.2 16.3 %collective-permute-start.3 = (f32[32,4096]{1,0:T(8,128)}, f32[32,4096]{1,0:T(8,128)S(1)}, u32[]{:S(2)}, u32[]{:S(2)}) collective-permute-start(f32[32,4096]{1,0:T(8,128)} %collective-permute-done.refs_1_), channel_id=1, source_target_pairs={{0,2},{1,3},{2,4},{3,5},{4,6},{5,7},{6,0},{7,1},{8,10},{9,11},{10,... | collective-permute-start | bytes 1572872 | tf_op jit(solution)/shard_map/ppermute | solution.py:323
  15.3 27.4 %collective-permute-start.2 = (f32[32,4096]{1,0:T(8,128)S(1)}, f32[32,4096]{1,0:T(8,128)S(1)}, u32[]{:S(2)}, u32[]{:S(2)}) collective-permute-start(f32[32,4096]{1,0:T(8,128)S(1)} %pad_maximum_fusion.4.refs_0_), channel_id=1, source_target_pairs={{0,2},{1,3},{2,4},{3,5},{4,6},{5,7},{6,0},{7,1},{8,10},{9,11},{10,... | collective-permute-start | bytes 1572872 | tf_op jit(solution)/shard_map/ppermute | solution.py:323
  15.3 26.2 %collective-permute-start.4 = (f32[32,4096]{1,0:T(8,128)S(1)}, f32[32,4096]{1,0:T(8,128)S(1)}, u32[]{:S(2)}, u32[]{:S(2)}) collective-permute-start(f32[32,4096]{1,0:T(8,128)S(1)} %pad_maximum_fusion.4.refs_0_), channel_id=1, source_target_pairs={{0,6},{1,7},{2,0},{3,1},{4,2},{5,3},{6,4},{7,5},{8,14},{9,15},{10,... | collective-permute-start | bytes 1572872 | tf_op jit(solution)/shard_map/ppermute | solution.py:323
  23.7 54.0 %copy-start.4 = (f32[32,4096]{1,0:T(8,128)}, f32[32,4096]{1,0:T(8,128)S(1)}, u32[]{:S(2)}) copy-start(f32[32,4096]{1,0:T(8,128)S(1)} %collective-permute-done.7.refs_7_) | copy-start | bytes 1572868
  23.7 14.6 %collective-permute-start.6 = (f32[32,4096]{1,0:T(8,128)S(1)}, f32[32,4096]{1,0:T(8,128)S(1)}, u32[]{:S(2)}, u32[]{:S(2)}) collective-permute-start(f32[32,4096]{1,0:T(8,128)S(1)} %pad_maximum_fusion.4.refs_0_), channel_id=1, source_target_pairs={{0,8},{1,9},{2,10},{3,11},{4,12},{5,13},{6,14},{7,15},{8,0},{9,1},... | collective-permute-start | bytes 1572872 | tf_op jit(solution)/shard_map/ppermute | solution.py:323
  27.8 49.9 %copy-start.5 = (f32[32,4096]{1,0:T(8,128)}, f32[32,4096]{1,0:T(8,128)S(1)}, u32[]{:S(2)}) copy-start(f32[32,4096]{1,0:T(8,128)S(1)} %collective-permute-done.5.refs_5_) | copy-start | bytes 1572868
  27.9 26.6 %copy-start = (f32[8192,128]{1,0:T(8,128)S(1)}, f32[8192,128]{1,0:T(8,128)}, u32[]{:S(2)}) copy-start(f32[8192,128]{1,0:T(8,128)} %refs_18_.3) | copy-start | bytes 12582916
  31.5 46.3 %copy-start.2 = (f32[32,4096]{1,0:T(8,128)}, f32[32,4096]{1,0:T(8,128)S(1)}, u32[]{:S(2)}) copy-start(f32[32,4096]{1,0:T(8,128)S(1)} %collective-permute-done.3.refs_3_) | copy-start | bytes 1572868
  31.7 22.2 %collective-permute-start.13 = (f32[64,2048]{1,0:T(8,128)S(1)}, f32[64,2048]{1,0:T(8,128)S(1)}, u32[]{:S(2)}, u32[]{:S(2)}) collective-permute-start(f32[64,2048]{1,0:T(8,128)S(1)} %get-tuple-element.37), channel_id=1, source_target_pairs={{0,2},{1,3},{2,4},{3,5},{4,6},{5,7},{6,0},{7,1},{8,10},{9,11},{10,... | collective-permute-start | bytes 1572872 | tf_op jit(solution)/shard_map/ppermute | solution.py:323
  31.8 28.9 %collective-permute-start.14 = (f32[64,2048]{1,0:T(8,128)S(1)}, f32[64,2048]{1,0:T(8,128)S(1)}, u32[]{:S(2)}, u32[]{:S(2)}) collective-permute-start(f32[64,2048]{1,0:T(8,128)S(1)} %get-tuple-element.36), channel_id=1, source_target_pairs={{0,6},{1,7},{2,0},{3,1},{4,2},{5,3},{6,4},{7,5},{8,14},{9,15},{10,... | collective-permute-start | bytes 1572872 | tf_op jit(solution)/shard_map/ppermute | solution.py:323
  38.4 39.4 %copy-start.7 = (f32[32,4096]{1,0:T(8,128)}, f32[32,4096]{1,0:T(8,128)S(1)}, u32[]{:S(2)}) copy-start(f32[32,4096]{1,0:T(8,128)S(1)} %collective-permute-done.6.refs_6_) | copy-start | bytes 1572868
  38.4 27.0 %collective-permute-start.15 = (f32[64,2048]{1,0:T(8,128)S(1)}, f32[64,2048]{1,0:T(8,128)S(1)}, u32[]{:S(2)}, u32[]{:S(2)}) collective-permute-start(f32[64,2048]{1,0:T(8,128)S(1)} %get-tuple-element.35), channel_id=1, source_target_pairs={{0,8},{1,9},{2,10},{3,11},{4,12},{5,13},{6,14},{7,15},{8,0},{9,1},... | collective-permute-start | bytes 1572872 | tf_op jit(solution)/shard_map/ppermute | solution.py:323
  41.5 36.2 %copy-start.6 = (f32[32,4096]{1,0:T(8,128)}, f32[32,4096]{1,0:T(8,128)S(1)}, u32[]{:S(2)}) copy-start(f32[32,4096]{1,0:T(8,128)S(1)} %collective-permute-done.4.refs_4_) | copy-start | bytes 1572868
  42.7 35.1 %copy-start.3 = (f32[32,4096]{1,0:T(8,128)}, f32[32,4096]{1,0:T(8,128)S(1)}, u32[]{:S(2)}) copy-start(f32[32,4096]{1,0:T(8,128)S(1)} %collective-permute-done.2.refs_2_) | copy-start | bytes 1572868
  42.9 22.3 %collective-permute-start.8 = (f32[64,2048]{1,0:T(8,128)S(1)}, f32[64,2048]{1,0:T(8,128)S(1)}, u32[]{:S(2)}, u32[]{:S(2)}) collective-permute-start(f32[64,2048]{1,0:T(8,128)S(1)} %get-tuple-element.40), channel_id=1, source_target_pairs={{0,2},{1,3},{2,4},{3,5},{4,6},{5,7},{6,0},{7,1},{8,10},{9,11},{10,... | collective-permute-start | bytes 1572872 | tf_op jit(solution)/shard_map/ppermute | solution.py:323
  43.8 21.4 %collective-permute-start.9 = (f32[64,2048]{1,0:T(8,128)S(1)}, f32[64,2048]{1,0:T(8,128)S(1)}, u32[]{:S(2)}, u32[]{:S(2)}) collective-permute-start(f32[64,2048]{1,0:T(8,128)S(1)} %get-tuple-element.39), channel_id=1, source_target_pairs={{0,6},{1,7},{2,0},{3,1},{4,2},{5,3},{6,4},{7,5},{8,14},{9,15},{10,... | collective-permute-start | bytes 1572872 | tf_op jit(solution)/shard_map/ppermute | solution.py:323
  53.9 23.8 %copy-start.8 = (f32[64,2048]{1,0:T(8,128)}, f32[64,2048]{1,0:T(8,128)S(1)}, u32[]{:S(2)}) copy-start(f32[64,2048]{1,0:T(8,128)S(1)} %collective-permute-done.13.refs_13_) | copy-start | bytes 1572868
  53.9 15.0 %collective-permute-start.10 = (f32[64,2048]{1,0:T(8,128)S(1)}, f32[64,2048]{1,0:T(8,128)S(1)}, u32[]{:S(2)}, u32[]{:S(2)}) collective-permute-start(f32[64,2048]{1,0:T(8,128)S(1)} %get-tuple-element.38), channel_id=1, source_target_pairs={{0,8},{1,9},{2,10},{3,11},{4,12},{5,13},{6,14},{7,15},{8,0},{9,1},... | collective-permute-start | bytes 1572872 | tf_op jit(solution)/shard_map/ppermute | solution.py:323
  60.6 26.2 %copy-start.9 = (f32[64,2048]{1,0:T(8,128)}, f32[64,2048]{1,0:T(8,128)S(1)}, u32[]{:S(2)}) copy-start(f32[64,2048]{1,0:T(8,128)S(1)} %collective-permute-done.14.refs_14_) | copy-start | bytes 1572868
  60.7 10.5 %collective-permute-start.16 = (f32[32,2048]{1,0:T(8,128)S(1)}, f32[32,2048]{1,0:T(8,128)S(1)}, u32[]{:S(2)}, u32[]{:S(2)}) collective-permute-start(f32[32,2048]{1,0:T(8,128)S(1)} %slice.50), channel_id=1, source_target_pairs={{0,2},{1,3},{2,4},{3,5},{4,6},{5,7},{6,0},{7,1},{8,10},{9,11},{10,... | collective-permute-start | bytes 786440 | tf_op jit(solution)/shard_map/ppermute | solution.py:323
  65.2 21.7 %copy-start.10 = (f32[64,2048]{1,0:T(8,128)}, f32[64,2048]{1,0:T(8,128)S(1)}, u32[]{:S(2)}) copy-start(f32[64,2048]{1,0:T(8,128)S(1)} %collective-permute-done.8.refs_8_) | copy-start | bytes 1572868
  65.2 9.7 %collective-permute-start.17 = (f32[32,2048]{1,0:T(8,128)S(1)}, f32[32,2048]{1,0:T(8,128)S(1)}, u32[]{:S(2)}, u32[]{:S(2)}) collective-permute-start(f32[32,2048]{1,0:T(8,128)S(1)} %slice.51), channel_id=1, source_target_pairs={{0,8},{1,9},{2,10},{3,11},{4,12},{5,13},{6,14},{7,15},{8,0},{9,1},... | collective-permute-start | bytes 786440 | tf_op jit(solution)/shard_map/ppermute | solution.py:323
  65.2 21.7 %copy-start.11 = (f32[64,2048]{1,0:T(8,128)}, f32[64,2048]{1,0:T(8,128)S(1)}, u32[]{:S(2)}) copy-start(f32[64,2048]{1,0:T(8,128)S(1)} %collective-permute-done.9.refs_9_) | copy-start | bytes 1572868
  65.2 9.7 %collective-permute-start.11 = (f32[32,2048]{1,0:T(8,128)S(1)}, f32[32,2048]{1,0:T(8,128)S(1)}, u32[]{:S(2)}, u32[]{:S(2)}) collective-permute-start(f32[32,2048]{1,0:T(8,128)S(1)} %slice.44), channel_id=1, source_target_pairs={{0,2},{1,3},{2,4},{3,5},{4,6},{5,7},{6,0},{7,1},{8,10},{9,11},{10,... | collective-permute-start | bytes 786440 | tf_op jit(solution)/shard_map/ppermute | solution.py:323
  65.3 21.5 %copy-start.12 = (f32[64,2048]{1,0:T(8,128)}, f32[64,2048]{1,0:T(8,128)S(1)}, u32[]{:S(2)}) copy-start(f32[64,2048]{1,0:T(8,128)S(1)} %collective-permute-done.15.refs_15_) | copy-start | bytes 1572868
  65.4 12.4 %collective-permute-start.12 = (f32[32,2048]{1,0:T(8,128)S(1)}, f32[32,2048]{1,0:T(8,128)S(1)}, u32[]{:S(2)}, u32[]{:S(2)}) collective-permute-start(f32[32,2048]{1,0:T(8,128)S(1)} %slice.45), channel_id=1, source_target_pairs={{0,8},{1,9},{2,10},{3,11},{4,12},{5,13},{6,14},{7,15},{8,0},{9,1},... | collective-permute-start | bytes 786440 | tf_op jit(solution)/shard_map/ppermute | solution.py:323
  68.9 17.9 %copy-start.13 = (f32[64,2048]{1,0:T(8,128)}, f32[64,2048]{1,0:T(8,128)S(1)}, u32[]{:S(2)}) copy-start(f32[64,2048]{1,0:T(8,128)S(1)} %collective-permute-done.10.refs_10_) | copy-start | bytes 1572868
  71.2 15.7 %copy-start.14 = (f32[32,2048]{1,0:T(8,128)}, f32[32,2048]{1,0:T(8,128)S(1)}, u32[]{:S(2)}) copy-start(f32[32,2048]{1,0:T(8,128)S(1)} %collective-permute-done.16.refs_16_) | copy-start | bytes 786436
  74.9 12.0 %copy-start.15 = (f32[32,2048]{1,0:T(8,128)}, f32[32,2048]{1,0:T(8,128)S(1)}, u32[]{:S(2)}) copy-start(f32[32,2048]{1,0:T(8,128)S(1)} %collective-permute-done.17.refs_17_) | copy-start | bytes 786436
  75.0 11.9 %copy-start.16 = (f32[32,2048]{1,0:T(8,128)}, f32[32,2048]{1,0:T(8,128)S(1)}, u32[]{:S(2)}) copy-start(f32[32,2048]{1,0:T(8,128)S(1)} %collective-permute-done.11.refs_11_) | copy-start | bytes 786436
  77.8 9.1 %copy-start.17 = (f32[32,2048]{1,0:T(8,128)}, f32[32,2048]{1,0:T(8,128)S(1)}, u32[]{:S(2)}) copy-start(f32[32,2048]{1,0:T(8,128)S(1)} %collective-permute-done.12.refs_12_) | copy-start | bytes 786436
  86.9 2.1 %collective-permute-start.18 = (f32[1152,128]{1,0:T(8,128)S(1)}, f32[1152,128]{1,0:T(8,128)S(1)}, u32[]{:S(2)}, u32[]{:S(2)}) collective-permute-start(f32[1152,128]{1,0:T(8,128)S(1)} %get-tuple-element.24), channel_id=1, source_target_pairs={{0,1},{1,0},{2,3},{3,2},{4,5},{5,4},{6,7},{7,6},{8,9},{9,8},{10,11... | collective-permute-start | bytes 1769480 | tf_op jit(solution)/shard_map/ppermute | solution.py:323
  117.7 2.0 %collective-permute-start.19 = (f32[1152,128]{1,0:T(8,128)S(1)}, f32[1152,128]{1,0:T(8,128)S(1)}, u32[]{:S(2)}, u32[]{:S(2)}) collective-permute-start(f32[1152,128]{1,0:T(8,128)S(1)} %bitcast.19), channel_id=1, source_target_pairs={{0,1},{1,0},{2,3},{3,2},{4,5},{5,4},{6,7},{7,6},{8,9},{9,8},{10,11... | collective-permute-start | bytes 1769480 | tf_op jit(solution)/shard_map/ppermute | solution.py:323
  131.8 4.2 %collective-permute-start.20 = (f32[4096,128]{1,0:T(8,128)S(1)}, f32[4096,128]{1,0:T(8,128)S(1)}, u32[]{:S(2)}, u32[]{:S(2)}) collective-permute-start(f32[4096,128]{1,0:T(8,128)S(1)} %get-tuple-element.26), channel_id=1, source_target_pairs={{0,1},{1,0},{2,3},{3,2},{4,5},{5,4},{6,7},{7,6},{8,9},{9,8},{10,11... | collective-permute-start | bytes 6291464 | tf_op jit(solution)/shard_map/ppermute | solution.py:323
  132.5 3.6 %copy-start.18 = (f32[8192,128]{1,0:T(8,128)}, f32[8192,128]{1,0:T(8,128)S(1)}, u32[]{:S(2)}) copy-start(f32[8192,128]{1,0:T(8,128)S(1)} %constant_dynamic-update-slice_fusion.1) | copy-start | bytes 12582916

commit v11 on v9

--- a/solution.py
+++ b/solution.py
@@ -13,8 +13,8 @@
 PLANES, DEPTH, CORES = 2, 4, 2
 CHIPS = PLANES * DEPTH
 WIDE = 128
-TILE = 1024
-LIMIT = 24 << 20
+TILE = 2048
+LIMIT = 32 << 20
 PIECES = ((0, 0), (0, 1), (1, 1), (0, 2), (0, 3)), ((1, 2), (1, 3), (2, 2), (2, 3), (3, 3))
 
 

time: 133 us -> 133 us (level)
  no operation moved by 1% of the time
where the time goes in v11:
time: 133 us; the launch traced here: 131 us
  waiting for transfers between devices  42.4 us (32%)
  blocking collectives  29.2 us (22%)
  Pallas kernels  26.5 us (20%)
  starting transfers between devices  24.7 us (19%)
  local copies, waits for them, and re-layouts  7.75 us (6%)
    ppermute x16, waiting for transfers between devices, permute(): return lax.ppermute(value, 'col', pairs)  42.4 us
    ppermute x16, starting transfers between devices, permute(): return lax.ppermute(value, 'col', pairs)  24.7 us
    all_to_all x1, blocking collectives, per_device(): lax.all_to_all(mine.reshape(members, length // members, WIDE), 'row', 0, 0)  16.2 us
    pallas_call x2, Pallas kernels, gram(): pl.pallas_call(functools.partial(gram_kernel, first=first), out_shape=sha...  14.4 us
    all_to_all x1, blocking collectives, per_device(): mine = lax.all_to_all(spread, 'row', 0, 0).reshape(length, WIDE)  13 us
    pallas_call x1, Pallas kernels, per_device(): pl.pallas_call(apply_kernel, out_shape=[jax.ShapeDtypeStruct((half, colum...  12.1 us
    unnamed x36, local copies, waits for them, and re-layouts  4.22 us
  transfers between devices with their start and end apart: 16, of which 10 were waited for; matrix products, arithmetic and copies ran while one was open for 2% of the time, Pallas kernels for 5%

profile of v11, /device:TPU:0, one launch (start us, length us, event | category | flops | bytes accessed | tf_op | source)
XLA Modules:
  0.0 131.3 jit_solution(4351028043612770773)
XLA Ops:
  0.0 0.0 collective-permute-start.1
  0.0 1.3 dynamic-slice_bitcast_fusion
  1.3 0.6 collective-permute-start
  1.9 0.0 copy-start.3
  1.9 2.1 %collective-permute-start.2 = (f32[32,4096]{1,0:T(8,128)S(1)}, f32[32,4096]{1,0:T(8,128)S(1)}, u32[]{:S(2)}, u32[]{:S(2)}) collective-permute-start(f32[32,4096]{1,0:T(8,128)S(1)} %pad_maximum_fusion.5.refs_0_), channel_id=1, source_target_pairs={{0,2},{1,3},{2,4},{3,5},{4,6},{5,7},{6,0},{7,1},{8,10},{9,11},{10,... | collective-permute-start | bytes 1572872 | tf_op jit(solution)/shard_map/ppermute | solution.py:322
  4.0 3.0 %collective-permute-start.6 = (f32[32,4096]{1,0:T(8,128)S(1)}, f32[32,4096]{1,0:T(8,128)S(1)}, u32[]{:S(2)}, u32[]{:S(2)}) collective-permute-start(f32[32,4096]{1,0:T(8,128)S(1)} %pad_maximum_fusion.5.refs_0_), channel_id=1, source_target_pairs={{0,8},{1,9},{2,10},{3,11},{4,12},{5,13},{6,14},{7,15},{8,0},{9,1},... | collective-permute-start | bytes 1572872 | tf_op jit(solution)/shard_map/ppermute | solution.py:322
  7.0 2.2 %collective-permute-start.4 = (f32[32,4096]{1,0:T(8,128)S(1)}, f32[32,4096]{1,0:T(8,128)S(1)}, u32[]{:S(2)}, u32[]{:S(2)}) collective-permute-start(f32[32,4096]{1,0:T(8,128)S(1)} %pad_maximum_fusion.5.refs_0_), channel_id=1, source_target_pairs={{0,6},{1,7},{2,0},{3,1},{4,2},{5,3},{6,4},{7,5},{8,14},{9,15},{10,... | collective-permute-start | bytes 1572872 | tf_op jit(solution)/shard_map/ppermute | solution.py:322
  9.3 0.0 collective-permute-done.refs_1_
  9.3 0.0 collective-permute-done.1.refs_9_.refs_14_
  9.3 1.9 %collective-permute-start.7 = (f32[32,4096]{1,0:T(8,128)}, f32[32,4096]{1,0:T(8,128)S(1)}, u32[]{:S(2)}, u32[]{:S(2)}) collective-permute-start(f32[32,4096]{1,0:T(8,128)} %collective-permute-done.refs_1_), channel_id=1, source_target_pairs={{0,8},{1,9},{2,10},{3,11},{4,12},{5,13},{6,14},{7,15},{8,0},{9,1},... | collective-permute-start | bytes 1572872 | tf_op jit(solution)/shard_map/ppermute | solution.py:322
  11.2 1.9 %collective-permute-start.3 = (f32[32,4096]{1,0:T(8,128)}, f32[32,4096]{1,0:T(8,128)S(1)}, u32[]{:S(2)}, u32[]{:S(2)}) collective-permute-start(f32[32,4096]{1,0:T(8,128)} %collective-permute-done.refs_1_), channel_id=1, source_target_pairs={{0,2},{1,3},{2,4},{3,5},{4,6},{5,7},{6,0},{7,1},{8,10},{9,11},{10,... | collective-permute-start | bytes 1572872 | tf_op jit(solution)/shard_map/ppermute | solution.py:322
  13.1 0.1 stack.39.where_ref
  13.2 5.7 %collective-permute-done.2.refs_2_ = f32[32,4096]{1,0:T(8,128)S(1)} collective-permute-done((f32[32,4096]{1,0:T(8,128)S(1)}, f32[32,4096]{1,0:T(8,128)S(1)}, u32[]{:S(2)}, u32[]{:S(2)}) %collective-permute-start.2) | collective-permute-done | bytes 524320 | tf_op jit(solution)/shard_map/ppermute | solution.py:322
  18.9 2.1 %collective-permute-start.5 = (f32[32,4096]{1,0:T(8,128)}, f32[32,4096]{1,0:T(8,128)S(1)}, u32[]{:S(2)}, u32[]{:S(2)}) collective-permute-start(f32[32,4096]{1,0:T(8,128)} %collective-permute-done.refs_1_), channel_id=1, source_target_pairs={{0,6},{1,7},{2,0},{3,1},{4,2},{5,3},{6,4},{7,5},{8,14},{9,15},{10,... | collective-permute-start | bytes 1572872 | tf_op jit(solution)/shard_map/ppermute | solution.py:322
  21.0 0.0 copy-start
  21.0 0.0 collective-permute-done.6.refs_6_
  21.0 0.0 copy-start.7
  21.0 0.1 collective-permute-done.4.refs_4_
  21.2 9.2 %collective-permute-done.7.refs_7_ = f32[32,4096]{1,0:T(8,128)S(1)} collective-permute-done((f32[32,4096]{1,0:T(8,128)}, f32[32,4096]{1,0:T(8,128)S(1)}, u32[]{:S(2)}, u32[]{:S(2)}) %collective-permute-start.7) | collective-permute-done | bytes 524320 | tf_op jit(solution)/shard_map/ppermute | solution.py:322
  30.4 0.0 collective-permute-done.3.refs_3_
  30.4 0.0 copy-start.5
  30.4 1.4 %collective-permute-done.5.refs_5_ = f32[32,4096]{1,0:T(8,128)S(1)} collective-permute-done((f32[32,4096]{1,0:T(8,128)}, f32[32,4096]{1,0:T(8,128)S(1)}, u32[]{:S(2)}, u32[]{:S(2)}) %collective-permute-start.5) | collective-permute-done | bytes 524320 | tf_op jit(solution)/shard_map/ppermute | solution.py:322
  31.8 0.4 pad_maximum_fusion.4
  32.2 0.0 copy-done.7
  32.2 0.0 copy-done.5
  32.2 1.8 %collective-permute-start.8 = (f32[128,2048]{1,0:T(8,128)S(1)}, f32[128,2048]{1,0:T(8,128)S(1)}, u32[]{:S(2)}, u32[]{:S(2)}) collective-permute-start(f32[128,2048]{1,0:T(8,128)S(1)} %get-tuple-element.25), channel_id=1, source_target_pairs={{0,2},{1,3},{2,4},{3,5},{4,6},{5,7},{6,0},{7,1},{8,10},{9,11},{10,... | collective-permute-start | bytes 3145736 | tf_op jit(solution)/shard_map/ppermute | solution.py:322
  34.0 0.0 copy-done.9
  34.0 0.0 copy-done.11
  34.0 1.9 %collective-permute-start.9 = (f32[128,2048]{1,0:T(8,128)S(1)}, f32[128,2048]{1,0:T(8,128)S(1)}, u32[]{:S(2)}, u32[]{:S(2)}) collective-permute-start(f32[128,2048]{1,0:T(8,128)S(1)} %get-tuple-element.24), channel_id=1, source_target_pairs={{0,6},{1,7},{2,0},{3,1},{4,2},{5,3},{6,4},{7,5},{8,14},{9,15},{10,... | collective-permute-start | bytes 3145736 | tf_op jit(solution)/shard_map/ppermute | solution.py:322
  35.9 2.7 %collective-permute-start.10 = (f32[128,2048]{1,0:T(8,128)S(1)}, f32[128,2048]{1,0:T(8,128)S(1)}, u32[]{:S(2)}, u32[]{:S(2)}) collective-permute-start(f32[128,2048]{1,0:T(8,128)S(1)} %get-tuple-element.23), channel_id=1, source_target_pairs={{0,8},{1,9},{2,10},{3,11},{4,12},{5,13},{6,14},{7,15},{8,0},{9,1},... | collective-permute-start | bytes 3145736 | tf_op jit(solution)/shard_map/ppermute | solution.py:322
  38.6 0.0 copy-done
  38.6 1.0 copy-done.6
  39.6 1.0 copy-done.8
  40.7 1.0 copy-done.10
  41.7 1.0 copy-done.12
  42.7 6.0 %gram_near.1.refs_15_ = f32[2,640,128]{2,1,0:T(8,128)S(1)} custom-call(s32[9]{0:T(128)S(1)} %stack.39.where_ref, f32[32,4096]{1,0:T(8,128)S(1)} %pad_maximum_fusion.5.refs_0_, f32[32,4096]{1,0:T(8,128)} %collective-permute-done.refs_1_, f32[32,4096]{1,0:T(8,128)S(1)} %collective-permute-done.2.refs_2_, f32[32,4096]{1,0:T(8,128)S(1)} %copy-done.6, ...), custom_call_target="tpu_custom_call" | custom-call | flops 16106127360 | bytes 8388608 | tf_op jit(solution)/shard_map/gram_near/pallas_call | solution.py:390
  48.8 8.5 %collective-permute-done.8.refs_8_ = f32[128,2048]{1,0:T(8,128)S(1)} collective-permute-done((f32[128,2048]{1,0:T(8,128)S(1)}, f32[128,2048]{1,0:T(8,128)S(1)}, u32[]{:S(2)}, u32[]{:S(2)}) %collective-permute-start.8) | collective-permute-done | bytes 1048608 | tf_op jit(solution)/shard_map/ppermute | solution.py:322
  57.3 0.0 collective-permute-done.9.refs_9_
  57.4 1.7 %collective-permute-start.11 = (f32[64,2048]{1,0:T(8,128)S(1)}, f32[64,2048]{1,0:T(8,128)S(1)}, u32[]{:S(2)}, u32[]{:S(2)}) collective-permute-start(f32[64,2048]{1,0:T(8,128)S(1)} %slice.42), channel_id=1, source_target_pairs={{0,2},{1,3},{2,4},{3,5},{4,6},{5,7},{6,0},{7,1},{8,10},{9,11},{10,... | collective-permute-start | bytes 1572872 | tf_op jit(solution)/shard_map/ppermute | solution.py:322
  59.1 2.6 %collective-permute-start.12 = (f32[64,2048]{1,0:T(8,128)S(1)}, f32[64,2048]{1,0:T(8,128)S(1)}, u32[]{:S(2)}, u32[]{:S(2)}) collective-permute-start(f32[64,2048]{1,0:T(8,128)S(1)} %slice.43), channel_id=1, source_target_pairs={{0,8},{1,9},{2,10},{3,11},{4,12},{5,13},{6,14},{7,15},{8,0},{9,1},... | collective-permute-start | bytes 1572872 | tf_op jit(solution)/shard_map/ppermute | solution.py:322
  61.7 0.0 collective-permute-done.10.refs_10_
  61.7 8.3 %collective-permute-done.11.refs_11_ = f32[64,2048]{1,0:T(8,128)S(1)} collective-permute-done((f32[64,2048]{1,0:T(8,128)S(1)}, f32[64,2048]{1,0:T(8,128)S(1)}, u32[]{:S(2)}, u32[]{:S(2)}) %collective-permute-start.11) | collective-permute-done | bytes 524320 | tf_op jit(solution)/shard_map/ppermute | solution.py:322
  70.0 1.6 %collective-permute-done.12.refs_12_ = f32[64,2048]{1,0:T(8,128)S(1)} collective-permute-done((f32[64,2048]{1,0:T(8,128)S(1)}, f32[64,2048]{1,0:T(8,128)S(1)}, u32[]{:S(2)}, u32[]{:S(2)}) %collective-permute-start.12) | collective-permute-done | bytes 524320 | tf_op jit(solution)/shard_map/ppermute | solution.py:322
  71.6 0.0 copy-done.3
  71.6 0.0 copy-done.4
  71.6 0.0 copy-done.13
  71.6 0.0 copy-start.16
  71.6 8.4 %gram_far.1 = (f32[1152,128]{1,0:T(8,128)S(1)}, f32[1152,128]{1,0:T(8,128)S(1)}) custom-call(s32[9]{0:T(128)S(1)} %stack.39.where_ref, f32[32,4096]{1,0:T(8,128)S(1)} %pad_maximum_fusion.5.refs_0_, f32[32,4096]{1,0:T(8,128)} %collective-permute-done.refs_1_, f32[32,4096]{1,0:T(8,128)S(1)} %collective-permute-done.2.refs_2_, f32[32,4096]{1,0:T(8,128)S(1)} %copy-done.6, ...), custom_call_target="tpu_custom_call" | custom-call | flops 25769803776 | bytes 12582912 | tf_op jit(solution)/shard_map/gram_far/pallas_call | solution.py:390
  80.0 0.0 copy-done.1
  80.1 0.0 copy-done.2
  80.1 0.1 collective-permute-start.13
  80.2 2.0 %collective-permute-done.13 = f32[1152,128]{1,0:T(8,128)S(1)} collective-permute-done((f32[1152,128]{1,0:T(8,128)S(1)}, f32[1152,128]{1,0:T(8,128)S(1)}, u32[]{:S(2)}, u32[]{:S(2)}) %collective-permute-start.13) | collective-permute-done | bytes 589856 | tf_op jit(solution)/shard_map/ppermute | solution.py:322
  82.2 0.1 add.93
  82.2 16.2 %all_to_all.10 = f32[8,144,128]{2,1,0:T(8,128)S(1)} all-to-all(f32[8,144,128]{2,1,0:T(8,128)S(1)} %bitcast.21), channel_id=1, replica_groups=mesh['row'=8,'col'=16] {'row'}, dimensions={0} | all-to-all | bytes 1179648 | tf_op jit(solution)/shard_map/all_to_all | solution.py:429
  98.5 13.0 %all_to_all.11 = f32[8,144,128]{2,1,0:T(8,128)S(1)} all-to-all(f32[8,144,128]{2,1,0:T(8,128)S(1)} %broadcast_in_dim.10), channel_id=1, replica_groups=mesh['row'=8,'col'=16] {'row'}, dimensions={0} | all-to-all | bytes 1179648 | tf_op jit(solution)/shard_map/all_to_all | solution.py:432
  111.5 0.0 collective-permute-start.14
  111.5 2.0 %collective-permute-done.14.refs_16_ = f32[1152,128]{1,0:T(8,128)S(1)} collective-permute-done((f32[1152,128]{1,0:T(8,128)S(1)}, f32[1152,128]{1,0:T(8,128)S(1)}, u32[]{:S(2)}, u32[]{:S(2)}) %collective-permute-start.14) | collective-permute-done | bytes 589856 | tf_op jit(solution)/shard_map/ppermute | solution.py:322
  113.5 12.1 %solve_apply.1 = (f32[4096,128]{1,0:T(8,128)S(1)}, f32[4096,128]{1,0:T(8,128)S(1)}) custom-call(s32[9]{0:T(128)S(1)} %stack.39.where_ref, f32[32,4096]{1,0:T(8,128)} %copy-done.3, f32[32,4096]{1,0:T(8,128)} %collective-permute-done.refs_1_, f32[32,4096]{1,0:T(8,128)} %copy-done.4, f32[32,4096]{1,0:T(8,128)} %copy-done.5, f32[32,4096]{1,0:T(8,128)} %copy-done.9, ...), custom_call_target="tpu_custom_call" | custom-call | tf_op jit(solution)/shard_map/solve_apply/pallas_call | solution.py:438
  125.6 0.2 collective-permute-start.15
  125.8 0.3 broadcast_in_dim.4
  126.1 0.2 constant_dynamic-update-slice_fusion.1
  126.3 0.0 copy-start.17
  126.3 3.5 %collective-permute-done.15 = f32[4096,128]{1,0:T(8,128)S(1)} collective-permute-done((f32[4096,128]{1,0:T(8,128)S(1)}, f32[4096,128]{1,0:T(8,128)S(1)}, u32[]{:S(2)}, u32[]{:S(2)}) %collective-permute-start.15) | collective-permute-done | bytes 2097184 | tf_op jit(solution)/shard_map/ppermute | solution.py:322
  129.8 1.5 %constant_dynamic-update-slice_fusion = f32[8192,128]{1,0:T(8,128)} fusion(f32[8192,128]{1,0:T(8,128)} %copy-done.17, f32[4096,128]{1,0:T(8,128)S(1)} %collective-permute-done.15, s32[]{:T(128)S(6)} %select_n.61), kind=kLoop, calls=%fused_computation.11 | loop fusion | bytes 4194308 | tf_op jit(solution)/shard_map/dynamic_update_slice | solution.py:464
  (28 shorter events, 0.4 us)
Async XLA Ops:
  0.0 9.3 %collective-permute-start.1 = (f32[8192,128]{1,0:T(8,128)}, f32[8192,128]{1,0:T(8,128)}, u32[]{:S(2)}, u32[]{:S(2)}) collective-permute-start(f32[8192,128]{1,0:T(8,128)} %refs_13_.3), channel_id=1, source_target_pairs={{0,1},{1,0},{2,3},{3,2},{4,5},{5,4},{6,7},{7,6},{8,9},{9,8},{10,11... | collective-permute-start | bytes 12582920 | tf_op jit(solution)/shard_map/ppermute | solution.py:322
  1.3 7.9 %collective-permute-start = (f32[32,4096]{1,0:T(8,128)S(1)}, f32[32,4096]{1,0:T(8,128)}, u32[]{:S(2)}, u32[]{:S(2)}) collective-permute-start(f32[32,4096]{1,0:T(8,128)S(1)} %pad_maximum_fusion.6), channel_id=1, source_target_pairs={{0,1},{1,0},{2,3},{3,2},{4,5},{5,4},{6,7},{7,6},{8,9},{9,8},{10,11... | collective-permute-start | bytes 1572872 | tf_op jit(solution)/shard_map/ppermute | solution.py:322
  1.9 69.7 %copy-start.3 = (f32[32,4096]{1,0:T(8,128)}, f32[32,4096]{1,0:T(8,128)S(1)}, u32[]{:S(2)}) copy-start(f32[32,4096]{1,0:T(8,128)S(1)} %pad_maximum_fusion.5.refs_0_) | copy-start | bytes 1572868
  1.9 16.9 %collective-permute-start.2 = (f32[32,4096]{1,0:T(8,128)S(1)}, f32[32,4096]{1,0:T(8,128)S(1)}, u32[]{:S(2)}, u32[]{:S(2)}) collective-permute-start(f32[32,4096]{1,0:T(8,128)S(1)} %pad_maximum_fusion.5.refs_0_), channel_id=1, source_target_pairs={{0,2},{1,3},{2,4},{3,5},{4,6},{5,7},{6,0},{7,1},{8,10},{9,11},{10,... | collective-permute-start | bytes 1572872 | tf_op jit(solution)/shard_map/ppermute | solution.py:322
  4.0 17.0 %collective-permute-start.6 = (f32[32,4096]{1,0:T(8,128)S(1)}, f32[32,4096]{1,0:T(8,128)S(1)}, u32[]{:S(2)}, u32[]{:S(2)}) collective-permute-start(f32[32,4096]{1,0:T(8,128)S(1)} %pad_maximum_fusion.5.refs_0_), channel_id=1, source_target_pairs={{0,8},{1,9},{2,10},{3,11},{4,12},{5,13},{6,14},{7,15},{8,0},{9,1},... | collective-permute-start | bytes 1572872 | tf_op jit(solution)/shard_map/ppermute | solution.py:322
  7.0 14.1 %collective-permute-start.4 = (f32[32,4096]{1,0:T(8,128)S(1)}, f32[32,4096]{1,0:T(8,128)S(1)}, u32[]{:S(2)}, u32[]{:S(2)}) collective-permute-start(f32[32,4096]{1,0:T(8,128)S(1)} %pad_maximum_fusion.5.refs_0_), channel_id=1, source_target_pairs={{0,6},{1,7},{2,0},{3,1},{4,2},{5,3},{6,4},{7,5},{8,14},{9,15},{10,... | collective-permute-start | bytes 1572872 | tf_op jit(solution)/shard_map/ppermute | solution.py:322
  9.3 21.1 %collective-permute-start.7 = (f32[32,4096]{1,0:T(8,128)}, f32[32,4096]{1,0:T(8,128)S(1)}, u32[]{:S(2)}, u32[]{:S(2)}) collective-permute-start(f32[32,4096]{1,0:T(8,128)} %collective-permute-done.refs_1_), channel_id=1, source_target_pairs={{0,8},{1,9},{2,10},{3,11},{4,12},{5,13},{6,14},{7,15},{8,0},{9,1},... | collective-permute-start | bytes 1572872 | tf_op jit(solution)/shard_map/ppermute | solution.py:322
  11.2 19.2 %collective-permute-start.3 = (f32[32,4096]{1,0:T(8,128)}, f32[32,4096]{1,0:T(8,128)S(1)}, u32[]{:S(2)}, u32[]{:S(2)}) collective-permute-start(f32[32,4096]{1,0:T(8,128)} %collective-permute-done.refs_1_), channel_id=1, source_target_pairs={{0,2},{1,3},{2,4},{3,5},{4,6},{5,7},{6,0},{7,1},{8,10},{9,11},{10,... | collective-permute-start | bytes 1572872 | tf_op jit(solution)/shard_map/ppermute | solution.py:322
  18.9 52.7 %copy-start.4 = (f32[32,4096]{1,0:T(8,128)}, f32[32,4096]{1,0:T(8,128)S(1)}, u32[]{:S(2)}) copy-start(f32[32,4096]{1,0:T(8,128)S(1)} %collective-permute-done.2.refs_2_) | copy-start | bytes 1572868
  18.9 12.9 %collective-permute-start.5 = (f32[32,4096]{1,0:T(8,128)}, f32[32,4096]{1,0:T(8,128)S(1)}, u32[]{:S(2)}, u32[]{:S(2)}) collective-permute-start(f32[32,4096]{1,0:T(8,128)} %collective-permute-done.refs_1_), channel_id=1, source_target_pairs={{0,6},{1,7},{2,0},{3,1},{4,2},{5,3},{6,4},{7,5},{8,14},{9,15},{10,... | collective-permute-start | bytes 1572872 | tf_op jit(solution)/shard_map/ppermute | solution.py:322
  21.0 17.6 %copy-start = (f32[8192,128]{1,0:T(8,128)S(1)}, f32[8192,128]{1,0:T(8,128)}, u32[]{:S(2)}) copy-start(f32[8192,128]{1,0:T(8,128)} %refs_13_.3) | copy-start | bytes 12582916
  21.0 11.2 %copy-start.7 = (f32[32,4096]{1,0:T(8,128)}, f32[32,4096]{1,0:T(8,128)S(1)}, u32[]{:S(2)}) copy-start(f32[32,4096]{1,0:T(8,128)S(1)} %collective-permute-done.6.refs_6_) | copy-start | bytes 1572868
  21.1 12.9 %copy-start.9 = (f32[32,4096]{1,0:T(8,128)}, f32[32,4096]{1,0:T(8,128)S(1)}, u32[]{:S(2)}) copy-start(f32[32,4096]{1,0:T(8,128)S(1)} %collective-permute-done.4.refs_4_) | copy-start | bytes 1572868
  30.3 3.7 %copy-start.11 = (f32[32,4096]{1,0:T(8,128)}, f32[32,4096]{1,0:T(8,128)S(1)}, u32[]{:S(2)}) copy-start(f32[32,4096]{1,0:T(8,128)S(1)} %collective-permute-done.7.refs_7_) | copy-start | bytes 1572868
  30.4 1.9 %copy-start.5 = (f32[32,4096]{1,0:T(8,128)}, f32[32,4096]{1,0:T(8,128)S(1)}, u32[]{:S(2)}) copy-start(f32[32,4096]{1,0:T(8,128)S(1)} %collective-permute-done.3.refs_3_) | copy-start | bytes 1572868
  31.8 39.8 %copy-start.13 = (f32[32,4096]{1,0:T(8,128)}, f32[32,4096]{1,0:T(8,128)S(1)}, u32[]{:S(2)}) copy-start(f32[32,4096]{1,0:T(8,128)S(1)} %collective-permute-done.5.refs_5_) | copy-start | bytes 1572868
  32.2 25.1 %collective-permute-start.8 = (f32[128,2048]{1,0:T(8,128)S(1)}, f32[128,2048]{1,0:T(8,128)S(1)}, u32[]{:S(2)}, u32[]{:S(2)}) collective-permute-start(f32[128,2048]{1,0:T(8,128)S(1)} %get-tuple-element.25), channel_id=1, source_target_pairs={{0,2},{1,3},{2,4},{3,5},{4,6},{5,7},{6,0},{7,1},{8,10},{9,11},{10,... | collective-permute-start | bytes 3145736 | tf_op jit(solution)/shard_map/ppermute | solution.py:322
  34.0 23.3 %collective-permute-start.9 = (f32[128,2048]{1,0:T(8,128)S(1)}, f32[128,2048]{1,0:T(8,128)S(1)}, u32[]{:S(2)}, u32[]{:S(2)}) collective-permute-start(f32[128,2048]{1,0:T(8,128)S(1)} %get-tuple-element.24), channel_id=1, source_target_pairs={{0,6},{1,7},{2,0},{3,1},{4,2},{5,3},{6,4},{7,5},{8,14},{9,15},{10,... | collective-permute-start | bytes 3145736 | tf_op jit(solution)/shard_map/ppermute | solution.py:322
  35.9 25.8 %collective-permute-start.10 = (f32[128,2048]{1,0:T(8,128)S(1)}, f32[128,2048]{1,0:T(8,128)S(1)}, u32[]{:S(2)}, u32[]{:S(2)}) collective-permute-start(f32[128,2048]{1,0:T(8,128)S(1)} %get-tuple-element.23), channel_id=1, source_target_pairs={{0,8},{1,9},{2,10},{3,11},{4,12},{5,13},{6,14},{7,15},{8,0},{9,1},... | collective-permute-start | bytes 3145736 | tf_op jit(solution)/shard_map/ppermute | solution.py:322
  38.6 1.0 copy-start.6
  39.6 1.0 copy-start.8
  40.7 1.0 copy-start.10
  41.7 1.0 copy-start.12
  57.3 22.8 %copy-start.1 = (f32[128,2048]{1,0:T(8,128)}, f32[128,2048]{1,0:T(8,128)S(1)}, u32[]{:S(2)}) copy-start(f32[128,2048]{1,0:T(8,128)S(1)} %collective-permute-done.8.refs_8_) | copy-start | bytes 3145732
  57.3 22.7 %copy-start.2 = (f32[128,2048]{1,0:T(8,128)}, f32[128,2048]{1,0:T(8,128)S(1)}, u32[]{:S(2)}) copy-start(f32[128,2048]{1,0:T(8,128)S(1)} %collective-permute-done.9.refs_9_) | copy-start | bytes 3145732
  57.4 12.6 %collective-permute-start.11 = (f32[64,2048]{1,0:T(8,128)S(1)}, f32[64,2048]{1,0:T(8,128)S(1)}, u32[]{:S(2)}, u32[]{:S(2)}) collective-permute-start(f32[64,2048]{1,0:T(8,128)S(1)} %slice.42), channel_id=1, source_target_pairs={{0,2},{1,3},{2,4},{3,5},{4,6},{5,7},{6,0},{7,1},{8,10},{9,11},{10,... | collective-permute-start | bytes 1572872 | tf_op jit(solution)/shard_map/ppermute | solution.py:322
  59.1 12.5 %collective-permute-start.12 = (f32[64,2048]{1,0:T(8,128)S(1)}, f32[64,2048]{1,0:T(8,128)S(1)}, u32[]{:S(2)}, u32[]{:S(2)}) collective-permute-start(f32[64,2048]{1,0:T(8,128)S(1)} %slice.43), channel_id=1, source_target_pairs={{0,8},{1,9},{2,10},{3,11},{4,12},{5,13},{6,14},{7,15},{8,0},{9,1},... | collective-permute-start | bytes 1572872 | tf_op jit(solution)/shard_map/ppermute | solution.py:322
  61.7 18.4 %copy-start.14 = (f32[128,2048]{1,0:T(8,128)}, f32[128,2048]{1,0:T(8,128)S(1)}, u32[]{:S(2)}) copy-start(f32[128,2048]{1,0:T(8,128)S(1)} %collective-permute-done.10.refs_10_) | copy-start | bytes 3145732
  70.0 10.1 %copy-start.15 = (f32[64,2048]{1,0:T(8,128)}, f32[64,2048]{1,0:T(8,128)S(1)}, u32[]{:S(2)}) copy-start(f32[64,2048]{1,0:T(8,128)S(1)} %collective-permute-done.11.refs_11_) | copy-start | bytes 1572868
  71.6 8.5 %copy-start.16 = (f32[64,2048]{1,0:T(8,128)}, f32[64,2048]{1,0:T(8,128)S(1)}, u32[]{:S(2)}) copy-start(f32[64,2048]{1,0:T(8,128)S(1)} %collective-permute-done.12.refs_12_) | copy-start | bytes 1572868
  80.1 2.1 %collective-permute-start.13 = (f32[1152,128]{1,0:T(8,128)S(1)}, f32[1152,128]{1,0:T(8,128)S(1)}, u32[]{:S(2)}, u32[]{:S(2)}) collective-permute-start(f32[1152,128]{1,0:T(8,128)S(1)} %get-tuple-element.20), channel_id=1, source_target_pairs={{0,1},{1,0},{2,3},{3,2},{4,5},{5,4},{6,7},{7,6},{8,9},{9,8},{10,11... | collective-permute-start | bytes 1769480 | tf_op jit(solution)/shard_map/ppermute | solution.py:322
  111.5 2.0 %collective-permute-start.14 = (f32[1152,128]{1,0:T(8,128)S(1)}, f32[1152,128]{1,0:T(8,128)S(1)}, u32[]{:S(2)}, u32[]{:S(2)}) collective-permute-start(f32[1152,128]{1,0:T(8,128)S(1)} %bitcast.19), channel_id=1, source_target_pairs={{0,1},{1,0},{2,3},{3,2},{4,5},{5,4},{6,7},{7,6},{8,9},{9,8},{10,11... | collective-permute-start | bytes 1769480 | tf_op jit(solution)/shard_map/ppermute | solution.py:322
  125.6 4.2 %collective-permute-start.15 = (f32[4096,128]{1,0:T(8,128)S(1)}, f32[4096,128]{1,0:T(8,128)S(1)}, u32[]{:S(2)}, u32[]{:S(2)}) collective-permute-start(f32[4096,128]{1,0:T(8,128)S(1)} %get-tuple-element.22), channel_id=1, source_target_pairs={{0,1},{1,0},{2,3},{3,2},{4,5},{5,4},{6,7},{7,6},{8,9},{9,8},{10,11... | collective-permute-start | bytes 6291464 | tf_op jit(solution)/shard_map/ppermute | solution.py:322
  126.3 3.5 %copy-start.17 = (f32[8192,128]{1,0:T(8,128)}, f32[8192,128]{1,0:T(8,128)S(1)}, u32[]{:S(2)}) copy-start(f32[8192,128]{1,0:T(8,128)S(1)} %constant_dynamic-update-slice_fusion.1) | copy-start | bytes 12582916

commit v12 on v8

--- a/solution.py
+++ b/solution.py
@@ -13,8 +13,8 @@
 PLANES, DEPTH, CORES = 2, 4, 2
 CHIPS = PLANES * DEPTH
 WIDE = 128
-TILE = 1024
-LIMIT = 24 << 20
+TILE = 2048
+LIMIT = 32 << 20
 PIECES = ((0, 0), (0, 1), (1, 1), (0, 2), (0, 3)), ((1, 2), (1, 3), (2, 2), (2, 3), (3, 3))
 
 
@@ -392,6 +392,7 @@
     b_own = core_swap(half_of(1 - core))
     own = jnp.concatenate([a_own, b_own], axis=0)
     a_away, a_below, a_above = across(a_own), up(a_own), down(a_own)
+    b_own, other = lax.optimization_barrier((b_own, core_swap(vectors)))
     b_away, b_below, b_above = across(b_own), up(b_own), down(b_own)
     near = (a_own, b_own, a_below, b_below, a_above, b_above, a_away, b_away)
 
@@ -407,8 +408,6 @@
     )
     to_across = jnp.concatenate(late_half(a_below, b_below, a_above, b_above), axis=0)
     sent_up, sent_down, sent_across = up(to_up), down(to_down), across(to_across)
-    vectors_late, _ = lax.optimization_barrier((vectors, to_up))
-    other = core_swap(vectors_late)
 
     chips = []
     for x_step, z_step in ((0, 0), (0, -1), (0, 1), (1, 0), (0, 2), (1, -1), (1, 1), (1, 2)):
@@ -464,9 +463,7 @@
         functools.partial(gram_kernel, first=True), near, whole, (),
         [(2 * span, span)], split_scratch(span) + [square] * 3, 10, "gram_near",
     )
-    before, sent_up, sent_down, sent_across = lax.optimization_barrier(
-        (before, sent_up, sent_down, sent_across)
-    )
+    before, sent_up, sent_down = lax.optimization_barrier((before, sent_up, sent_down))
     end_up = up(sent_up[chunk:])
     end_across = across(sent_down[:chunk])
     middle = (sent_up, sent_down, sent_across)
@@ -491,7 +488,9 @@
     mine = lax.all_to_all(spread, "row", 0, 0).reshape(length, WIDE)
     theirs = core_swap(mine)
 
-    held = [pltpu.with_memory_space_constraint(v, pltpu.HBM) for v in near + far]
+    *held, vectors_held, other_held = [
+        pltpu.with_memory_space_constraint(v, pltpu.HBM) for v in near + far + (vectors, other)
+    ]
     result_own, result_other = pl.pallas_call(
         apply_kernel,
         out_shape=[jax.ShapeDtypeStruct((half, columns), F32)] * 2,
@@ -513,7 +512,7 @@
             dimension_semantics=("arbitrary",), vmem_limit_bytes=LIMIT
         ),
         name="solve_apply",
-    )(where, *held, vectors, other, mine, theirs)
+    )(where, *held, vectors_held, other_held, mine, theirs)
 
     returned = core_swap(result_other)
     result = jnp.zeros((rows, columns), F32)

time: 140 us -> 132 us (0.943)
  waiting for transfers between devices: 40.7 us -> 33.7 us
  starting transfers between devices: 20.2 us -> 24.9 us
  local copies, waits for them, and re-layouts: 11.5 us -> 7.75 us
    ppermute x16, waiting for transfers between devices: 40.7 us -> 33.7 us  [permute(): return lax.ppermute(value, 'col', pairs)]
    ppermute x16, starting transfers between devices: 20.2 us -> 24.9 us  [permute(): return lax.ppermute(value, 'col', pairs)]
    unnamed x40 -> x36, local copies, waits for them, and re-layouts: 7.99 us -> 4.22 us
  transfers between devices with their start and end apart: 16 -> 16, of which waited for: 12 -> 9; matrix products, arithmetic and copies ran while one was open for 1% -> 2% of each run, Pallas kernels for 11% -> 11%
where the time goes in v12:
time: 132 us; the launch traced here: 130 us
  waiting for transfers between devices  33.7 us (26%)
  Pallas kernels  33.7 us (26%)
  blocking collectives  29.2 us (22%)
  starting transfers between devices  24.9 us (19%)
  local copies, waits for them, and re-layouts  7.75 us (6%)
    ppermute x16, waiting for transfers between devices, permute(): return lax.ppermute(value, 'col', pairs)  33.7 us
    ppermute x16, starting transfers between devices, permute(): return lax.ppermute(value, 'col', pairs)  24.9 us
    pallas_call x3, Pallas kernels, products(): pl.pallas_call(kernel, out_shape=[jax.ShapeDtypeStruct(v, F32) for v in s...  21.6 us
    all_to_all x1, blocking collectives, per_device(): lax.all_to_all(mine.reshape(members, length // members, WIDE), 'row', 0, 0)  16.2 us
    all_to_all x1, blocking collectives, per_device(): mine = lax.all_to_all(spread, 'row', 0, 0).reshape(length, WIDE)  13 us
    pallas_call x1, Pallas kernels, per_device(): pl.pallas_call(apply_kernel, out_shape=[jax.ShapeDtypeStruct((half, colum...  12.1 us
    unnamed x36, local copies, waits for them, and re-layouts  4.22 us
  transfers between devices with their start and end apart: 16, of which 9 were waited for; matrix products, arithmetic and copies ran while one was open for 2% of the time, Pallas kernels for 11%

profile of v12, /device:TPU:0, one launch (start us, length us, event | category | flops | bytes accessed | tf_op | source)
XLA Modules:
  0.0 130.1 jit_solution(12829979966501609593)
XLA Ops:
  0.0 0.0 collective-permute-start.1
  0.0 1.3 dynamic-slice_bitcast_fusion
  1.3 0.6 collective-permute-start
  1.9 0.0 copy-start.3
  1.9 2.1 %collective-permute-start.2 = (f32[32,4096]{1,0:T(8,128)S(1)}, f32[32,4096]{1,0:T(8,128)S(1)}, u32[]{:S(2)}, u32[]{:S(2)}) collective-permute-start(f32[32,4096]{1,0:T(8,128)S(1)} %pad_maximum_fusion.5.refs_0_), channel_id=1, source_target_pairs={{0,2},{1,3},{2,4},{3,5},{4,6},{5,7},{6,0},{7,1},{8,10},{9,11},{10,... | collective-permute-start | bytes 1572872 | tf_op jit(solution)/shard_map/ppermute | solution.py:373
  4.0 3.0 %collective-permute-start.6 = (f32[32,4096]{1,0:T(8,128)S(1)}, f32[32,4096]{1,0:T(8,128)S(1)}, u32[]{:S(2)}, u32[]{:S(2)}) collective-permute-start(f32[32,4096]{1,0:T(8,128)S(1)} %pad_maximum_fusion.5.refs_0_), channel_id=1, source_target_pairs={{0,8},{1,9},{2,10},{3,11},{4,12},{5,13},{6,14},{7,15},{8,0},{9,1},... | collective-permute-start | bytes 1572872 | tf_op jit(solution)/shard_map/ppermute | solution.py:373
  7.0 2.2 %collective-permute-start.4 = (f32[32,4096]{1,0:T(8,128)S(1)}, f32[32,4096]{1,0:T(8,128)S(1)}, u32[]{:S(2)}, u32[]{:S(2)}) collective-permute-start(f32[32,4096]{1,0:T(8,128)S(1)} %pad_maximum_fusion.5.refs_0_), channel_id=1, source_target_pairs={{0,6},{1,7},{2,0},{3,1},{4,2},{5,3},{6,4},{7,5},{8,14},{9,15},{10,... | collective-permute-start | bytes 1572872 | tf_op jit(solution)/shard_map/ppermute | solution.py:373
  9.3 0.0 collective-permute-done.refs_1_
  9.3 0.0 collective-permute-done.1.refs_9_.refs_12_.refs_14_
  9.3 1.9 %collective-permute-start.7 = (f32[32,4096]{1,0:T(8,128)}, f32[32,4096]{1,0:T(8,128)S(1)}, u32[]{:S(2)}, u32[]{:S(2)}) collective-permute-start(f32[32,4096]{1,0:T(8,128)} %collective-permute-done.refs_1_), channel_id=1, source_target_pairs={{0,8},{1,9},{2,10},{3,11},{4,12},{5,13},{6,14},{7,15},{8,0},{9,1},... | collective-permute-start | bytes 1572872 | tf_op jit(solution)/shard_map/ppermute | solution.py:373
  11.2 1.9 %collective-permute-start.3 = (f32[32,4096]{1,0:T(8,128)}, f32[32,4096]{1,0:T(8,128)S(1)}, u32[]{:S(2)}, u32[]{:S(2)}) collective-permute-start(f32[32,4096]{1,0:T(8,128)} %collective-permute-done.refs_1_), channel_id=1, source_target_pairs={{0,2},{1,3},{2,4},{3,5},{4,6},{5,7},{6,0},{7,1},{8,10},{9,11},{10,... | collective-permute-start | bytes 1572872 | tf_op jit(solution)/shard_map/ppermute | solution.py:373
  13.1 0.1 stack.39.where_ref
  13.2 5.7 %collective-permute-done.2.refs_2_ = f32[32,4096]{1,0:T(8,128)S(1)} collective-permute-done((f32[32,4096]{1,0:T(8,128)S(1)}, f32[32,4096]{1,0:T(8,128)S(1)}, u32[]{:S(2)}, u32[]{:S(2)}) %collective-permute-start.2) | collective-permute-done | bytes 524320 | tf_op jit(solution)/shard_map/ppermute | solution.py:373
  18.9 2.1 %collective-permute-start.5 = (f32[32,4096]{1,0:T(8,128)}, f32[32,4096]{1,0:T(8,128)S(1)}, u32[]{:S(2)}, u32[]{:S(2)}) collective-permute-start(f32[32,4096]{1,0:T(8,128)} %collective-permute-done.refs_1_), channel_id=1, source_target_pairs={{0,6},{1,7},{2,0},{3,1},{4,2},{5,3},{6,4},{7,5},{8,14},{9,15},{10,... | collective-permute-start | bytes 1572872 | tf_op jit(solution)/shard_map/ppermute | solution.py:373
  21.0 0.0 copy-start
  21.0 0.0 collective-permute-done.6.refs_6_
  21.0 0.0 copy-start.7
  21.0 0.1 collective-permute-done.4.refs_4_
  21.2 9.2 %collective-permute-done.7.refs_7_ = f32[32,4096]{1,0:T(8,128)S(1)} collective-permute-done((f32[32,4096]{1,0:T(8,128)}, f32[32,4096]{1,0:T(8,128)S(1)}, u32[]{:S(2)}, u32[]{:S(2)}) %collective-permute-start.7) | collective-permute-done | bytes 524320 | tf_op jit(solution)/shard_map/ppermute | solution.py:373
  30.4 0.0 collective-permute-done.3.refs_3_
  30.4 0.0 copy-start.5
  30.4 1.4 %collective-permute-done.5.refs_5_ = f32[32,4096]{1,0:T(8,128)S(1)} collective-permute-done((f32[32,4096]{1,0:T(8,128)}, f32[32,4096]{1,0:T(8,128)S(1)}, u32[]{:S(2)}, u32[]{:S(2)}) %collective-permute-start.5) | collective-permute-done | bytes 524320 | tf_op jit(solution)/shard_map/ppermute | solution.py:373
  31.8 0.4 pad_maximum_fusion.4
  32.2 0.0 copy-done.7
  32.2 0.0 copy-done.5
  32.2 1.8 %collective-permute-start.8 = (f32[128,2048]{1,0:T(8,128)S(1)}, f32[128,2048]{1,0:T(8,128)S(1)}, u32[]{:S(2)}, u32[]{:S(2)}) collective-permute-start(f32[128,2048]{1,0:T(8,128)S(1)} %get-tuple-element.31), channel_id=1, source_target_pairs={{0,2},{1,3},{2,4},{3,5},{4,6},{5,7},{6,0},{7,1},{8,10},{9,11},{10,... | collective-permute-start | bytes 3145736 | tf_op jit(solution)/shard_map/ppermute | solution.py:373
  34.0 0.0 copy-done.9
  34.0 0.0 copy-done.11
  34.0 1.9 %collective-permute-start.9 = (f32[128,2048]{1,0:T(8,128)S(1)}, f32[128,2048]{1,0:T(8,128)S(1)}, u32[]{:S(2)}, u32[]{:S(2)}) collective-permute-start(f32[128,2048]{1,0:T(8,128)S(1)} %get-tuple-element.30), channel_id=1, source_target_pairs={{0,6},{1,7},{2,0},{3,1},{4,2},{5,3},{6,4},{7,5},{8,14},{9,15},{10,... | collective-permute-start | bytes 3145736 | tf_op jit(solution)/shard_map/ppermute | solution.py:373
  35.9 2.7 %collective-permute-start.10 = (f32[128,2048]{1,0:T(8,128)S(1)}, f32[128,2048]{1,0:T(8,128)S(1)}, u32[]{:S(2)}, u32[]{:S(2)}) collective-permute-start(f32[128,2048]{1,0:T(8,128)S(1)} %get-tuple-element.29), channel_id=1, source_target_pairs={{0,8},{1,9},{2,10},{3,11},{4,12},{5,13},{6,14},{7,15},{8,0},{9,1},... | collective-permute-start | bytes 3145736 | tf_op jit(solution)/shard_map/ppermute | solution.py:373
  38.5 0.0 copy-done
  38.5 1.0 copy-done.6
  39.6 1.0 copy-done.8
  40.6 1.0 copy-done.10
  41.7 1.0 copy-done.12
  42.7 6.3 %gram_near.1.refs_15_ = f32[512,256]{1,0:T(8,128)S(1)} custom-call(s32[9]{0:T(128)S(1)} %stack.39.where_ref, f32[32,4096]{1,0:T(8,128)S(1)} %pad_maximum_fusion.5.refs_0_, f32[32,4096]{1,0:T(8,128)} %collective-permute-done.refs_1_, f32[32,4096]{1,0:T(8,128)S(1)} %collective-permute-done.2.refs_2_, f32[32,4096]{1,0:T(8,128)S(1)} %copy-done.6, ...), custom_call_target="tpu_custom_call" | custom-call | flops 16106127360 | bytes 12582912 | tf_op jit(solution)/shard_map/gram_near/pallas_call | solution.py:435
  49.0 8.3 %collective-permute-done.8.refs_8_ = f32[128,2048]{1,0:T(8,128)S(1)} collective-permute-done((f32[128,2048]{1,0:T(8,128)S(1)}, f32[128,2048]{1,0:T(8,128)S(1)}, u32[]{:S(2)}, u32[]{:S(2)}) %collective-permute-start.8) | collective-permute-done | bytes 1048608 | tf_op jit(solution)/shard_map/ppermute | solution.py:373
  57.3 0.0 collective-permute-done.9.refs_9_
  57.3 1.7 %collective-permute-start.11 = (f32[64,2048]{1,0:T(8,128)S(1)}, f32[64,2048]{1,0:T(8,128)S(1)}, u32[]{:S(2)}, u32[]{:S(2)}) collective-permute-start(f32[64,2048]{1,0:T(8,128)S(1)} %slice.42), channel_id=1, source_target_pairs={{0,2},{1,3},{2,4},{3,5},{4,6},{5,7},{6,0},{7,1},{8,10},{9,11},{10,... | collective-permute-start | bytes 1572872 | tf_op jit(solution)/shard_map/ppermute | solution.py:373
  59.1 2.8 %collective-permute-start.12 = (f32[64,2048]{1,0:T(8,128)S(1)}, f32[64,2048]{1,0:T(8,128)S(1)}, u32[]{:S(2)}, u32[]{:S(2)}) collective-permute-start(f32[64,2048]{1,0:T(8,128)S(1)} %slice.43), channel_id=1, source_target_pairs={{0,8},{1,9},{2,10},{3,11},{4,12},{5,13},{6,14},{7,15},{8,0},{9,1},... | collective-permute-start | bytes 1572872 | tf_op jit(solution)/shard_map/ppermute | solution.py:373
  61.9 0.0 collective-permute-done.10.refs_10_
  61.9 8.3 %gram_middle.1.refs_16_ = f32[768,256]{1,0:T(8,128)S(1)} custom-call(s32[9]{0:T(128)S(1)} %stack.39.where_ref, f32[32,4096]{1,0:T(8,128)S(1)} %pad_maximum_fusion.5.refs_0_, f32[32,4096]{1,0:T(8,128)} %collective-permute-done.refs_1_, f32[32,4096]{1,0:T(8,128)S(1)} %collective-permute-done.2.refs_2_, f32[32,4096]{1,0:T(8,128)S(1)} %copy-done.6, ...), custom_call_target="tpu_custom_call" | custom-call | flops 25769803776 | bytes 12582912 | tf_op jit(solution)/shard_map/gram_middle/pallas_call | solution.py:435
  70.2 0.0 collective-permute-done.11.refs_11_
  70.2 0.0 copy-start.15
  70.2 1.5 %collective-permute-done.12.refs_12_ = f32[64,2048]{1,0:T(8,128)S(1)} collective-permute-done((f32[64,2048]{1,0:T(8,128)S(1)}, f32[64,2048]{1,0:T(8,128)S(1)}, u32[]{:S(2)}, u32[]{:S(2)}) %collective-permute-start.12) | collective-permute-done | bytes 524320 | tf_op jit(solution)/shard_map/ppermute | solution.py:373
  71.7 0.0 copy-done.3
  71.7 0.0 copy-done.4
  71.7 0.0 copy-done.13
  71.8 7.0 %gram_last.1 = (f32[1152,128]{1,0:T(8,128)S(1)}, f32[1152,128]{1,0:T(8,128)S(1)}) custom-call(s32[9]{0:T(128)S(1)} %stack.39.where_ref, f32[32,4096]{1,0:T(8,128)S(1)} %pad_maximum_fusion.5.refs_0_, f32[32,4096]{1,0:T(8,128)} %collective-permute-done.refs_1_, f32[32,4096]{1,0:T(8,128)S(1)} %collective-permute-done.2.refs_2_, f32[32,4096]{1,0:T(8,128)S(1)} %copy-done.6, ...), custom_call_target="tpu_custom_call" | custom-call | flops 12884901888 | bytes 12582912 | tf_op jit(solution)/shard_map/gram_last/pallas_call | solution.py:435
  78.8 0.1 collective-permute-start.13
  78.9 2.0 %collective-permute-done.13 = f32[1152,128]{1,0:T(8,128)S(1)} collective-permute-done((f32[1152,128]{1,0:T(8,128)S(1)}, f32[1152,128]{1,0:T(8,128)S(1)}, u32[]{:S(2)}, u32[]{:S(2)}) %collective-permute-start.13) | collective-permute-done | bytes 589856 | tf_op jit(solution)/shard_map/ppermute | solution.py:373
  80.9 0.1 add.93
  81.0 16.2 %all_to_all.10 = f32[8,144,128]{2,1,0:T(8,128)S(1)} all-to-all(f32[8,144,128]{2,1,0:T(8,128)S(1)} %bitcast.21), channel_id=1, replica_groups=mesh['row'=8,'col'=16] {'row'}, dimensions={0} | all-to-all | bytes 1179648 | tf_op jit(solution)/shard_map/all_to_all | solution.py:485
  97.3 13.0 %all_to_all.11 = f32[8,144,128]{2,1,0:T(8,128)S(1)} all-to-all(f32[8,144,128]{2,1,0:T(8,128)S(1)} %broadcast_in_dim.10), channel_id=1, replica_groups=mesh['row'=8,'col'=16] {'row'}, dimensions={0} | all-to-all | bytes 1179648 | tf_op jit(solution)/shard_map/all_to_all | solution.py:488
  110.3 0.0 collective-permute-start.14
  110.3 2.0 %collective-permute-done.14.refs_16_ = f32[1152,128]{1,0:T(8,128)S(1)} collective-permute-done((f32[1152,128]{1,0:T(8,128)S(1)}, f32[1152,128]{1,0:T(8,128)S(1)}, u32[]{:S(2)}, u32[]{:S(2)}) %collective-permute-start.14) | collective-permute-done | bytes 589856 | tf_op jit(solution)/shard_map/ppermute | solution.py:373
  112.3 12.1 %solve_apply.1 = (f32[4096,128]{1,0:T(8,128)S(1)}, f32[4096,128]{1,0:T(8,128)S(1)}) custom-call(s32[9]{0:T(128)S(1)} %stack.39.where_ref, f32[32,4096]{1,0:T(8,128)} %copy-done.3, f32[32,4096]{1,0:T(8,128)} %collective-permute-done.refs_1_, f32[32,4096]{1,0:T(8,128)} %copy-done.4, f32[32,4096]{1,0:T(8,128)} %copy-done.5, f32[32,4096]{1,0:T(8,128)} %copy-done.9, ...), custom_call_target="tpu_custom_call" | custom-call | tf_op jit(solution)/shard_map/solve_apply/pallas_call | solution.py:494
  124.4 0.2 collective-permute-start.15
  124.6 0.3 broadcast_in_dim.4
  124.9 0.2 constant_dynamic-update-slice_fusion.1
  125.1 0.0 copy-start.17
  125.1 3.5 %collective-permute-done.15 = f32[4096,128]{1,0:T(8,128)S(1)} collective-permute-done((f32[4096,128]{1,0:T(8,128)S(1)}, f32[4096,128]{1,0:T(8,128)S(1)}, u32[]{:S(2)}, u32[]{:S(2)}) %collective-permute-start.15) | collective-permute-done | bytes 2097184 | tf_op jit(solution)/shard_map/ppermute | solution.py:373
  128.6 0.0 copy-done.17
  128.6 1.5 %constant_dynamic-update-slice_fusion = f32[8192,128]{1,0:T(8,128)} fusion(f32[8192,128]{1,0:T(8,128)} %copy-done.17, f32[4096,128]{1,0:T(8,128)S(1)} %collective-permute-done.15, s32[]{:T(128)S(6)} %select_n.61), kind=kLoop, calls=%fused_computation.11 | loop fusion | bytes 4194308 | tf_op jit(solution)/shard_map/dynamic_update_slice | solution.py:520
  (29 shorter events, 0.4 us)
Async XLA Ops:
  0.0 9.3 %collective-permute-start.1 = (f32[8192,128]{1,0:T(8,128)}, f32[8192,128]{1,0:T(8,128)}, u32[]{:S(2)}, u32[]{:S(2)}) collective-permute-start(f32[8192,128]{1,0:T(8,128)} %refs_13_.3), channel_id=1, source_target_pairs={{0,1},{1,0},{2,3},{3,2},{4,5},{5,4},{6,7},{7,6},{8,9},{9,8},{10,11... | collective-permute-start | bytes 12582920 | tf_op jit(solution)/shard_map/ppermute | solution.py:373
  1.3 7.9 %collective-permute-start = (f32[32,4096]{1,0:T(8,128)S(1)}, f32[32,4096]{1,0:T(8,128)}, u32[]{:S(2)}, u32[]{:S(2)}) collective-permute-start(f32[32,4096]{1,0:T(8,128)S(1)} %pad_maximum_fusion.6), channel_id=1, source_target_pairs={{0,1},{1,0},{2,3},{3,2},{4,5},{5,4},{6,7},{7,6},{8,9},{9,8},{10,11... | collective-permute-start | bytes 1572872 | tf_op jit(solution)/shard_map/ppermute | solution.py:373
  1.9 69.8 %copy-start.3 = (f32[32,4096]{1,0:T(8,128)}, f32[32,4096]{1,0:T(8,128)S(1)}, u32[]{:S(2)}) copy-start(f32[32,4096]{1,0:T(8,128)S(1)} %pad_maximum_fusion.5.refs_0_) | copy-start | bytes 1572868
  1.9 16.9 %collective-permute-start.2 = (f32[32,4096]{1,0:T(8,128)S(1)}, f32[32,4096]{1,0:T(8,128)S(1)}, u32[]{:S(2)}, u32[]{:S(2)}) collective-permute-start(f32[32,4096]{1,0:T(8,128)S(1)} %pad_maximum_fusion.5.refs_0_), channel_id=1, source_target_pairs={{0,2},{1,3},{2,4},{3,5},{4,6},{5,7},{6,0},{7,1},{8,10},{9,11},{10,... | collective-permute-start | bytes 1572872 | tf_op jit(solution)/shard_map/ppermute | solution.py:373
  4.0 17.0 %collective-permute-start.6 = (f32[32,4096]{1,0:T(8,128)S(1)}, f32[32,4096]{1,0:T(8,128)S(1)}, u32[]{:S(2)}, u32[]{:S(2)}) collective-permute-start(f32[32,4096]{1,0:T(8,128)S(1)} %pad_maximum_fusion.5.refs_0_), channel_id=1, source_target_pairs={{0,8},{1,9},{2,10},{3,11},{4,12},{5,13},{6,14},{7,15},{8,0},{9,1},... | collective-permute-start | bytes 1572872 | tf_op jit(solution)/shard_map/ppermute | solution.py:373
  7.0 14.1 %collective-permute-start.4 = (f32[32,4096]{1,0:T(8,128)S(1)}, f32[32,4096]{1,0:T(8,128)S(1)}, u32[]{:S(2)}, u32[]{:S(2)}) collective-permute-start(f32[32,4096]{1,0:T(8,128)S(1)} %pad_maximum_fusion.5.refs_0_), channel_id=1, source_target_pairs={{0,6},{1,7},{2,0},{3,1},{4,2},{5,3},{6,4},{7,5},{8,14},{9,15},{10,... | collective-permute-start | bytes 1572872 | tf_op jit(solution)/shard_map/ppermute | solution.py:373
  9.3 21.1 %collective-permute-start.7 = (f32[32,4096]{1,0:T(8,128)}, f32[32,4096]{1,0:T(8,128)S(1)}, u32[]{:S(2)}, u32[]{:S(2)}) collective-permute-start(f32[32,4096]{1,0:T(8,128)} %collective-permute-done.refs_1_), channel_id=1, source_target_pairs={{0,8},{1,9},{2,10},{3,11},{4,12},{5,13},{6,14},{7,15},{8,0},{9,1},... | collective-permute-start | bytes 1572872 | tf_op jit(solution)/shard_map/ppermute | solution.py:373
  11.2 19.2 %collective-permute-start.3 = (f32[32,4096]{1,0:T(8,128)}, f32[32,4096]{1,0:T(8,128)S(1)}, u32[]{:S(2)}, u32[]{:S(2)}) collective-permute-start(f32[32,4096]{1,0:T(8,128)} %collective-permute-done.refs_1_), channel_id=1, source_target_pairs={{0,2},{1,3},{2,4},{3,5},{4,6},{5,7},{6,0},{7,1},{8,10},{9,11},{10,... | collective-permute-start | bytes 1572872 | tf_op jit(solution)/shard_map/ppermute | solution.py:373
  18.9 52.9 %copy-start.4 = (f32[32,4096]{1,0:T(8,128)}, f32[32,4096]{1,0:T(8,128)S(1)}, u32[]{:S(2)}) copy-start(f32[32,4096]{1,0:T(8,128)S(1)} %collective-permute-done.2.refs_2_) | copy-start | bytes 1572868
  18.9 12.9 %collective-permute-start.5 = (f32[32,4096]{1,0:T(8,128)}, f32[32,4096]{1,0:T(8,128)S(1)}, u32[]{:S(2)}, u32[]{:S(2)}) collective-permute-start(f32[32,4096]{1,0:T(8,128)} %collective-permute-done.refs_1_), channel_id=1, source_target_pairs={{0,6},{1,7},{2,0},{3,1},{4,2},{5,3},{6,4},{7,5},{8,14},{9,15},{10,... | collective-permute-start | bytes 1572872 | tf_op jit(solution)/shard_map/ppermute | solution.py:373
  21.0 17.6 %copy-start = (f32[8192,128]{1,0:T(8,128)S(1)}, f32[8192,128]{1,0:T(8,128)}, u32[]{:S(2)}) copy-start(f32[8192,128]{1,0:T(8,128)} %refs_13_.3) | copy-start | bytes 12582916
  21.0 11.2 %copy-start.7 = (f32[32,4096]{1,0:T(8,128)}, f32[32,4096]{1,0:T(8,128)S(1)}, u32[]{:S(2)}) copy-start(f32[32,4096]{1,0:T(8,128)S(1)} %collective-permute-done.6.refs_6_) | copy-start | bytes 1572868
  21.1 12.8 %copy-start.9 = (f32[32,4096]{1,0:T(8,128)}, f32[32,4096]{1,0:T(8,128)S(1)}, u32[]{:S(2)}) copy-start(f32[32,4096]{1,0:T(8,128)S(1)} %collective-permute-done.4.refs_4_) | copy-start | bytes 1572868
  30.3 3.7 %copy-start.11 = (f32[32,4096]{1,0:T(8,128)}, f32[32,4096]{1,0:T(8,128)S(1)}, u32[]{:S(2)}) copy-start(f32[32,4096]{1,0:T(8,128)S(1)} %collective-permute-done.7.refs_7_) | copy-start | bytes 1572868
  30.4 1.8 %copy-start.5 = (f32[32,4096]{1,0:T(8,128)}, f32[32,4096]{1,0:T(8,128)S(1)}, u32[]{:S(2)}) copy-start(f32[32,4096]{1,0:T(8,128)S(1)} %collective-permute-done.3.refs_3_) | copy-start | bytes 1572868
  31.8 40.0 %copy-start.13 = (f32[32,4096]{1,0:T(8,128)}, f32[32,4096]{1,0:T(8,128)S(1)}, u32[]{:S(2)}) copy-start(f32[32,4096]{1,0:T(8,128)S(1)} %collective-permute-done.5.refs_5_) | copy-start | bytes 1572868
  32.2 25.1 %collective-permute-start.8 = (f32[128,2048]{1,0:T(8,128)S(1)}, f32[128,2048]{1,0:T(8,128)S(1)}, u32[]{:S(2)}, u32[]{:S(2)}) collective-permute-start(f32[128,2048]{1,0:T(8,128)S(1)} %get-tuple-element.31), channel_id=1, source_target_pairs={{0,2},{1,3},{2,4},{3,5},{4,6},{5,7},{6,0},{7,1},{8,10},{9,11},{10,... | collective-permute-start | bytes 3145736 | tf_op jit(solution)/shard_map/ppermute | solution.py:373
  34.0 23.3 %collective-permute-start.9 = (f32[128,2048]{1,0:T(8,128)S(1)}, f32[128,2048]{1,0:T(8,128)S(1)}, u32[]{:S(2)}, u32[]{:S(2)}) collective-permute-start(f32[128,2048]{1,0:T(8,128)S(1)} %get-tuple-element.30), channel_id=1, source_target_pairs={{0,6},{1,7},{2,0},{3,1},{4,2},{5,3},{6,4},{7,5},{8,14},{9,15},{10,... | collective-permute-start | bytes 3145736 | tf_op jit(solution)/shard_map/ppermute | solution.py:373
  35.9 26.0 %collective-permute-start.10 = (f32[128,2048]{1,0:T(8,128)S(1)}, f32[128,2048]{1,0:T(8,128)S(1)}, u32[]{:S(2)}, u32[]{:S(2)}) collective-permute-start(f32[128,2048]{1,0:T(8,128)S(1)} %get-tuple-element.29), channel_id=1, source_target_pairs={{0,8},{1,9},{2,10},{3,11},{4,12},{5,13},{6,14},{7,15},{8,0},{9,1},... | collective-permute-start | bytes 3145736 | tf_op jit(solution)/shard_map/ppermute | solution.py:373
  38.5 1.0 copy-start.6
  39.6 1.0 copy-start.8
  40.6 1.0 copy-start.10
  41.7 1.0 copy-start.12
  57.3 14.5 %copy-start.1 = (f32[128,2048]{1,0:T(8,128)}, f32[128,2048]{1,0:T(8,128)S(1)}, u32[]{:S(2)}) copy-start(f32[128,2048]{1,0:T(8,128)S(1)} %collective-permute-done.8.refs_8_) | copy-start | bytes 3145732
  57.3 14.4 %copy-start.2 = (f32[128,2048]{1,0:T(8,128)}, f32[128,2048]{1,0:T(8,128)S(1)}, u32[]{:S(2)}) copy-start(f32[128,2048]{1,0:T(8,128)S(1)} %collective-permute-done.9.refs_9_) | copy-start | bytes 3145732
  57.3 12.8 %collective-permute-start.11 = (f32[64,2048]{1,0:T(8,128)S(1)}, f32[64,2048]{1,0:T(8,128)S(1)}, u32[]{:S(2)}, u32[]{:S(2)}) collective-permute-start(f32[64,2048]{1,0:T(8,128)S(1)} %slice.42), channel_id=1, source_target_pairs={{0,2},{1,3},{2,4},{3,5},{4,6},{5,7},{6,0},{7,1},{8,10},{9,11},{10,... | collective-permute-start | bytes 1572872 | tf_op jit(solution)/shard_map/ppermute | solution.py:373
  59.1 12.6 %collective-permute-start.12 = (f32[64,2048]{1,0:T(8,128)S(1)}, f32[64,2048]{1,0:T(8,128)S(1)}, u32[]{:S(2)}, u32[]{:S(2)}) collective-permute-start(f32[64,2048]{1,0:T(8,128)S(1)} %slice.43), channel_id=1, source_target_pairs={{0,8},{1,9},{2,10},{3,11},{4,12},{5,13},{6,14},{7,15},{8,0},{9,1},... | collective-permute-start | bytes 1572872 | tf_op jit(solution)/shard_map/ppermute | solution.py:373
  61.9 9.9 %copy-start.14 = (f32[128,2048]{1,0:T(8,128)}, f32[128,2048]{1,0:T(8,128)S(1)}, u32[]{:S(2)}) copy-start(f32[128,2048]{1,0:T(8,128)S(1)} %collective-permute-done.10.refs_10_) | copy-start | bytes 3145732
  70.2 8.6 %copy-start.15 = (f32[64,2048]{1,0:T(8,128)}, f32[64,2048]{1,0:T(8,128)S(1)}, u32[]{:S(2)}) copy-start(f32[64,2048]{1,0:T(8,128)S(1)} %collective-permute-done.11.refs_11_) | copy-start | bytes 1572868
  71.8 7.1 %copy-start.16 = (f32[64,2048]{1,0:T(8,128)}, f32[64,2048]{1,0:T(8,128)S(1)}, u32[]{:S(2)}) copy-start(f32[64,2048]{1,0:T(8,128)S(1)} %collective-permute-done.12.refs_12_) | copy-start | bytes 1572868
  78.8 2.1 %collective-permute-start.13 = (f32[1152,128]{1,0:T(8,128)S(1)}, f32[1152,128]{1,0:T(8,128)S(1)}, u32[]{:S(2)}, u32[]{:S(2)}) collective-permute-start(f32[1152,128]{1,0:T(8,128)S(1)} %get-tuple-element.26), channel_id=1, source_target_pairs={{0,1},{1,0},{2,3},{3,2},{4,5},{5,4},{6,7},{7,6},{8,9},{9,8},{10,11... | collective-permute-start | bytes 1769480 | tf_op jit(solution)/shard_map/ppermute | solution.py:373
  110.3 2.0 %collective-permute-start.14 = (f32[1152,128]{1,0:T(8,128)S(1)}, f32[1152,128]{1,0:T(8,128)S(1)}, u32[]{:S(2)}, u32[]{:S(2)}) collective-permute-start(f32[1152,128]{1,0:T(8,128)S(1)} %bitcast.19), channel_id=1, source_target_pairs={{0,1},{1,0},{2,3},{3,2},{4,5},{5,4},{6,7},{7,6},{8,9},{9,8},{10,11... | collective-permute-start | bytes 1769480 | tf_op jit(solution)/shard_map/ppermute | solution.py:373
  124.4 4.2 %collective-permute-start.15 = (f32[4096,128]{1,0:T(8,128)S(1)}, f32[4096,128]{1,0:T(8,128)S(1)}, u32[]{:S(2)}, u32[]{:S(2)}) collective-permute-start(f32[4096,128]{1,0:T(8,128)S(1)} %get-tuple-element.28), channel_id=1, source_target_pairs={{0,1},{1,0},{2,3},{3,2},{4,5},{5,4},{6,7},{7,6},{8,9},{9,8},{10,11... | collective-permute-start | bytes 6291464 | tf_op jit(solution)/shard_map/ppermute | solution.py:373
  125.1 3.5 %copy-start.17 = (f32[8192,128]{1,0:T(8,128)}, f32[8192,128]{1,0:T(8,128)S(1)}, u32[]{:S(2)}) copy-start(f32[8192,128]{1,0:T(8,128)S(1)} %constant_dynamic-update-slice_fusion.1) | copy-start | bytes 12582916

commit v13 on v12

--- a/solution.py
+++ b/solution.py
@@ -489,7 +489,7 @@
     theirs = core_swap(mine)
 
     *held, vectors_held, other_held = [
-        pltpu.with_memory_space_constraint(v, pltpu.HBM) for v in near + far + (vectors, other)
+        pltpu.with_memory_space_constraint(v, pltpu.HBM) for v in near[2:4] + far + (vectors, other)
     ]
     result_own, result_other = pl.pallas_call(
         apply_kernel,
@@ -512,7 +512,7 @@
             dimension_semantics=("arbitrary",), vmem_limit_bytes=LIMIT
         ),
         name="solve_apply",
-    )(where, *held, vectors_held, other_held, mine, theirs)
+    )(where, *near[:2], *held[:2], *near[4:], *held[2:], vectors_held, other_held, mine, theirs)
 
     returned = core_swap(result_other)
     result = jnp.zeros((rows, columns), F32)

time: 132 us -> 132 us (level)
    unnamed x36 -> x42, local copies, waits for them, and re-layouts: 4.22 us -> 4.24 us
where the time goes in v13:
time: 132 us; the launch traced here: 131 us
  waiting for transfers between devices  34.1 us (26%)
  Pallas kernels  32.9 us (25%)
  blocking collectives  29.3 us (22%)
  starting transfers between devices  24.9 us (19%)
  local copies, waits for them, and re-layouts  7.74 us (6%)
  other arithmetic  1.61 us (1%)
    ppermute x16, waiting for transfers between devices, permute(): return lax.ppermute(value, 'col', pairs)  34.1 us
    ppermute x16, starting transfers between devices, permute(): return lax.ppermute(value, 'col', pairs)  24.9 us
    pallas_call x3, Pallas kernels, products(): pl.pallas_call(kernel, out_shape=[jax.ShapeDtypeStruct(v, F32) for v in s...  21.1 us
    all_to_all x1, blocking collectives, per_device(): lax.all_to_all(mine.reshape(members, length // members, WIDE), 'row', 0, 0)  16.3 us
    all_to_all x1, blocking collectives, per_device(): mine = lax.all_to_all(spread, 'row', 0, 0).reshape(length, WIDE)  13 us
    pallas_call x1, Pallas kernels, per_device(): pl.pallas_call(apply_kernel, out_shape=[jax.ShapeDtypeStruct((half, colum...  11.8 us
    unnamed x42, local copies, waits for them, and re-layouts  4.24 us
  transfers between devices with their start and end apart: 16, of which 9 were waited for; matrix products, arithmetic and copies ran while one was open for 2% of the time, Pallas kernels for 11%

profile of v13, /device:TPU:0, one launch (start us, length us, event | category | flops | bytes accessed | tf_op | source)
XLA Modules:
  0.0 130.8 jit_solution(4200500973189901612)
XLA Ops:
  0.0 0.0 collective-permute-start.1
  0.0 1.3 dynamic-slice_bitcast_fusion
  1.3 0.6 collective-permute-start
  1.9 2.1 %collective-permute-start.2 = (f32[32,4096]{1,0:T(8,128)S(1)}, f32[32,4096]{1,0:T(8,128)S(1)}, u32[]{:S(2)}, u32[]{:S(2)}) collective-permute-start(f32[32,4096]{1,0:T(8,128)S(1)} %pad_maximum_fusion.5.refs_0_), channel_id=1, source_target_pairs={{0,2},{1,3},{2,4},{3,5},{4,6},{5,7},{6,0},{7,1},{8,10},{9,11},{10,... | collective-permute-start | bytes 1572872 | tf_op jit(solution)/shard_map/ppermute | solution.py:373
  4.0 3.0 %collective-permute-start.6 = (f32[32,4096]{1,0:T(8,128)S(1)}, f32[32,4096]{1,0:T(8,128)S(1)}, u32[]{:S(2)}, u32[]{:S(2)}) collective-permute-start(f32[32,4096]{1,0:T(8,128)S(1)} %pad_maximum_fusion.5.refs_0_), channel_id=1, source_target_pairs={{0,8},{1,9},{2,10},{3,11},{4,12},{5,13},{6,14},{7,15},{8,0},{9,1},... | collective-permute-start | bytes 1572872 | tf_op jit(solution)/shard_map/ppermute | solution.py:373
  7.0 2.2 %collective-permute-start.4 = (f32[32,4096]{1,0:T(8,128)S(1)}, f32[32,4096]{1,0:T(8,128)S(1)}, u32[]{:S(2)}, u32[]{:S(2)}) collective-permute-start(f32[32,4096]{1,0:T(8,128)S(1)} %pad_maximum_fusion.5.refs_0_), channel_id=1, source_target_pairs={{0,6},{1,7},{2,0},{3,1},{4,2},{5,3},{6,4},{7,5},{8,14},{9,15},{10,... | collective-permute-start | bytes 1572872 | tf_op jit(solution)/shard_map/ppermute | solution.py:373
  9.2 0.0 collective-permute-done.refs_1_
  9.2 0.0 collective-permute-done.1.refs_9_.refs_12_.refs_14_
  9.3 1.9 %collective-permute-start.7 = (f32[32,4096]{1,0:T(8,128)}, f32[32,4096]{1,0:T(8,128)S(1)}, u32[]{:S(2)}, u32[]{:S(2)}) collective-permute-start(f32[32,4096]{1,0:T(8,128)} %collective-permute-done.refs_1_), channel_id=1, source_target_pairs={{0,8},{1,9},{2,10},{3,11},{4,12},{5,13},{6,14},{7,15},{8,0},{9,1},... | collective-permute-start | bytes 1572872 | tf_op jit(solution)/shard_map/ppermute | solution.py:373
  11.2 1.9 %collective-permute-start.3 = (f32[32,4096]{1,0:T(8,128)}, f32[32,4096]{1,0:T(8,128)S(1)}, u32[]{:S(2)}, u32[]{:S(2)}) collective-permute-start(f32[32,4096]{1,0:T(8,128)} %collective-permute-done.refs_1_), channel_id=1, source_target_pairs={{0,2},{1,3},{2,4},{3,5},{4,6},{5,7},{6,0},{7,1},{8,10},{9,11},{10,... | collective-permute-start | bytes 1572872 | tf_op jit(solution)/shard_map/ppermute | solution.py:373
  13.1 0.1 stack.39.where_ref
  13.2 5.7 %collective-permute-done.2.refs_2_ = f32[32,4096]{1,0:T(8,128)S(1)} collective-permute-done((f32[32,4096]{1,0:T(8,128)S(1)}, f32[32,4096]{1,0:T(8,128)S(1)}, u32[]{:S(2)}, u32[]{:S(2)}) %collective-permute-start.2) | collective-permute-done | bytes 524320 | tf_op jit(solution)/shard_map/ppermute | solution.py:373
  18.9 2.1 %collective-permute-start.5 = (f32[32,4096]{1,0:T(8,128)}, f32[32,4096]{1,0:T(8,128)S(1)}, u32[]{:S(2)}, u32[]{:S(2)}) collective-permute-start(f32[32,4096]{1,0:T(8,128)} %collective-permute-done.refs_1_), channel_id=1, source_target_pairs={{0,6},{1,7},{2,0},{3,1},{4,2},{5,3},{6,4},{7,5},{8,14},{9,15},{10,... | collective-permute-start | bytes 1572872 | tf_op jit(solution)/shard_map/ppermute | solution.py:373
  21.0 0.0 copy-start
  21.0 0.0 collective-permute-done.6.refs_6_
  21.0 0.0 copy-start.6
  21.0 0.1 collective-permute-done.4.refs_4_
  21.1 9.2 %collective-permute-done.7.refs_7_ = f32[32,4096]{1,0:T(8,128)S(1)} collective-permute-done((f32[32,4096]{1,0:T(8,128)}, f32[32,4096]{1,0:T(8,128)S(1)}, u32[]{:S(2)}, u32[]{:S(2)}) %collective-permute-start.7) | collective-permute-done | bytes 524320 | tf_op jit(solution)/shard_map/ppermute | solution.py:373
  30.3 0.0 collective-permute-done.3.refs_3_
  30.4 0.0 copy-start.4
  30.4 1.4 %collective-permute-done.5.refs_5_ = f32[32,4096]{1,0:T(8,128)S(1)} collective-permute-done((f32[32,4096]{1,0:T(8,128)}, f32[32,4096]{1,0:T(8,128)S(1)}, u32[]{:S(2)}, u32[]{:S(2)}) %collective-permute-start.5) | collective-permute-done | bytes 524320 | tf_op jit(solution)/shard_map/ppermute | solution.py:373
  31.8 0.4 pad_maximum_fusion.4
  32.2 0.0 copy-done.6
  32.2 0.0 copy-done.4
  32.2 1.8 %collective-permute-start.8 = (f32[128,2048]{1,0:T(8,128)S(1)}, f32[128,2048]{1,0:T(8,128)S(1)}, u32[]{:S(2)}, u32[]{:S(2)}) collective-permute-start(f32[128,2048]{1,0:T(8,128)S(1)} %get-tuple-element.31), channel_id=1, source_target_pairs={{0,2},{1,3},{2,4},{3,5},{4,6},{5,7},{6,0},{7,1},{8,10},{9,11},{10,... | collective-permute-start | bytes 3145736 | tf_op jit(solution)/shard_map/ppermute | solution.py:373
  34.0 0.0 copy-done.9
  34.0 0.0 copy-done.12
  34.0 1.9 %collective-permute-start.9 = (f32[128,2048]{1,0:T(8,128)S(1)}, f32[128,2048]{1,0:T(8,128)S(1)}, u32[]{:S(2)}, u32[]{:S(2)}) collective-permute-start(f32[128,2048]{1,0:T(8,128)S(1)} %get-tuple-element.30), channel_id=1, source_target_pairs={{0,6},{1,7},{2,0},{3,1},{4,2},{5,3},{6,4},{7,5},{8,14},{9,15},{10,... | collective-permute-start | bytes 3145736 | tf_op jit(solution)/shard_map/ppermute | solution.py:373
  35.9 2.7 %collective-permute-start.10 = (f32[128,2048]{1,0:T(8,128)S(1)}, f32[128,2048]{1,0:T(8,128)S(1)}, u32[]{:S(2)}, u32[]{:S(2)}) collective-permute-start(f32[128,2048]{1,0:T(8,128)S(1)} %get-tuple-element.29), channel_id=1, source_target_pairs={{0,8},{1,9},{2,10},{3,11},{4,12},{5,13},{6,14},{7,15},{8,0},{9,1},... | collective-permute-start | bytes 3145736 | tf_op jit(solution)/shard_map/ppermute | solution.py:373
  38.5 0.0 copy-done
  38.5 1.0 copy-done.5
  39.6 1.0 copy-done.7
  40.6 1.0 copy-done.10
  41.7 1.0 copy-done.13
  42.7 6.1 %gram_near.1.refs_15_ = f32[512,256]{1,0:T(8,128)S(1)} custom-call(s32[9]{0:T(128)S(1)} %stack.39.where_ref, f32[32,4096]{1,0:T(8,128)S(1)} %pad_maximum_fusion.5.refs_0_, f32[32,4096]{1,0:T(8,128)} %collective-permute-done.refs_1_, f32[32,4096]{1,0:T(8,128)S(1)} %collective-permute-done.2.refs_2_, f32[32,4096]{1,0:T(8,128)S(1)} %copy-done.5, ...), custom_call_target="tpu_custom_call" | custom-call | flops 16106127360 | bytes 12582912 | tf_op jit(solution)/shard_map/gram_near/pallas_call | solution.py:435
  48.8 8.4 %collective-permute-done.8.refs_8_ = f32[128,2048]{1,0:T(8,128)S(1)} collective-permute-done((f32[128,2048]{1,0:T(8,128)S(1)}, f32[128,2048]{1,0:T(8,128)S(1)}, u32[]{:S(2)}, u32[]{:S(2)}) %collective-permute-start.8) | collective-permute-done | bytes 1048608 | tf_op jit(solution)/shard_map/ppermute | solution.py:373
  57.2 0.0 collective-permute-done.9.refs_9_
  57.3 1.7 %collective-permute-start.11 = (f32[64,2048]{1,0:T(8,128)S(1)}, f32[64,2048]{1,0:T(8,128)S(1)}, u32[]{:S(2)}, u32[]{:S(2)}) collective-permute-start(f32[64,2048]{1,0:T(8,128)S(1)} %slice.42), channel_id=1, source_target_pairs={{0,2},{1,3},{2,4},{3,5},{4,6},{5,7},{6,0},{7,1},{8,10},{9,11},{10,... | collective-permute-start | bytes 1572872 | tf_op jit(solution)/shard_map/ppermute | solution.py:373
  59.1 2.8 %collective-permute-start.12 = (f32[64,2048]{1,0:T(8,128)S(1)}, f32[64,2048]{1,0:T(8,128)S(1)}, u32[]{:S(2)}, u32[]{:S(2)}) collective-permute-start(f32[64,2048]{1,0:T(8,128)S(1)} %slice.43), channel_id=1, source_target_pairs={{0,8},{1,9},{2,10},{3,11},{4,12},{5,13},{6,14},{7,15},{8,0},{9,1},... | collective-permute-start | bytes 1572872 | tf_op jit(solution)/shard_map/ppermute | solution.py:373
  61.8 0.0 collective-permute-done.10.refs_10_
  61.8 8.1 %gram_middle.1.refs_16_ = f32[768,256]{1,0:T(8,128)S(1)} custom-call(s32[9]{0:T(128)S(1)} %stack.39.where_ref, f32[32,4096]{1,0:T(8,128)S(1)} %pad_maximum_fusion.5.refs_0_, f32[32,4096]{1,0:T(8,128)} %collective-permute-done.refs_1_, f32[32,4096]{1,0:T(8,128)S(1)} %collective-permute-done.2.refs_2_, f32[32,4096]{1,0:T(8,128)S(1)} %copy-done.5, ...), custom_call_target="tpu_custom_call" | custom-call | flops 25769803776 | bytes 12582912 | tf_op jit(solution)/shard_map/gram_middle/pallas_call | solution.py:435
  70.0 0.0 collective-permute-done.11.refs_11_
  70.0 0.0 copy-start.18
  70.0 1.7 %collective-permute-done.12.refs_12_ = f32[64,2048]{1,0:T(8,128)S(1)} collective-permute-done((f32[64,2048]{1,0:T(8,128)S(1)}, f32[64,2048]{1,0:T(8,128)S(1)}, u32[]{:S(2)}, u32[]{:S(2)}) %collective-permute-start.12) | collective-permute-done | bytes 524320 | tf_op jit(solution)/shard_map/ppermute | solution.py:373
  71.7 0.0 copy-done.3
  71.7 0.0 copy-done.15
  71.7 0.0 copy-done.1
  71.8 6.9 %gram_last.1 = (f32[1152,128]{1,0:T(8,128)S(1)}, f32[1152,128]{1,0:T(8,128)S(1)}) custom-call(s32[9]{0:T(128)S(1)} %stack.39.where_ref, f32[32,4096]{1,0:T(8,128)S(1)} %pad_maximum_fusion.5.refs_0_, f32[32,4096]{1,0:T(8,128)} %collective-permute-done.refs_1_, f32[32,4096]{1,0:T(8,128)S(1)} %collective-permute-done.2.refs_2_, f32[32,4096]{1,0:T(8,128)S(1)} %copy-done.5, ...), custom_call_target="tpu_custom_call" | custom-call | flops 12884901888 | bytes 12582912 | tf_op jit(solution)/shard_map/gram_last/pallas_call | solution.py:435
  78.7 0.1 collective-permute-start.13
  78.8 2.0 %collective-permute-done.13 = f32[1152,128]{1,0:T(8,128)S(1)} collective-permute-done((f32[1152,128]{1,0:T(8,128)S(1)}, f32[1152,128]{1,0:T(8,128)S(1)}, u32[]{:S(2)}, u32[]{:S(2)}) %collective-permute-start.13) | collective-permute-done | bytes 589856 | tf_op jit(solution)/shard_map/ppermute | solution.py:373
  80.8 0.1 add.93
  80.9 16.3 %all_to_all.10 = f32[8,144,128]{2,1,0:T(8,128)} all-to-all(f32[8,144,128]{2,1,0:T(8,128)S(1)} %bitcast.21), channel_id=1, replica_groups=mesh['row'=8,'col'=16] {'row'}, dimensions={0} | all-to-all | bytes 1179648 | tf_op jit(solution)/shard_map/all_to_all | solution.py:485
  97.2 1.1 reduce_sum.9
  98.3 13.0 %all_to_all.11 = f32[8,144,128]{2,1,0:T(8,128)S(1)} all-to-all(f32[8,144,128]{2,1,0:T(8,128)S(1)} %broadcast_in_dim.10), channel_id=1, replica_groups=mesh['row'=8,'col'=16] {'row'}, dimensions={0} | all-to-all | bytes 1179648 | tf_op jit(solution)/shard_map/all_to_all | solution.py:488
  111.3 0.0 collective-permute-start.14
  111.3 2.0 %collective-permute-done.14.refs_16_ = f32[1152,128]{1,0:T(8,128)S(1)} collective-permute-done((f32[1152,128]{1,0:T(8,128)S(1)}, f32[1152,128]{1,0:T(8,128)S(1)}, u32[]{:S(2)}, u32[]{:S(2)}) %collective-permute-start.14) | collective-permute-done | bytes 589856 | tf_op jit(solution)/shard_map/ppermute | solution.py:373
  113.3 11.8 %solve_apply.1 = (f32[4096,128]{1,0:T(8,128)S(1)}, f32[4096,128]{1,0:T(8,128)S(1)}) custom-call(s32[9]{0:T(128)S(1)} %stack.39.where_ref, f32[32,4096]{1,0:T(8,128)S(1)} %pad_maximum_fusion.5.refs_0_, f32[32,4096]{1,0:T(8,128)} %collective-permute-done.refs_1_, f32[32,4096]{1,0:T(8,128)} %copy-done.3, f32[32,4096]{1,0:T(8,128)} %copy-done.4, ...), custom_call_target="tpu_custom_call" | custom-call | tf_op jit(solution)/shard_map/solve_apply/pallas_call | solution.py:494
  125.1 0.2 collective-permute-start.15
  125.3 0.3 broadcast_in_dim.4
  125.6 0.2 constant_dynamic-update-slice_fusion.1
  125.8 0.0 copy-start.20
  125.8 3.6 %collective-permute-done.15 = f32[4096,128]{1,0:T(8,128)S(1)} collective-permute-done((f32[4096,128]{1,0:T(8,128)S(1)}, f32[4096,128]{1,0:T(8,128)S(1)}, u32[]{:S(2)}, u32[]{:S(2)}) %collective-permute-start.15) | collective-permute-done | bytes 2097184 | tf_op jit(solution)/shard_map/ppermute | solution.py:373
  129.4 0.0 copy-done.20
  129.4 1.5 %constant_dynamic-update-slice_fusion = f32[8192,128]{1,0:T(8,128)} fusion(f32[8192,128]{1,0:T(8,128)} %copy-done.20, f32[4096,128]{1,0:T(8,128)S(1)} %collective-permute-done.15, s32[]{:T(128)S(6)} %select_n.61), kind=kLoop, calls=%fused_computation.11 | loop fusion | bytes 4194308 | tf_op jit(solution)/shard_map/dynamic_update_slice | solution.py:520
  (35 shorter events, 0.4 us)
Async XLA Ops:
  0.0 9.2 %collective-permute-start.1 = (f32[8192,128]{1,0:T(8,128)}, f32[8192,128]{1,0:T(8,128)}, u32[]{:S(2)}, u32[]{:S(2)}) collective-permute-start(f32[8192,128]{1,0:T(8,128)} %refs_13_.3), channel_id=1, source_target_pairs={{0,1},{1,0},{2,3},{3,2},{4,5},{5,4},{6,7},{7,6},{8,9},{9,8},{10,11... | collective-permute-start | bytes 12582920 | tf_op jit(solution)/shard_map/ppermute | solution.py:373
  1.3 7.9 %collective-permute-start = (f32[32,4096]{1,0:T(8,128)S(1)}, f32[32,4096]{1,0:T(8,128)}, u32[]{:S(2)}, u32[]{:S(2)}) collective-permute-start(f32[32,4096]{1,0:T(8,128)S(1)} %pad_maximum_fusion.6), channel_id=1, source_target_pairs={{0,1},{1,0},{2,3},{3,2},{4,5},{5,4},{6,7},{7,6},{8,9},{9,8},{10,11... | collective-permute-start | bytes 1572872 | tf_op jit(solution)/shard_map/ppermute | solution.py:373
  1.9 16.9 %collective-permute-start.2 = (f32[32,4096]{1,0:T(8,128)S(1)}, f32[32,4096]{1,0:T(8,128)S(1)}, u32[]{:S(2)}, u32[]{:S(2)}) collective-permute-start(f32[32,4096]{1,0:T(8,128)S(1)} %pad_maximum_fusion.5.refs_0_), channel_id=1, source_target_pairs={{0,2},{1,3},{2,4},{3,5},{4,6},{5,7},{6,0},{7,1},{8,10},{9,11},{10,... | collective-permute-start | bytes 1572872 | tf_op jit(solution)/shard_map/ppermute | solution.py:373
  4.0 17.0 %collective-permute-start.6 = (f32[32,4096]{1,0:T(8,128)S(1)}, f32[32,4096]{1,0:T(8,128)S(1)}, u32[]{:S(2)}, u32[]{:S(2)}) collective-permute-start(f32[32,4096]{1,0:T(8,128)S(1)} %pad_maximum_fusion.5.refs_0_), channel_id=1, source_target_pairs={{0,8},{1,9},{2,10},{3,11},{4,12},{5,13},{6,14},{7,15},{8,0},{9,1},... | collective-permute-start | bytes 1572872 | tf_op jit(solution)/shard_map/ppermute | solution.py:373
  7.0 14.1 %collective-permute-start.4 = (f32[32,4096]{1,0:T(8,128)S(1)}, f32[32,4096]{1,0:T(8,128)S(1)}, u32[]{:S(2)}, u32[]{:S(2)}) collective-permute-start(f32[32,4096]{1,0:T(8,128)S(1)} %pad_maximum_fusion.5.refs_0_), channel_id=1, source_target_pairs={{0,6},{1,7},{2,0},{3,1},{4,2},{5,3},{6,4},{7,5},{8,14},{9,15},{10,... | collective-permute-start | bytes 1572872 | tf_op jit(solution)/shard_map/ppermute | solution.py:373
  9.3 21.1 %collective-permute-start.7 = (f32[32,4096]{1,0:T(8,128)}, f32[32,4096]{1,0:T(8,128)S(1)}, u32[]{:S(2)}, u32[]{:S(2)}) collective-permute-start(f32[32,4096]{1,0:T(8,128)} %collective-permute-done.refs_1_), channel_id=1, source_target_pairs={{0,8},{1,9},{2,10},{3,11},{4,12},{5,13},{6,14},{7,15},{8,0},{9,1},... | collective-permute-start | bytes 1572872 | tf_op jit(solution)/shard_map/ppermute | solution.py:373
  11.2 19.2 %collective-permute-start.3 = (f32[32,4096]{1,0:T(8,128)}, f32[32,4096]{1,0:T(8,128)S(1)}, u32[]{:S(2)}, u32[]{:S(2)}) collective-permute-start(f32[32,4096]{1,0:T(8,128)} %collective-permute-done.refs_1_), channel_id=1, source_target_pairs={{0,2},{1,3},{2,4},{3,5},{4,6},{5,7},{6,0},{7,1},{8,10},{9,11},{10,... | collective-permute-start | bytes 1572872 | tf_op jit(solution)/shard_map/ppermute | solution.py:373
  18.9 52.9 %copy-start.3 = (f32[32,4096]{1,0:T(8,128)}, f32[32,4096]{1,0:T(8,128)S(1)}, u32[]{:S(2)}) copy-start(f32[32,4096]{1,0:T(8,128)S(1)} %collective-permute-done.2.refs_2_) | copy-start | bytes 1572868
  18.9 12.9 %collective-permute-start.5 = (f32[32,4096]{1,0:T(8,128)}, f32[32,4096]{1,0:T(8,128)S(1)}, u32[]{:S(2)}, u32[]{:S(2)}) collective-permute-start(f32[32,4096]{1,0:T(8,128)} %collective-permute-done.refs_1_), channel_id=1, source_target_pairs={{0,6},{1,7},{2,0},{3,1},{4,2},{5,3},{6,4},{7,5},{8,14},{9,15},{10,... | collective-permute-start | bytes 1572872 | tf_op jit(solution)/shard_map/ppermute | solution.py:373
  21.0 17.6 %copy-start = (f32[8192,128]{1,0:T(8,128)S(1)}, f32[8192,128]{1,0:T(8,128)}, u32[]{:S(2)}) copy-start(f32[8192,128]{1,0:T(8,128)} %refs_13_.3) | copy-start | bytes 12582916
  21.0 11.2 %copy-start.6 = (f32[32,4096]{1,0:T(8,128)}, f32[32,4096]{1,0:T(8,128)S(1)}, u32[]{:S(2)}) copy-start(f32[32,4096]{1,0:T(8,128)S(1)} %collective-permute-done.6.refs_6_) | copy-start | bytes 1572868
  21.1 12.8 %copy-start.9 = (f32[32,4096]{1,0:T(8,128)}, f32[32,4096]{1,0:T(8,128)S(1)}, u32[]{:S(2)}) copy-start(f32[32,4096]{1,0:T(8,128)S(1)} %collective-permute-done.4.refs_4_) | copy-start | bytes 1572868
  30.3 3.7 %copy-start.12 = (f32[32,4096]{1,0:T(8,128)}, f32[32,4096]{1,0:T(8,128)S(1)}, u32[]{:S(2)}) copy-start(f32[32,4096]{1,0:T(8,128)S(1)} %collective-permute-done.7.refs_7_) | copy-start | bytes 1572868
  30.4 1.8 %copy-start.4 = (f32[32,4096]{1,0:T(8,128)}, f32[32,4096]{1,0:T(8,128)S(1)}, u32[]{:S(2)}) copy-start(f32[32,4096]{1,0:T(8,128)S(1)} %collective-permute-done.3.refs_3_) | copy-start | bytes 1572868
  31.8 39.9 %copy-start.15 = (f32[32,4096]{1,0:T(8,128)}, f32[32,4096]{1,0:T(8,128)S(1)}, u32[]{:S(2)}) copy-start(f32[32,4096]{1,0:T(8,128)S(1)} %collective-permute-done.5.refs_5_) | copy-start | bytes 1572868
  32.2 25.1 %collective-permute-start.8 = (f32[128,2048]{1,0:T(8,128)S(1)}, f32[128,2048]{1,0:T(8,128)S(1)}, u32[]{:S(2)}, u32[]{:S(2)}) collective-permute-start(f32[128,2048]{1,0:T(8,128)S(1)} %get-tuple-element.31), channel_id=1, source_target_pairs={{0,2},{1,3},{2,4},{3,5},{4,6},{5,7},{6,0},{7,1},{8,10},{9,11},{10,... | collective-permute-start | bytes 3145736 | tf_op jit(solution)/shard_map/ppermute | solution.py:373
  34.0 23.3 %collective-permute-start.9 = (f32[128,2048]{1,0:T(8,128)S(1)}, f32[128,2048]{1,0:T(8,128)S(1)}, u32[]{:S(2)}, u32[]{:S(2)}) collective-permute-start(f32[128,2048]{1,0:T(8,128)S(1)} %get-tuple-element.30), channel_id=1, source_target_pairs={{0,6},{1,7},{2,0},{3,1},{4,2},{5,3},{6,4},{7,5},{8,14},{9,15},{10,... | collective-permute-start | bytes 3145736 | tf_op jit(solution)/shard_map/ppermute | solution.py:373
  35.9 26.0 %collective-permute-start.10 = (f32[128,2048]{1,0:T(8,128)S(1)}, f32[128,2048]{1,0:T(8,128)S(1)}, u32[]{:S(2)}, u32[]{:S(2)}) collective-permute-start(f32[128,2048]{1,0:T(8,128)S(1)} %get-tuple-element.29), channel_id=1, source_target_pairs={{0,8},{1,9},{2,10},{3,11},{4,12},{5,13},{6,14},{7,15},{8,0},{9,1},... | collective-permute-start | bytes 3145736 | tf_op jit(solution)/shard_map/ppermute | solution.py:373
  38.5 1.0 copy-start.5
  39.6 1.0 copy-start.7
  40.6 1.0 copy-start.10
  41.7 1.0 copy-start.13
  57.2 14.5 %copy-start.1 = (f32[128,2048]{1,0:T(8,128)}, f32[128,2048]{1,0:T(8,128)S(1)}, u32[]{:S(2)}) copy-start(f32[128,2048]{1,0:T(8,128)S(1)} %collective-permute-done.8.refs_8_) | copy-start | bytes 3145732
  57.3 14.4 %copy-start.2 = (f32[128,2048]{1,0:T(8,128)}, f32[128,2048]{1,0:T(8,128)S(1)}, u32[]{:S(2)}) copy-start(f32[128,2048]{1,0:T(8,128)S(1)} %collective-permute-done.9.refs_9_) | copy-start | bytes 3145732
  57.3 12.6 %collective-permute-start.11 = (f32[64,2048]{1,0:T(8,128)S(1)}, f32[64,2048]{1,0:T(8,128)S(1)}, u32[]{:S(2)}, u32[]{:S(2)}) collective-permute-start(f32[64,2048]{1,0:T(8,128)S(1)} %slice.42), channel_id=1, source_target_pairs={{0,2},{1,3},{2,4},{3,5},{4,6},{5,7},{6,0},{7,1},{8,10},{9,11},{10,... | collective-permute-start | bytes 1572872 | tf_op jit(solution)/shard_map/ppermute | solution.py:373
  59.1 12.6 %collective-permute-start.12 = (f32[64,2048]{1,0:T(8,128)S(1)}, f32[64,2048]{1,0:T(8,128)S(1)}, u32[]{:S(2)}, u32[]{:S(2)}) collective-permute-start(f32[64,2048]{1,0:T(8,128)S(1)} %slice.43), channel_id=1, source_target_pairs={{0,8},{1,9},{2,10},{3,11},{4,12},{5,13},{6,14},{7,15},{8,0},{9,1},... | collective-permute-start | bytes 1572872 | tf_op jit(solution)/shard_map/ppermute | solution.py:373
  61.8 9.9 %copy-start.17 = (f32[128,2048]{1,0:T(8,128)}, f32[128,2048]{1,0:T(8,128)S(1)}, u32[]{:S(2)}) copy-start(f32[128,2048]{1,0:T(8,128)S(1)} %collective-permute-done.10.refs_10_) | copy-start | bytes 3145732
  70.0 8.7 %copy-start.18 = (f32[64,2048]{1,0:T(8,128)}, f32[64,2048]{1,0:T(8,128)S(1)}, u32[]{:S(2)}) copy-start(f32[64,2048]{1,0:T(8,128)S(1)} %collective-permute-done.11.refs_11_) | copy-start | bytes 1572868
  71.7 6.9 %copy-start.19 = (f32[64,2048]{1,0:T(8,128)}, f32[64,2048]{1,0:T(8,128)S(1)}, u32[]{:S(2)}) copy-start(f32[64,2048]{1,0:T(8,128)S(1)} %collective-permute-done.12.refs_12_) | copy-start | bytes 1572868
  78.7 34.6 %copy-start.8 = (f32[32,4096]{1,0:T(8,128)S(1)}, f32[32,4096]{1,0:T(8,128)}, u32[]{:S(2)}) copy-start(f32[32,4096]{1,0:T(8,128)} %copy-done.6) | copy-start | bytes 1572868
  78.7 34.6 %copy-start.11 = (f32[32,4096]{1,0:T(8,128)S(1)}, f32[32,4096]{1,0:T(8,128)}, u32[]{:S(2)}) copy-start(f32[32,4096]{1,0:T(8,128)} %copy-done.9) | copy-start | bytes 1572868
  78.7 34.6 %copy-start.14 = (f32[32,4096]{1,0:T(8,128)S(1)}, f32[32,4096]{1,0:T(8,128)}, u32[]{:S(2)}) copy-start(f32[32,4096]{1,0:T(8,128)} %copy-done.12) | copy-start | bytes 1572868
  78.7 34.6 %copy-start.16 = (f32[32,4096]{1,0:T(8,128)S(1)}, f32[32,4096]{1,0:T(8,128)}, u32[]{:S(2)}) copy-start(f32[32,4096]{1,0:T(8,128)} %copy-done.15) | copy-start | bytes 1572868
  78.7 2.1 %collective-permute-start.13 = (f32[1152,128]{1,0:T(8,128)S(1)}, f32[1152,128]{1,0:T(8,128)S(1)}, u32[]{:S(2)}, u32[]{:S(2)}) collective-permute-start(f32[1152,128]{1,0:T(8,128)S(1)} %get-tuple-element.26), channel_id=1, source_target_pairs={{0,1},{1,0},{2,3},{3,2},{4,5},{5,4},{6,7},{7,6},{8,9},{9,8},{10,11... | collective-permute-start | bytes 1769480 | tf_op jit(solution)/shard_map/ppermute | solution.py:373
  111.3 2.0 %collective-permute-start.14 = (f32[1152,128]{1,0:T(8,128)S(1)}, f32[1152,128]{1,0:T(8,128)S(1)}, u32[]{:S(2)}, u32[]{:S(2)}) collective-permute-start(f32[1152,128]{1,0:T(8,128)S(1)} %bitcast.19), channel_id=1, source_target_pairs={{0,1},{1,0},{2,3},{3,2},{4,5},{5,4},{6,7},{7,6},{8,9},{9,8},{10,11... | collective-permute-start | bytes 1769480 | tf_op jit(solution)/shard_map/ppermute | solution.py:373
  125.1 4.2 %collective-permute-start.15 = (f32[4096,128]{1,0:T(8,128)S(1)}, f32[4096,128]{1,0:T(8,128)S(1)}, u32[]{:S(2)}, u32[]{:S(2)}) collective-permute-start(f32[4096,128]{1,0:T(8,128)S(1)} %get-tuple-element.28), channel_id=1, source_target_pairs={{0,1},{1,0},{2,3},{3,2},{4,5},{5,4},{6,7},{7,6},{8,9},{9,8},{10,11... | collective-permute-start | bytes 6291464 | tf_op jit(solution)/shard_map/ppermute | solution.py:373
  125.8 3.6 %copy-start.20 = (f32[8192,128]{1,0:T(8,128)}, f32[8192,128]{1,0:T(8,128)S(1)}, u32[]{:S(2)}) copy-start(f32[8192,128]{1,0:T(8,128)S(1)} %constant_dynamic-update-slice_fusion.1) | copy-start | bytes 12582916

commit v14 on v12

--- a/solution.py
+++ b/solution.py
@@ -255,7 +255,7 @@
             jnp.where(row < column, value, jnp.where(row == column, value * 0.5, 0.0))
         )
     lane = lax.broadcasted_iota(jnp.int32, (base, WIDE), 1) % base
-    ones = jnp.where(same, 1.0, 0.0).astype(F32)
+    ones = jnp.where(same, 1.0, 0.0).astype(BF16)
     spread = []
     for i in range(count):
         flipped = jnp.where(same, diagonals[i], 0.0).T
@@ -263,7 +263,11 @@
         for k in range(1, WIDE // base):
             folded = folded + flipped[k * base : (k + 1) * base]
         stacked = jnp.concatenate([jnp.where(lane == k, folded, 0.0) for k in range(base)], axis=0)
-        spread.append(full(stacked, ones))
+        high = stacked.astype(BF16)
+        rest = stacked - high.astype(F32)
+        middle = rest.astype(BF16)
+        low = (rest - middle.astype(F32)).astype(BF16)
+        spread.append((nn(low, ones) + nn(middle, ones)) + nn(high, ones))
     wide_lane = lax.broadcasted_iota(jnp.int32, (1, size), 1) % base
     wide_row = lax.broadcasted_iota(jnp.int32, (base, size), 0)
     solved = jnp.zeros((base, size), F32)

time: 132 us -> 131 us (level)
  no operation moved by 1% of the time
where the time goes in v14:
time: 131 us; the launch traced here: 130 us
  waiting for transfers between devices  33.8 us (26%)
  Pallas kernels  33.5 us (26%)
  blocking collectives  29.2 us (22%)
  starting transfers between devices  24.9 us (19%)
  local copies, waits for them, and re-layouts  7.75 us (6%)
    ppermute x16, waiting for transfers between devices, permute(): return lax.ppermute(value, 'col', pairs)  33.8 us
    ppermute x16, starting transfers between devices, permute(): return lax.ppermute(value, 'col', pairs)  24.9 us
    pallas_call x3, Pallas kernels, products(): pl.pallas_call(kernel, out_shape=[jax.ShapeDtypeStruct(v, F32) for v in s...  21.6 us
    all_to_all x1, blocking collectives, per_device(): lax.all_to_all(mine.reshape(members, length // members, WIDE), 'row', 0, 0)  16.2 us
    all_to_all x1, blocking collectives, per_device(): mine = lax.all_to_all(spread, 'row', 0, 0).reshape(length, WIDE)  13 us
    pallas_call x1, Pallas kernels, per_device(): pl.pallas_call(apply_kernel, out_shape=[jax.ShapeDtypeStruct((half, colum...  11.9 us
    unnamed x36, local copies, waits for them, and re-layouts  4.22 us
  transfers between devices with their start and end apart: 16, of which 9 were waited for; matrix products, arithmetic and copies ran while one was open for 2% of the time, Pallas kernels for 11%

profile of v14, /device:TPU:0, one launch (start us, length us, event | category | flops | bytes accessed | tf_op | source)
XLA Modules:
  0.0 129.9 jit_solution(4548233594348596435)
XLA Ops:
  0.0 0.0 collective-permute-start.1
  0.0 1.3 dynamic-slice_bitcast_fusion
  1.3 0.6 collective-permute-start
  1.9 0.0 copy-start.3
  1.9 2.1 %collective-permute-start.2 = (f32[32,4096]{1,0:T(8,128)S(1)}, f32[32,4096]{1,0:T(8,128)S(1)}, u32[]{:S(2)}, u32[]{:S(2)}) collective-permute-start(f32[32,4096]{1,0:T(8,128)S(1)} %pad_maximum_fusion.5.refs_0_), channel_id=1, source_target_pairs={{0,2},{1,3},{2,4},{3,5},{4,6},{5,7},{6,0},{7,1},{8,10},{9,11},{10,... | collective-permute-start | bytes 1572872 | tf_op jit(solution)/shard_map/ppermute | solution.py:377
  4.0 3.0 %collective-permute-start.6 = (f32[32,4096]{1,0:T(8,128)S(1)}, f32[32,4096]{1,0:T(8,128)S(1)}, u32[]{:S(2)}, u32[]{:S(2)}) collective-permute-start(f32[32,4096]{1,0:T(8,128)S(1)} %pad_maximum_fusion.5.refs_0_), channel_id=1, source_target_pairs={{0,8},{1,9},{2,10},{3,11},{4,12},{5,13},{6,14},{7,15},{8,0},{9,1},... | collective-permute-start | bytes 1572872 | tf_op jit(solution)/shard_map/ppermute | solution.py:377
  7.0 2.2 %collective-permute-start.4 = (f32[32,4096]{1,0:T(8,128)S(1)}, f32[32,4096]{1,0:T(8,128)S(1)}, u32[]{:S(2)}, u32[]{:S(2)}) collective-permute-start(f32[32,4096]{1,0:T(8,128)S(1)} %pad_maximum_fusion.5.refs_0_), channel_id=1, source_target_pairs={{0,6},{1,7},{2,0},{3,1},{4,2},{5,3},{6,4},{7,5},{8,14},{9,15},{10,... | collective-permute-start | bytes 1572872 | tf_op jit(solution)/shard_map/ppermute | solution.py:377
  9.3 0.0 collective-permute-done.refs_1_
  9.3 0.0 collective-permute-done.1.refs_9_.refs_12_.refs_14_
  9.3 1.9 %collective-permute-start.7 = (f32[32,4096]{1,0:T(8,128)}, f32[32,4096]{1,0:T(8,128)S(1)}, u32[]{:S(2)}, u32[]{:S(2)}) collective-permute-start(f32[32,4096]{1,0:T(8,128)} %collective-permute-done.refs_1_), channel_id=1, source_target_pairs={{0,8},{1,9},{2,10},{3,11},{4,12},{5,13},{6,14},{7,15},{8,0},{9,1},... | collective-permute-start | bytes 1572872 | tf_op jit(solution)/shard_map/ppermute | solution.py:377
  11.2 1.9 %collective-permute-start.3 = (f32[32,4096]{1,0:T(8,128)}, f32[32,4096]{1,0:T(8,128)S(1)}, u32[]{:S(2)}, u32[]{:S(2)}) collective-permute-start(f32[32,4096]{1,0:T(8,128)} %collective-permute-done.refs_1_), channel_id=1, source_target_pairs={{0,2},{1,3},{2,4},{3,5},{4,6},{5,7},{6,0},{7,1},{8,10},{9,11},{10,... | collective-permute-start | bytes 1572872 | tf_op jit(solution)/shard_map/ppermute | solution.py:377
  13.1 0.1 stack.39.where_ref
  13.2 5.7 %collective-permute-done.2.refs_2_ = f32[32,4096]{1,0:T(8,128)S(1)} collective-permute-done((f32[32,4096]{1,0:T(8,128)S(1)}, f32[32,4096]{1,0:T(8,128)S(1)}, u32[]{:S(2)}, u32[]{:S(2)}) %collective-permute-start.2) | collective-permute-done | bytes 524320 | tf_op jit(solution)/shard_map/ppermute | solution.py:377
  18.9 2.1 %collective-permute-start.5 = (f32[32,4096]{1,0:T(8,128)}, f32[32,4096]{1,0:T(8,128)S(1)}, u32[]{:S(2)}, u32[]{:S(2)}) collective-permute-start(f32[32,4096]{1,0:T(8,128)} %collective-permute-done.refs_1_), channel_id=1, source_target_pairs={{0,6},{1,7},{2,0},{3,1},{4,2},{5,3},{6,4},{7,5},{8,14},{9,15},{10,... | collective-permute-start | bytes 1572872 | tf_op jit(solution)/shard_map/ppermute | solution.py:377
  21.0 0.0 copy-start
  21.0 0.0 collective-permute-done.6.refs_6_
  21.0 0.0 copy-start.7
  21.0 0.1 collective-permute-done.4.refs_4_
  21.2 9.2 %collective-permute-done.7.refs_7_ = f32[32,4096]{1,0:T(8,128)S(1)} collective-permute-done((f32[32,4096]{1,0:T(8,128)}, f32[32,4096]{1,0:T(8,128)S(1)}, u32[]{:S(2)}, u32[]{:S(2)}) %collective-permute-start.7) | collective-permute-done | bytes 524320 | tf_op jit(solution)/shard_map/ppermute | solution.py:377
  30.4 0.0 collective-permute-done.3.refs_3_
  30.4 0.0 copy-start.5
  30.4 1.4 %collective-permute-done.5.refs_5_ = f32[32,4096]{1,0:T(8,128)S(1)} collective-permute-done((f32[32,4096]{1,0:T(8,128)}, f32[32,4096]{1,0:T(8,128)S(1)}, u32[]{:S(2)}, u32[]{:S(2)}) %collective-permute-start.5) | collective-permute-done | bytes 524320 | tf_op jit(solution)/shard_map/ppermute | solution.py:377
  31.8 0.4 pad_maximum_fusion.4
  32.2 0.0 copy-done.7
  32.2 0.0 copy-done.5
  32.2 1.8 %collective-permute-start.8 = (f32[128,2048]{1,0:T(8,128)S(1)}, f32[128,2048]{1,0:T(8,128)S(1)}, u32[]{:S(2)}, u32[]{:S(2)}) collective-permute-start(f32[128,2048]{1,0:T(8,128)S(1)} %get-tuple-element.31), channel_id=1, source_target_pairs={{0,2},{1,3},{2,4},{3,5},{4,6},{5,7},{6,0},{7,1},{8,10},{9,11},{10,... | collective-permute-start | bytes 3145736 | tf_op jit(solution)/shard_map/ppermute | solution.py:377
  34.0 0.0 copy-done.9
  34.0 0.0 copy-done.11
  34.0 1.9 %collective-permute-start.9 = (f32[128,2048]{1,0:T(8,128)S(1)}, f32[128,2048]{1,0:T(8,128)S(1)}, u32[]{:S(2)}, u32[]{:S(2)}) collective-permute-start(f32[128,2048]{1,0:T(8,128)S(1)} %get-tuple-element.30), channel_id=1, source_target_pairs={{0,6},{1,7},{2,0},{3,1},{4,2},{5,3},{6,4},{7,5},{8,14},{9,15},{10,... | collective-permute-start | bytes 3145736 | tf_op jit(solution)/shard_map/ppermute | solution.py:377
  35.9 2.7 %collective-permute-start.10 = (f32[128,2048]{1,0:T(8,128)S(1)}, f32[128,2048]{1,0:T(8,128)S(1)}, u32[]{:S(2)}, u32[]{:S(2)}) collective-permute-start(f32[128,2048]{1,0:T(8,128)S(1)} %get-tuple-element.29), channel_id=1, source_target_pairs={{0,8},{1,9},{2,10},{3,11},{4,12},{5,13},{6,14},{7,15},{8,0},{9,1},... | collective-permute-start | bytes 3145736 | tf_op jit(solution)/shard_map/ppermute | solution.py:377
  38.5 0.0 copy-done
  38.5 1.0 copy-done.6
  39.6 1.0 copy-done.8
  40.6 1.0 copy-done.10
  41.7 1.0 copy-done.12
  42.7 6.3 %gram_near.1.refs_15_ = f32[512,256]{1,0:T(8,128)S(1)} custom-call(s32[9]{0:T(128)S(1)} %stack.39.where_ref, f32[32,4096]{1,0:T(8,128)S(1)} %pad_maximum_fusion.5.refs_0_, f32[32,4096]{1,0:T(8,128)} %collective-permute-done.refs_1_, f32[32,4096]{1,0:T(8,128)S(1)} %collective-permute-done.2.refs_2_, f32[32,4096]{1,0:T(8,128)S(1)} %copy-done.6, ...), custom_call_target="tpu_custom_call" | custom-call | flops 16106127360 | bytes 12582912 | tf_op jit(solution)/shard_map/gram_near/pallas_call | solution.py:439
  49.0 8.3 %collective-permute-done.8.refs_8_ = f32[128,2048]{1,0:T(8,128)S(1)} collective-permute-done((f32[128,2048]{1,0:T(8,128)S(1)}, f32[128,2048]{1,0:T(8,128)S(1)}, u32[]{:S(2)}, u32[]{:S(2)}) %collective-permute-start.8) | collective-permute-done | bytes 1048608 | tf_op jit(solution)/shard_map/ppermute | solution.py:377
  57.3 0.0 collective-permute-done.9.refs_9_
  57.3 1.7 %collective-permute-start.11 = (f32[64,2048]{1,0:T(8,128)S(1)}, f32[64,2048]{1,0:T(8,128)S(1)}, u32[]{:S(2)}, u32[]{:S(2)}) collective-permute-start(f32[64,2048]{1,0:T(8,128)S(1)} %slice.42), channel_id=1, source_target_pairs={{0,2},{1,3},{2,4},{3,5},{4,6},{5,7},{6,0},{7,1},{8,10},{9,11},{10,... | collective-permute-start | bytes 1572872 | tf_op jit(solution)/shard_map/ppermute | solution.py:377
  59.1 2.8 %collective-permute-start.12 = (f32[64,2048]{1,0:T(8,128)S(1)}, f32[64,2048]{1,0:T(8,128)S(1)}, u32[]{:S(2)}, u32[]{:S(2)}) collective-permute-start(f32[64,2048]{1,0:T(8,128)S(1)} %slice.43), channel_id=1, source_target_pairs={{0,8},{1,9},{2,10},{3,11},{4,12},{5,13},{6,14},{7,15},{8,0},{9,1},... | collective-permute-start | bytes 1572872 | tf_op jit(solution)/shard_map/ppermute | solution.py:377
  61.9 0.0 collective-permute-done.10.refs_10_
  61.9 8.3 %gram_middle.1.refs_16_ = f32[768,256]{1,0:T(8,128)S(1)} custom-call(s32[9]{0:T(128)S(1)} %stack.39.where_ref, f32[32,4096]{1,0:T(8,128)S(1)} %pad_maximum_fusion.5.refs_0_, f32[32,4096]{1,0:T(8,128)} %collective-permute-done.refs_1_, f32[32,4096]{1,0:T(8,128)S(1)} %collective-permute-done.2.refs_2_, f32[32,4096]{1,0:T(8,128)S(1)} %copy-done.6, ...), custom_call_target="tpu_custom_call" | custom-call | flops 25769803776 | bytes 12582912 | tf_op jit(solution)/shard_map/gram_middle/pallas_call | solution.py:439
  70.2 0.0 collective-permute-done.11.refs_11_
  70.2 0.0 copy-start.15
  70.2 1.5 %collective-permute-done.12.refs_12_ = f32[64,2048]{1,0:T(8,128)S(1)} collective-permute-done((f32[64,2048]{1,0:T(8,128)S(1)}, f32[64,2048]{1,0:T(8,128)S(1)}, u32[]{:S(2)}, u32[]{:S(2)}) %collective-permute-start.12) | collective-permute-done | bytes 524320 | tf_op jit(solution)/shard_map/ppermute | solution.py:377
  71.7 0.0 copy-done.3
  71.7 0.0 copy-done.4
  71.7 0.0 copy-done.13
  71.7 0.0 copy-done.1
  71.8 7.0 %gram_last.1 = (f32[1152,128]{1,0:T(8,128)S(1)}, f32[1152,128]{1,0:T(8,128)S(1)}) custom-call(s32[9]{0:T(128)S(1)} %stack.39.where_ref, f32[32,4096]{1,0:T(8,128)S(1)} %pad_maximum_fusion.5.refs_0_, f32[32,4096]{1,0:T(8,128)} %collective-permute-done.refs_1_, f32[32,4096]{1,0:T(8,128)S(1)} %collective-permute-done.2.refs_2_, f32[32,4096]{1,0:T(8,128)S(1)} %copy-done.6, ...), custom_call_target="tpu_custom_call" | custom-call | flops 12884901888 | bytes 12582912 | tf_op jit(solution)/shard_map/gram_last/pallas_call | solution.py:439
  78.8 0.1 collective-permute-start.13
  78.9 2.0 %collective-permute-done.13 = f32[1152,128]{1,0:T(8,128)S(1)} collective-permute-done((f32[1152,128]{1,0:T(8,128)S(1)}, f32[1152,128]{1,0:T(8,128)S(1)}, u32[]{:S(2)}, u32[]{:S(2)}) %collective-permute-start.13) | collective-permute-done | bytes 589856 | tf_op jit(solution)/shard_map/ppermute | solution.py:377
  80.9 0.1 add.93
  81.0 16.2 %all_to_all.10 = f32[8,144,128]{2,1,0:T(8,128)S(1)} all-to-all(f32[8,144,128]{2,1,0:T(8,128)S(1)} %bitcast.21), channel_id=1, replica_groups=mesh['row'=8,'col'=16] {'row'}, dimensions={0} | all-to-all | bytes 1179648 | tf_op jit(solution)/shard_map/all_to_all | solution.py:489
  97.3 13.0 %all_to_all.11 = f32[8,144,128]{2,1,0:T(8,128)S(1)} all-to-all(f32[8,144,128]{2,1,0:T(8,128)S(1)} %broadcast_in_dim.10), channel_id=1, replica_groups=mesh['row'=8,'col'=16] {'row'}, dimensions={0} | all-to-all | bytes 1179648 | tf_op jit(solution)/shard_map/all_to_all | solution.py:492
  110.3 0.0 collective-permute-start.14
  110.3 2.0 %collective-permute-done.14.refs_16_ = f32[1152,128]{1,0:T(8,128)S(1)} collective-permute-done((f32[1152,128]{1,0:T(8,128)S(1)}, f32[1152,128]{1,0:T(8,128)S(1)}, u32[]{:S(2)}, u32[]{:S(2)}) %collective-permute-start.14) | collective-permute-done | bytes 589856 | tf_op jit(solution)/shard_map/ppermute | solution.py:377
  112.3 11.9 %solve_apply.1 = (f32[4096,128]{1,0:T(8,128)S(1)}, f32[4096,128]{1,0:T(8,128)S(1)}) custom-call(s32[9]{0:T(128)S(1)} %stack.39.where_ref, f32[32,4096]{1,0:T(8,128)} %copy-done.3, f32[32,4096]{1,0:T(8,128)} %collective-permute-done.refs_1_, f32[32,4096]{1,0:T(8,128)} %copy-done.4, f32[32,4096]{1,0:T(8,128)} %copy-done.5, f32[32,4096]{1,0:T(8,128)} %copy-done.9, ...), custom_call_target="tpu_custom_call" | custom-call | tf_op jit(solution)/shard_map/solve_apply/pallas_call | solution.py:498
  124.2 0.2 collective-permute-start.15
  124.4 0.3 broadcast_in_dim.4
  124.7 0.2 constant_dynamic-update-slice_fusion.1
  124.9 0.0 copy-start.17
  124.9 3.5 %collective-permute-done.15 = f32[4096,128]{1,0:T(8,128)S(1)} collective-permute-done((f32[4096,128]{1,0:T(8,128)S(1)}, f32[4096,128]{1,0:T(8,128)S(1)}, u32[]{:S(2)}, u32[]{:S(2)}) %collective-permute-start.15) | collective-permute-done | bytes 2097184 | tf_op jit(solution)/shard_map/ppermute | solution.py:377
  128.5 1.5 %constant_dynamic-update-slice_fusion = f32[8192,128]{1,0:T(8,128)} fusion(f32[8192,128]{1,0:T(8,128)} %copy-done.17, f32[4096,128]{1,0:T(8,128)S(1)} %collective-permute-done.15, s32[]{:T(128)S(6)} %select_n.61), kind=kLoop, calls=%fused_computation.11 | loop fusion | bytes 4194308 | tf_op jit(solution)/shard_map/dynamic_update_slice | solution.py:524
  (29 shorter events, 0.4 us)
Async XLA Ops:
  0.0 9.3 %collective-permute-start.1 = (f32[8192,128]{1,0:T(8,128)}, f32[8192,128]{1,0:T(8,128)}, u32[]{:S(2)}, u32[]{:S(2)}) collective-permute-start(f32[8192,128]{1,0:T(8,128)} %refs_13_.3), channel_id=1, source_target_pairs={{0,1},{1,0},{2,3},{3,2},{4,5},{5,4},{6,7},{7,6},{8,9},{9,8},{10,11... | collective-permute-start | bytes 12582920 | tf_op jit(solution)/shard_map/ppermute | solution.py:377
  1.3 7.9 %collective-permute-start = (f32[32,4096]{1,0:T(8,128)S(1)}, f32[32,4096]{1,0:T(8,128)}, u32[]{:S(2)}, u32[]{:S(2)}) collective-permute-start(f32[32,4096]{1,0:T(8,128)S(1)} %pad_maximum_fusion.6), channel_id=1, source_target_pairs={{0,1},{1,0},{2,3},{3,2},{4,5},{5,4},{6,7},{7,6},{8,9},{9,8},{10,11... | collective-permute-start | bytes 1572872 | tf_op jit(solution)/shard_map/ppermute | solution.py:377
  1.9 69.8 %copy-start.3 = (f32[32,4096]{1,0:T(8,128)}, f32[32,4096]{1,0:T(8,128)S(1)}, u32[]{:S(2)}) copy-start(f32[32,4096]{1,0:T(8,128)S(1)} %pad_maximum_fusion.5.refs_0_) | copy-start | bytes 1572868
  1.9 16.9 %collective-permute-start.2 = (f32[32,4096]{1,0:T(8,128)S(1)}, f32[32,4096]{1,0:T(8,128)S(1)}, u32[]{:S(2)}, u32[]{:S(2)}) collective-permute-start(f32[32,4096]{1,0:T(8,128)S(1)} %pad_maximum_fusion.5.refs_0_), channel_id=1, source_target_pairs={{0,2},{1,3},{2,4},{3,5},{4,6},{5,7},{6,0},{7,1},{8,10},{9,11},{10,... | collective-permute-start | bytes 1572872 | tf_op jit(solution)/shard_map/ppermute | solution.py:377
  4.0 17.0 %collective-permute-start.6 = (f32[32,4096]{1,0:T(8,128)S(1)}, f32[32,4096]{1,0:T(8,128)S(1)}, u32[]{:S(2)}, u32[]{:S(2)}) collective-permute-start(f32[32,4096]{1,0:T(8,128)S(1)} %pad_maximum_fusion.5.refs_0_), channel_id=1, source_target_pairs={{0,8},{1,9},{2,10},{3,11},{4,12},{5,13},{6,14},{7,15},{8,0},{9,1},... | collective-permute-start | bytes 1572872 | tf_op jit(solution)/shard_map/ppermute | solution.py:377
  7.0 14.1 %collective-permute-start.4 = (f32[32,4096]{1,0:T(8,128)S(1)}, f32[32,4096]{1,0:T(8,128)S(1)}, u32[]{:S(2)}, u32[]{:S(2)}) collective-permute-start(f32[32,4096]{1,0:T(8,128)S(1)} %pad_maximum_fusion.5.refs_0_), channel_id=1, source_target_pairs={{0,6},{1,7},{2,0},{3,1},{4,2},{5,3},{6,4},{7,5},{8,14},{9,15},{10,... | collective-permute-start | bytes 1572872 | tf_op jit(solution)/shard_map/ppermute | solution.py:377
  9.3 21.1 %collective-permute-start.7 = (f32[32,4096]{1,0:T(8,128)}, f32[32,4096]{1,0:T(8,128)S(1)}, u32[]{:S(2)}, u32[]{:S(2)}) collective-permute-start(f32[32,4096]{1,0:T(8,128)} %collective-permute-done.refs_1_), channel_id=1, source_target_pairs={{0,8},{1,9},{2,10},{3,11},{4,12},{5,13},{6,14},{7,15},{8,0},{9,1},... | collective-permute-start | bytes 1572872 | tf_op jit(solution)/shard_map/ppermute | solution.py:377
  11.2 19.2 %collective-permute-start.3 = (f32[32,4096]{1,0:T(8,128)}, f32[32,4096]{1,0:T(8,128)S(1)}, u32[]{:S(2)}, u32[]{:S(2)}) collective-permute-start(f32[32,4096]{1,0:T(8,128)} %collective-permute-done.refs_1_), channel_id=1, source_target_pairs={{0,2},{1,3},{2,4},{3,5},{4,6},{5,7},{6,0},{7,1},{8,10},{9,11},{10,... | collective-permute-start | bytes 1572872 | tf_op jit(solution)/shard_map/ppermute | solution.py:377
  18.9 52.9 %copy-start.4 = (f32[32,4096]{1,0:T(8,128)}, f32[32,4096]{1,0:T(8,128)S(1)}, u32[]{:S(2)}) copy-start(f32[32,4096]{1,0:T(8,128)S(1)} %collective-permute-done.2.refs_2_) | copy-start | bytes 1572868
  18.9 12.9 %collective-permute-start.5 = (f32[32,4096]{1,0:T(8,128)}, f32[32,4096]{1,0:T(8,128)S(1)}, u32[]{:S(2)}, u32[]{:S(2)}) collective-permute-start(f32[32,4096]{1,0:T(8,128)} %collective-permute-done.refs_1_), channel_id=1, source_target_pairs={{0,6},{1,7},{2,0},{3,1},{4,2},{5,3},{6,4},{7,5},{8,14},{9,15},{10,... | collective-permute-start | bytes 1572872 | tf_op jit(solution)/shard_map/ppermute | solution.py:377
  21.0 17.6 %copy-start = (f32[8192,128]{1,0:T(8,128)S(1)}, f32[8192,128]{1,0:T(8,128)}, u32[]{:S(2)}) copy-start(f32[8192,128]{1,0:T(8,128)} %refs_13_.3) | copy-start | bytes 12582916
  21.0 11.2 %copy-start.7 = (f32[32,4096]{1,0:T(8,128)}, f32[32,4096]{1,0:T(8,128)S(1)}, u32[]{:S(2)}) copy-start(f32[32,4096]{1,0:T(8,128)S(1)} %collective-permute-done.6.refs_6_) | copy-start | bytes 1572868
  21.1 12.8 %copy-start.9 = (f32[32,4096]{1,0:T(8,128)}, f32[32,4096]{1,0:T(8,128)S(1)}, u32[]{:S(2)}) copy-start(f32[32,4096]{1,0:T(8,128)S(1)} %collective-permute-done.4.refs_4_) | copy-start | bytes 1572868
  30.3 3.7 %copy-start.11 = (f32[32,4096]{1,0:T(8,128)}, f32[32,4096]{1,0:T(8,128)S(1)}, u32[]{:S(2)}) copy-start(f32[32,4096]{1,0:T(8,128)S(1)} %collective-permute-done.7.refs_7_) | copy-start | bytes 1572868
  30.4 1.8 %copy-start.5 = (f32[32,4096]{1,0:T(8,128)}, f32[32,4096]{1,0:T(8,128)S(1)}, u32[]{:S(2)}) copy-start(f32[32,4096]{1,0:T(8,128)S(1)} %collective-permute-done.3.refs_3_) | copy-start | bytes 1572868
  31.8 40.0 %copy-start.13 = (f32[32,4096]{1,0:T(8,128)}, f32[32,4096]{1,0:T(8,128)S(1)}, u32[]{:S(2)}) copy-start(f32[32,4096]{1,0:T(8,128)S(1)} %collective-permute-done.5.refs_5_) | copy-start | bytes 1572868
  32.2 25.1 %collective-permute-start.8 = (f32[128,2048]{1,0:T(8,128)S(1)}, f32[128,2048]{1,0:T(8,128)S(1)}, u32[]{:S(2)}, u32[]{:S(2)}) collective-permute-start(f32[128,2048]{1,0:T(8,128)S(1)} %get-tuple-element.31), channel_id=1, source_target_pairs={{0,2},{1,3},{2,4},{3,5},{4,6},{5,7},{6,0},{7,1},{8,10},{9,11},{10,... | collective-permute-start | bytes 3145736 | tf_op jit(solution)/shard_map/ppermute | solution.py:377
  34.0 23.3 %collective-permute-start.9 = (f32[128,2048]{1,0:T(8,128)S(1)}, f32[128,2048]{1,0:T(8,128)S(1)}, u32[]{:S(2)}, u32[]{:S(2)}) collective-permute-start(f32[128,2048]{1,0:T(8,128)S(1)} %get-tuple-element.30), channel_id=1, source_target_pairs={{0,6},{1,7},{2,0},{3,1},{4,2},{5,3},{6,4},{7,5},{8,14},{9,15},{10,... | collective-permute-start | bytes 3145736 | tf_op jit(solution)/shard_map/ppermute | solution.py:377
  35.9 26.0 %collective-permute-start.10 = (f32[128,2048]{1,0:T(8,128)S(1)}, f32[128,2048]{1,0:T(8,128)S(1)}, u32[]{:S(2)}, u32[]{:S(2)}) collective-permute-start(f32[128,2048]{1,0:T(8,128)S(1)} %get-tuple-element.29), channel_id=1, source_target_pairs={{0,8},{1,9},{2,10},{3,11},{4,12},{5,13},{6,14},{7,15},{8,0},{9,1},... | collective-permute-start | bytes 3145736 | tf_op jit(solution)/shard_map/ppermute | solution.py:377
  38.5 1.0 copy-start.6
  39.6 1.0 copy-start.8
  40.6 1.0 copy-start.10
  41.7 1.0 copy-start.12
  57.3 14.5 %copy-start.1 = (f32[128,2048]{1,0:T(8,128)}, f32[128,2048]{1,0:T(8,128)S(1)}, u32[]{:S(2)}) copy-start(f32[128,2048]{1,0:T(8,128)S(1)} %collective-permute-done.8.refs_8_) | copy-start | bytes 3145732
  57.3 14.4 %copy-start.2 = (f32[128,2048]{1,0:T(8,128)}, f32[128,2048]{1,0:T(8,128)S(1)}, u32[]{:S(2)}) copy-start(f32[128,2048]{1,0:T(8,128)S(1)} %collective-permute-done.9.refs_9_) | copy-start | bytes 3145732
  57.3 12.8 %collective-permute-start.11 = (f32[64,2048]{1,0:T(8,128)S(1)}, f32[64,2048]{1,0:T(8,128)S(1)}, u32[]{:S(2)}, u32[]{:S(2)}) collective-permute-start(f32[64,2048]{1,0:T(8,128)S(1)} %slice.42), channel_id=1, source_target_pairs={{0,2},{1,3},{2,4},{3,5},{4,6},{5,7},{6,0},{7,1},{8,10},{9,11},{10,... | collective-permute-start | bytes 1572872 | tf_op jit(solution)/shard_map/ppermute | solution.py:377
  59.1 12.6 %collective-permute-start.12 = (f32[64,2048]{1,0:T(8,128)S(1)}, f32[64,2048]{1,0:T(8,128)S(1)}, u32[]{:S(2)}, u32[]{:S(2)}) collective-permute-start(f32[64,2048]{1,0:T(8,128)S(1)} %slice.43), channel_id=1, source_target_pairs={{0,8},{1,9},{2,10},{3,11},{4,12},{5,13},{6,14},{7,15},{8,0},{9,1},... | collective-permute-start | bytes 1572872 | tf_op jit(solution)/shard_map/ppermute | solution.py:377
  61.9 9.9 %copy-start.14 = (f32[128,2048]{1,0:T(8,128)}, f32[128,2048]{1,0:T(8,128)S(1)}, u32[]{:S(2)}) copy-start(f32[128,2048]{1,0:T(8,128)S(1)} %collective-permute-done.10.refs_10_) | copy-start | bytes 3145732
  70.2 8.6 %copy-start.15 = (f32[64,2048]{1,0:T(8,128)}, f32[64,2048]{1,0:T(8,128)S(1)}, u32[]{:S(2)}) copy-start(f32[64,2048]{1,0:T(8,128)S(1)} %collective-permute-done.11.refs_11_) | copy-start | bytes 1572868
  71.8 7.1 %copy-start.16 = (f32[64,2048]{1,0:T(8,128)}, f32[64,2048]{1,0:T(8,128)S(1)}, u32[]{:S(2)}) copy-start(f32[64,2048]{1,0:T(8,128)S(1)} %collective-permute-done.12.refs_12_) | copy-start | bytes 1572868
  78.8 2.1 %collective-permute-start.13 = (f32[1152,128]{1,0:T(8,128)S(1)}, f32[1152,128]{1,0:T(8,128)S(1)}, u32[]{:S(2)}, u32[]{:S(2)}) collective-permute-start(f32[1152,128]{1,0:T(8,128)S(1)} %get-tuple-element.26), channel_id=1, source_target_pairs={{0,1},{1,0},{2,3},{3,2},{4,5},{5,4},{6,7},{7,6},{8,9},{9,8},{10,11... | collective-permute-start | bytes 1769480 | tf_op jit(solution)/shard_map/ppermute | solution.py:377
  110.3 2.0 %collective-permute-start.14 = (f32[1152,128]{1,0:T(8,128)S(1)}, f32[1152,128]{1,0:T(8,128)S(1)}, u32[]{:S(2)}, u32[]{:S(2)}) collective-permute-start(f32[1152,128]{1,0:T(8,128)S(1)} %bitcast.19), channel_id=1, source_target_pairs={{0,1},{1,0},{2,3},{3,2},{4,5},{5,4},{6,7},{7,6},{8,9},{9,8},{10,11... | collective-permute-start | bytes 1769480 | tf_op jit(solution)/shard_map/ppermute | solution.py:377
  124.2 4.2 %collective-permute-start.15 = (f32[4096,128]{1,0:T(8,128)S(1)}, f32[4096,128]{1,0:T(8,128)S(1)}, u32[]{:S(2)}, u32[]{:S(2)}) collective-permute-start(f32[4096,128]{1,0:T(8,128)S(1)} %get-tuple-element.28), channel_id=1, source_target_pairs={{0,1},{1,0},{2,3},{3,2},{4,5},{5,4},{6,7},{7,6},{8,9},{9,8},{10,11... | collective-permute-start | bytes 6291464 | tf_op jit(solution)/shard_map/ppermute | solution.py:377
  124.9 3.6 %copy-start.17 = (f32[8192,128]{1,0:T(8,128)}, f32[8192,128]{1,0:T(8,128)S(1)}, u32[]{:S(2)}) copy-start(f32[8192,128]{1,0:T(8,128)S(1)} %constant_dynamic-update-slice_fusion.1) | copy-start | bytes 12582916
